TPU v7x, 32 devices: a whole 2x2x4 slice. The times are simulated.
32 devices in a mesh: ctx: 8 (over z, x), tp: 4 (over y, core).
Axes of the slice: x: 2, y: 2, z: 4, core: 2. Of those that a mesh axis runs over, the one named last changes fastest.
Arguments:
- qkv: bfloat16 [3, 1024, 8192], P(None, 'ctx', 'tp'), may hold values from -6 to 6
- cotangent: bfloat16 [1024, 8192], P('ctx', 'tp'), may hold values from -6 to 6
- doc_ids: int32 [1024], P('ctx'), may hold values from 0 to 3, never falling along the last dimension, each value on 1 to 512 neighbouring positions
- short_filter: float32 [3, 8192, 7], P(None, 'tp'), may hold values from -2 to 2
- long_filter: float32 [512, 128], P('tp'), may hold values from -0.5 to 0.5
Outputs:
- layer_output: bfloat16 [1024, 8192], P('ctx', 'tp')
- qkv_grad: bfloat16 [3, 1024, 8192], P(None, 'ctx', 'tp')
- long_filter_grad: float32 [512, 128], P(('tp', 'ctx'))
- short_filter_grad: float32 [3, 8192, 7], P(None, ('tp', 'ctx'))
Inputs may be any that keep to these rules, and one draw needn't show every extreme that they name: `doc_ids`: document ids never decrease along the tokens; every id in the range is used; a document holds at most 512 tokens and one holds exactly that many.
All inputs are finite; a program needn't handle non-finite values.
Results may differ from a plain program's by a relative error of at most 0.005.
Values may be sent and summed in bfloat16 or wider, within the bound.
No kernel may reach another device: no remote copies, remote signals or barrier semaphores. Data moves between devices by JAX's collectives and lax.ppermute only.
A program may use at most 128 MiB of HBM per device.

v0:
```python
import math

import jax
import jax.numpy as jnp
from jax import lax
from jax.sharding import PartitionSpec as P

PRECISE = lax.Precision.HIGHEST


def passed_along(block, axis, distance):
    devices = range(lax.axis_size(axis))
    route = [(i - distance, i) for i in devices if i - distance in devices]
    return lax.ppermute(block, axis, route)


def for_sending(x):

    def short(part):
        return part.astype(jnp.bfloat16) if part.dtype == jnp.float32 else part

    return jax.tree.map(short, x)


def causal_short(extended, filters, ids_before, row_count):
    tap_count = filters.shape[2]
    ids_now = ids_before[tap_count - 1 :]
    summed = jnp.zeros((3, row_count, extended.shape[2]), jnp.float32)
    for tap_index in range(tap_count):
        first_row = tap_count - 1 - tap_index
        same_doc = (ids_before[first_row : first_row + row_count] == ids_now).astype(jnp.float32)
        summed = (
            summed
            + filters[:, None, :, tap_index]
            * extended[:, first_row : first_row + row_count, :]
            * same_doc[None, :, None]
        )
    return summed


def anti_short(extended, filters, ids_after, row_count):
    tap_count = filters.shape[2]
    ids_now = ids_after[:row_count]
    summed = jnp.zeros((3, row_count, extended.shape[2]), jnp.float32)
    for tap_index in range(tap_count):
        same_doc = (ids_after[tap_index : tap_index + row_count] == ids_now).astype(jnp.float32)
        summed = (
            summed
            + filters[:, None, :, tap_index]
            * extended[:, tap_index : tap_index + row_count, :]
            * same_doc[None, :, None]
        )
    return summed


def short_grad(grad_feats, extended, ids_before, tap_count, row_count):
    ids_now = ids_before[tap_count - 1 :]
    columns = []
    for tap_index in range(tap_count):
        first_row = tap_count - 1 - tap_index
        same_doc = (ids_before[first_row : first_row + row_count] == ids_now).astype(jnp.float32)
        columns.append(
            jnp.sum(
                grad_feats
                * extended[:, first_row : first_row + row_count, :]
                * same_doc[None, :, None],
                axis=1,
            )
        )
    return jnp.stack(columns, -1)


def long_apply(filters, extended, ids_ext, row_count, causal):
    group_count, tap_count = filters.shape
    if causal:
        ids_now = ids_ext[tap_count - 1 :]
    else:
        ids_now = ids_ext[:row_count]
    summed = jnp.zeros((row_count,) + extended.shape[1:], jnp.float32)
    for tap_index in range(tap_count):
        first_row = tap_count - 1 - tap_index if causal else tap_index
        same_doc = (ids_ext[first_row : first_row + row_count] == ids_now).astype(jnp.float32)
        summed = (
            summed
            + filters[None, :, tap_index, None]
            * extended[first_row : first_row + row_count]
            * same_doc[:, None, None]
        )
    return summed


def long_grad(tap_count, grad_rows, extended, ids_before, row_count):
    group_count = grad_rows.shape[1]
    block_rows = min(row_count, 256)
    block_groups = math.gcd(group_count, 32)
    window = block_rows + tap_count - 1

    def one_block(block_index):
        same_doc = (ids_before[tap_count - 1 :][:, None] == ids_before[None, :]).astype(jnp.float32)

        def one_group(group_index):
            part_rows = lax.dynamic_slice_in_dim(
                extended, group_index * block_groups, block_groups, 1
            )
            part_grads = lax.dynamic_slice_in_dim(
                grad_rows, group_index * block_groups, block_groups, 1
            )
            products = (
                jnp.einsum("rgc,wgc->grw", part_grads, part_rows, precision=PRECISE)
                * same_doc[None]
            )
            flattened = products.reshape(block_groups, block_rows * window)
            flattened = jnp.concatenate(
                [flattened, jnp.zeros((block_groups, block_rows), jnp.float32)], 1
            )
            diagonals = flattened.reshape(block_groups, block_rows, window + 1)[:, :, :tap_count]
            return jnp.sum(diagonals, 1)[:, ::-1]

        results = lax.map(one_group, jnp.arange(group_count // block_groups, dtype=jnp.int32))
        return results.reshape(group_count, tap_count)

    return jnp.sum(lax.map(one_block, jnp.arange(row_count // block_rows, dtype=jnp.int32)), 0)


def hyena_mix(qkv, cotangent, doc_ids, short_filter, long_filter):
    row_count = qkv.shape[1]
    chan_count = qkv.shape[2]
    short_count = short_filter.shape[2]
    group_count, long_count = long_filter.shape
    group_size = chan_count // group_count
    raw_tail, ids_tail = passed_along(
        (qkv[:, row_count - (short_count - 1) :, :], doc_ids[row_count - (long_count - 1) :]),
        "ctx",
        1,
    )
    raw_before = jnp.concatenate([raw_tail, qkv], 1)
    ids_before = jnp.concatenate([ids_tail, doc_ids], 0)
    ids_short = ids_before[long_count - short_count :]
    features = causal_short(raw_before, short_filter, ids_short, row_count)
    kv_product = features[1] * features[2]
    mix_tail = passed_along(kv_product[row_count - (long_count - 1) :], "ctx", 1)
    mix_before = jnp.concatenate([mix_tail, kv_product], 0).reshape(-1, group_count, group_size)
    long_conv = long_apply(long_filter, mix_before, ids_before, row_count, True).reshape(
        row_count, chan_count
    )
    output = (features[0] * long_conv).astype(jnp.bfloat16)
    grad_q = cotangent * long_conv
    grad_conv = cotangent * features[0]
    grad_head, ids_head = (
        passed_along(grad_conv[: long_count - 1].astype(jnp.bfloat16), "ctx", -1).astype(
            jnp.float32
        ),
        passed_along(doc_ids[: long_count - 1], "ctx", -1),
    )
    grad_after = jnp.concatenate([grad_conv, grad_head], 0).reshape(-1, group_count, group_size)
    ids_after = jnp.concatenate([doc_ids, ids_head], 0)
    grad_mix = long_apply(long_filter, grad_after, ids_after, row_count, False).reshape(
        row_count, chan_count
    )
    grad_feats = jnp.stack([grad_q, grad_mix * features[2], grad_mix * features[1]], 0)
    feat_head = passed_along(for_sending(grad_feats[:, : short_count - 1, :]), "ctx", -1)
    feats_after = jnp.concatenate([grad_feats, feat_head], 1)
    grad_raw = anti_short(
        feats_after, short_filter, ids_after[: row_count + short_count - 1], row_count
    ).astype(jnp.bfloat16)
    long_part = long_grad(
        long_count,
        grad_conv.reshape(row_count, group_count, group_size),
        mix_before,
        ids_before,
        row_count,
    )
    short_part = short_grad(grad_feats, raw_before, ids_short, short_count, row_count)
    return (output, grad_raw, long_part, short_part)


def shards(qkv, cotangent, doc_ids, short_filter, long_filter):
    row_count = qkv.shape[1]
    devices = lax.axis_size("ctx")
    grad_scale = 1.0 / math.sqrt(row_count * devices)
    output, grad_raw, long_part, short_part = hyena_mix(
        qkv, cotangent, doc_ids, short_filter, long_filter
    )
    long_part, short_part = (
        lax.psum_scatter(long_part, "ctx", scatter_dimension=0, tiled=True),
        lax.psum_scatter(short_part, "ctx", scatter_dimension=1, tiled=True),
    )
    return (output, grad_raw, long_part * grad_scale, short_part * grad_scale)


def solution(mesh):
    in_specs = (P(None, "ctx", "tp"), P("ctx", "tp"), P("ctx"), P(None, "tp", None), P("tp", None))
    out_specs = (
        P("ctx", "tp"),
        P(None, "ctx", "tp"),
        P(("tp", "ctx"), None),
        P(None, ("tp", "ctx"), None),
    )
    return jax.shard_map(shards, mesh=mesh, in_specs=in_specs, out_specs=out_specs, check_vma=False)
```

profile of v0, /device:TPU:0, one launch (start us, length us, event | category | flops | bytes accessed | tf_op | source)
XLA Modules:
  0.0 709.0 jit_solution(2259839419204158659)
XLA Ops:
  8.5 5.4 collective-permute-start.1
  15.1 1.5 slice.2441
  16.7 4.5 collective-permute-start
  21.2 2.3 slice_reduce_fusion.123
  23.5 2.8 slice_reduce_fusion.124
  28.1 1.3 slice_reduce_fusion.127
  29.4 1.3 slice_reduce_fusion.128
  30.8 1.3 slice_reduce_fusion.67
  32.1 1.4 copy.18
  148.1 10.8 %fusion.10 = f32[3,128,2048]{1,2,0:T(8,128)S(1)} fusion(bf16[3,128,2048]{1,2,0:T(8,128)(2,1)S(1)} %copy.18, f32[128]{0:T(128)S(1)} %get-tuple-element.497, f32[3,2048]{1,0:T(4,128)S(1)} %get-tuple-element.502, f32[128]{0:T(128)S(1)} %get-tuple-element.498, f32[3,2048]{1,0:T(4,128)S(1)} %get-tuple-element.503, f32[128]{0:T(128)S(1)} %get-tuple-element.499, ...), kind=kLoop, calls=%fused_computation.545 | loop fusion | flops 34603008 | bytes 4967424 | tf_op jit(solution)/shard_map/add | solution.py:33
  159.6 1.4 collective-permute-start.3
  162.5 12.1 %collective-permute-done.3 = bf16[127,2048]{0,1:T(8,128)(2,1)S(1)} collective-permute-done((bf16[127,2048]{0,1:T(8,128)(2,1)S(1)}, bf16[127,2048]{0,1:T(8,128)(2,1)S(1)}, u32[]{:S(2)}, u32[]{:S(2)}) %collective-permute-start.3) | collective-permute-done | bytes 520224 | tf_op jit(solution)/shard_map/ppermute | solution.py:14
  174.8 70.8 %fusion.236 = f32[128,2048]{0,1:T(8,128)S(1)} fusion(f32[128,2048]{0,1:T(8,128)S(1)} %convert_multiply_fusion.14, f32[127,2048]{0,1:T(8,128)S(1)} %convert_element_type.973, f32[128]{0:T(128)} %get-tuple-element.320, f32[128]{0:T(128)} %get-tuple-element.321, f32[128]{0:T(128)} %get-tuple-element.323, f32[128]{0:T(128)} %get-tuple-element.324, ...), kind=kLoop, calls=%fused_computation.782 | loop fusion | flops 63176704 | bytes 3667968 | tf_op jit(solution)/shard_map/add | solution.py:84
  245.9 73.1 %multiply_bitcast_fusion.1 = (f32[1,128,2048]{1,2,0:T(8,128)S(1)}, f32[128,2048]{0,1:T(8,128)S(1)}) fusion(f32[3,128,2048]{1,2,0:T(8,128)S(1)} %fusion.10, f32[127,2048]{0,1:T(8,128)S(1)} %convert_element_type.973, f32[128,2048]{0,1:T(8,128)S(1)} %convert_multiply_fusion.14, f32[128,2048]{0,1:T(8,128)S(1)} %fusion.236, f32[128]{0:T(128)} %get-tuple-element.251, ...), kind=kLoop, calls=%fused_computation.1616 | loop fusion | flops 70516736 | bytes 6866432 | tf_op jit(solution)/shard_map/stack | solution.py:160
  320.0 4.6 collective-permute-start.2
  327.0 18.2 %collective-permute-done.2 = f32[127,2048]{0,1:T(8,128)S(1)} collective-permute-done((f32[127,2048]{0,1:T(8,128)S(1)}, f32[127,2048]{0,1:T(8,128)S(1)}, u32[]{:S(2)}, u32[]{:S(2)}) %collective-permute-start.2) | collective-permute-done | bytes 1040416 | tf_op jit(solution)/shard_map/ppermute | solution.py:14
  345.5 61.9 %fusion.736 = f32[128,2048]{0,1:T(8,128)} fusion(f32[127,2048]{0,1:T(8,128)S(1)} %collective-permute-done.2, f32[128,2048]{0,1:T(8,128)S(1)} %get-tuple-element.242, f32[128]{0:T(128)} %get-tuple-element.446, f32[2048]{0:T(1024)S(1)} %copy-done.59, f32[128]{0:T(128)} %get-tuple-element.447, f32[2048]{0:T(1024)S(1)} %copy-done.61, ...), kind=kLoop, calls=%fused_computation.1282 | loop fusion | flops 63176704 | bytes 3667968 | tf_op jit(solution)/shard_map/add | solution.py:84
  407.5 73.9 %fusion.48 = (f32[1,128,2048]{1,2,0:T(8,128)S(1)}, f32[128,2048]{0,1:T(8,128)S(1)}) fusion(bf16[128,2048]{0,1:T(8,128)(2,1)} %copy.21, f32[128,2048]{0,1:T(8,128)} %fusion.736, f32[128,2048]{0,1:T(8,128)S(1)} %get-tuple-element.242, f32[127,2048]{0,1:T(8,128)S(1)} %collective-permute-done.2, f32[128]{0:T(128)} %get-tuple-element.377, f32[2048]{0:T(1024)} %mul.6347, ...), kind=kLoop, calls=%fused_computation.594 | loop fusion | flops 70778880 | bytes 6342144 | tf_op jit(solution)/shard_map/stack | solution.py:160
  481.5 6.1 fusion.29
  487.6 6.9 fusion.26
  494.5 1.5 pad_maximum_fusion.2
  496.0 2.1 multiply_convert_fusion
  498.1 2.0 pad_maximum_fusion
  500.1 71.1 %while.18 = (s32[]{:T(128)}, f32[4,32,128]{2,1,0:T(8,128)}, s32[4]{0:T(128)S(1)}, f32[128,128,16]{0,2,1:T(8,128)}, f32[255,128,16]{0,2,1:T(8,128)}, /*index=5*/s...) while((s32[]{:T(128)}, f32[4,32,128]{2,1,0:T(8,128)}, ...), condition=%wide.region_2.3_spmd.clone, body=%wide.region_0.2_spmd.clone.sunk | while | flops 202170112 | bytes 32523964 | solution.py:119
  501.7 6.6 convolution_multiply_fusion.2
  508.3 5.2 reshape.1081
  513.5 2.5 concatenate.29
  519.4 6.6 convolution_multiply_fusion.2
  526.0 5.2 reshape.1081
  531.2 2.5 concatenate.29
  533.7 1.3 copy.46
  537.2 6.6 convolution_multiply_fusion.2
  543.7 5.2 reshape.1081
  548.9 2.5 concatenate.29
  554.9 6.6 convolution_multiply_fusion.2
  561.4 5.2 reshape.1081
  566.7 2.5 concatenate.29
  572.1 2.4 copy.22
  580.4 2.0 copy.24
  582.4 4.7 copy.27
  587.1 6.4 reshape.950
  593.5 2.8 copy.23
  596.4 2.2 pad_maximum_fusion.1
  598.7 12.7 %fusion.32 = bf16[3,128,2048]{1,2,0:T(8,128)(2,1)} fusion(f32[3,134,2048]{1,2,0:T(8,128)S(1)} %pad_maximum_fusion.1, f32[128]{0:T(128)S(1)} %copy-done.103, f32[128]{0:T(128)S(1)} %copy-done.104, f32[128]{0:T(128)S(1)} %copy-done.105, f32[128]{0:T(128)S(1)} %copy-done.106, f32[128]{0:T(128)S(1)} %copy-done.107, f32[128]{0:T(128)S(1)} %copy-done.109, ...), kind=kLoop, calls=%fused_computation.568 | loop fusion | flops 17301504 | bytes 23768064 | tf_op jit(solution)/shard_map/convert_element_type | solution.py:165
  611.3 2.6 copy.25
  613.9 20.0 %reduce-scatter.5.cloned.1.call-done = f32[16,128]{1,0:T(8,128)} async-done(((f32[128,128]{1,0:T(8,128)}), f32[16,128]{1,0:T(8,128)}) %reduce-scatter.5.cloned.1.call-update) | async-done | bytes 8208 | tf_op jit(solution)/shard_map/reduce_scatter | solution.py:185
  634.0 1.3 broadcast_multiply_fusion.1
  635.3 64.5 %reduce-scatter.7.cloned.1.call-done = f32[256,21]{1,0:T(8,128)} async-done(((f32[2048,21]{1,0:T(8,128)}), f32[256,21]{1,0:T(8,128)}) %reduce-scatter.7.cloned.1.call-update) | async-done | bytes 21520
  (639 shorter events, 142.2 us)
Async XLA Ops:
  7.2 626.8 %reduce-scatter.5.cloned.1.call-start = ((), (), s32[]{:S(2)}) async-start(), calls=%async_computation.2 | async-start | bytes 73728 | tf_op jit(solution)/shard_map/reduce_scatter | solution.py:185
  8.5 137.2 %collective-permute-start.1 = (s32[127]{0:T(128)}, s32[127]{0:T(128)}, u32[]{:S(2)}, u32[]{:S(2)}) collective-permute-start(s32[127]{0:T(128)} %slice.2443), channel_id=1, source_target_pairs={{0,4},{4,8},{8,12},{12,16},{16,20},{20,24},{24,28},{1,5},{5,9},{9,... | collective-permute-start | bytes 1532 | tf_op jit(solution)/shard_map/ppermute | solution.py:14
  13.8 126.8 %collective-permute-start.4 = (s32[127]{0:T(128)}, s32[127]{0:T(128)}, u32[]{:S(2)}, u32[]{:S(2)}) collective-permute-start(s32[127]{0:T(128)} %bitcast.83), channel_id=1, source_target_pairs={{4,0},{8,4},{12,8},{16,12},{20,16},{24,20},{28,24},{5,1},{9,5},{13... | collective-permute-start | bytes 1532 | tf_op jit(solution)/shard_map/ppermute | solution.py:14
  16.7 130.5 %collective-permute-start = (bf16[3,6,2048]{2,1,0:T(8,128)(2,1)}, bf16[3,6,2048]{2,1,0:T(8,128)(2,1)S(1)}, u32[]{:S(2)}, u32[]{:S(2)}) collective-permute-start(bf16[3,6,2048]{2,1,0:T(8,128)(2,1)} %slice.2441), channel_id=1, source_target_pairs={{0,4},{4,8},{8,12},{12,16},{16,20},{20,24},{24,28},{1,5},{5,9},{9,... | collective-permute-start | bytes 221192 | tf_op jit(solution)/shard_map/ppermute | solution.py:14
  33.5 114.5 %copy-start.1 = (bf16[3,128,2048]{1,2,0:T(8,128)(2,1)}, bf16[3,128,2048]{1,2,0:T(8,128)(2,1)S(1)}, u32[]{:S(2)}) copy-start(bf16[3,128,2048]{1,2,0:T(8,128)(2,1)S(1)} %copy.18) | copy-start | bytes 4718596
  33.9 42.1 %copy-start.127 = (f32[128]{0:T(128)S(1)}, f32[128]{0:T(128)}, u32[]{:S(2)}) copy-start(f32[128]{0:T(128)} %get-tuple-element.135) | copy-start | bytes 1540
  159.0 160.1 %copy-start.6 = (f32[3,128,2048]{1,2,0:T(8,128)}, f32[3,128,2048]{1,2,0:T(8,128)S(1)}, u32[]{:S(2)}) copy-start(f32[3,128,2048]{1,2,0:T(8,128)S(1)} %fusion.10) | copy-start | bytes 9437188
  159.2 160.8 %copy-start.5 = (f32[128,2048]{0,1:T(8,128)}, f32[128,2048]{0,1:T(8,128)S(1)}, u32[]{:S(2)}) copy-start(f32[128,2048]{0,1:T(8,128)S(1)} %convert_multiply_fusion.14) | copy-start | bytes 3145732
  159.2 86.4 %copy-start.16 = (f32[2048]{0:T(1024)S(1)}, f32[2048]{0:T(1024)}, u32[]{:S(2)}) copy-start(f32[2048]{0:T(1024)} %mul.6312) | copy-start | bytes 24580
  159.2 86.4 %copy-start.17 = (f32[2048]{0:T(1024)S(1)}, f32[2048]{0:T(1024)}, u32[]{:S(2)}) copy-start(f32[2048]{0:T(1024)} %mul.6305) | copy-start | bytes 24580
  159.2 86.4 %copy-start.18 = (f32[2048]{0:T(1024)S(1)}, f32[2048]{0:T(1024)}, u32[]{:S(2)}) copy-start(f32[2048]{0:T(1024)} %mul.6298) | copy-start | bytes 24580
  159.2 86.4 %copy-start.19 = (f32[2048]{0:T(1024)S(1)}, f32[2048]{0:T(1024)}, u32[]{:S(2)}) copy-start(f32[2048]{0:T(1024)} %mul.6291) | copy-start | bytes 24580
  159.2 86.4 %copy-start.20 = (f32[2048]{0:T(1024)S(1)}, f32[2048]{0:T(1024)}, u32[]{:S(2)}) copy-start(f32[2048]{0:T(1024)} %mul.6284) | copy-start | bytes 24580
  159.2 86.4 %copy-start.21 = (f32[2048]{0:T(1024)S(1)}, f32[2048]{0:T(1024)}, u32[]{:S(2)}) copy-start(f32[2048]{0:T(1024)} %mul.6277) | copy-start | bytes 24580
  159.3 86.4 %copy-start.22 = (f32[2048]{0:T(1024)S(1)}, f32[2048]{0:T(1024)}, u32[]{:S(2)}) copy-start(f32[2048]{0:T(1024)} %mul.6270) | copy-start | bytes 24580
  159.3 86.4 %copy-start.23 = (f32[2048]{0:T(1024)S(1)}, f32[2048]{0:T(1024)}, u32[]{:S(2)}) copy-start(f32[2048]{0:T(1024)} %mul.6263) | copy-start | bytes 24580
  159.3 86.4 %copy-start.24 = (f32[2048]{0:T(1024)S(1)}, f32[2048]{0:T(1024)}, u32[]{:S(2)}) copy-start(f32[2048]{0:T(1024)} %mul.6256) | copy-start | bytes 24580
  159.3 86.4 %copy-start.25 = (f32[2048]{0:T(1024)S(1)}, f32[2048]{0:T(1024)}, u32[]{:S(2)}) copy-start(f32[2048]{0:T(1024)} %mul.6249) | copy-start | bytes 24580
  159.3 86.4 %copy-start.26 = (f32[2048]{0:T(1024)S(1)}, f32[2048]{0:T(1024)}, u32[]{:S(2)}) copy-start(f32[2048]{0:T(1024)} %mul.6242) | copy-start | bytes 24580
  159.3 86.4 %copy-start.27 = (f32[2048]{0:T(1024)S(1)}, f32[2048]{0:T(1024)}, u32[]{:S(2)}) copy-start(f32[2048]{0:T(1024)} %mul.6235) | copy-start | bytes 24580
  159.3 86.4 %copy-start.28 = (f32[2048]{0:T(1024)S(1)}, f32[2048]{0:T(1024)}, u32[]{:S(2)}) copy-start(f32[2048]{0:T(1024)} %mul.6228) | copy-start | bytes 24580
  159.3 86.4 %copy-start.29 = (f32[2048]{0:T(1024)S(1)}, f32[2048]{0:T(1024)}, u32[]{:S(2)}) copy-start(f32[2048]{0:T(1024)} %mul.6221) | copy-start | bytes 24580
  159.3 86.4 %copy-start.30 = (f32[2048]{0:T(1024)S(1)}, f32[2048]{0:T(1024)}, u32[]{:S(2)}) copy-start(f32[2048]{0:T(1024)} %mul.6214) | copy-start | bytes 24580
  159.3 86.4 %copy-start.31 = (f32[2048]{0:T(1024)S(1)}, f32[2048]{0:T(1024)}, u32[]{:S(2)}) copy-start(f32[2048]{0:T(1024)} %mul.6207) | copy-start | bytes 24580
  159.4 86.4 %copy-start.32 = (f32[2048]{0:T(1024)S(1)}, f32[2048]{0:T(1024)}, u32[]{:S(2)}) copy-start(f32[2048]{0:T(1024)} %mul.6200) | copy-start | bytes 24580
  159.4 86.4 %copy-start.33 = (f32[2048]{0:T(1024)S(1)}, f32[2048]{0:T(1024)}, u32[]{:S(2)}) copy-start(f32[2048]{0:T(1024)} %mul.6193) | copy-start | bytes 24580
  159.4 86.4 %copy-start.34 = (f32[2048]{0:T(1024)S(1)}, f32[2048]{0:T(1024)}, u32[]{:S(2)}) copy-start(f32[2048]{0:T(1024)} %mul.6186) | copy-start | bytes 24580
  159.4 86.4 %copy-start.35 = (f32[2048]{0:T(1024)S(1)}, f32[2048]{0:T(1024)}, u32[]{:S(2)}) copy-start(f32[2048]{0:T(1024)} %mul.6179) | copy-start | bytes 24580
  159.4 86.4 %copy-start.36 = (f32[2048]{0:T(1024)S(1)}, f32[2048]{0:T(1024)}, u32[]{:S(2)}) copy-start(f32[2048]{0:T(1024)} %mul.6172) | copy-start | bytes 24580
  159.4 86.4 %copy-start.37 = (f32[2048]{0:T(1024)S(1)}, f32[2048]{0:T(1024)}, u32[]{:S(2)}) copy-start(f32[2048]{0:T(1024)} %mul.6165) | copy-start | bytes 24580
  159.4 86.4 %copy-start.38 = (f32[2048]{0:T(1024)S(1)}, f32[2048]{0:T(1024)}, u32[]{:S(2)}) copy-start(f32[2048]{0:T(1024)} %mul.6158) | copy-start | bytes 24580
  159.4 86.4 %copy-start.39 = (f32[2048]{0:T(1024)S(1)}, f32[2048]{0:T(1024)}, u32[]{:S(2)}) copy-start(f32[2048]{0:T(1024)} %mul.6151) | copy-start | bytes 24580
  159.4 86.4 %copy-start.40 = (f32[2048]{0:T(1024)S(1)}, f32[2048]{0:T(1024)}, u32[]{:S(2)}) copy-start(f32[2048]{0:T(1024)} %mul.6144) | copy-start | bytes 24580
  159.4 86.4 %copy-start.41 = (f32[2048]{0:T(1024)S(1)}, f32[2048]{0:T(1024)}, u32[]{:S(2)}) copy-start(f32[2048]{0:T(1024)} %mul.6137) | copy-start | bytes 24580
  159.5 86.4 %copy-start.42 = (f32[2048]{0:T(1024)S(1)}, f32[2048]{0:T(1024)}, u32[]{:S(2)}) copy-start(f32[2048]{0:T(1024)} %mul.6130) | copy-start | bytes 24580
  159.5 86.4 %copy-start.43 = (f32[2048]{0:T(1024)S(1)}, f32[2048]{0:T(1024)}, u32[]{:S(2)}) copy-start(f32[2048]{0:T(1024)} %mul.6123) | copy-start | bytes 24580
  159.5 86.4 %copy-start.44 = (f32[2048]{0:T(1024)S(1)}, f32[2048]{0:T(1024)}, u32[]{:S(2)}) copy-start(f32[2048]{0:T(1024)} %mul.6116) | copy-start | bytes 24580
  159.5 86.4 %copy-start.45 = (f32[2048]{0:T(1024)S(1)}, f32[2048]{0:T(1024)}, u32[]{:S(2)}) copy-start(f32[2048]{0:T(1024)} %mul.6109) | copy-start | bytes 24580
  159.6 15.0 %collective-permute-start.3 = (bf16[127,2048]{0,1:T(8,128)(2,1)S(1)}, bf16[127,2048]{0,1:T(8,128)(2,1)S(1)}, u32[]{:S(2)}, u32[]{:S(2)}) collective-permute-start(bf16[127,2048]{0,1:T(8,128)(2,1)S(1)} %slice.8638), channel_id=1, source_target_pairs={{4,0},{8,4},{12,8},{16,12},{20,16},{24,20},{28,24},{5,1},{9,5},{13... | collective-permute-start | bytes 1560584 | tf_op jit(solution)/shard_map/ppermute | solution.py:14
  161.8 83.8 %copy-start.108 = (f32[128]{0:T(128)}, f32[128]{0:T(128)S(1)}, u32[]{:S(2)}) copy-start(f32[128]{0:T(128)S(1)} %get-tuple-element.268) | copy-start | bytes 1540
  161.8 84.1 %copy-start.150 = (f32[128]{0:T(128)S(1)}, f32[128]{0:T(128)}, u32[]{:S(2)}) copy-start(f32[128]{0:T(128)} %get-tuple-element.269) | copy-start | bytes 1540
  320.0 25.2 %collective-permute-start.2 = (f32[127,2048]{0,1:T(8,128)S(1)}, f32[127,2048]{0,1:T(8,128)S(1)}, u32[]{:S(2)}, u32[]{:S(2)}) collective-permute-start(f32[127,2048]{0,1:T(8,128)S(1)} %slice.3118), channel_id=1, source_target_pairs={{0,4},{4,8},{8,12},{12,16},{16,20},{20,24},{24,28},{1,5},{5,9},{9,... | collective-permute-start | bytes 3121160 | tf_op jit(solution)/shard_map/ppermute | solution.py:14
  407.5 74.0 %copy-start.2 = (bf16[3,128,2048]{1,2,0:T(8,128)(2,1)S(1)}, bf16[3,128,2048]{1,2,0:T(8,128)(2,1)}, u32[]{:S(2)}) copy-start(bf16[3,128,2048]{1,2,0:T(8,128)(2,1)} %copy-done.1) | copy-start | bytes 4718596
  407.5 74.0 %copy-start.4 = (bf16[3,6,2048]{1,2,0:T(8,128)(2,1)S(1)}, bf16[3,6,2048]{1,2,0:T(8,128)(2,1)}, u32[]{:S(2)}) copy-start(bf16[3,6,2048]{1,2,0:T(8,128)(2,1)} %copy-done.3) | copy-start | bytes 221188
  407.5 74.0 %copy-start.100 = (f32[128]{0:T(128)S(1)}, f32[128]{0:T(128)}, u32[]{:S(2)}) copy-start(f32[128]{0:T(128)} %copy-done.99) | copy-start | bytes 1540
  407.5 74.0 %copy-start.102 = (f32[128]{0:T(128)S(1)}, f32[128]{0:T(128)}, u32[]{:S(2)}) copy-start(f32[128]{0:T(128)} %copy-done.101) | copy-start | bytes 1540
  571.3 128.5 %reduce-scatter.7.cloned.1.call-start = ((), (), s32[]{:S(2)}) async-start(), calls=%async_computation.3 | async-start | bytes 1179648
  574.5 19.0 %collective-permute-start.5 = (bf16[3,6,2048]{2,1,0:T(8,128)(2,1)}, bf16[3,6,2048]{2,1,0:T(8,128)(2,1)}, u32[]{:S(2)}, u32[]{:S(2)}) collective-permute-start(bf16[3,6,2048]{2,1,0:T(8,128)(2,1)} %copy.22), channel_id=1, source_target_pairs={{4,0},{8,4},{12,8},{16,12},{20,16},{24,20},{28,24},{5,1},{9,5},{13... | collective-permute-start | bytes 221192 | tf_op jit(solution)/shard_map/ppermute | solution.py:14
  (111 other events, 2827.2 us)
Sparse Core Ops, SparseCore 0:
  571.4 62.5 reduce-scatter.4
  637.4 62.3 reduce-scatter.6
where the time goes:
time: 715 us; the launch traced here: 709 us
  other arithmetic  336 us (47%)
  local copies, waits for them, and re-layouts  193 us (27%)
  waiting for transfers between devices  115 us (16%)
  matrix products  26.2 us (4%)
  starting transfers between devices  18.6 us (3%)
  between operations  16.7 us (2%)
    another operation x4, other arithmetic, hyena_mix(): jnp.stack([grad_q, grad_mix * features[2], grad_mix * features[1]], 0)  149 us
    add x2, other arithmetic, long_apply(): summed + filters[None, :, tap_index, None] * extended[first_row:first_row...  133 us
    mul x256, local copies, waits for them, and re-layouts, long_apply(): filters[None, :, tap_index, None]  105 us
    unnamed x3, waiting for transfers between devices  64.5 us
    ppermute x6, waiting for transfers between devices, passed_along(): return lax.ppermute(block, axis, route)  30.3 us
    dot_general x4, matrix products, one_group(): jnp.einsum('rgc,wgc->grw', part_grads, part_rows, precision=PRECISE)  26.2 us
    unnamed x322, local copies, waits for them, and re-layouts  25.6 us
    reshape x4, local copies, waits for them, and re-layouts, one_group(): flattened = products.reshape(block_groups, block_rows * window)  20.9 us
  transfers between devices with their start and end apart: 8, of which 4 were waited for; matrix products, arithmetic and copies ran while one was open for 24% of the time, Pallas kernels for 0%

commit v1 on v0

v1 whole, which is shorter than its diff:
```python
import functools
import math

import jax
import jax.numpy as jnp
from jax import lax
from jax.experimental import pallas as pl
from jax.experimental.pallas import tpu as pltpu
from jax.sharding import PartitionSpec as P

F32 = jnp.float32
BF16 = jnp.bfloat16
EDGE = 8
TILE = 256


def passed_along(block, distance):
    devices = range(lax.axis_size("ctx"))
    route = [(i - distance, i) for i in devices if i - distance in devices]
    return lax.ppermute(block, "ctx", route)


def iota2(shape, dim):
    return lax.broadcasted_iota(jnp.int32, shape, dim)


def dot(a, b):
    return jnp.dot(a, b, preferred_element_type=F32)


def feature_kernel(ids_ref, sf_ref, x_ref, cot_ref, edge_ref, ids_edge_ref,
                   feat_ref, kv_ref, g_ref, shift, shift_edge):
    rows = x_ref.shape[1]
    taps = sf_ref.shape[1]

    @pl.when(pl.program_id(0) == 0)
    def _():
        id_row = jnp.broadcast_to(ids_ref[...], (rows, rows)).astype(F32)
        id_col = id_row.T
        lag = iota2((rows, rows), 0) - iota2((rows, rows), 1)
        same = id_row == id_col
        before = jnp.broadcast_to(ids_edge_ref[0, 0:1, 0:rows].astype(F32), (EDGE, rows))
        before = pltpu.roll(before, EDGE, 1)
        lag_edge = iota2((EDGE, rows), 0) + EDGE - iota2((EDGE, rows), 1)
        same_edge = before == id_col[0:EDGE]
        for t in range(1, taps):
            shift[(t - 1) * rows : t * rows] = jnp.where((lag == t) & same, 1.0, 0.0).astype(BF16)
            shift_edge[(t - 1) * EDGE : t * EDGE] = jnp.where((lag_edge == t) & same_edge, 1.0, 0.0)

    feats = []
    for i in range(3):
        x = x_ref[i]
        w = sf_ref[i]
        moved = dot(shift[...], x)
        acc = w[0:1] * x.astype(F32)
        for t in range(1, taps):
            acc = acc + w[t : t + 1] * moved[(t - 1) * rows : t * rows]
        edge = jnp.concatenate([edge_ref[i].astype(F32), jnp.zeros((rows - EDGE, x.shape[1]), F32)], 0)
        moved_edge = dot(shift_edge[...].astype(BF16), edge.astype(BF16))
        fix = w[1:2] * moved_edge[0:EDGE]
        for t in range(2, taps):
            fix = fix + w[t : t + 1] * moved_edge[(t - 1) * EDGE : t * EDGE]
        acc = jnp.concatenate([acc[0:EDGE] + fix, acc[EDGE:]], 0)
        feat_ref[i] = acc
        feats.append(acc)
    kv_ref[...] = (feats[1] * feats[2]).astype(BF16)
    g = cot_ref[...].astype(F32) * feats[0]
    id_wide = jnp.concatenate([ids_ref[...].astype(F32)] * (g.shape[1] // rows), 1)
    last = iota2(g.shape, 0) == rows - 1
    g_ref[...] = jnp.where(last, jnp.broadcast_to(id_wide, g.shape), g).astype(BF16)


def mixer_kernel(ids_ref, sf_ref, lf_ref, lfr_ref, x_ref, cot_ref, edge_ref, ids_edge_ref, feat_ref,
                 kvp_ref, gn_ref, out_ref, qg_ref, tail_ref, part_ref, long_ref, short_ref,
                 shift, mask_y, mask_g, mask_a, w_kv, w_g, g_rev, y_ref, gm_ref, dh_ref):
    rows = x_ref.shape[1]
    taps = sf_ref.shape[1]
    lanes = x_ref.shape[2]
    groups = lf_ref.shape[0]
    width = lanes // groups
    lag = iota2((rows, rows), 0) - iota2((rows, rows), 1)
    flip = jnp.where(iota2((rows, rows), 0) + iota2((rows, rows), 1) == rows - 1, 1.0, 0.0)
    mirror = flip.astype(BF16)

    @pl.when(pl.program_id(0) == 0)
    def _():
        id_row = jnp.broadcast_to(ids_ref[...], (rows, rows)).astype(F32)
        id_col = id_row.T
        prev_row = jnp.broadcast_to(ids_edge_ref[0, 0:1, 0:rows].astype(F32), (rows, rows))
        prev_col = prev_row.T
        next_row = jnp.broadcast_to(gn_ref[rows - 1 : rows, 0:rows].astype(F32), (rows, rows))
        same = id_row == id_col
        own = jnp.where((lag >= 0) & same, 1.0, 0.0)
        prev = jnp.where((lag < 0) & (prev_row == id_col), 1.0, 0.0)
        mask_y[:, 0:rows] = own.astype(BF16)
        mask_y[:, rows:] = prev.astype(BF16)
        mask_a[...] = dot(mirror, mask_y[...])
        mask_g[:, 0:rows] = jnp.where((lag <= 0) & same, 1.0, 0.0).astype(BF16)
        mask_g[:, rows:] = jnp.where((lag > 0) & (next_row == id_col), 1.0, 0.0).astype(BF16)
        for t in range(1, taps):
            shift[(t - 1) * rows : t * rows] = jnp.where((lag == -t) & same, 1.0, 0.0).astype(BF16)
        base = (taps - 1) * rows
        lag_edge = iota2((EDGE, rows), 1) + EDGE - iota2((EDGE, rows), 0)
        same_edge = prev_col[rows - EDGE :] == id_row[0:EDGE]
        pieces = [jnp.where((lag_edge == t) & same_edge, 1.0, 0.0) for t in range(1, taps)]
        shift[base : base + (taps - 1) * EDGE] = jnp.concatenate(pieces, 0).astype(BF16)

    cot = cot_ref[...].astype(F32)
    g32 = cot * feat_ref[0]
    w_kv[0:rows] = (feat_ref[1] * feat_ref[2]).astype(BF16)
    w_kv[rows:] = kvp_ref[...]
    w_g[0:rows] = g32.astype(BF16)
    w_g[rows:] = gn_ref[...]
    g_rev[...] = dot(mirror, w_g[0:rows]).astype(BF16)

    half = rows
    for part in range(lanes // half):
        cols = slice(part * half, (part + 1) * half)
        per = half // width

        def one_group(j, carry, part=part, cols=cols, per=per):
            g = part * per + j
            mine = iota2((rows, half), 1) // width == j
            fwd = jnp.broadcast_to(lfr_ref[pl.ds(g, 1), :], (rows, rows))
            fwd = pltpu.roll(fwd, 0, 1, stride=1, stride_axis=0).astype(BF16)
            t_y = jnp.concatenate([fwd, fwd], 1) * mask_y[...]
            res = dot(t_y, w_kv[:, cols])
            y_ref[:, cols] = jnp.where(mine, res, y_ref[:, cols])
            bwd = jnp.broadcast_to(lf_ref[pl.ds(g, 1), :], (rows, rows))
            bwd = pltpu.roll(bwd, 0, 1, stride=1, stride_axis=0).astype(BF16)
            t_g = jnp.concatenate([bwd, bwd], 1) * mask_g[...]
            res = dot(t_g, w_g[:, cols])
            gm_ref[:, cols] = jnp.where(mine, res, gm_ref[:, cols])
            g_sel = jnp.where(mine, g_rev[:, cols], jnp.zeros((rows, half), BF16))
            cross = lax.dot_general(
                g_sel, w_kv[:, cols], (((1,), (1,)), ((), ())), preferred_element_type=F32
            ) * mask_a[...]
            folded = cross[:, 0:rows] + cross[:, rows:]
            folded = pltpu.roll(folded, 0, 1, stride=1, stride_axis=0)
            dh_ref[pl.ds(g, 1), :] = jnp.sum(folded, 0, keepdims=True)
            return carry

        lax.fori_loop(0, per, one_group, 0, unroll=2)

    long_ref[...] = jnp.dot(dh_ref[...], flip, preferred_element_type=F32, precision=lax.Precision.HIGHEST)

    y = y_ref[...]
    gm = gm_ref[...]
    out_ref[...] = (feat_ref[0] * y).astype(BF16)
    for i in range(3):
        gf = cot * y if i == 0 else gm * feat_ref[3 - i]
        w = sf_ref[i]
        x = x_ref[i].astype(F32)
        xe = edge_ref[i].astype(F32)
        moved = dot(shift[...], gf.astype(BF16))
        base = (taps - 1) * rows
        acc = w[0:1] * gf
        short_ref[i, 0:1] = jnp.sum(x * gf, 0, keepdims=True)
        sent = jnp.zeros((EDGE, lanes), F32)
        for t in range(1, taps):
            piece = moved[(t - 1) * rows : t * rows]
            piece_edge = moved[base + (t - 1) * EDGE : base + t * EDGE]
            acc = acc + w[t : t + 1] * piece
            sent = sent + w[t : t + 1] * piece_edge
            short_ref[i, t : t + 1] = (
                jnp.sum(x * piece, 0, keepdims=True) + jnp.sum(xe * piece_edge, 0, keepdims=True)
            )
        short_ref[i, taps:] = jnp.zeros((short_ref.shape[1] - taps, lanes), F32)
        qg_ref[i] = acc.astype(BF16)
        tail_ref[i] = acc[rows - EDGE :]
        part_ref[i] = sent.astype(BF16)


def shards(qkv, cotangent, doc_ids, short_filter, long_filter):
    _, rows, chans = qkv.shape
    groups, long_taps = long_filter.shape
    taps = short_filter.shape[2]
    devices = lax.axis_size("ctx")
    grad_scale = 1.0 / math.sqrt(rows * devices)
    tile_groups = TILE * groups // chans
    padded_taps = 8
    params = pltpu.CompilerParams(vmem_limit_bytes=48 << 20, dimension_semantics=("arbitrary",))

    ids = doc_ids.reshape(1, rows)
    sf = jnp.transpose(short_filter, (0, 2, 1))
    lf_rev = jnp.roll(jnp.flip(long_filter, 1), 1, 1)

    edge = qkv[:, rows - EDGE :, :]
    edge = edge.at[0, 0, :rows].set(doc_ids.astype(BF16))
    edge = passed_along(edge, 1)

    fixed = lambda shape: pl.BlockSpec(shape, lambda c: (0,) * len(shape))
    wide3 = lambda n: pl.BlockSpec((3, n, TILE), lambda c: (0, 0, c))
    wide2 = lambda n: pl.BlockSpec((n, TILE), lambda c: (0, c))
    feats, kv, grad = pl.pallas_call(
        feature_kernel,
        grid=(chans // TILE,),
        in_specs=[fixed((1, rows)), wide3(taps), wide3(rows), wide2(rows), wide3(EDGE), fixed((3, EDGE, TILE))],
        out_specs=[wide3(rows), wide2(rows), wide2(rows)],
        out_shape=[
            jax.ShapeDtypeStruct((3, rows, chans), F32),
            jax.ShapeDtypeStruct((rows, chans), BF16),
            jax.ShapeDtypeStruct((rows, chans), BF16),
        ],
        scratch_shapes=[
            pltpu.VMEM(((taps - 1) * rows, rows), BF16),
            pltpu.VMEM(((taps - 1) * EDGE, rows), F32),
        ],
        compiler_params=params,
        name="features",
    )(ids, sf, qkv, cotangent, edge, edge)

    kv_prev = passed_along(kv, 1)
    grad_next = passed_along(grad, -1)

    out, qg, tail, part, long_part, short_part = pl.pallas_call(
        mixer_kernel,
        grid=(chans // TILE,),
        in_specs=[
            fixed((1, rows)), wide3(taps),
            pl.BlockSpec((tile_groups, long_taps), lambda c: (c, 0)),
            pl.BlockSpec((tile_groups, long_taps), lambda c: (c, 0)),
            wide3(rows), wide2(rows), wide3(EDGE), fixed((3, EDGE, TILE)), wide3(rows),
            wide2(rows), wide2(rows),
        ],
        out_specs=[
            wide2(rows), wide3(rows), wide3(EDGE), wide3(EDGE),
            pl.BlockSpec((tile_groups, long_taps), lambda c: (c, 0)),
            wide3(padded_taps),
        ],
        out_shape=[
            jax.ShapeDtypeStruct((rows, chans), BF16),
            jax.ShapeDtypeStruct((3, rows, chans), BF16),
            jax.ShapeDtypeStruct((3, EDGE, chans), F32),
            jax.ShapeDtypeStruct((3, EDGE, chans), BF16),
            jax.ShapeDtypeStruct((groups, long_taps), F32),
            jax.ShapeDtypeStruct((3, padded_taps, chans), F32),
        ],
        scratch_shapes=[
            pltpu.VMEM(((taps - 1) * (rows + EDGE), rows), BF16),
            pltpu.VMEM((rows, 2 * rows), BF16),
            pltpu.VMEM((rows, 2 * rows), BF16),
            pltpu.VMEM((rows, 2 * rows), F32),
            pltpu.VMEM((2 * rows, TILE), BF16),
            pltpu.VMEM((2 * rows, TILE), BF16),
            pltpu.VMEM((rows, TILE), BF16),
            pltpu.VMEM((rows, TILE), F32),
            pltpu.VMEM((rows, TILE), F32),
            pltpu.VMEM((tile_groups, long_taps), F32),
        ],
        compiler_params=params,
        name="mixer",
    )(ids, sf, long_filter, lf_rev, qkv, cotangent, edge, edge, feats, kv_prev, grad_next)

    part = passed_along(part, -1)
    qg = lax.dynamic_update_slice(qg, (tail + part.astype(F32)).astype(BF16), (0, rows - EDGE, 0))

    per = chans // devices
    packed = jnp.concatenate(
        [
            short_part.reshape(3 * padded_taps, devices, per).transpose(1, 0, 2),
            long_part.reshape(devices, -1, per),
        ],
        1,
    )
    packed = lax.all_to_all(packed, "ctx", 0, 0)
    total = jnp.sum(packed, 0) * grad_scale
    short_grad = total[: 3 * padded_taps].reshape(3, padded_taps, per)[:, :taps].transpose(0, 2, 1)
    long_grad = total[3 * padded_taps :].reshape(groups // devices, long_taps)
    return (out, qg, long_grad, short_grad)


def solution(mesh):
    in_specs = (P(None, "ctx", "tp"), P("ctx", "tp"), P("ctx"), P(None, "tp", None), P("tp", None))
    out_specs = (
        P("ctx", "tp"),
        P(None, "ctx", "tp"),
        P(("tp", "ctx"), None),
        P(None, ("tp", "ctx"), None),
    )
    return jax.shard_map(shards, mesh=mesh, in_specs=in_specs, out_specs=out_specs, check_vma=False)
```

time: 715 us -> 106 us (0.15)
  other arithmetic: 336 us -> 2.98 us
  local copies, waits for them, and re-layouts: 193 us -> 13.1 us
  waiting for transfers between devices: 115 us -> 27.4 us
  Pallas kernels: 0 us -> 39.8 us
  matrix products: 26.2 us -> 0 us
  between operations: 16.7 us -> 0.77 us
    another operation x5 -> x1, other arithmetic: 149 us -> 0.66 us  [the longest x4 149 us: hyena_mix(): jnp.stack([grad_q, grad_mix * features[2], grad_mix * features[1]], 0)]
    add x3 -> x0, other arithmetic: 144 us -> none  [the longest x2 133 us: long_apply(): summed + filters[None, :, tap_index, None] * extended[first_row:first_row...]
    mul x256 -> x0, local copies, waits for them, and re-layouts: 105 us -> none  [long_apply(): filters[None, :, tap_index, None]]
    unnamed x3 -> x0, waiting for transfers between devices: 64.5 us -> none
    pallas_call x0 -> x2, Pallas kernels: none -> 39.8 us  [the longest x1 33.8 us: shards(): pl.pallas_call(mixer_kernel, grid=(chans // TILE,), in_specs=[fixed((1, r...]
    dot_general x4 -> x0, matrix products: 26.2 us -> none  [one_group(): jnp.einsum('rgc,wgc->grw', part_grads, part_rows, precision=PRECISE)]
    convert_element_type x23 -> x0, other arithmetic: 24.2 us -> none  [the longest x1 12.7 us: hyena_mix(): grad_raw = anti_short(feats_after, short_filter, ids_after[:row_count + s...]
    reduce_scatter x1 -> x0, waiting for transfers between devices: 20 us -> none  [shards(): lax.psum_scatter(long_part, 'ctx', scatter_dimension=0, tiled=True)]
  transfers between devices with their start and end apart: 8 -> 5, of which waited for: 4 -> 3; matrix products, arithmetic and copies ran while one was open for 24% -> 5% of each run, Pallas kernels for 0% -> 0%
where the time goes in v1:
time: 106 us
  Pallas kernels  39.8 us (38%)
  waiting for transfers between devices  27.4 us (26%)
  starting transfers between devices  21.4 us (20%)
  local copies, waits for them, and re-layouts  13.1 us (12%)
  other arithmetic  2.98 us (3%)
    pallas_call x1, Pallas kernels, shards(): pl.pallas_call(mixer_kernel, grid=(chans // TILE,), in_specs=[fixed((1, r...  33.8 us
    ppermute x4, waiting for transfers between devices, passed_along(): return lax.ppermute(block, 'ctx', route)  19.3 us
    ppermute x4, starting transfers between devices, passed_along(): return lax.ppermute(block, 'ctx', route)  11.8 us
    all_to_all x1, starting transfers between devices, shards(): packed = lax.all_to_all(packed, 'ctx', 0, 0)  9.64 us
    all_to_all x1, waiting for transfers between devices, shards(): packed = lax.all_to_all(packed, 'ctx', 0, 0)  8.14 us
    unnamed x29, local copies, waits for them, and re-layouts  7.64 us
    pallas_call x1, Pallas kernels, shards(): pl.pallas_call(feature_kernel, grid=(chans // TILE,), in_specs=[fixed((1,...  6.04 us
    slice x2, local copies, waits for them, and re-layouts, shards(): lf_rev = jnp.roll(jnp.flip(long_filter, 1), 1, 1)  2.24 us
  transfers between devices with their start and end apart: 5, of which 3 were waited for; matrix products, arithmetic and copies ran while one was open for 5% of the time, Pallas kernels for 0%

profile of v1, /device:TPU:0, one launch (start us, length us, event | category | flops | bytes accessed | tf_op | source)
XLA Modules:
  0.0 105.5 jit_solution(9604635885862471083)
XLA Ops:
  0.6 0.7 convert_bitcast_fusion
  1.3 0.0 copy-start.5
  1.3 0.0 copy-start.12
  1.3 0.9 slice.50
  2.2 0.1 scatter.4
  2.4 4.8 %collective-permute-start = (bf16[3,8,2048]{2,1,0:T(8,128)(2,1)S(1)}, bf16[3,8,2048]{2,1,0:T(8,128)(2,1)S(1)}, u32[]{:S(2)}, u32[]{:S(2)}) collective-permute-start(bf16[3,8,2048]{2,1,0:T(8,128)(2,1)S(1)} %scatter.4), channel_id=1, source_target_pairs={{0,4},{4,8},{8,12},{12,16},{16,20},{20,24},{24,28},{1,5},{5,9},{9,... | collective-permute-start | bytes 294920 | tf_op jit(solution)/shard_map/ppermute | solution.py:20
  7.2 2.2 %collective-permute-done.edge_ref.ids_edge_ref = bf16[3,8,2048]{2,1,0:T(8,128)(2,1)S(1)} collective-permute-done((bf16[3,8,2048]{2,1,0:T(8,128)(2,1)S(1)}, bf16[3,8,2048]{2,1,0:T(8,128)(2,1)S(1)}, u32[]{:S(2)}, u32[]{:S(2)}) %collective-permute-start) | collective-permute-done | bytes 98336 | tf_op jit(solution)/shard_map/ppermute | solution.py:20
  9.4 0.0 copy-start
  9.4 1.4 %copy-done = bf16[3,128,2048]{2,1,0:T(8,128)(2,1)S(1)} copy-done((bf16[3,128,2048]{2,1,0:T(8,128)(2,1)S(1)}, bf16[3,128,2048]{2,1,0:T(8,128)(2,1)}, u32[]{:S(2)}) %copy-start) | copy-done | bytes 1572888
  10.8 0.0 copy-start.2
  10.8 1.0 copy-done.2
  11.9 0.0 copy-start.4
  11.9 0.9 copy-done.4
  12.8 0.0 copy-start.11
  12.8 0.7 copy-done.11
  13.5 0.0 copy-start.6
  13.5 0.0 copy-start.1
  13.5 0.0 copy-start.3
  13.5 6.0 %features.1 = (f32[3,128,2048]{2,1,0:T(8,128)}, bf16[128,2048]{1,0:T(8,128)(2,1)}, bf16[128,2048]{1,0:T(8,128)(2,1)}) custom-call(s32[1,128]{1,0:T(1,128)S(1)} %bitcast.19, f32[3,7,2048]{2,1,0:T(8,128)S(1)} %bitcast.15, bf16[3,128,2048]{2,1,0:T(8,128)(2,1)S(1)} %copy-done, bf16[128,2048]{1,0:T(8,128)(2,1)S(1)} %copy-done.2, ...), custom_call_target="tpu_custom_call" | custom-call | tf_op jit(solution)/shard_map/features/pallas_call | solution.py:195
  19.5 4.3 %collective-permute-start.1 = (bf16[128,2048]{1,0:T(8,128)(2,1)}, bf16[128,2048]{1,0:T(8,128)(2,1)S(1)}, u32[]{:S(2)}, u32[]{:S(2)}) collective-permute-start(bf16[128,2048]{1,0:T(8,128)(2,1)} %get-tuple-element.26), channel_id=1, source_target_pairs={{0,4},{4,8},{8,12},{12,16},{16,20},{20,24},{24,28},{1,5},{5,9},{9,... | collective-permute-start | bytes 1572872 | tf_op jit(solution)/shard_map/ppermute | solution.py:20
  23.8 1.3 %collective-permute-start.2 = (bf16[128,2048]{1,0:T(8,128)(2,1)}, bf16[128,2048]{1,0:T(8,128)(2,1)S(1)}, u32[]{:S(2)}, u32[]{:S(2)}) collective-permute-start(bf16[128,2048]{1,0:T(8,128)(2,1)} %get-tuple-element.27), channel_id=1, source_target_pairs={{4,0},{8,4},{12,8},{16,12},{20,16},{24,20},{28,24},{5,1},{9,5},{13... | collective-permute-start | bytes 1572872 | tf_op jit(solution)/shard_map/ppermute | solution.py:20
  25.1 0.0 copy-done.6
  25.1 0.7 slice.48
  25.9 1.5 %slice.49 = f32[128,127]{1,0:T(8,128)} reverse(f32[128,127]{1,0:T(8,128)} %slice.48), dimensions={1} | reverse | bytes 130048 | tf_op jit(solution)/shard_map/jit(_roll_static)/slice | solution.py:186
  27.4 0.9 pad_maximum_fusion.1.lfr_ref
  28.3 17.1 %collective-permute-done.1.kvp_ref = bf16[128,2048]{1,0:T(8,128)(2,1)S(1)} collective-permute-done((bf16[128,2048]{1,0:T(8,128)(2,1)}, bf16[128,2048]{1,0:T(8,128)(2,1)S(1)}, u32[]{:S(2)}, u32[]{:S(2)}) %collective-permute-start.1) | collective-permute-done | bytes 524320 | tf_op jit(solution)/shard_map/ppermute | solution.py:20
  45.4 0.0 collective-permute-done.2.gn_ref
  45.4 0.0 copy-done.5
  45.4 0.0 copy-done.12
  45.4 0.0 copy-done.1
  45.4 0.0 copy-done.3
  45.4 33.8 %mixer.1 = (bf16[128,2048]{1,0:T(8,128)(2,1)}, bf16[3,128,2048]{2,1,0:T(8,128)(2,1)}, f32[3,8,2048]{2,1,0:T(8,128)S(1)}, bf16[3,8,2048]{2,1,0:T(8,128)(2,1)S(1)}...) custom-call(s32[1,128]{1,0:T(1,128)S(1)} %bitcast.20, f32[3,7,2048]{2,1,0:T(8,128)S(1)} %bitcast.16, ...), custom_call_target="tpu_custom_call" | custom-call | tf_op jit(solution)/shard_map/mixer/pallas_call | solution.py:216
  79.2 0.7 copy-done.7
  79.9 0.7 copy-done.9
  80.5 0.6 copy-done.10
  81.2 0.6 copy-done.13
  81.8 0.9 reshape.59
  82.7 1.3 %collective-permute-start.3 = (bf16[3,8,2048]{2,1,0:T(8,128)(2,1)}, bf16[3,8,2048]{2,1,0:T(8,128)(2,1)S(1)}, u32[]{:S(2)}, u32[]{:S(2)}) collective-permute-start(bf16[3,8,2048]{2,1,0:T(8,128)(2,1)} %copy-done.13), channel_id=1, source_target_pairs={{4,0},{8,4},{12,8},{16,12},{20,16},{24,20},{28,24},{5,1},{9,5},{13... | collective-permute-start | bytes 294920 | tf_op jit(solution)/shard_map/ppermute | solution.py:20
  84.0 1.0 copy.11
  85.0 0.1 copy.13
  85.1 0.7 pad_maximum_fusion
  85.8 9.6 %all-to-all-start = ((f32[8,32,256]{2,1,0:T(8,128)}), f32[8,32,256]{2,1,0:T(8,128)S(1)}, u32[]{:S(2)}, u32[]{:S(2)}) async-start(f32[8,32,256]{2,1,0:T(8,128)} %pad_maximum_fusion), calls=%async_computation | async-start | bytes 524288 | tf_op jit(solution)/shard_map/all_to_all | solution.py:266
  95.4 0.0 collective-permute-done.3
  95.4 0.0 copy-done.8
  95.4 0.7 fusion
  96.1 8.1 %all-to-all-done = f32[8,32,256]{2,1,0:T(8,128)S(1)} async-done(((f32[8,32,256]{2,1,0:T(8,128)}), f32[8,32,256]{2,1,0:T(8,128)S(1)}, u32[]{:S(2)}, u32[]{:S(2)}) %all-to-all-start) | async-done | bytes 262176 | tf_op jit(solution)/shard_map/all_to_all | solution.py:266
  104.3 0.6 slice_bitcast_fusion
  104.9 0.6 reshape.60
  (9 shorter events, 0.0 us)
Async XLA Ops:
  1.3 44.1 %copy-start.5 = (f32[3,2048,7]{1,2,0:T(8,128)S(1)}, f32[3,2048,7]{1,2,0:T(8,128)}, u32[]{:S(2)}) copy-start(f32[3,2048,7]{1,2,0:T(8,128)} %param.10) | copy-start | bytes 516100
  1.3 44.1 %copy-start.12 = (s32[128]{0:T(128)S(1)}, s32[128]{0:T(128)}, u32[]{:S(2)}) copy-start(s32[128]{0:T(128)} %param.9) | copy-start | bytes 1540
  2.4 7.0 %collective-permute-start = (bf16[3,8,2048]{2,1,0:T(8,128)(2,1)S(1)}, bf16[3,8,2048]{2,1,0:T(8,128)(2,1)S(1)}, u32[]{:S(2)}, u32[]{:S(2)}) collective-permute-start(bf16[3,8,2048]{2,1,0:T(8,128)(2,1)S(1)} %scatter.4), channel_id=1, source_target_pairs={{0,4},{4,8},{8,12},{12,16},{16,20},{20,24},{24,28},{1,5},{5,9},{9,... | collective-permute-start | bytes 294920 | tf_op jit(solution)/shard_map/ppermute | solution.py:20
  9.4 1.4 %copy-start = (bf16[3,128,2048]{2,1,0:T(8,128)(2,1)S(1)}, bf16[3,128,2048]{2,1,0:T(8,128)(2,1)}, u32[]{:S(2)}) copy-start(bf16[3,128,2048]{2,1,0:T(8,128)(2,1)} %x_ref.3) | copy-start | bytes 4718596
  10.8 1.0 copy-start.2
  11.9 0.9 copy-start.4
  12.8 0.7 copy-start.11
  13.5 11.7 %copy-start.6 = (f32[128,128]{1,0:T(8,128)S(1)}, f32[128,128]{1,0:T(8,128)}, u32[]{:S(2)}) copy-start(f32[128,128]{1,0:T(8,128)} %lf_ref.1) | copy-start | bytes 196612
  13.5 31.9 %copy-start.1 = (bf16[3,128,2048]{2,1,0:T(8,128)(2,1)S(1)}, bf16[3,128,2048]{2,1,0:T(8,128)(2,1)}, u32[]{:S(2)}) copy-start(bf16[3,128,2048]{2,1,0:T(8,128)(2,1)} %x_ref.3) | copy-start | bytes 4718596
  13.5 31.9 %copy-start.3 = (bf16[128,2048]{1,0:T(8,128)(2,1)S(1)}, bf16[128,2048]{1,0:T(8,128)(2,1)}, u32[]{:S(2)}) copy-start(bf16[128,2048]{1,0:T(8,128)(2,1)} %cot_ref.3) | copy-start | bytes 1572868
  19.5 25.9 %collective-permute-start.1 = (bf16[128,2048]{1,0:T(8,128)(2,1)}, bf16[128,2048]{1,0:T(8,128)(2,1)S(1)}, u32[]{:S(2)}, u32[]{:S(2)}) collective-permute-start(bf16[128,2048]{1,0:T(8,128)(2,1)} %get-tuple-element.26), channel_id=1, source_target_pairs={{0,4},{4,8},{8,12},{12,16},{16,20},{20,24},{24,28},{1,5},{5,9},{9,... | collective-permute-start | bytes 1572872 | tf_op jit(solution)/shard_map/ppermute | solution.py:20
  23.8 21.5 %collective-permute-start.2 = (bf16[128,2048]{1,0:T(8,128)(2,1)}, bf16[128,2048]{1,0:T(8,128)(2,1)S(1)}, u32[]{:S(2)}, u32[]{:S(2)}) collective-permute-start(bf16[128,2048]{1,0:T(8,128)(2,1)} %get-tuple-element.27), channel_id=1, source_target_pairs={{4,0},{8,4},{12,8},{16,12},{20,16},{24,20},{28,24},{5,1},{9,5},{13... | collective-permute-start | bytes 1572872 | tf_op jit(solution)/shard_map/ppermute | solution.py:20
  79.2 0.7 copy-start.7
  79.9 0.7 copy-start.9
  80.5 0.6 copy-start.10
  81.2 0.6 copy-start.13
  81.8 13.6 %copy-start.8 = (f32[3,8,2048]{2,1,0:T(8,128)S(1)}, f32[3,8,2048]{2,1,0:T(8,128)}, u32[]{:S(2)}) copy-start(f32[3,8,2048]{2,1,0:T(8,128)} %copy-done.7) | copy-start | bytes 589828
  82.7 12.7 %collective-permute-start.3 = (bf16[3,8,2048]{2,1,0:T(8,128)(2,1)}, bf16[3,8,2048]{2,1,0:T(8,128)(2,1)S(1)}, u32[]{:S(2)}, u32[]{:S(2)}) collective-permute-start(bf16[3,8,2048]{2,1,0:T(8,128)(2,1)} %copy-done.13), channel_id=1, source_target_pairs={{4,0},{8,4},{12,8},{16,12},{20,16},{24,20},{28,24},{5,1},{9,5},{13... | collective-permute-start | bytes 294920 | tf_op jit(solution)/shard_map/ppermute | solution.py:20
  85.8 18.5 %all-to-all-start = ((f32[8,32,256]{2,1,0:T(8,128)}), f32[8,32,256]{2,1,0:T(8,128)S(1)}, u32[]{:S(2)}, u32[]{:S(2)}) async-start(f32[8,32,256]{2,1,0:T(8,128)} %pad_maximum_fusion), calls=%async_computation | async-start | bytes 524288 | tf_op jit(solution)/shard_map/all_to_all | solution.py:266

commit v2 on v1

--- a/solution.py
+++ b/solution.py
@@ -11,7 +11,7 @@
 F32 = jnp.float32
 BF16 = jnp.bfloat16
 EDGE = 8
-TILE = 256
+TILE = 512
 
 
 def passed_along(block, distance):
@@ -70,9 +70,9 @@
     g_ref[...] = jnp.where(last, jnp.broadcast_to(id_wide, g.shape), g).astype(BF16)
 
 
-def mixer_kernel(ids_ref, sf_ref, lf_ref, lfr_ref, x_ref, cot_ref, edge_ref, ids_edge_ref, feat_ref,
-                 kvp_ref, gn_ref, out_ref, qg_ref, tail_ref, part_ref, long_ref, short_ref,
-                 shift, mask_y, mask_g, mask_a, w_kv, w_g, g_rev, y_ref, gm_ref, dh_ref):
+def mixer_kernel(ids_ref, sf_ref, lf_ref, x_ref, cot_ref, edge_ref, ids_edge_ref, feat_ref,
+                 kvp_ref, gn_ref, out_ref, qg_ref, tail_ref, part_ref, packed_ref,
+                 shift, mask_y, mask_g, mask_a, w_kv, w_g, g_rev, y_ref, gm_ref, dh_ref, lfr_ref, short_ref):
     rows = x_ref.shape[1]
     taps = sf_ref.shape[1]
     lanes = x_ref.shape[2]
@@ -114,35 +114,43 @@
     g_rev[...] = dot(mirror, w_g[0:rows]).astype(BF16)
 
     half = rows
-    for part in range(lanes // half):
-        cols = slice(part * half, (part + 1) * half)
-        per = half // width
-
-        def one_group(j, carry, part=part, cols=cols, per=per):
+    per = half // width
+    backward = jnp.where((iota2((rows, rows), 0) + iota2((rows, rows), 1)) % rows == 0, 1.0, 0.0)
+    lfr_ref[...] = dot(lf_ref[...].astype(BF16), backward.astype(BF16))
+    owner = iota2((rows, half), 1) // width
+
+    def one_part(part, carry):
+        cols = pl.ds(pl.multiple_of(part * half, half), half)
+        w_kv_part = w_kv[:, cols]
+        w_g_part = w_g[:, cols]
+        g_part = g_rev[:, cols]
+        y_part = jnp.zeros((rows, half), F32)
+        gm_part = jnp.zeros((rows, half), F32)
+        for j in range(per):
             g = part * per + j
-            mine = iota2((rows, half), 1) // width == j
+            mine = owner == j
             fwd = jnp.broadcast_to(lfr_ref[pl.ds(g, 1), :], (rows, rows))
             fwd = pltpu.roll(fwd, 0, 1, stride=1, stride_axis=0).astype(BF16)
             t_y = jnp.concatenate([fwd, fwd], 1) * mask_y[...]
-            res = dot(t_y, w_kv[:, cols])
-            y_ref[:, cols] = jnp.where(mine, res, y_ref[:, cols])
+            y_part = jnp.where(mine, dot(t_y, w_kv_part), y_part)
             bwd = jnp.broadcast_to(lf_ref[pl.ds(g, 1), :], (rows, rows))
             bwd = pltpu.roll(bwd, 0, 1, stride=1, stride_axis=0).astype(BF16)
             t_g = jnp.concatenate([bwd, bwd], 1) * mask_g[...]
-            res = dot(t_g, w_g[:, cols])
-            gm_ref[:, cols] = jnp.where(mine, res, gm_ref[:, cols])
-            g_sel = jnp.where(mine, g_rev[:, cols], jnp.zeros((rows, half), BF16))
+            gm_part = jnp.where(mine, dot(t_g, w_g_part), gm_part)
+            g_sel = jnp.where(mine, g_part, jnp.zeros((rows, half), BF16))
             cross = lax.dot_general(
-                g_sel, w_kv[:, cols], (((1,), (1,)), ((), ())), preferred_element_type=F32
+                g_sel, w_kv_part, (((1,), (1,)), ((), ())), preferred_element_type=F32
             ) * mask_a[...]
             folded = cross[:, 0:rows] + cross[:, rows:]
             folded = pltpu.roll(folded, 0, 1, stride=1, stride_axis=0)
             dh_ref[pl.ds(g, 1), :] = jnp.sum(folded, 0, keepdims=True)
-            return carry
-
-        lax.fori_loop(0, per, one_group, 0, unroll=2)
-
-    long_ref[...] = jnp.dot(dh_ref[...], flip, preferred_element_type=F32, precision=lax.Precision.HIGHEST)
+        y_ref[:, cols] = y_part
+        gm_ref[:, cols] = gm_part
+        return carry
+
+    lax.fori_loop(0, lanes // half, one_part, 0)
+
+    dh = jnp.dot(dh_ref[...], flip, preferred_element_type=F32, precision=lax.Precision.HIGHEST)
 
     y = y_ref[...]
     gm = gm_ref[...]
@@ -170,6 +178,29 @@
         tail_ref[i] = acc[rows - EDGE :]
         part_ref[i] = sent.astype(BF16)
 
+    chunk = packed_ref.shape[2]
+    pairs = chunk // rows
+    size = groups * rows // lanes
+    for k in range(lanes // chunk):
+        heads = [short_ref[i, :, k * chunk : (k + 1) * chunk] for i in range(3)]
+        first = k * pairs * size
+        rest = [dh[first + p * size : first + (p + 1) * size] for p in range(pairs)]
+        packed_ref[k] = jnp.concatenate(heads + [jnp.concatenate(rest, 1)], 0).astype(BF16)
+
+
+def finish_kernel(scale, taps, got_ref, long_ref, short_ref):
+    total = got_ref[0].astype(F32)
+    for k in range(1, got_ref.shape[0]):
+        total = total + got_ref[k].astype(F32)
+    total = total * scale
+    padded = short_ref.shape[1] + 1
+    for i in range(3):
+        short_ref[i] = total[i * padded : i * padded + taps]
+    size = total.shape[0] - 3 * padded
+    lags = long_ref.shape[1]
+    for p in range(total.shape[1] // lags):
+        long_ref[p * size : (p + 1) * size] = total[3 * padded :, p * lags : (p + 1) * lags]
+
 
 def shards(qkv, cotangent, doc_ids, short_filter, long_filter):
     _, rows, chans = qkv.shape
@@ -179,14 +210,17 @@
     grad_scale = 1.0 / math.sqrt(rows * devices)
     tile_groups = TILE * groups // chans
     padded_taps = 8
-    params = pltpu.CompilerParams(vmem_limit_bytes=48 << 20, dimension_semantics=("arbitrary",))
+    params = pltpu.CompilerParams(vmem_limit_bytes=60 << 20, dimension_semantics=("arbitrary",))
 
     ids = doc_ids.reshape(1, rows)
     sf = jnp.transpose(short_filter, (0, 2, 1))
-    lf_rev = jnp.roll(jnp.flip(long_filter, 1), 1, 1)
+    chunk = 2 * rows
+    packed_rows = 3 * padded_taps + groups * long_taps // chans
 
     edge = qkv[:, rows - EDGE :, :]
-    edge = edge.at[0, 0, :rows].set(doc_ids.astype(BF16))
+    id_lanes = jnp.pad(doc_ids.astype(BF16), (0, chans - rows))
+    first = (lax.broadcasted_iota(jnp.int32, edge.shape, 0) + lax.broadcasted_iota(jnp.int32, edge.shape, 1)) == 0
+    edge = jnp.where(first, id_lanes[None, None, :], edge)
     edge = passed_along(edge, 1)
 
     fixed = lambda shape: pl.BlockSpec(shape, lambda c: (0,) * len(shape))
@@ -213,28 +247,25 @@
     kv_prev = passed_along(kv, 1)
     grad_next = passed_along(grad, -1)
 
-    out, qg, tail, part, long_part, short_part = pl.pallas_call(
+    out, qg, tail, part, packed = pl.pallas_call(
         mixer_kernel,
         grid=(chans // TILE,),
         in_specs=[
             fixed((1, rows)), wide3(taps),
             pl.BlockSpec((tile_groups, long_taps), lambda c: (c, 0)),
-            pl.BlockSpec((tile_groups, long_taps), lambda c: (c, 0)),
             wide3(rows), wide2(rows), wide3(EDGE), fixed((3, EDGE, TILE)), wide3(rows),
             wide2(rows), wide2(rows),
         ],
         out_specs=[
             wide2(rows), wide3(rows), wide3(EDGE), wide3(EDGE),
-            pl.BlockSpec((tile_groups, long_taps), lambda c: (c, 0)),
-            wide3(padded_taps),
+            pl.BlockSpec((TILE // chunk, packed_rows, chunk), lambda c: (c, 0, 0)),
         ],
         out_shape=[
             jax.ShapeDtypeStruct((rows, chans), BF16),
             jax.ShapeDtypeStruct((3, rows, chans), BF16),
             jax.ShapeDtypeStruct((3, EDGE, chans), F32),
             jax.ShapeDtypeStruct((3, EDGE, chans), BF16),
-            jax.ShapeDtypeStruct((groups, long_taps), F32),
-            jax.ShapeDtypeStruct((3, padded_taps, chans), F32),
+            jax.ShapeDtypeStruct((chans // chunk, packed_rows, chunk), BF16),
         ],
         scratch_shapes=[
             pltpu.VMEM(((taps - 1) * (rows + EDGE), rows), BF16),
@@ -247,26 +278,37 @@
             pltpu.VMEM((rows, TILE), F32),
             pltpu.VMEM((rows, TILE), F32),
             pltpu.VMEM((tile_groups, long_taps), F32),
+            pltpu.VMEM((tile_groups, long_taps), F32),
+            pltpu.VMEM((3, padded_taps, TILE), F32),
         ],
         compiler_params=params,
         name="mixer",
-    )(ids, sf, long_filter, lf_rev, qkv, cotangent, edge, edge, feats, kv_prev, grad_next)
+    )(ids, sf, long_filter, qkv, cotangent, edge, edge, feats, kv_prev, grad_next)
 
     part = passed_along(part, -1)
     qg = lax.dynamic_update_slice(qg, (tail + part.astype(F32)).astype(BF16), (0, rows - EDGE, 0))
 
     per = chans // devices
-    packed = jnp.concatenate(
-        [
-            short_part.reshape(3 * padded_taps, devices, per).transpose(1, 0, 2),
-            long_part.reshape(devices, -1, per),
-        ],
-        1,
-    )
-    packed = lax.all_to_all(packed, "ctx", 0, 0)
-    total = jnp.sum(packed, 0) * grad_scale
-    short_grad = total[: 3 * padded_taps].reshape(3, padded_taps, per)[:, :taps].transpose(0, 2, 1)
-    long_grad = total[3 * padded_taps :].reshape(groups // devices, long_taps)
+    if per == chunk:
+        got = lax.all_to_all(packed, "ctx", 0, 0)
+        long_grad, short_grad = pl.pallas_call(
+            functools.partial(finish_kernel, grad_scale, taps),
+            out_shape=[
+                jax.ShapeDtypeStruct((groups // devices, long_taps), F32),
+                jax.ShapeDtypeStruct((3, taps, per), F32),
+            ],
+            name="finish",
+        )(got)
+        return (out, qg, long_grad, short_grad.transpose(0, 2, 1))
+    head = 3 * padded_taps
+    short_part = packed[:, :head].transpose(1, 0, 2).reshape(head, devices, per)
+    long_part = packed[:, head:].reshape(-1, packed_rows - head, chunk // long_taps, long_taps)
+    long_part = long_part.transpose(0, 2, 1, 3).reshape(devices, -1, per)
+    got = jnp.concatenate([short_part.transpose(1, 0, 2), long_part], 1)
+    got = lax.all_to_all(got, "ctx", 0, 0)
+    total = jnp.sum(got.astype(F32), 0) * grad_scale
+    short_grad = total[:head].reshape(3, padded_taps, per)[:, :taps].transpose(0, 2, 1)
+    long_grad = total[head:].reshape(groups // devices, long_taps)
     return (out, qg, long_grad, short_grad)
 
 

time: 106 us -> 83.4 us (0.79)
  Pallas kernels: 39.8 us -> 27.5 us
  local copies, waits for them, and re-layouts: 13.1 us -> 2.3 us
    pallas_call x1, Pallas kernels: 33.8 us -> 19.7 us  [shards(): pl.pallas_call(mixer_kernel, grid=(chans // TILE,), in_specs=[fixed((1, r...]
    unnamed x29 -> x8, local copies, waits for them, and re-layouts: 7.64 us -> 2.29 us
    ppermute x4, waiting for transfers between devices: 19.3 us -> 22.4 us  [passed_along(): return lax.ppermute(block, 'ctx', route)]
    slice x4 -> x0, local copies, waits for them, and re-layouts: 3.18 us -> none  [the longest x2 2.24 us: shards(): lf_rev = jnp.roll(jnp.flip(long_filter, 1), 1, 1)]
    all_to_all x1, waiting for transfers between devices: 8.14 us -> 5.75 us  [shards(): got = lax.all_to_all(packed, 'ctx', 0, 0)]
    concatenate x2 -> x0, other arithmetic: 1.63 us -> none  [the longest x1 0.92 us: shards(): lf_rev = jnp.roll(jnp.flip(long_filter, 1), 1, 1)]
    reshape x4 -> x0, local copies, waits for them, and re-layouts: 1.57 us -> none  [the longest x1 0.9 us: shards(): long_part.reshape(devices, -1, per)]
    pallas_call x0 -> x1, Pallas kernels: none -> 1.53 us  [shards(): pl.pallas_call(functools.partial(finish_kernel, grad_scale, taps), out_sh...]
  transfers between devices with their start and end apart: 5 -> 5, of which waited for: 3 -> 3; matrix products, arithmetic and copies ran while one was open for 5% -> 2% of each run, Pallas kernels for 0% -> 0%
where the time goes in v2:
time: 83.4 us; the launch traced here: 83 us
  waiting for transfers between devices  28.2 us (34%)
  Pallas kernels  27.5 us (33%)
  starting transfers between devices  21.2 us (25%)
  other arithmetic  3.16 us (4%)
  local copies, waits for them, and re-layouts  2.3 us (3%)
    ppermute x4, waiting for transfers between devices, passed_along(): return lax.ppermute(block, 'ctx', route)  22.4 us
    pallas_call x1, Pallas kernels, shards(): pl.pallas_call(mixer_kernel, grid=(chans // TILE,), in_specs=[fixed((1, r...  19.7 us
    ppermute x4, starting transfers between devices, passed_along(): return lax.ppermute(block, 'ctx', route)  11.8 us
    all_to_all x1, starting transfers between devices, shards(): got = lax.all_to_all(packed, 'ctx', 0, 0)  9.44 us
    pallas_call x1, Pallas kernels, shards(): pl.pallas_call(feature_kernel, grid=(chans // TILE,), in_specs=[fixed((1,...  6.2 us
    all_to_all x1, waiting for transfers between devices, shards(): got = lax.all_to_all(packed, 'ctx', 0, 0)  5.75 us
    unnamed x8, local copies, waits for them, and re-layouts  2.29 us
  transfers between devices with their start and end apart: 5, of which 3 were waited for; matrix products, arithmetic and copies ran while one was open for 2% of the time, Pallas kernels for 0%

profile of v2, /device:TPU:0, one launch (start us, length us, event | category | flops | bytes accessed | tf_op | source)
XLA Modules:
  0.0 83.0 jit_solution(3032748622633220647)
XLA Ops:
  0.6 0.7 convert_element_type.11
  1.3 0.9 %fusion = bf16[3,8,2048]{2,1,0:T(8,128)(2,1)S(1)} fusion(bf16[3,128,2048]{2,1,0:T(8,128)(2,1)} %x_ref.3, bf16[2048]{0:T(1024)(128)(2,1)S(1)} %pad.4), kind=kLoop, calls=%fused_computation.2 | loop fusion | flops 147456 | bytes 200704 | tf_op jit(solution)/shard_map/jit(_where)/select_n | solution.py:223
  2.2 4.8 %collective-permute-start = (bf16[3,8,2048]{2,1,0:T(8,128)(2,1)S(1)}, bf16[3,8,2048]{2,1,0:T(8,128)(2,1)S(1)}, u32[]{:S(2)}, u32[]{:S(2)}) collective-permute-start(bf16[3,8,2048]{2,1,0:T(8,128)(2,1)S(1)} %fusion), channel_id=1, source_target_pairs={{0,4},{4,8},{8,12},{12,16},{16,20},{20,24},{24,28},{1,5},{5,9},{9,... | collective-permute-start | bytes 294920 | tf_op jit(solution)/shard_map/ppermute | solution.py:20
  7.1 2.2 %collective-permute-done.edge_ref.ids_edge_ref = bf16[3,8,2048]{2,1,0:T(8,128)(2,1)S(1)} collective-permute-done((bf16[3,8,2048]{2,1,0:T(8,128)(2,1)S(1)}, bf16[3,8,2048]{2,1,0:T(8,128)(2,1)S(1)}, u32[]{:S(2)}, u32[]{:S(2)}) %collective-permute-start) | collective-permute-done | bytes 98336 | tf_op jit(solution)/shard_map/ppermute | solution.py:20
  9.3 0.0 copy-start
  9.3 0.6 copy-done
  9.9 6.2 %features.1 = (f32[3,128,2048]{2,1,0:T(8,128)}, bf16[128,2048]{1,0:T(8,128)(2,1)}, bf16[128,2048]{1,0:T(8,128)(2,1)}) custom-call(s32[1,128]{1,0:T(1,128)} %bitcast.5, f32[3,7,2048]{2,1,0:T(8,128)} %bitcast.3, bf16[3,128,2048]{2,1,0:T(8,128)(2,1)} %x_ref.3, bf16[128,2048]{1,0:T(8,128)(2,1)} %cot_ref.3, bf16[3,8,2048]{2,1,0:T(8,128)(2,1)} %copy-done, ...), custom_call_target="tpu_custom_call" | custom-call | tf_op jit(solution)/shard_map/features/pallas_call | solution.py:229
  16.1 4.3 %collective-permute-start.1 = (bf16[128,2048]{1,0:T(8,128)(2,1)}, bf16[128,2048]{1,0:T(8,128)(2,1)S(1)}, u32[]{:S(2)}, u32[]{:S(2)}) collective-permute-start(bf16[128,2048]{1,0:T(8,128)(2,1)} %get-tuple-element.15), channel_id=1, source_target_pairs={{0,4},{4,8},{8,12},{12,16},{16,20},{20,24},{24,28},{1,5},{5,9},{9,... | collective-permute-start | bytes 1572872 | tf_op jit(solution)/shard_map/ppermute | solution.py:20
  20.4 1.3 %collective-permute-start.2 = (bf16[128,2048]{1,0:T(8,128)(2,1)}, bf16[128,2048]{1,0:T(8,128)(2,1)S(1)}, u32[]{:S(2)}, u32[]{:S(2)}) collective-permute-start(bf16[128,2048]{1,0:T(8,128)(2,1)} %get-tuple-element.16), channel_id=1, source_target_pairs={{4,0},{8,4},{12,8},{16,12},{20,16},{24,20},{28,24},{5,1},{9,5},{13... | collective-permute-start | bytes 1572872 | tf_op jit(solution)/shard_map/ppermute | solution.py:20
  21.7 20.2 %collective-permute-done.1.kvp_ref = bf16[128,2048]{1,0:T(8,128)(2,1)S(1)} collective-permute-done((bf16[128,2048]{1,0:T(8,128)(2,1)}, bf16[128,2048]{1,0:T(8,128)(2,1)S(1)}, u32[]{:S(2)}, u32[]{:S(2)}) %collective-permute-start.1) | collective-permute-done | bytes 524320 | tf_op jit(solution)/shard_map/ppermute | solution.py:20
  42.0 0.0 copy-start.2
  42.0 0.0 collective-permute-done.2.gn_ref
  42.0 0.0 copy-start.3
  42.0 0.8 copy-done.2
  42.8 0.2 copy-done.3
  43.0 19.7 %mixer.1 = (bf16[128,2048]{1,0:T(8,128)(2,1)}, bf16[3,128,2048]{2,1,0:T(8,128)(2,1)}, f32[3,8,2048]{2,1,0:T(8,128)}, bf16[3,8,2048]{2,1,0:T(8,128)(2,1)}, bf16[8,32,256]{2,1,0:T(8,128)(2,1)}) custom-call(s32[1,128]{1,0:T(1,128)} %bitcast.6, f32[3,7,2048]{2,1,0:T(8,128)} %bitcast.4, f32[128,128]{1,0:T(8,128)} %lf_ref.1, bf16[3,128,2048]{2,1,0:T(8,128)(2,1)} %x_ref.3, ...), custom_call_target="tpu_custom_call" | custom-call | tf_op jit(solution)/shard_map/mixer/pallas_call | solution.py:250
  62.7 1.3 %collective-permute-start.3 = (bf16[3,8,2048]{2,1,0:T(8,128)(2,1)}, bf16[3,8,2048]{2,1,0:T(8,128)(2,1)S(1)}, u32[]{:S(2)}, u32[]{:S(2)}) collective-permute-start(bf16[3,8,2048]{2,1,0:T(8,128)(2,1)} %get-tuple-element.20), channel_id=1, source_target_pairs={{4,0},{8,4},{12,8},{16,12},{20,16},{24,20},{28,24},{5,1},{9,5},{13... | collective-permute-start | bytes 294920 | tf_op jit(solution)/shard_map/ppermute | solution.py:20
  64.0 9.4 %all-to-all-start = ((bf16[8,32,256]{2,1,0:T(8,128)(2,1)}), bf16[8,32,256]{2,1,0:T(8,128)(2,1)S(1)}, u32[]{:S(2)}, u32[]{:S(2)}) async-start(bf16[8,32,256]{2,1,0:T(8,128)(2,1)} %get-tuple-element.21), calls=%async_computation | async-start | bytes 262144 | tf_op jit(solution)/shard_map/all_to_all | solution.py:293
  73.4 0.0 collective-permute-done.3
  73.5 1.6 %fusion.1 = bf16[3,128,2048]{2,1,0:T(8,128)(2,1)} fusion(bf16[3,128,2048]{2,1,0:T(8,128)(2,1)} %get-tuple-element.18, f32[3,8,2048]{2,1,0:T(8,128)} %get-tuple-element.19, bf16[3,8,2048]{2,1,0:T(8,128)(2,1)S(1)} %collective-permute-done.3), kind=kLoop, calls=%fused_computation.3 | loop fusion | flops 147456 | bytes 393216 | tf_op jit(solution)/shard_map/dynamic_update_slice | solution.py:289
  75.0 5.7 %all-to-all-done.got_ref = bf16[8,32,256]{2,1,0:T(8,128)(2,1)S(1)} async-done(((bf16[8,32,256]{2,1,0:T(8,128)(2,1)}), bf16[8,32,256]{2,1,0:T(8,128)(2,1)S(1)}, u32[]{:S(2)}, u32[]{:S(2)}) %all-to-all-start) | async-done | bytes 131104 | tf_op jit(solution)/shard_map/all_to_all | solution.py:293
  80.8 0.0 copy-start.1
  80.8 0.6 copy-done.1
  81.4 1.5 %finish.1 = (f32[16,128]{1,0:T(8,128)}, f32[3,7,256]{2,1,0:T(8,128)}) custom-call(bf16[8,32,256]{2,1,0:T(8,128)(2,1)} %copy-done.1), custom_call_target="tpu_custom_call" | custom-call | tf_op jit(solution)/shard_map/finish/pallas_call | solution.py:294
  (1 shorter events, 0.0 us)
Async XLA Ops:
  2.2 7.0 %collective-permute-start = (bf16[3,8,2048]{2,1,0:T(8,128)(2,1)S(1)}, bf16[3,8,2048]{2,1,0:T(8,128)(2,1)S(1)}, u32[]{:S(2)}, u32[]{:S(2)}) collective-permute-start(bf16[3,8,2048]{2,1,0:T(8,128)(2,1)S(1)} %fusion), channel_id=1, source_target_pairs={{0,4},{4,8},{8,12},{12,16},{16,20},{20,24},{24,28},{1,5},{5,9},{9,... | collective-permute-start | bytes 294920 | tf_op jit(solution)/shard_map/ppermute | solution.py:20
  9.3 0.7 copy-start
  16.1 25.9 %collective-permute-start.1 = (bf16[128,2048]{1,0:T(8,128)(2,1)}, bf16[128,2048]{1,0:T(8,128)(2,1)S(1)}, u32[]{:S(2)}, u32[]{:S(2)}) collective-permute-start(bf16[128,2048]{1,0:T(8,128)(2,1)} %get-tuple-element.15), channel_id=1, source_target_pairs={{0,4},{4,8},{8,12},{12,16},{16,20},{20,24},{24,28},{1,5},{5,9},{9,... | collective-permute-start | bytes 1572872 | tf_op jit(solution)/shard_map/ppermute | solution.py:20
  20.4 21.5 %collective-permute-start.2 = (bf16[128,2048]{1,0:T(8,128)(2,1)}, bf16[128,2048]{1,0:T(8,128)(2,1)S(1)}, u32[]{:S(2)}, u32[]{:S(2)}) collective-permute-start(bf16[128,2048]{1,0:T(8,128)(2,1)} %get-tuple-element.16), channel_id=1, source_target_pairs={{4,0},{8,4},{12,8},{16,12},{20,16},{24,20},{28,24},{5,1},{9,5},{13... | collective-permute-start | bytes 1572872 | tf_op jit(solution)/shard_map/ppermute | solution.py:20
  42.0 0.8 copy-start.2
  42.0 1.0 %copy-start.3 = (bf16[128,2048]{1,0:T(8,128)(2,1)}, bf16[128,2048]{1,0:T(8,128)(2,1)S(1)}, u32[]{:S(2)}) copy-start(bf16[128,2048]{1,0:T(8,128)(2,1)S(1)} %collective-permute-done.2.gn_ref) | copy-start | bytes 1572868
  62.7 10.7 %collective-permute-start.3 = (bf16[3,8,2048]{2,1,0:T(8,128)(2,1)}, bf16[3,8,2048]{2,1,0:T(8,128)(2,1)S(1)}, u32[]{:S(2)}, u32[]{:S(2)}) collective-permute-start(bf16[3,8,2048]{2,1,0:T(8,128)(2,1)} %get-tuple-element.20), channel_id=1, source_target_pairs={{4,0},{8,4},{12,8},{16,12},{20,16},{24,20},{28,24},{5,1},{9,5},{13... | collective-permute-start | bytes 294920 | tf_op jit(solution)/shard_map/ppermute | solution.py:20
  64.0 16.8 %all-to-all-start = ((bf16[8,32,256]{2,1,0:T(8,128)(2,1)}), bf16[8,32,256]{2,1,0:T(8,128)(2,1)S(1)}, u32[]{:S(2)}, u32[]{:S(2)}) async-start(bf16[8,32,256]{2,1,0:T(8,128)(2,1)} %get-tuple-element.21), calls=%async_computation | async-start | bytes 262144 | tf_op jit(solution)/shard_map/all_to_all | solution.py:293
  80.8 0.7 copy-start.1

commit v3 on v2

v3 whole, which is shorter than its diff:
```python
import functools
import math

import jax
import jax.numpy as jnp
from jax import lax
from jax.experimental import pallas as pl
from jax.experimental.pallas import tpu as pltpu
from jax.sharding import PartitionSpec as P

F32 = jnp.float32
BF16 = jnp.bfloat16
EDGE = 8
LANES = 512
CHUNK = 256
PADDED = 8
PARTS = 2

VMEM = pl.BlockSpec(memory_space=pltpu.VMEM)
ANY = pl.BlockSpec(memory_space=pl.ANY)
HBM = pl.BlockSpec(memory_space=pltpu.HBM)


def passed_along(block, distance):
    devices = range(lax.axis_size("ctx"))
    route = [(i - distance, i) for i in devices if i - distance in devices]
    return lax.ppermute(block, "ctx", route)


def iota2(shape, dim):
    return lax.broadcasted_iota(jnp.int32, shape, dim)


def dot(a, b):
    return jnp.dot(a, b, preferred_element_type=F32)


def lane_range(start, size):
    return pl.ds(pl.multiple_of(start, size), size)


def ones_where(cond):
    return jnp.where(cond, 1.0, 0.0)


def prepare_kernel(ids_ref, lf_ref, delay_ref, advance_ref, lfr_ref):
    rows = delay_ref.shape[1]
    taps = delay_ref.shape[0] // rows + 1
    id_row = jnp.broadcast_to(ids_ref[...], (rows, rows)).astype(F32)
    same = id_row == id_row.T
    lag = iota2((rows, rows), 0) - iota2((rows, rows), 1)
    for t in range(1, taps):
        delay_ref[(t - 1) * rows : t * rows] = ones_where((lag == t) & same).astype(BF16)
        advance_ref[(t - 1) * rows : t * rows] = ones_where((lag == -t) & same).astype(BF16)
    backward = ones_where((iota2((rows, rows), 0) + iota2((rows, rows), 1)) % rows == 0)
    lfr_ref[...] = dot(lf_ref[...].astype(BF16), backward.astype(BF16))


def feature_kernel(first, ids_ref, delay_ref, edge_ref, sf_hbm, x_hbm, cot_hbm,
                   feat_ref, kv_ref, g_ref, edge_shift, sf_ref, x_ref, cot_ref, sems):
    rows = x_ref.shape[1]
    taps = sf_ref.shape[1]
    steps = kv_ref.shape[1] // LANES

    def loads(p):
        near = lane_range(p * LANES, LANES)
        cols = lane_range(first + p * LANES, LANES)
        pairs = [
            (sf_hbm.at[:, :, cols], sf_ref.at[:, :, near]),
            (x_hbm.at[:, :, cols], x_ref.at[:, :, near]),
            (cot_hbm.at[:, cols], cot_ref.at[:, near]),
        ]
        return [pltpu.make_async_copy(src, dst, sems.at[k, p]) for k, (src, dst) in enumerate(pairs)]

    for p in range(steps):
        for copy in loads(p):
            copy.start()
    id_row = jnp.broadcast_to(ids_ref[...], (rows, rows)).astype(F32)
    head_ids = id_row.T[0:EDGE]
    before = jnp.broadcast_to(edge_ref[0, 0:1, 0:rows].astype(F32), (EDGE, rows))
    before = pltpu.roll(before, EDGE, 1)
    lag = iota2((EDGE, rows), 0) + EDGE - iota2((EDGE, rows), 1)
    for t in range(1, taps):
        edge_shift[(t - 1) * EDGE : t * EDGE] = ones_where((lag == t) & (before == head_ids))
    id_wide = jnp.concatenate([ids_ref[...].astype(F32)] * (LANES // rows), 1)

    def one_step(p, carry):
        near = lane_range(p * LANES, LANES)
        cols = lane_range(first + p * LANES, LANES)
        for copy in loads(p):
            copy.wait()
        feats = []
        for i in range(3):
            x = x_ref[i, :, near]
            w = sf_ref[i, :, near]
            moved = dot(delay_ref[...], x)
            acc = w[0:1] * x.astype(F32)
            for t in range(1, taps):
                acc = acc + w[t : t + 1] * moved[(t - 1) * rows : t * rows]
            edge = edge_ref[i, :, cols].astype(F32)
            edge = jnp.concatenate([edge, jnp.zeros((rows - EDGE, LANES), F32)], 0)
            moved = dot(edge_shift[...].astype(BF16), edge.astype(BF16))
            fix = w[1:2] * moved[0:EDGE]
            for t in range(2, taps):
                fix = fix + w[t : t + 1] * moved[(t - 1) * EDGE : t * EDGE]
            acc = jnp.concatenate([acc[0:EDGE] + fix, acc[EDGE:]], 0)
            feat_ref[i, :, near] = acc
            feats.append(acc)
        kv_ref[:, near] = (feats[1] * feats[2]).astype(BF16)
        g = cot_ref[:, near].astype(F32) * feats[0]
        last = iota2(g.shape, 0) == rows - 1
        g_ref[:, near] = jnp.where(last, jnp.broadcast_to(id_wide, g.shape), g).astype(BF16)
        return carry

    lax.fori_loop(0, steps, one_step, 0)


def mixer_kernel(first, filled, ids_ref, sf_ref, lf_ref, lfr_ref, advance_ref, x_ref, cot_ref, edge_ref,
                 feat_ref, kvp_ref, gn_ref, *refs):
    (out_hbm, qg_hbm, tail_hbm, part_hbm, packed_hbm, out_ref, qg_ref, tail_ref, part_ref, packed_ref,
     edge_shift, mask_y, mask_g, mask_a, w_kv, w_g, g_rev, dh_ref, y_ref, gm_ref, sems) = refs[filled:]
    rows = x_ref.shape[1]
    taps = sf_ref.shape[1]
    count = kvp_ref.shape[1]
    width = x_ref.shape[2] // lf_ref.shape[0]
    half = rows
    per = half // width
    lag = iota2((rows, rows), 0) - iota2((rows, rows), 1)
    flip = ones_where(iota2((rows, rows), 0) + iota2((rows, rows), 1) == rows - 1)
    mirror = flip.astype(BF16)
    id_row = jnp.broadcast_to(ids_ref[...], (rows, rows)).astype(F32)
    id_col = id_row.T
    prev_row = jnp.broadcast_to(edge_ref[0, 0:1, 0:rows].astype(F32), (rows, rows))
    next_row = jnp.broadcast_to(gn_ref[rows - 1 : rows, 0:rows].astype(F32), (rows, rows))
    same = id_row == id_col
    mask_y[:, 0:rows] = ones_where((lag >= 0) & same).astype(BF16)
    mask_y[:, rows:] = ones_where((lag < 0) & (prev_row == id_col)).astype(BF16)
    mask_g[:, 0:rows] = ones_where((lag <= 0) & same).astype(BF16)
    mask_g[:, rows:] = ones_where((lag > 0) & (next_row == id_col)).astype(BF16)
    mask_a[...] = dot(mirror, mask_y[...])
    lag_edge = iota2((EDGE, rows), 1) + EDGE - iota2((EDGE, rows), 0)
    same_edge = prev_row.T[rows - EDGE :] == id_row[0:EDGE]
    pieces = [ones_where((lag_edge == t) & same_edge) for t in range(1, taps)]
    edge_shift[...] = jnp.concatenate(pieces, 0).astype(BF16)
    owner = iota2((rows, half), 1) // width
    blocks = LANES // CHUNK

    def copies(p):
        near = lane_range(p * LANES, LANES)
        cols = lane_range(first + p * LANES, LANES)
        pairs = [
            (out_ref.at[:, near], out_hbm.at[:, cols]),
            (qg_ref.at[:, :, near], qg_hbm.at[:, :, cols]),
            (tail_ref.at[:, :, near], tail_hbm.at[:, :, cols]),
            (part_ref.at[:, :, near], part_hbm.at[:, :, cols]),
            (packed_ref.at[pl.ds(p * blocks, blocks)], packed_hbm.at[pl.ds(first // CHUNK + p * blocks, blocks)]),
        ]
        return [pltpu.make_async_copy(src, dst, sems.at[k, p]) for k, (src, dst) in enumerate(pairs)]

    def one_step(p, carry):
        near = lane_range(p * LANES, LANES)
        cols = lane_range(first + p * LANES, LANES)
        cot = cot_ref[:, cols].astype(F32)
        w_kv[0:rows] = (feat_ref[1, :, near] * feat_ref[2, :, near]).astype(BF16)
        w_kv[rows:] = kvp_ref[:, near]
        w_g[0:rows] = (cot * feat_ref[0, :, near]).astype(BF16)
        w_g[rows:] = gn_ref[:, near]
        g_rev[...] = dot(mirror, w_g[0:rows]).astype(BF16)
        for q in range(LANES // half):
            part = slice(q * half, (q + 1) * half)
            base = pl.multiple_of((first // half) * per + p * (LANES // width) + q * per, per)
            for j in range(per):
                mine = owner == j
                fwd = jnp.broadcast_to(lfr_ref[pl.ds(base + j, 1), :], (rows, rows))
                fwd = pltpu.roll(fwd, 0, 1, stride=1, stride_axis=0).astype(BF16)
                t_y = jnp.concatenate([fwd, fwd], 1) * mask_y[...]
                pltpu.store(y_ref.at[:, part], dot(t_y, w_kv[:, part]), mask=mine)
                bwd = jnp.broadcast_to(lf_ref[pl.ds(base + j, 1), :], (rows, rows))
                bwd = pltpu.roll(bwd, 0, 1, stride=1, stride_axis=0).astype(BF16)
                t_g = jnp.concatenate([bwd, bwd], 1) * mask_g[...]
                pltpu.store(gm_ref.at[:, part], dot(t_g, w_g[:, part]), mask=mine)
                g_sel = jnp.where(mine, g_rev[:, part], jnp.zeros((rows, half), BF16))
                cross = lax.dot_general(
                    g_sel, w_kv[:, part], (((1,), (1,)), ((), ())), preferred_element_type=F32
                ) * mask_a[...]
                folded = cross[:, 0:rows] + cross[:, rows:]
                folded = pltpu.roll(folded, 0, 1, stride=1, stride_axis=0)
                dh_ref[q * per + j : q * per + j + 1] = jnp.sum(folded, 0, keepdims=True)
        dh = jnp.dot(dh_ref[...], flip, preferred_element_type=F32, precision=lax.Precision.HIGHEST)
        y = y_ref[...]
        gm = gm_ref[...]
        out_ref[:, near] = (feat_ref[0, :, near] * y).astype(BF16)
        heads = []
        for i in range(3):
            gf = cot * y if i == 0 else gm * feat_ref[3 - i, :, near]
            w = sf_ref[i, :, cols]
            x = x_ref[i, :, cols].astype(F32)
            xe = edge_ref[i, :, cols].astype(F32)
            gf_sent = gf.astype(BF16)
            moved = dot(advance_ref[...], gf_sent)
            moved_edge = dot(edge_shift[...], gf_sent)
            acc = w[0:1] * gf
            sums = [jnp.sum(x * gf, 0, keepdims=True)]
            sent = jnp.zeros((EDGE, LANES), F32)
            for t in range(1, taps):
                piece = moved[(t - 1) * rows : t * rows]
                piece_edge = moved_edge[(t - 1) * EDGE : t * EDGE]
                acc = acc + w[t : t + 1] * piece
                sent = sent + w[t : t + 1] * piece_edge
                sums.append(jnp.sum(x * piece, 0, keepdims=True) + jnp.sum(xe * piece_edge, 0, keepdims=True))
            sums.append(jnp.zeros((PADDED - taps, LANES), F32))
            qg_ref[i, :, near] = acc.astype(BF16)
            tail_ref[i, :, near] = acc[rows - EDGE :]
            part_ref[i, :, near] = sent.astype(BF16)
            heads.append(jnp.concatenate(sums, 0))
        size = dh.shape[0] * rows // LANES
        for k in range(blocks):
            picked = [head[:, k * CHUNK : (k + 1) * CHUNK] for head in heads]
            lines = range(k * (CHUNK // rows), (k + 1) * (CHUNK // rows))
            picked.append(jnp.concatenate([dh[e * size : (e + 1) * size] for e in lines], 1))
            packed_ref[p * blocks + k] = jnp.concatenate(picked, 0).astype(BF16)
        for copy in copies(p):
            copy.start()
        return carry

    def drain(p, carry):
        for copy in copies(p):
            copy.wait()
        return carry

    lax.fori_loop(0, count // LANES, one_step, 0)
    lax.fori_loop(0, count // LANES, drain, 0)


def finish_kernel(scale, taps, got_ref, long_ref, short_ref):
    total = got_ref[0].astype(F32)
    for k in range(1, got_ref.shape[0]):
        total = total + got_ref[k].astype(F32)
    total = total * scale
    for i in range(3):
        short_ref[i] = total[i * PADDED : i * PADDED + taps]
    size = total.shape[0] - 3 * PADDED
    lags = long_ref.shape[1]
    for p in range(total.shape[1] // lags):
        long_ref[p * size : (p + 1) * size] = total[3 * PADDED :, p * lags : (p + 1) * lags]


def shards(qkv, cotangent, doc_ids, short_filter, long_filter):
    _, rows, chans = qkv.shape
    groups, long_taps = long_filter.shape
    taps = short_filter.shape[2]
    devices = lax.axis_size("ctx")
    grad_scale = 1.0 / math.sqrt(rows * devices)
    packed_rows = 3 * PADDED + groups * long_taps // chans
    step_groups = LANES * groups // chans
    params = pltpu.CompilerParams(vmem_limit_bytes=24 << 20)

    ids = doc_ids.reshape(1, rows)
    sf = jnp.transpose(short_filter, (0, 2, 1))

    edge = qkv[:, rows - EDGE :, :]
    id_lanes = jnp.broadcast_to(doc_ids.astype(BF16), (chans // rows, rows)).reshape(chans)
    first = (lax.broadcasted_iota(jnp.int32, edge.shape, 0) + lax.broadcasted_iota(jnp.int32, edge.shape, 1)) == 0
    edge = jnp.where(first, id_lanes[None, None, :], edge)
    edge = passed_along(edge, 1)

    shifts = ((taps - 1) * rows, rows)
    delay, advance, lf_rev = pl.pallas_call(
        prepare_kernel,
        in_specs=[VMEM] * 2,
        out_specs=[VMEM] * 3,
        out_shape=[
            jax.ShapeDtypeStruct(shifts, BF16),
            jax.ShapeDtypeStruct(shifts, BF16),
            jax.ShapeDtypeStruct((groups, long_taps), F32),
        ],
        cost_estimate=pl.CostEstimate(flops=6_000_000_000, bytes_accessed=16_000_000, transcendentals=0),
        compiler_params=pltpu.CompilerParams(vmem_limit_bytes=8 << 20),
        name="prepare",
    )(ids, long_filter)

    count = chans // PARTS
    sent = []
    for part in range(PARTS):
        feats, kv, grad = pl.pallas_call(
            functools.partial(feature_kernel, part * count),
            in_specs=[VMEM] * 3 + [HBM] * 3,
            out_specs=[VMEM] * 3,
            out_shape=[
                jax.ShapeDtypeStruct((3, rows, count), F32),
                jax.ShapeDtypeStruct((rows, count), BF16),
                jax.ShapeDtypeStruct((rows, count), BF16),
            ],
            scratch_shapes=[
                pltpu.VMEM(((taps - 1) * EDGE, rows), F32),
                pltpu.VMEM((3, taps, count), F32),
                pltpu.VMEM((3, rows, count), BF16),
                pltpu.VMEM((rows, count), BF16),
                pltpu.SemaphoreType.DMA((3, count // LANES)),
            ],
            compiler_params=params,
            cost_estimate=pl.CostEstimate(flops=2_000_000_000, bytes_accessed=4_000_000, transcendentals=0),
            name="features",
        )(ids, delay, edge, sf, qkv, cotangent)
        sent.append((feats, passed_along(kv, 1), passed_along(grad, -1)))

    results = []
    full = [
        jax.ShapeDtypeStruct((rows, chans), BF16),
        jax.ShapeDtypeStruct((3, rows, chans), BF16),
        jax.ShapeDtypeStruct((3, EDGE, chans), F32),
        jax.ShapeDtypeStruct((3, EDGE, chans), BF16),
        jax.ShapeDtypeStruct((chans // CHUNK, packed_rows, CHUNK), BF16),
    ]
    for part in range(PARTS):
        feats, kv_prev, grad_next = sent[part]
        filled = len(results)
        results = pl.pallas_call(
            functools.partial(mixer_kernel, part * count, filled),
            in_specs=[VMEM] * 11 + [ANY] * filled,
            out_specs=[ANY] * 5,
            out_shape=full,
            input_output_aliases={11 + k: k for k in range(filled)},
            scratch_shapes=[
                pltpu.VMEM((rows, count), BF16),
                pltpu.VMEM((3, rows, count), BF16),
                pltpu.VMEM((3, EDGE, count), F32),
                pltpu.VMEM((3, EDGE, count), BF16),
                pltpu.VMEM((count // CHUNK, packed_rows, CHUNK), BF16),
                pltpu.VMEM(((taps - 1) * EDGE, rows), BF16),
                pltpu.VMEM((rows, 2 * rows), BF16),
                pltpu.VMEM((rows, 2 * rows), BF16),
                pltpu.VMEM((rows, 2 * rows), F32),
                pltpu.VMEM((2 * rows, LANES), BF16),
                pltpu.VMEM((2 * rows, LANES), BF16),
                pltpu.VMEM((rows, LANES), BF16),
                pltpu.VMEM((step_groups, long_taps), F32),
                pltpu.VMEM((rows, LANES), F32),
                pltpu.VMEM((rows, LANES), F32),
                pltpu.SemaphoreType.DMA((5, count // LANES)),
            ],
            compiler_params=params,
            cost_estimate=pl.CostEstimate(flops=8_000_000_000, bytes_accessed=8_000_000, transcendentals=0),
            name="mixer",
        )(ids, sf, long_filter, lf_rev, advance, qkv, cotangent, edge, feats, kv_prev, grad_next, *results)
    out, qg, tail, part, packed = results

    part = passed_along(part, -1)
    qg = lax.dynamic_update_slice(qg, (tail + part.astype(F32)).astype(BF16), (0, rows - EDGE, 0))

    per = chans // devices
    if per == CHUNK:
        got = lax.all_to_all(packed, "ctx", 0, 0)
        long_grad, short_grad = pl.pallas_call(
            functools.partial(finish_kernel, grad_scale, taps),
            in_specs=[VMEM],
            out_specs=[VMEM] * 2,
            out_shape=[
                jax.ShapeDtypeStruct((groups // devices, long_taps), F32),
                jax.ShapeDtypeStruct((3, taps, per), F32),
            ],
            compiler_params=pltpu.CompilerParams(vmem_limit_bytes=8 << 20),
            cost_estimate=pl.CostEstimate(flops=1_000_000, bytes_accessed=200_000, transcendentals=0),
            name="finish",
        )(got)
        return (out, qg, long_grad, short_grad.transpose(0, 2, 1))
    head = 3 * PADDED
    short_part = packed[:, :head].transpose(1, 0, 2).reshape(head, devices, per)
    long_part = packed[:, head:].reshape(-1, packed_rows - head, CHUNK // long_taps, long_taps)
    long_part = long_part.transpose(0, 2, 1, 3).reshape(devices, -1, per)
    got = jnp.concatenate([short_part.transpose(1, 0, 2), long_part], 1)
    got = lax.all_to_all(got, "ctx", 0, 0)
    total = jnp.sum(got.astype(F32), 0) * grad_scale
    short_grad = total[:head].reshape(3, PADDED, per)[:, :taps].transpose(0, 2, 1)
    long_grad = total[head:].reshape(groups // devices, long_taps)
    return (out, qg, long_grad, short_grad)


def solution(mesh):
    in_specs = (P(None, "ctx", "tp"), P("ctx", "tp"), P("ctx"), P(None, "tp", None), P("tp", None))
    out_specs = (
        P("ctx", "tp"),
        P(None, "ctx", "tp"),
        P(("tp", "ctx"), None),
        P(None, ("tp", "ctx"), None),
    )
    return jax.shard_map(shards, mesh=mesh, in_specs=in_specs, out_specs=out_specs, check_vma=False)
```

time: 83.4 us -> 65.4 us (0.78)
  waiting for transfers between devices: 28.2 us -> 12.3 us
  Pallas kernels: 27.5 us -> 19.2 us
  starting transfers between devices: 21.2 us -> 28 us
  other arithmetic: 3.16 us -> 2.23 us
    ppermute x4 -> x6, waiting for transfers between devices: 22.4 us -> 5.59 us  [passed_along(): return lax.ppermute(block, 'ctx', route)]
    pallas_call x3 -> x6, Pallas kernels: 27.5 us -> 19.2 us  [the longest x2 14.5 us: shards(): pl.pallas_call(functools.partial(mixer_kernel, part * count, filled), in_...]
    ppermute x4 -> x6, starting transfers between devices: 11.8 us -> 17.3 us  [passed_along(): return lax.ppermute(block, 'ctx', route)]
    all_to_all x1, starting transfers between devices: 9.44 us -> 10.7 us  [shards(): got = lax.all_to_all(packed, 'ctx', 0, 0)]
    dynamic_update_slice x1, other arithmetic: 1.59 us -> 0.66 us  [shards(): lax.dynamic_update_slice(qg, (tail + part.astype(F32)).astype(BF16), (0,...]
    all_to_all x1, waiting for transfers between devices: 5.75 us -> 6.67 us  [shards(): got = lax.all_to_all(packed, 'ctx', 0, 0)]
    unnamed x8 -> x14, local copies, waits for them, and re-layouts: 2.29 us -> 2.37 us
  transfers between devices with their start and end apart: 5 -> 7, of which waited for: 3 -> 4; matrix products, arithmetic and copies ran while one was open for 2% -> 1% of each run, Pallas kernels for 0% -> 14%
where the time goes in v3:
time: 65.4 us; the launch traced here: 64.9 us
  starting transfers between devices  28 us (43%)
  Pallas kernels  19.2 us (29%)
  waiting for transfers between devices  12.3 us (19%)
  local copies, waits for them, and re-layouts  2.37 us (4%)
  other arithmetic  2.23 us (3%)
  between operations  0.75 us (1%)
    ppermute x6, starting transfers between devices, passed_along(): return lax.ppermute(block, 'ctx', route)  17.3 us
    pallas_call x2, Pallas kernels, shards(): pl.pallas_call(functools.partial(mixer_kernel, part * count, filled), in_...  14.5 us
    all_to_all x1, starting transfers between devices, shards(): got = lax.all_to_all(packed, 'ctx', 0, 0)  10.7 us
    all_to_all x1, waiting for transfers between devices, shards(): got = lax.all_to_all(packed, 'ctx', 0, 0)  6.67 us
    ppermute x6, waiting for transfers between devices, passed_along(): return lax.ppermute(block, 'ctx', route)  5.59 us
    pallas_call x2, Pallas kernels, shards(): pl.pallas_call(functools.partial(feature_kernel, part * count), in_specs=...  3.93 us
    unnamed x14, local copies, waits for them, and re-layouts  2.37 us
  transfers between devices with their start and end apart: 7, of which 4 were waited for; matrix products, arithmetic and copies ran while one was open for 1% of the time, Pallas kernels for 14%

profile of v3, /device:TPU:0, one launch (start us, length us, event | category | flops | bytes accessed | tf_op | source)
XLA Modules:
  0.0 64.9 jit_solution(6838446606714676982)
XLA Ops:
  0.6 0.7 %convert_element_type.9 = bf16[128]{0:T(256)(128)(2,1)S(1)} convert(s32[128]{0:T(128)} %param.7) | non-fusion elementwise | flops 128 | bytes 768 | tf_op jit(solution)/shard_map/convert_element_type | solution.py:262
  1.3 0.9 %fusion = bf16[3,8,2048]{2,1,0:T(8,128)(2,1)S(1)} fusion(bf16[3,128,2048]{2,1,0:T(8,128)(2,1)} %x_ref.3, bf16[2048]{0:T(1024)(128)(2,1)S(1)} %broadcast_bitcast_fusion), kind=kLoop, calls=%fused_computation.2 | loop fusion | flops 147456 | bytes 200704 | tf_op jit(solution)/shard_map/jit(_where)/select_n | solution.py:264
  2.2 4.8 %collective-permute-start = (bf16[3,8,2048]{2,1,0:T(8,128)(2,1)S(1)}, bf16[3,8,2048]{2,1,0:T(8,128)(2,1)S(1)}, u32[]{:S(2)}, u32[]{:S(2)}) collective-permute-start(bf16[3,8,2048]{2,1,0:T(8,128)(2,1)S(1)} %fusion), channel_id=1, source_target_pairs={{0,4},{4,8},{8,12},{12,16},{16,20},{20,24},{24,28},{1,5},{5,9},{9,... | collective-permute-start | bytes 294920 | tf_op jit(solution)/shard_map/ppermute | solution.py:27
  7.1 0.0 copy-start.3
  7.1 0.8 %copy-done.3 = f32[128,128]{1,0:T(8,128)S(1)} copy-done((f32[128,128]{1,0:T(8,128)S(1)}, f32[128,128]{1,0:T(8,128)}, u32[]{:S(2)}) %copy-start.3) | copy-done | bytes 65560
  7.9 0.0 copy-start.5
  7.9 0.7 %copy-done.5 = s32[128]{0:T(128)S(1)} copy-done((s32[128]{0:T(128)S(1)}, s32[128]{0:T(128)}, u32[]{:S(2)}) %copy-start.5) | copy-done | bytes 536
  8.6 0.0 copy-start
  8.6 0.0 copy-start.1
  8.6 0.0 copy-start.2
  8.6 0.0 copy-start.6
  8.6 0.2 prepare.1
  8.7 0.5 collective-permute-done.edge_ref
  9.3 0.7 %copy-done = bf16[3,128,2048]{2,1,0:T(8,128)(2,1)S(1)} copy-done((bf16[3,128,2048]{2,1,0:T(8,128)(2,1)S(1)}, bf16[3,128,2048]{2,1,0:T(8,128)(2,1)}, u32[]{:S(2)}) %copy-start) | copy-done | bytes 1572888
  10.0 0.1 copy-done.1
  10.1 0.0 copy-done.2
  10.1 0.0 copy-done.6
  10.1 2.0 %features.3 = (f32[3,128,1024]{2,1,0:T(8,128)S(1)}, bf16[128,1024]{1,0:T(8,128)(2,1)S(1)}, bf16[128,1024]{1,0:T(8,128)(2,1)S(1)}) custom-call(s32[1,128]{1,0:T(1,128)S(1)} %bitcast.10, bf16[768,128]{1,0:T(8,128)(2,1)S(1)} %get-tuple-element.27.delay_ref, bf16[3,8,2048]{2,1,0:T(8,128)(2,1)S(1)} %collective-permute-done.edge_ref, f32[3,7,2048]{2,1,0:T(8,128)S(1)} %bitcast.5, ...), custom_call_target="tpu_custom_call" | custom-call | flops 2000000000 | bytes 4000000 | tf_op jit(solution)/shard_map/features/pallas_call | solution.py:285
  12.1 3.5 %collective-permute-start.3 = (bf16[128,1024]{1,0:T(8,128)(2,1)S(1)}, bf16[128,1024]{1,0:T(8,128)(2,1)S(1)}, u32[]{:S(2)}, u32[]{:S(2)}) collective-permute-start(bf16[128,1024]{1,0:T(8,128)(2,1)S(1)} %get-tuple-element.32), channel_id=1, source_target_pairs={{0,4},{4,8},{8,12},{12,16},{16,20},{20,24},{24,28},{1,5},{5,9},{9,... | collective-permute-start | bytes 786440 | tf_op jit(solution)/shard_map/ppermute | solution.py:27
  15.6 0.0 copy-start.4
  15.6 1.4 %collective-permute-start.4 = (bf16[128,1024]{1,0:T(8,128)(2,1)S(1)}, bf16[128,1024]{1,0:T(8,128)(2,1)S(1)}, u32[]{:S(2)}, u32[]{:S(2)}) collective-permute-start(bf16[128,1024]{1,0:T(8,128)(2,1)S(1)} %get-tuple-element.33), channel_id=1, source_target_pairs={{4,0},{8,4},{12,8},{16,12},{20,16},{24,20},{28,24},{5,1},{9,5},{13... | collective-permute-start | bytes 786440 | tf_op jit(solution)/shard_map/ppermute | solution.py:27
  17.0 2.0 %features.2 = (f32[3,128,1024]{2,1,0:T(8,128)S(1)}, bf16[128,1024]{1,0:T(8,128)(2,1)S(1)}, bf16[128,1024]{1,0:T(8,128)(2,1)S(1)}) custom-call(s32[1,128]{1,0:T(1,128)S(1)} %bitcast.11, bf16[768,128]{1,0:T(8,128)(2,1)S(1)} %get-tuple-element.27.delay_ref, bf16[3,8,2048]{2,1,0:T(8,128)(2,1)S(1)} %collective-permute-done.edge_ref, f32[3,7,2048]{2,1,0:T(8,128)S(1)} %bitcast.6, ...), custom_call_target="tpu_custom_call" | custom-call | flops 2000000000 | bytes 4000000 | tf_op jit(solution)/shard_map/features/pallas_call | solution.py:285
  19.0 5.0 %collective-permute-start.1 = (bf16[128,1024]{1,0:T(8,128)(2,1)S(1)}, bf16[128,1024]{1,0:T(8,128)(2,1)S(1)}, u32[]{:S(2)}, u32[]{:S(2)}) collective-permute-start(bf16[128,1024]{1,0:T(8,128)(2,1)S(1)} %get-tuple-element.29), channel_id=1, source_target_pairs={{0,4},{4,8},{8,12},{12,16},{16,20},{20,24},{24,28},{1,5},{5,9},{9,... | collective-permute-start | bytes 786440 | tf_op jit(solution)/shard_map/ppermute | solution.py:27
  24.0 1.3 %collective-permute-start.2 = (bf16[128,1024]{1,0:T(8,128)(2,1)S(1)}, bf16[128,1024]{1,0:T(8,128)(2,1)S(1)}, u32[]{:S(2)}, u32[]{:S(2)}) collective-permute-start(bf16[128,1024]{1,0:T(8,128)(2,1)S(1)} %get-tuple-element.30), channel_id=1, source_target_pairs={{4,0},{8,4},{12,8},{16,12},{20,16},{24,20},{28,24},{5,1},{9,5},{13... | collective-permute-start | bytes 786440 | tf_op jit(solution)/shard_map/ppermute | solution.py:27
  25.3 2.3 %collective-permute-done.3.kvp_ref = bf16[128,1024]{1,0:T(8,128)(2,1)S(1)} collective-permute-done((bf16[128,1024]{1,0:T(8,128)(2,1)S(1)}, bf16[128,1024]{1,0:T(8,128)(2,1)S(1)}, u32[]{:S(2)}, u32[]{:S(2)}) %collective-permute-start.3) | collective-permute-done | bytes 262176 | tf_op jit(solution)/shard_map/ppermute | solution.py:27
  27.6 0.0 collective-permute-done.4.gn_ref
  27.6 0.0 copy-done.4
  27.6 7.3 %mixer.2 = (bf16[128,2048]{1,0:T(8,128)(2,1)}, bf16[3,128,2048]{2,1,0:T(8,128)(2,1)}, f32[3,8,2048]{2,1,0:T(8,128)S(1)}, bf16[3,8,2048]{2,1,0:T(8,128)(2,1)S(1)}, bf16[8,32,256]{2,1,0:T(8,128)(2,1)}) custom-call(s32[1,128]{1,0:T(1,128)S(1)} %bitcast.12, f32[3,7,2048]{2,1,0:T(8,128)S(1)} %bitcast.7, f32[128,128]{1,0:T(8,128)S(1)} %copy-done.4, ...), custom_call_target="tpu_custom_call" | custom-call | flops 8000000000 | bytes 8000000 | tf_op jit(solution)/shard_map/mixer/pallas_call | solution.py:318
  34.9 2.8 %collective-permute-done.1.kvp_ref = bf16[128,1024]{1,0:T(8,128)(2,1)S(1)} collective-permute-done((bf16[128,1024]{1,0:T(8,128)(2,1)S(1)}, bf16[128,1024]{1,0:T(8,128)(2,1)S(1)}, u32[]{:S(2)}, u32[]{:S(2)}) %collective-permute-start.1) | collective-permute-done | bytes 262176 | tf_op jit(solution)/shard_map/ppermute | solution.py:27
  37.7 0.0 collective-permute-done.2.gn_ref
  37.7 7.2 %mixer.3 = (bf16[128,2048]{1,0:T(8,128)(2,1)}, bf16[3,128,2048]{2,1,0:T(8,128)(2,1)}, f32[3,8,2048]{2,1,0:T(8,128)S(1)}, bf16[3,8,2048]{2,1,0:T(8,128)(2,1)S(1)}, bf16[8,32,256]{2,1,0:T(8,128)(2,1)}) custom-call(s32[1,128]{1,0:T(1,128)S(1)} %bitcast.13, ...), custom_call_target="tpu_custom_call", output_to_operand_aliasing={{0}: (11, {}), {1}: (12, {}), {2}: (13, {}), {3}: (14, {}),... | custom-call | flops 8000000000 | bytes 8000000 | tf_op jit(solution)/shard_map/mixer/pallas_call | solution.py:318
  44.9 1.3 %collective-permute-start.5 = (bf16[3,8,2048]{2,1,0:T(8,128)(2,1)S(1)}, bf16[3,8,2048]{2,1,0:T(8,128)(2,1)S(1)}, u32[]{:S(2)}, u32[]{:S(2)}) collective-permute-start(bf16[3,8,2048]{2,1,0:T(8,128)(2,1)S(1)} %get-tuple-element.42), channel_id=1, source_target_pairs={{4,0},{8,4},{12,8},{16,12},{20,16},{24,20},{28,24},{5,1},{9,5},{13... | collective-permute-start | bytes 294920 | tf_op jit(solution)/shard_map/ppermute | solution.py:27
  46.2 10.7 %all-to-all-start = ((bf16[8,32,256]{2,1,0:T(8,128)(2,1)}), bf16[8,32,256]{2,1,0:T(8,128)(2,1)S(1)}, u32[]{:S(2)}, u32[]{:S(2)}) async-start(bf16[8,32,256]{2,1,0:T(8,128)(2,1)} %get-tuple-element.43), calls=%async_computation | async-start | bytes 262144 | tf_op jit(solution)/shard_map/all_to_all | solution.py:353
  56.9 0.0 collective-permute-done.5
  56.9 0.7 %fusion.1 = bf16[3,128,2048]{2,1,0:T(8,128)(2,1)} fusion(bf16[3,128,2048]{2,1,0:T(8,128)(2,1)} %get-tuple-element.40, f32[3,8,2048]{2,1,0:T(8,128)S(1)} %get-tuple-element.41, bf16[3,8,2048]{2,1,0:T(8,128)(2,1)S(1)} %collective-permute-done.5), kind=kLoop, calls=%fused_computation.3 | loop fusion | flops 147456 | bytes 393216 | tf_op jit(solution)/shard_map/dynamic_update_slice | solution.py:349
  57.6 6.7 %all-to-all-done.got_ref = bf16[8,32,256]{2,1,0:T(8,128)(2,1)S(1)} async-done(((bf16[8,32,256]{2,1,0:T(8,128)(2,1)}), bf16[8,32,256]{2,1,0:T(8,128)(2,1)S(1)}, u32[]{:S(2)}, u32[]{:S(2)}) %all-to-all-start) | async-done | bytes 131104 | tf_op jit(solution)/shard_map/all_to_all | solution.py:353
  64.3 0.6 finish.1
  (1 shorter events, 0.0 us)
Async XLA Ops:
  2.2 7.0 %collective-permute-start = (bf16[3,8,2048]{2,1,0:T(8,128)(2,1)S(1)}, bf16[3,8,2048]{2,1,0:T(8,128)(2,1)S(1)}, u32[]{:S(2)}, u32[]{:S(2)}) collective-permute-start(bf16[3,8,2048]{2,1,0:T(8,128)(2,1)S(1)} %fusion), channel_id=1, source_target_pairs={{0,4},{4,8},{8,12},{12,16},{16,20},{20,24},{24,28},{1,5},{5,9},{9,... | collective-permute-start | bytes 294920 | tf_op jit(solution)/shard_map/ppermute | solution.py:27
  7.1 0.8 %copy-start.3 = (f32[128,128]{1,0:T(8,128)S(1)}, f32[128,128]{1,0:T(8,128)}, u32[]{:S(2)}) copy-start(f32[128,128]{1,0:T(8,128)} %lf_ref.5) | copy-start | bytes 196612
  7.9 0.7 %copy-start.5 = (s32[128]{0:T(128)S(1)}, s32[128]{0:T(128)}, u32[]{:S(2)}) copy-start(s32[128]{0:T(128)} %param.7) | copy-start | bytes 1540
  8.6 1.4 %copy-start = (bf16[3,128,2048]{2,1,0:T(8,128)(2,1)S(1)}, bf16[3,128,2048]{2,1,0:T(8,128)(2,1)}, u32[]{:S(2)}) copy-start(bf16[3,128,2048]{2,1,0:T(8,128)(2,1)} %x_ref.3) | copy-start | bytes 4718596
  8.6 1.5 %copy-start.1 = (bf16[128,2048]{1,0:T(8,128)(2,1)S(1)}, bf16[128,2048]{1,0:T(8,128)(2,1)}, u32[]{:S(2)}) copy-start(bf16[128,2048]{1,0:T(8,128)(2,1)} %cot_ref.3) | copy-start | bytes 1572868
  8.6 1.6 %copy-start.2 = (f32[3,2048,7]{1,2,0:T(8,128)S(1)}, f32[3,2048,7]{1,2,0:T(8,128)}, u32[]{:S(2)}) copy-start(f32[3,2048,7]{1,2,0:T(8,128)} %param.8) | copy-start | bytes 516100
  8.6 1.6 %copy-start.6 = (s32[128]{0:T(128)S(1)}, s32[128]{0:T(128)}, u32[]{:S(2)}) copy-start(s32[128]{0:T(128)} %param.7) | copy-start | bytes 1540
  12.1 15.5 %collective-permute-start.3 = (bf16[128,1024]{1,0:T(8,128)(2,1)S(1)}, bf16[128,1024]{1,0:T(8,128)(2,1)S(1)}, u32[]{:S(2)}, u32[]{:S(2)}) collective-permute-start(bf16[128,1024]{1,0:T(8,128)(2,1)S(1)} %get-tuple-element.32), channel_id=1, source_target_pairs={{0,4},{4,8},{8,12},{12,16},{16,20},{20,24},{24,28},{1,5},{5,9},{9,... | collective-permute-start | bytes 786440 | tf_op jit(solution)/shard_map/ppermute | solution.py:27
  15.6 12.0 %copy-start.4 = (f32[128,128]{1,0:T(8,128)S(1)}, f32[128,128]{1,0:T(8,128)}, u32[]{:S(2)}) copy-start(f32[128,128]{1,0:T(8,128)} %lf_ref.5) | copy-start | bytes 196612
  15.6 12.0 %collective-permute-start.4 = (bf16[128,1024]{1,0:T(8,128)(2,1)S(1)}, bf16[128,1024]{1,0:T(8,128)(2,1)S(1)}, u32[]{:S(2)}, u32[]{:S(2)}) collective-permute-start(bf16[128,1024]{1,0:T(8,128)(2,1)S(1)} %get-tuple-element.33), channel_id=1, source_target_pairs={{4,0},{8,4},{12,8},{16,12},{20,16},{24,20},{28,24},{5,1},{9,5},{13... | collective-permute-start | bytes 786440 | tf_op jit(solution)/shard_map/ppermute | solution.py:27
  19.0 18.7 %collective-permute-start.1 = (bf16[128,1024]{1,0:T(8,128)(2,1)S(1)}, bf16[128,1024]{1,0:T(8,128)(2,1)S(1)}, u32[]{:S(2)}, u32[]{:S(2)}) collective-permute-start(bf16[128,1024]{1,0:T(8,128)(2,1)S(1)} %get-tuple-element.29), channel_id=1, source_target_pairs={{0,4},{4,8},{8,12},{12,16},{16,20},{20,24},{24,28},{1,5},{5,9},{9,... | collective-permute-start | bytes 786440 | tf_op jit(solution)/shard_map/ppermute | solution.py:27
  24.0 13.7 %collective-permute-start.2 = (bf16[128,1024]{1,0:T(8,128)(2,1)S(1)}, bf16[128,1024]{1,0:T(8,128)(2,1)S(1)}, u32[]{:S(2)}, u32[]{:S(2)}) collective-permute-start(bf16[128,1024]{1,0:T(8,128)(2,1)S(1)} %get-tuple-element.30), channel_id=1, source_target_pairs={{4,0},{8,4},{12,8},{16,12},{20,16},{24,20},{28,24},{5,1},{9,5},{13... | collective-permute-start | bytes 786440 | tf_op jit(solution)/shard_map/ppermute | solution.py:27
  44.9 12.0 %collective-permute-start.5 = (bf16[3,8,2048]{2,1,0:T(8,128)(2,1)S(1)}, bf16[3,8,2048]{2,1,0:T(8,128)(2,1)S(1)}, u32[]{:S(2)}, u32[]{:S(2)}) collective-permute-start(bf16[3,8,2048]{2,1,0:T(8,128)(2,1)S(1)} %get-tuple-element.42), channel_id=1, source_target_pairs={{4,0},{8,4},{12,8},{16,12},{20,16},{24,20},{28,24},{5,1},{9,5},{13... | collective-permute-start | bytes 294920 | tf_op jit(solution)/shard_map/ppermute | solution.py:27
  46.2 18.1 %all-to-all-start = ((bf16[8,32,256]{2,1,0:T(8,128)(2,1)}), bf16[8,32,256]{2,1,0:T(8,128)(2,1)S(1)}, u32[]{:S(2)}, u32[]{:S(2)}) async-start(bf16[8,32,256]{2,1,0:T(8,128)(2,1)} %get-tuple-element.43), calls=%async_computation | async-start | bytes 262144 | tf_op jit(solution)/shard_map/all_to_all | solution.py:353

commit v4 on v3

--- a/solution.py
+++ b/solution.py
@@ -54,6 +54,16 @@
         advance_ref[(t - 1) * rows : t * rows] = ones_where((lag == -t) & same).astype(BF16)
     backward = ones_where((iota2((rows, rows), 0) + iota2((rows, rows), 1)) % rows == 0)
     lfr_ref[...] = dot(lf_ref[...].astype(BF16), backward.astype(BF16))
+
+
+def edge_kernel(ids_ref, x_hbm, edge_ref, sem):
+    rows = x_hbm.shape[1]
+    copy = pltpu.make_async_copy(x_hbm.at[:, rows - EDGE :, :], edge_ref, sem)
+    copy.start()
+    copy.wait()
+    top = edge_ref[0].astype(F32)
+    id_wide = jnp.concatenate([ids_ref[...].astype(F32)] * (top.shape[1] // rows), 1)
+    edge_ref[0] = jnp.where(iota2(top.shape, 0) == 0, jnp.broadcast_to(id_wide, top.shape), top).astype(BF16)
 
 
 def feature_kernel(first, ids_ref, delay_ref, edge_ref, sf_hbm, x_hbm, cot_hbm,
@@ -118,7 +128,7 @@
 def mixer_kernel(first, filled, ids_ref, sf_ref, lf_ref, lfr_ref, advance_ref, x_ref, cot_ref, edge_ref,
                  feat_ref, kvp_ref, gn_ref, *refs):
     (out_hbm, qg_hbm, tail_hbm, part_hbm, packed_hbm, out_ref, qg_ref, tail_ref, part_ref, packed_ref,
-     edge_shift, mask_y, mask_g, mask_a, w_kv, w_g, g_rev, dh_ref, y_ref, gm_ref, sems) = refs[filled:]
+     edge_shift, mask_y, mask_g, mask_a, w_kv, w_g, g_rev, dh_ref, kv_turned, g_turned, y_turned, gm_turned, sems) = refs[filled:]
     rows = x_ref.shape[1]
     taps = sf_ref.shape[1]
     count = kvp_ref.shape[1]
@@ -133,11 +143,17 @@
     prev_row = jnp.broadcast_to(edge_ref[0, 0:1, 0:rows].astype(F32), (rows, rows))
     next_row = jnp.broadcast_to(gn_ref[rows - 1 : rows, 0:rows].astype(F32), (rows, rows))
     same = id_row == id_col
-    mask_y[:, 0:rows] = ones_where((lag >= 0) & same).astype(BF16)
-    mask_y[:, rows:] = ones_where((lag < 0) & (prev_row == id_col)).astype(BF16)
-    mask_g[:, 0:rows] = ones_where((lag <= 0) & same).astype(BF16)
-    mask_g[:, rows:] = ones_where((lag > 0) & (next_row == id_col)).astype(BF16)
-    mask_a[...] = dot(mirror, mask_y[...])
+    prev_col = prev_row.T
+    next_col = next_row.T
+    own_later = ones_where((lag <= 0) & same).astype(BF16)
+    own_earlier = ones_where((lag >= 0) & same).astype(BF16)
+    mask_y[0:rows] = own_later
+    mask_y[rows:] = ones_where((lag > 0) & (prev_col == id_row)).astype(BF16)
+    mask_g[0:rows] = own_earlier
+    mask_g[rows:] = ones_where((lag < 0) & (next_col == id_row)).astype(BF16)
+    mask_prev = ones_where((lag < 0) & (prev_row == id_col)).astype(BF16)
+    mask_a[:, 0:rows] = dot(mirror, own_earlier)
+    mask_a[:, rows:] = dot(mirror, mask_prev)
     lag_edge = iota2((EDGE, rows), 1) + EDGE - iota2((EDGE, rows), 0)
     same_edge = prev_row.T[rows - EDGE :] == id_row[0:EDGE]
     pieces = [ones_where((lag_edge == t) & same_edge) for t in range(1, taps)]
@@ -166,29 +182,31 @@
         w_g[0:rows] = (cot * feat_ref[0, :, near]).astype(BF16)
         w_g[rows:] = gn_ref[:, near]
         g_rev[...] = dot(mirror, w_g[0:rows]).astype(BF16)
+        kv_turned[...] = w_kv[...].T
+        g_turned[...] = w_g[...].T
         for q in range(LANES // half):
             part = slice(q * half, (q + 1) * half)
             base = pl.multiple_of((first // half) * per + p * (LANES // width) + q * per, per)
             for j in range(per):
-                mine = owner == j
+                bwd = jnp.broadcast_to(lf_ref[pl.ds(base + j, 1), :], (rows, rows))
+                bwd = pltpu.roll(bwd, 0, 1, stride=1, stride_axis=0).astype(BF16)
+                t_y = jnp.concatenate([bwd, bwd], 0) * mask_y[...]
+                mine = slice((q * per + j) * width, (q * per + j + 1) * width)
+                y_turned[mine] = dot(kv_turned[mine], t_y)
                 fwd = jnp.broadcast_to(lfr_ref[pl.ds(base + j, 1), :], (rows, rows))
                 fwd = pltpu.roll(fwd, 0, 1, stride=1, stride_axis=0).astype(BF16)
-                t_y = jnp.concatenate([fwd, fwd], 1) * mask_y[...]
-                pltpu.store(y_ref.at[:, part], dot(t_y, w_kv[:, part]), mask=mine)
-                bwd = jnp.broadcast_to(lf_ref[pl.ds(base + j, 1), :], (rows, rows))
-                bwd = pltpu.roll(bwd, 0, 1, stride=1, stride_axis=0).astype(BF16)
-                t_g = jnp.concatenate([bwd, bwd], 1) * mask_g[...]
-                pltpu.store(gm_ref.at[:, part], dot(t_g, w_g[:, part]), mask=mine)
-                g_sel = jnp.where(mine, g_rev[:, part], jnp.zeros((rows, half), BF16))
+                t_g = jnp.concatenate([fwd, fwd], 0) * mask_g[...]
+                gm_turned[mine] = dot(g_turned[mine], t_g)
+                g_sel = jnp.where(owner == j, g_rev[:, part], jnp.zeros((rows, half), BF16))
                 cross = lax.dot_general(
                     g_sel, w_kv[:, part], (((1,), (1,)), ((), ())), preferred_element_type=F32
                 ) * mask_a[...]
                 folded = cross[:, 0:rows] + cross[:, rows:]
                 folded = pltpu.roll(folded, 0, 1, stride=1, stride_axis=0)
                 dh_ref[q * per + j : q * per + j + 1] = jnp.sum(folded, 0, keepdims=True)
-        dh = jnp.dot(dh_ref[...], flip, preferred_element_type=F32, precision=lax.Precision.HIGHEST)
-        y = y_ref[...]
-        gm = gm_ref[...]
+        dh = dot(dh_ref[...].astype(BF16), mirror)
+        y = y_turned[...].T
+        gm = gm_turned[...].T
         out_ref[:, near] = (feat_ref[0, :, near] * y).astype(BF16)
         heads = []
         for i in range(3):
@@ -232,7 +250,11 @@
     lax.fori_loop(0, count // LANES, drain, 0)
 
 
-def finish_kernel(scale, taps, got_ref, long_ref, short_ref):
+def finish_kernel(scale, taps, got_ref, tail_ref, part_ref, qg_in, qg_hbm, long_ref, short_ref, last_ref, sem):
+    rows = qg_hbm.shape[1]
+    last_ref[...] = (tail_ref[...] + part_ref[...].astype(F32)).astype(BF16)
+    copy = pltpu.make_async_copy(last_ref, qg_hbm.at[:, rows - EDGE :, :], sem)
+    copy.start()
     total = got_ref[0].astype(F32)
     for k in range(1, got_ref.shape[0]):
         total = total + got_ref[k].astype(F32)
@@ -243,6 +265,7 @@
     lags = long_ref.shape[1]
     for p in range(total.shape[1] // lags):
         long_ref[p * size : (p + 1) * size] = total[3 * PADDED :, p * lags : (p + 1) * lags]
+    copy.wait()
 
 
 def shards(qkv, cotangent, doc_ids, short_filter, long_filter):
@@ -258,10 +281,17 @@
     ids = doc_ids.reshape(1, rows)
     sf = jnp.transpose(short_filter, (0, 2, 1))
 
-    edge = qkv[:, rows - EDGE :, :]
-    id_lanes = jnp.broadcast_to(doc_ids.astype(BF16), (chans // rows, rows)).reshape(chans)
-    first = (lax.broadcasted_iota(jnp.int32, edge.shape, 0) + lax.broadcasted_iota(jnp.int32, edge.shape, 1)) == 0
-    edge = jnp.where(first, id_lanes[None, None, :], edge)
+    small = pltpu.CompilerParams(vmem_limit_bytes=8 << 20)
+    edge = pl.pallas_call(
+        edge_kernel,
+        in_specs=[VMEM, HBM],
+        out_specs=VMEM,
+        out_shape=jax.ShapeDtypeStruct((3, EDGE, chans), BF16),
+        scratch_shapes=[pltpu.SemaphoreType.DMA],
+        compiler_params=pltpu.CompilerParams(vmem_limit_bytes=62 << 20),
+        cost_estimate=pl.CostEstimate(flops=100_000, bytes_accessed=200_000, transcendentals=0),
+        name="edge",
+    )(ids, qkv)
     edge = passed_along(edge, 1)
 
     shifts = ((taps - 1) * rows, rows)
@@ -275,7 +305,7 @@
             jax.ShapeDtypeStruct((groups, long_taps), F32),
         ],
         cost_estimate=pl.CostEstimate(flops=6_000_000_000, bytes_accessed=16_000_000, transcendentals=0),
-        compiler_params=pltpu.CompilerParams(vmem_limit_bytes=8 << 20),
+        compiler_params=small,
         name="prepare",
     )(ids, long_filter)
 
@@ -328,15 +358,17 @@
                 pltpu.VMEM((3, EDGE, count), BF16),
                 pltpu.VMEM((count // CHUNK, packed_rows, CHUNK), BF16),
                 pltpu.VMEM(((taps - 1) * EDGE, rows), BF16),
-                pltpu.VMEM((rows, 2 * rows), BF16),
-                pltpu.VMEM((rows, 2 * rows), BF16),
+                pltpu.VMEM((2 * rows, rows), BF16),
+                pltpu.VMEM((2 * rows, rows), BF16),
                 pltpu.VMEM((rows, 2 * rows), F32),
                 pltpu.VMEM((2 * rows, LANES), BF16),
                 pltpu.VMEM((2 * rows, LANES), BF16),
                 pltpu.VMEM((rows, LANES), BF16),
                 pltpu.VMEM((step_groups, long_taps), F32),
-                pltpu.VMEM((rows, LANES), F32),
-                pltpu.VMEM((rows, LANES), F32),
+                pltpu.VMEM((LANES, 2 * rows), BF16),
+                pltpu.VMEM((LANES, 2 * rows), BF16),
+                pltpu.VMEM((LANES, rows), F32),
+                pltpu.VMEM((LANES, rows), F32),
                 pltpu.SemaphoreType.DMA((5, count // LANES)),
             ],
             compiler_params=params,
@@ -346,24 +378,26 @@
     out, qg, tail, part, packed = results
 
     part = passed_along(part, -1)
-    qg = lax.dynamic_update_slice(qg, (tail + part.astype(F32)).astype(BF16), (0, rows - EDGE, 0))
-
     per = chans // devices
     if per == CHUNK:
         got = lax.all_to_all(packed, "ctx", 0, 0)
-        long_grad, short_grad = pl.pallas_call(
+        qg, long_grad, short_grad = pl.pallas_call(
             functools.partial(finish_kernel, grad_scale, taps),
-            in_specs=[VMEM],
-            out_specs=[VMEM] * 2,
+            in_specs=[VMEM, VMEM, VMEM, ANY],
+            out_specs=[ANY, VMEM, VMEM],
             out_shape=[
+                jax.ShapeDtypeStruct(qg.shape, BF16),
                 jax.ShapeDtypeStruct((groups // devices, long_taps), F32),
                 jax.ShapeDtypeStruct((3, taps, per), F32),
             ],
-            compiler_params=pltpu.CompilerParams(vmem_limit_bytes=8 << 20),
+            input_output_aliases={3: 0},
+            scratch_shapes=[pltpu.VMEM((3, EDGE, chans), BF16), pltpu.SemaphoreType.DMA],
+            compiler_params=small,
             cost_estimate=pl.CostEstimate(flops=1_000_000, bytes_accessed=200_000, transcendentals=0),
             name="finish",
-        )(got)
+        )(got, tail, part, qg)
         return (out, qg, long_grad, short_grad.transpose(0, 2, 1))
+    qg = lax.dynamic_update_slice(qg, (tail + part.astype(F32)).astype(BF16), (0, rows - EDGE, 0))
     head = 3 * PADDED
     short_part = packed[:, :head].transpose(1, 0, 2).reshape(head, devices, per)
     long_part = packed[:, head:].reshape(-1, packed_rows - head, CHUNK // long_taps, long_taps)

time: 65.4 us -> 62.3 us (0.953)
  local copies, waits for them, and re-layouts: 2.37 us -> 0.03 us
  other arithmetic: 2.23 us -> 0 us
  Pallas kernels: 19.2 us -> 20.8 us
  starting transfers between devices: 28 us -> 26.8 us
  waiting for transfers between devices: 12.3 us -> 13.5 us
    ppermute x6, waiting for transfers between devices: 5.59 us -> 13.1 us  [passed_along(): return lax.ppermute(block, 'ctx', route)]
    all_to_all x1, waiting for transfers between devices: 6.67 us -> 0.4 us  [shards(): got = lax.all_to_all(packed, 'ctx', 0, 0)]
    unnamed x14 -> x10, local copies, waits for them, and re-layouts: 2.37 us -> 0.03 us
    pallas_call x0 -> x1, Pallas kernels: none -> 2.26 us  [shards(): pl.pallas_call(edge_kernel, in_specs=[VMEM, HBM], out_specs=VMEM, out_sha...]
    all_to_all x1, starting transfers between devices: 10.7 us -> 8.75 us  [shards(): got = lax.all_to_all(packed, 'ctx', 0, 0)]
    pallas_call x2, Pallas kernels: 14.5 us -> 13.2 us  [shards(): pl.pallas_call(functools.partial(mixer_kernel, part * count, filled), in_...]
    select_n x1 -> x0, other arithmetic: 0.9 us -> none  [shards(): edge = jnp.where(first, id_lanes[None, None, :], edge)]
    ppermute x6, starting transfers between devices: 17.3 us -> 18.1 us  [passed_along(): return lax.ppermute(block, 'ctx', route)]
  transfers between devices with their start and end apart: 7 -> 7, of which waited for: 4 -> 5; matrix products, arithmetic and copies ran while one was open for 1% -> 0% of each run, Pallas kernels for 14% -> 14%
where the time goes in v4:
time: 62.3 us; the launch traced here: 61.9 us
  starting transfers between devices  26.8 us (43%)
  Pallas kernels  20.8 us (33%)
  waiting for transfers between devices  13.5 us (22%)
  between operations  0.79 us (1%)
    ppermute x6, starting transfers between devices, passed_along(): return lax.ppermute(block, 'ctx', route)  18.1 us
    pallas_call x2, Pallas kernels, shards(): pl.pallas_call(functools.partial(mixer_kernel, part * count, filled), in_...  13.2 us
    ppermute x6, waiting for transfers between devices, passed_along(): return lax.ppermute(block, 'ctx', route)  13.1 us
    all_to_all x1, starting transfers between devices, shards(): got = lax.all_to_all(packed, 'ctx', 0, 0)  8.75 us
    pallas_call x2, Pallas kernels, shards(): pl.pallas_call(functools.partial(feature_kernel, part * count), in_specs=...  3.91 us
    pallas_call x1, Pallas kernels, shards(): pl.pallas_call(edge_kernel, in_specs=[VMEM, HBM], out_specs=VMEM, out_sha...  2.26 us
    pallas_call x1, Pallas kernels, shards(): pl.pallas_call(functools.partial(finish_kernel, grad_scale, taps), in_spe...  1.28 us
  transfers between devices with their start and end apart: 7, of which 5 were waited for; matrix products, arithmetic and copies ran while one was open for 0% of the time, Pallas kernels for 14%

profile of v4, /device:TPU:0, one launch (start us, length us, event | category | flops | bytes accessed | tf_op | source)
XLA Modules:
  0.0 61.9 jit_solution(12628049319720601188)
XLA Ops:
  0.6 0.0 copy-start.1
  0.6 0.0 copy-start.4
  0.7 2.3 %edge.1 = bf16[3,8,2048]{2,1,0:T(8,128)(2,1)} custom-call(s32[1,128]{1,0:T(1,128)} %bitcast.3, bf16[3,128,2048]{2,1,0:T(8,128)(2,1)} %x_ref.3), custom_call_target="tpu_custom_call" | custom-call | flops 100000 | bytes 200000 | tf_op jit(solution)/shard_map/edge/pallas_call | solution.py:285
  2.9 0.0 copy-start
  2.9 0.0 copy-start.2
  2.9 0.0 copy-start.3
  3.0 5.0 %collective-permute-start = (bf16[3,8,2048]{2,1,0:T(8,128)(2,1)}, bf16[3,8,2048]{2,1,0:T(8,128)(2,1)S(1)}, u32[]{:S(2)}, u32[]{:S(2)}) collective-permute-start(bf16[3,8,2048]{2,1,0:T(8,128)(2,1)} %edge.1), channel_id=1, source_target_pairs={{0,4},{4,8},{8,12},{12,16},{16,20},{20,24},{24,28},{1,5},{5,9},{9,... | collective-permute-start | bytes 294920 | tf_op jit(solution)/shard_map/ppermute | solution.py:27
  7.9 0.0 copy-done.1
  7.9 0.0 copy-done.4
  8.0 0.2 prepare.1
  8.1 2.3 %collective-permute-done.edge_ref = bf16[3,8,2048]{2,1,0:T(8,128)(2,1)S(1)} collective-permute-done((bf16[3,8,2048]{2,1,0:T(8,128)(2,1)}, bf16[3,8,2048]{2,1,0:T(8,128)(2,1)S(1)}, u32[]{:S(2)}, u32[]{:S(2)}) %collective-permute-start) | collective-permute-done | bytes 98336 | tf_op jit(solution)/shard_map/ppermute | solution.py:27
  10.4 0.0 copy-done
  10.4 0.0 copy-done.2
  10.5 0.0 copy-done.3
  10.5 2.0 %features.3 = (f32[3,128,1024]{2,1,0:T(8,128)S(1)}, bf16[128,1024]{1,0:T(8,128)(2,1)S(1)}, bf16[128,1024]{1,0:T(8,128)(2,1)S(1)}) custom-call(s32[1,128]{1,0:T(1,128)S(1)} %bitcast.5, bf16[768,128]{1,0:T(8,128)(2,1)S(1)} %get-tuple-element.28.delay_ref, bf16[3,8,2048]{2,1,0:T(8,128)(2,1)S(1)} %collective-permute-done.edge_ref, f32[3,7,2048]{2,1,0:T(8,128)S(1)} %bitcast.9, ...), custom_call_target="tpu_custom_call" | custom-call | flops 2000000000 | bytes 4000000 | tf_op jit(solution)/shard_map/features/pallas_call | solution.py:315
  12.4 4.2 %collective-permute-start.3 = (bf16[128,1024]{1,0:T(8,128)(2,1)S(1)}, bf16[128,1024]{1,0:T(8,128)(2,1)S(1)}, u32[]{:S(2)}, u32[]{:S(2)}) collective-permute-start(bf16[128,1024]{1,0:T(8,128)(2,1)S(1)} %get-tuple-element.33), channel_id=1, source_target_pairs={{0,4},{4,8},{8,12},{12,16},{16,20},{20,24},{24,28},{1,5},{5,9},{9,... | collective-permute-start | bytes 786440 | tf_op jit(solution)/shard_map/ppermute | solution.py:27
  16.7 1.3 %collective-permute-start.4 = (bf16[128,1024]{1,0:T(8,128)(2,1)S(1)}, bf16[128,1024]{1,0:T(8,128)(2,1)S(1)}, u32[]{:S(2)}, u32[]{:S(2)}) collective-permute-start(bf16[128,1024]{1,0:T(8,128)(2,1)S(1)} %get-tuple-element.34), channel_id=1, source_target_pairs={{4,0},{8,4},{12,8},{16,12},{20,16},{24,20},{28,24},{5,1},{9,5},{13... | collective-permute-start | bytes 786440 | tf_op jit(solution)/shard_map/ppermute | solution.py:27
  18.0 2.0 %features.2 = (f32[3,128,1024]{2,1,0:T(8,128)S(1)}, bf16[128,1024]{1,0:T(8,128)(2,1)S(1)}, bf16[128,1024]{1,0:T(8,128)(2,1)S(1)}) custom-call(s32[1,128]{1,0:T(1,128)S(1)} %bitcast.6, bf16[768,128]{1,0:T(8,128)(2,1)S(1)} %get-tuple-element.28.delay_ref, bf16[3,8,2048]{2,1,0:T(8,128)(2,1)S(1)} %collective-permute-done.edge_ref, f32[3,7,2048]{2,1,0:T(8,128)S(1)} %bitcast.10, ...), custom_call_target="tpu_custom_call" | custom-call | flops 2000000000 | bytes 4000000 | tf_op jit(solution)/shard_map/features/pallas_call | solution.py:315
  19.9 5.0 %collective-permute-start.1 = (bf16[128,1024]{1,0:T(8,128)(2,1)S(1)}, bf16[128,1024]{1,0:T(8,128)(2,1)S(1)}, u32[]{:S(2)}, u32[]{:S(2)}) collective-permute-start(bf16[128,1024]{1,0:T(8,128)(2,1)S(1)} %get-tuple-element.30), channel_id=1, source_target_pairs={{0,4},{4,8},{8,12},{12,16},{16,20},{20,24},{24,28},{1,5},{5,9},{9,... | collective-permute-start | bytes 786440 | tf_op jit(solution)/shard_map/ppermute | solution.py:27
  24.9 1.3 %collective-permute-start.2 = (bf16[128,1024]{1,0:T(8,128)(2,1)S(1)}, bf16[128,1024]{1,0:T(8,128)(2,1)S(1)}, u32[]{:S(2)}, u32[]{:S(2)}) collective-permute-start(bf16[128,1024]{1,0:T(8,128)(2,1)S(1)} %get-tuple-element.31), channel_id=1, source_target_pairs={{4,0},{8,4},{12,8},{16,12},{20,16},{24,20},{28,24},{5,1},{9,5},{13... | collective-permute-start | bytes 786440 | tf_op jit(solution)/shard_map/ppermute | solution.py:27
  26.2 0.9 %collective-permute-done.3.kvp_ref = bf16[128,1024]{1,0:T(8,128)(2,1)S(1)} collective-permute-done((bf16[128,1024]{1,0:T(8,128)(2,1)S(1)}, bf16[128,1024]{1,0:T(8,128)(2,1)S(1)}, u32[]{:S(2)}, u32[]{:S(2)}) %collective-permute-start.3) | collective-permute-done | bytes 262176 | tf_op jit(solution)/shard_map/ppermute | solution.py:27
  27.1 0.0 collective-permute-done.4.gn_ref
  27.1 6.6 %mixer.2 = (bf16[128,2048]{1,0:T(8,128)(2,1)}, bf16[3,128,2048]{2,1,0:T(8,128)(2,1)}, f32[3,8,2048]{2,1,0:T(8,128)S(1)}, bf16[3,8,2048]{2,1,0:T(8,128)(2,1)S(1)}, bf16[8,32,256]{2,1,0:T(8,128)(2,1)}) custom-call(s32[1,128]{1,0:T(1,128)S(1)} %bitcast.7, f32[3,7,2048]{2,1,0:T(8,128)S(1)} %bitcast.11, f32[128,128]{1,0:T(8,128)S(1)} %copy-done.4, ...), custom_call_target="tpu_custom_call" | custom-call | flops 8000000000 | bytes 8000000 | tf_op jit(solution)/shard_map/mixer/pallas_call | solution.py:348
  33.7 4.2 %collective-permute-done.1.kvp_ref = bf16[128,1024]{1,0:T(8,128)(2,1)S(1)} collective-permute-done((bf16[128,1024]{1,0:T(8,128)(2,1)S(1)}, bf16[128,1024]{1,0:T(8,128)(2,1)S(1)}, u32[]{:S(2)}, u32[]{:S(2)}) %collective-permute-start.1) | collective-permute-done | bytes 262176 | tf_op jit(solution)/shard_map/ppermute | solution.py:27
  37.9 0.0 collective-permute-done.2.gn_ref
  37.9 6.6 %mixer.3 = (bf16[128,2048]{1,0:T(8,128)(2,1)}, bf16[3,128,2048]{2,1,0:T(8,128)(2,1)}, f32[3,8,2048]{2,1,0:T(8,128)S(1)}, bf16[3,8,2048]{2,1,0:T(8,128)(2,1)S(1)}, bf16[8,32,256]{2,1,0:T(8,128)(2,1)}) custom-call(s32[1,128]{1,0:T(1,128)S(1)} %bitcast.8, ...), custom_call_target="tpu_custom_call", output_to_operand_aliasing={{0}: (11, {}), {1}: (12, {}), {2}: (13, {}), {3}: (14, {}),... | custom-call | flops 8000000000 | bytes 8000000 | tf_op jit(solution)/shard_map/mixer/pallas_call | solution.py:348
  44.5 8.8 %all-to-all-start = ((bf16[8,32,256]{2,1,0:T(8,128)(2,1)}), bf16[8,32,256]{2,1,0:T(8,128)(2,1)S(1)}, u32[]{:S(2)}, u32[]{:S(2)}) async-start(bf16[8,32,256]{2,1,0:T(8,128)(2,1)} %get-tuple-element.41), calls=%async_computation | async-start | bytes 262144 | tf_op jit(solution)/shard_map/all_to_all | solution.py:383
  53.2 1.3 %collective-permute-start.5 = (bf16[3,8,2048]{2,1,0:T(8,128)(2,1)S(1)}, bf16[3,8,2048]{2,1,0:T(8,128)(2,1)S(1)}, u32[]{:S(2)}, u32[]{:S(2)}) collective-permute-start(bf16[3,8,2048]{2,1,0:T(8,128)(2,1)S(1)} %get-tuple-element.43), channel_id=1, source_target_pairs={{4,0},{8,4},{12,8},{16,12},{20,16},{24,20},{28,24},{5,1},{9,5},{13... | collective-permute-start | bytes 294920 | tf_op jit(solution)/shard_map/ppermute | solution.py:27
  54.5 5.7 %collective-permute-done.5.part_ref = bf16[3,8,2048]{2,1,0:T(8,128)(2,1)S(1)} collective-permute-done((bf16[3,8,2048]{2,1,0:T(8,128)(2,1)S(1)}, bf16[3,8,2048]{2,1,0:T(8,128)(2,1)S(1)}, u32[]{:S(2)}, u32[]{:S(2)}) %collective-permute-start.5) | collective-permute-done | bytes 98336 | tf_op jit(solution)/shard_map/ppermute | solution.py:27
  60.2 0.4 all-to-all-done.got_ref
  60.6 1.3 %finish.1 = (bf16[3,128,2048]{2,1,0:T(8,128)(2,1)}, f32[16,128]{1,0:T(8,128)}, f32[3,7,256]{2,1,0:T(8,128)}) custom-call(bf16[8,32,256]{2,1,0:T(8,128)(2,1)S(1)} %all-to-all-done.got_ref, f32[3,8,2048]{2,1,0:T(8,128)S(1)} %get-tuple-element.42.tail_ref, bf16[3,8,2048]{2,1,0:T(8,128)(2,1)S(1)} %collective-permute-done.5.part_ref, ...), custom_call_target="tpu_custom_call", output_to_operand_aliasing={{0}: (3, {})} | custom-call | flops 1000000 | bytes 200000 | tf_op jit(solution)/shard_map/finish/pallas_call | solution.py:384
Async XLA Ops:
  0.6 7.3 %copy-start.1 = (s32[128]{0:T(128)S(1)}, s32[128]{0:T(128)}, u32[]{:S(2)}) copy-start(s32[128]{0:T(128)} %param.7) | copy-start | bytes 1540
  0.6 7.3 %copy-start.4 = (f32[128,128]{1,0:T(8,128)S(1)}, f32[128,128]{1,0:T(8,128)}, u32[]{:S(2)}) copy-start(f32[128,128]{1,0:T(8,128)} %lf_ref.5) | copy-start | bytes 196612
  2.9 7.5 %copy-start = (bf16[3,128,2048]{2,1,0:T(8,128)(2,1)S(1)}, bf16[3,128,2048]{2,1,0:T(8,128)(2,1)}, u32[]{:S(2)}) copy-start(bf16[3,128,2048]{2,1,0:T(8,128)(2,1)} %x_ref.3) | copy-start | bytes 4718596
  2.9 7.5 %copy-start.2 = (bf16[128,2048]{1,0:T(8,128)(2,1)S(1)}, bf16[128,2048]{1,0:T(8,128)(2,1)}, u32[]{:S(2)}) copy-start(bf16[128,2048]{1,0:T(8,128)(2,1)} %cot_ref.3) | copy-start | bytes 1572868
  2.9 7.5 %copy-start.3 = (f32[3,2048,7]{1,2,0:T(8,128)S(1)}, f32[3,2048,7]{1,2,0:T(8,128)}, u32[]{:S(2)}) copy-start(f32[3,2048,7]{1,2,0:T(8,128)} %param.8) | copy-start | bytes 516100
  3.0 7.5 %collective-permute-start = (bf16[3,8,2048]{2,1,0:T(8,128)(2,1)}, bf16[3,8,2048]{2,1,0:T(8,128)(2,1)S(1)}, u32[]{:S(2)}, u32[]{:S(2)}) collective-permute-start(bf16[3,8,2048]{2,1,0:T(8,128)(2,1)} %edge.1), channel_id=1, source_target_pairs={{0,4},{4,8},{8,12},{12,16},{16,20},{20,24},{24,28},{1,5},{5,9},{9,... | collective-permute-start | bytes 294920 | tf_op jit(solution)/shard_map/ppermute | solution.py:27
  12.4 14.7 %collective-permute-start.3 = (bf16[128,1024]{1,0:T(8,128)(2,1)S(1)}, bf16[128,1024]{1,0:T(8,128)(2,1)S(1)}, u32[]{:S(2)}, u32[]{:S(2)}) collective-permute-start(bf16[128,1024]{1,0:T(8,128)(2,1)S(1)} %get-tuple-element.33), channel_id=1, source_target_pairs={{0,4},{4,8},{8,12},{12,16},{16,20},{20,24},{24,28},{1,5},{5,9},{9,... | collective-permute-start | bytes 786440 | tf_op jit(solution)/shard_map/ppermute | solution.py:27
  16.7 10.5 %collective-permute-start.4 = (bf16[128,1024]{1,0:T(8,128)(2,1)S(1)}, bf16[128,1024]{1,0:T(8,128)(2,1)S(1)}, u32[]{:S(2)}, u32[]{:S(2)}) collective-permute-start(bf16[128,1024]{1,0:T(8,128)(2,1)S(1)} %get-tuple-element.34), channel_id=1, source_target_pairs={{4,0},{8,4},{12,8},{16,12},{20,16},{24,20},{28,24},{5,1},{9,5},{13... | collective-permute-start | bytes 786440 | tf_op jit(solution)/shard_map/ppermute | solution.py:27
  19.9 18.0 %collective-permute-start.1 = (bf16[128,1024]{1,0:T(8,128)(2,1)S(1)}, bf16[128,1024]{1,0:T(8,128)(2,1)S(1)}, u32[]{:S(2)}, u32[]{:S(2)}) collective-permute-start(bf16[128,1024]{1,0:T(8,128)(2,1)S(1)} %get-tuple-element.30), channel_id=1, source_target_pairs={{0,4},{4,8},{8,12},{12,16},{16,20},{20,24},{24,28},{1,5},{5,9},{9,... | collective-permute-start | bytes 786440 | tf_op jit(solution)/shard_map/ppermute | solution.py:27
  24.9 13.0 %collective-permute-start.2 = (bf16[128,1024]{1,0:T(8,128)(2,1)S(1)}, bf16[128,1024]{1,0:T(8,128)(2,1)S(1)}, u32[]{:S(2)}, u32[]{:S(2)}) collective-permute-start(bf16[128,1024]{1,0:T(8,128)(2,1)S(1)} %get-tuple-element.31), channel_id=1, source_target_pairs={{4,0},{8,4},{12,8},{16,12},{20,16},{24,20},{28,24},{5,1},{9,5},{13... | collective-permute-start | bytes 786440 | tf_op jit(solution)/shard_map/ppermute | solution.py:27
  44.5 16.1 %all-to-all-start = ((bf16[8,32,256]{2,1,0:T(8,128)(2,1)}), bf16[8,32,256]{2,1,0:T(8,128)(2,1)S(1)}, u32[]{:S(2)}, u32[]{:S(2)}) async-start(bf16[8,32,256]{2,1,0:T(8,128)(2,1)} %get-tuple-element.41), calls=%async_computation | async-start | bytes 262144 | tf_op jit(solution)/shard_map/all_to_all | solution.py:383
  53.2 6.9 %collective-permute-start.5 = (bf16[3,8,2048]{2,1,0:T(8,128)(2,1)S(1)}, bf16[3,8,2048]{2,1,0:T(8,128)(2,1)S(1)}, u32[]{:S(2)}, u32[]{:S(2)}) collective-permute-start(bf16[3,8,2048]{2,1,0:T(8,128)(2,1)S(1)} %get-tuple-element.43), channel_id=1, source_target_pairs={{4,0},{8,4},{12,8},{16,12},{20,16},{24,20},{28,24},{5,1},{9,5},{13... | collective-permute-start | bytes 294920 | tf_op jit(solution)/shard_map/ppermute | solution.py:27

commit v5 on v4

--- a/solution.py
+++ b/solution.py
@@ -54,16 +54,6 @@
         advance_ref[(t - 1) * rows : t * rows] = ones_where((lag == -t) & same).astype(BF16)
     backward = ones_where((iota2((rows, rows), 0) + iota2((rows, rows), 1)) % rows == 0)
     lfr_ref[...] = dot(lf_ref[...].astype(BF16), backward.astype(BF16))
-
-
-def edge_kernel(ids_ref, x_hbm, edge_ref, sem):
-    rows = x_hbm.shape[1]
-    copy = pltpu.make_async_copy(x_hbm.at[:, rows - EDGE :, :], edge_ref, sem)
-    copy.start()
-    copy.wait()
-    top = edge_ref[0].astype(F32)
-    id_wide = jnp.concatenate([ids_ref[...].astype(F32)] * (top.shape[1] // rows), 1)
-    edge_ref[0] = jnp.where(iota2(top.shape, 0) == 0, jnp.broadcast_to(id_wide, top.shape), top).astype(BF16)
 
 
 def feature_kernel(first, ids_ref, delay_ref, edge_ref, sf_hbm, x_hbm, cot_hbm,
@@ -125,51 +115,81 @@
     lax.fori_loop(0, steps, one_step, 0)
 
 
-def mixer_kernel(first, filled, ids_ref, sf_ref, lf_ref, lfr_ref, advance_ref, x_ref, cot_ref, edge_ref,
-                 feat_ref, kvp_ref, gn_ref, *refs):
-    (out_hbm, qg_hbm, tail_hbm, part_hbm, packed_hbm, out_ref, qg_ref, tail_ref, part_ref, packed_ref,
-     edge_shift, mask_y, mask_g, mask_a, w_kv, w_g, g_rev, dh_ref, kv_turned, g_turned, y_turned, gm_turned, sems) = refs[filled:]
+def store_all(copies, steps):
+    def drain(p, carry):
+        for copy in copies(p):
+            copy.wait()
+        return carry
+
+    lax.fori_loop(0, steps, drain, 0)
+
+
+def edge_shifts(ids_ref, edge_ref, edge_shift):
+    rows = edge_shift.shape[1]
+    taps = edge_shift.shape[0] // EDGE + 1
+    id_head = jnp.broadcast_to(ids_ref[...], (EDGE, rows)).astype(F32)
+    prev = jnp.broadcast_to(edge_ref[0, 0:1, 0:rows].astype(F32), (rows, rows)).T
+    lag = iota2((EDGE, rows), 1) + EDGE - iota2((EDGE, rows), 0)
+    same = prev[rows - EDGE :] == id_head
+    pieces = [ones_where((lag == t) & same) for t in range(1, taps)]
+    edge_shift[...] = jnp.concatenate(pieces, 0).astype(BF16)
+
+
+def short_stage(gf, w, x, xe, advance_ref, edge_shift):
+    rows = gf.shape[0]
+    taps = w.shape[0]
+    gf_sent = gf.astype(BF16)
+    moved = dot(advance_ref[...], gf_sent)
+    moved_edge = dot(edge_shift[...], gf_sent)
+    acc = w[0:1] * gf
+    sums = [jnp.sum(x * gf, 0, keepdims=True)]
+    sent = jnp.zeros((EDGE, LANES), F32)
+    for t in range(1, taps):
+        piece = moved[(t - 1) * rows : t * rows]
+        piece_edge = moved_edge[(t - 1) * EDGE : t * EDGE]
+        acc = acc + w[t : t + 1] * piece
+        sent = sent + w[t : t + 1] * piece_edge
+        sums.append(jnp.sum(x * piece, 0, keepdims=True) + jnp.sum(xe * piece_edge, 0, keepdims=True))
+    sums.append(jnp.zeros((PADDED - taps, LANES), F32))
+    return acc, sent, jnp.concatenate(sums, 0)
+
+
+def query_kernel(first, filled, ids_ref, sf_ref, lf_ref, advance_ref, x_ref, cot_ref, edge_ref,
+                 feat_ref, kvp_ref, *refs):
+    (out_hbm, qg_hbm, tail_hbm, part_hbm, packed_hbm, out_ref, qg_ref, tail_ref, part_ref, short_ref, long_ref,
+     edge_shift, mask_y, mask_a, w_kv, g_rev, dh_ref, kv_turned, y_turned, sems) = refs[filled:]
     rows = x_ref.shape[1]
-    taps = sf_ref.shape[1]
     count = kvp_ref.shape[1]
     width = x_ref.shape[2] // lf_ref.shape[0]
     half = rows
     per = half // width
     lag = iota2((rows, rows), 0) - iota2((rows, rows), 1)
-    flip = ones_where(iota2((rows, rows), 0) + iota2((rows, rows), 1) == rows - 1)
-    mirror = flip.astype(BF16)
+    mirror = ones_where(iota2((rows, rows), 0) + iota2((rows, rows), 1) == rows - 1).astype(BF16)
     id_row = jnp.broadcast_to(ids_ref[...], (rows, rows)).astype(F32)
     id_col = id_row.T
     prev_row = jnp.broadcast_to(edge_ref[0, 0:1, 0:rows].astype(F32), (rows, rows))
-    next_row = jnp.broadcast_to(gn_ref[rows - 1 : rows, 0:rows].astype(F32), (rows, rows))
     same = id_row == id_col
-    prev_col = prev_row.T
-    next_col = next_row.T
-    own_later = ones_where((lag <= 0) & same).astype(BF16)
-    own_earlier = ones_where((lag >= 0) & same).astype(BF16)
-    mask_y[0:rows] = own_later
-    mask_y[rows:] = ones_where((lag > 0) & (prev_col == id_row)).astype(BF16)
-    mask_g[0:rows] = own_earlier
-    mask_g[rows:] = ones_where((lag < 0) & (next_col == id_row)).astype(BF16)
-    mask_prev = ones_where((lag < 0) & (prev_row == id_col)).astype(BF16)
-    mask_a[:, 0:rows] = dot(mirror, own_earlier)
-    mask_a[:, rows:] = dot(mirror, mask_prev)
-    lag_edge = iota2((EDGE, rows), 1) + EDGE - iota2((EDGE, rows), 0)
-    same_edge = prev_row.T[rows - EDGE :] == id_row[0:EDGE]
-    pieces = [ones_where((lag_edge == t) & same_edge) for t in range(1, taps)]
-    edge_shift[...] = jnp.concatenate(pieces, 0).astype(BF16)
+    mask_y[0:rows] = ones_where((lag <= 0) & same).astype(BF16)
+    mask_y[rows:] = ones_where((lag > 0) & (prev_row.T == id_row)).astype(BF16)
+    mask_a[:, 0:rows] = dot(mirror, ones_where((lag >= 0) & same).astype(BF16))
+    mask_a[:, rows:] = dot(mirror, ones_where((lag < 0) & (prev_row == id_col)).astype(BF16))
+    edge_shifts(ids_ref, edge_ref, edge_shift)
     owner = iota2((rows, half), 1) // width
     blocks = LANES // CHUNK
+    head = 3 * PADDED
 
     def copies(p):
         near = lane_range(p * LANES, LANES)
         cols = lane_range(first + p * LANES, LANES)
+        here = pl.ds(p * blocks, blocks)
+        there = pl.ds(first // CHUNK + p * blocks, blocks)
         pairs = [
             (out_ref.at[:, near], out_hbm.at[:, cols]),
-            (qg_ref.at[:, :, near], qg_hbm.at[:, :, cols]),
-            (tail_ref.at[:, :, near], tail_hbm.at[:, :, cols]),
-            (part_ref.at[:, :, near], part_hbm.at[:, :, cols]),
-            (packed_ref.at[pl.ds(p * blocks, blocks)], packed_hbm.at[pl.ds(first // CHUNK + p * blocks, blocks)]),
+            (qg_ref.at[:, near], qg_hbm.at[0, :, cols]),
+            (tail_ref.at[:, near], tail_hbm.at[0, :, cols]),
+            (part_ref.at[:, near], part_hbm.at[0, :, cols]),
+            (short_ref.at[here], packed_hbm.at[there, 0:PADDED]),
+            (long_ref.at[here], packed_hbm.at[there, head:]),
         ]
         return [pltpu.make_async_copy(src, dst, sems.at[k, p]) for k, (src, dst) in enumerate(pairs)]
 
@@ -179,24 +199,17 @@
         cot = cot_ref[:, cols].astype(F32)
         w_kv[0:rows] = (feat_ref[1, :, near] * feat_ref[2, :, near]).astype(BF16)
         w_kv[rows:] = kvp_ref[:, near]
-        w_g[0:rows] = (cot * feat_ref[0, :, near]).astype(BF16)
-        w_g[rows:] = gn_ref[:, near]
-        g_rev[...] = dot(mirror, w_g[0:rows]).astype(BF16)
         kv_turned[...] = w_kv[...].T
-        g_turned[...] = w_g[...].T
+        g_rev[...] = dot(mirror, (cot * feat_ref[0, :, near]).astype(BF16)).astype(BF16)
         for q in range(LANES // half):
             part = slice(q * half, (q + 1) * half)
             base = pl.multiple_of((first // half) * per + p * (LANES // width) + q * per, per)
             for j in range(per):
-                bwd = jnp.broadcast_to(lf_ref[pl.ds(base + j, 1), :], (rows, rows))
-                bwd = pltpu.roll(bwd, 0, 1, stride=1, stride_axis=0).astype(BF16)
-                t_y = jnp.concatenate([bwd, bwd], 0) * mask_y[...]
                 mine = slice((q * per + j) * width, (q * per + j + 1) * width)
-                y_turned[mine] = dot(kv_turned[mine], t_y)
-                fwd = jnp.broadcast_to(lfr_ref[pl.ds(base + j, 1), :], (rows, rows))
-                fwd = pltpu.roll(fwd, 0, 1, stride=1, stride_axis=0).astype(BF16)
-                t_g = jnp.concatenate([fwd, fwd], 0) * mask_g[...]
-                gm_turned[mine] = dot(g_turned[mine], t_g)
+                taps = jnp.broadcast_to(lf_ref[pl.ds(base + j, 1), :], (rows, rows))
+                taps = pltpu.roll(taps, 0, 1, stride=1, stride_axis=0).astype(BF16)
+                toeplitz = jnp.concatenate([taps, taps], 0) * mask_y[...]
+                y_turned[mine] = dot(kv_turned[mine], toeplitz)
                 g_sel = jnp.where(owner == j, g_rev[:, part], jnp.zeros((rows, half), BF16))
                 cross = lax.dot_general(
                     g_sel, w_kv[:, part], (((1,), (1,)), ((), ())), preferred_element_type=F32
@@ -206,48 +219,89 @@
                 dh_ref[q * per + j : q * per + j + 1] = jnp.sum(folded, 0, keepdims=True)
         dh = dot(dh_ref[...].astype(BF16), mirror)
         y = y_turned[...].T
-        gm = gm_turned[...].T
         out_ref[:, near] = (feat_ref[0, :, near] * y).astype(BF16)
-        heads = []
-        for i in range(3):
-            gf = cot * y if i == 0 else gm * feat_ref[3 - i, :, near]
-            w = sf_ref[i, :, cols]
-            x = x_ref[i, :, cols].astype(F32)
-            xe = edge_ref[i, :, cols].astype(F32)
-            gf_sent = gf.astype(BF16)
-            moved = dot(advance_ref[...], gf_sent)
-            moved_edge = dot(edge_shift[...], gf_sent)
-            acc = w[0:1] * gf
-            sums = [jnp.sum(x * gf, 0, keepdims=True)]
-            sent = jnp.zeros((EDGE, LANES), F32)
-            for t in range(1, taps):
-                piece = moved[(t - 1) * rows : t * rows]
-                piece_edge = moved_edge[(t - 1) * EDGE : t * EDGE]
-                acc = acc + w[t : t + 1] * piece
-                sent = sent + w[t : t + 1] * piece_edge
-                sums.append(jnp.sum(x * piece, 0, keepdims=True) + jnp.sum(xe * piece_edge, 0, keepdims=True))
-            sums.append(jnp.zeros((PADDED - taps, LANES), F32))
-            qg_ref[i, :, near] = acc.astype(BF16)
-            tail_ref[i, :, near] = acc[rows - EDGE :]
-            part_ref[i, :, near] = sent.astype(BF16)
-            heads.append(jnp.concatenate(sums, 0))
+        acc, sent, sums = short_stage(
+            cot * y, sf_ref[0, :, cols], x_ref[0, :, cols].astype(F32), edge_ref[0, :, cols].astype(F32),
+            advance_ref, edge_shift,
+        )
+        qg_ref[:, near] = acc.astype(BF16)
+        tail_ref[:, near] = acc[rows - EDGE :]
+        part_ref[:, near] = sent.astype(BF16)
         size = dh.shape[0] * rows // LANES
         for k in range(blocks):
-            picked = [head[:, k * CHUNK : (k + 1) * CHUNK] for head in heads]
+            short_ref[p * blocks + k] = sums[:, k * CHUNK : (k + 1) * CHUNK].astype(BF16)
             lines = range(k * (CHUNK // rows), (k + 1) * (CHUNK // rows))
-            picked.append(jnp.concatenate([dh[e * size : (e + 1) * size] for e in lines], 1))
-            packed_ref[p * blocks + k] = jnp.concatenate(picked, 0).astype(BF16)
+            long_ref[p * blocks + k] = jnp.concatenate([dh[e * size : (e + 1) * size] for e in lines], 1).astype(BF16)
         for copy in copies(p):
             copy.start()
         return carry
 
-    def drain(p, carry):
+    lax.fori_loop(0, count // LANES, one_step, 0)
+    store_all(copies, count // LANES)
+
+
+def pair_kernel(first, filled, ids_ref, sf_ref, lfr_ref, advance_ref, x_ref, cot_ref, edge_ref,
+                feat_ref, gn_ref, *refs):
+    (qg_hbm, tail_hbm, part_hbm, packed_hbm, qg_ref, tail_ref, part_ref, short_ref,
+     edge_shift, mask_g, w_g, g_turned, gm_turned, sems) = refs[filled:]
+    rows = x_ref.shape[1]
+    count = gn_ref.shape[1]
+    width = x_ref.shape[2] // lfr_ref.shape[0]
+    lag = iota2((rows, rows), 0) - iota2((rows, rows), 1)
+    id_row = jnp.broadcast_to(ids_ref[...], (rows, rows)).astype(F32)
+    next_col = jnp.broadcast_to(gn_ref[rows - 1 : rows, 0:rows].astype(F32), (rows, rows)).T
+    mask_g[0:rows] = ones_where((lag >= 0) & (id_row == id_row.T)).astype(BF16)
+    mask_g[rows:] = ones_where((lag < 0) & (next_col == id_row)).astype(BF16)
+    edge_shifts(ids_ref, edge_ref, edge_shift)
+    blocks = LANES // CHUNK
+
+    def copies(p):
+        near = lane_range(p * LANES, LANES)
+        cols = lane_range(first + p * LANES, LANES)
+        pairs = [
+            (qg_ref.at[:, :, near], qg_hbm.at[1:3, :, cols]),
+            (tail_ref.at[:, :, near], tail_hbm.at[1:3, :, cols]),
+            (part_ref.at[:, :, near], part_hbm.at[1:3, :, cols]),
+            (
+                short_ref.at[pl.ds(p * blocks, blocks)],
+                packed_hbm.at[pl.ds(first // CHUNK + p * blocks, blocks), PADDED : 3 * PADDED],
+            ),
+        ]
+        return [pltpu.make_async_copy(src, dst, sems.at[k, p]) for k, (src, dst) in enumerate(pairs)]
+
+    def one_step(p, carry):
+        near = lane_range(p * LANES, LANES)
+        cols = lane_range(first + p * LANES, LANES)
+        w_g[0:rows] = (cot_ref[:, cols].astype(F32) * feat_ref[0, :, near]).astype(BF16)
+        w_g[rows:] = gn_ref[:, near]
+        g_turned[...] = w_g[...].T
+        for j in range(LANES // width):
+            mine = slice(j * width, (j + 1) * width)
+            base = pl.multiple_of(first // width + p * (LANES // width), LANES // width)
+            taps = jnp.broadcast_to(lfr_ref[pl.ds(base + j, 1), :], (rows, rows))
+            taps = pltpu.roll(taps, 0, 1, stride=1, stride_axis=0).astype(BF16)
+            toeplitz = jnp.concatenate([taps, taps], 0) * mask_g[...]
+            gm_turned[mine] = dot(g_turned[mine], toeplitz)
+        gm = gm_turned[...].T
+        heads = []
+        for i in (1, 2):
+            acc, sent, sums = short_stage(
+                gm * feat_ref[3 - i, :, near], sf_ref[i, :, cols], x_ref[i, :, cols].astype(F32),
+                edge_ref[i, :, cols].astype(F32), advance_ref, edge_shift,
+            )
+            qg_ref[i - 1, :, near] = acc.astype(BF16)
+            tail_ref[i - 1, :, near] = acc[rows - EDGE :]
+            part_ref[i - 1, :, near] = sent.astype(BF16)
+            heads.append(sums)
+        for k in range(blocks):
+            picked = [head[:, k * CHUNK : (k + 1) * CHUNK] for head in heads]
+            short_ref[p * blocks + k] = jnp.concatenate(picked, 0).astype(BF16)
         for copy in copies(p):
-            copy.wait()
+            copy.start()
         return carry
 
     lax.fori_loop(0, count // LANES, one_step, 0)
-    lax.fori_loop(0, count // LANES, drain, 0)
+    store_all(copies, count // LANES)
 
 
 def finish_kernel(scale, taps, got_ref, tail_ref, part_ref, qg_in, qg_hbm, long_ref, short_ref, last_ref, sem):
@@ -282,16 +336,8 @@
     sf = jnp.transpose(short_filter, (0, 2, 1))
 
     small = pltpu.CompilerParams(vmem_limit_bytes=8 << 20)
-    edge = pl.pallas_call(
-        edge_kernel,
-        in_specs=[VMEM, HBM],
-        out_specs=VMEM,
-        out_shape=jax.ShapeDtypeStruct((3, EDGE, chans), BF16),
-        scratch_shapes=[pltpu.SemaphoreType.DMA],
-        compiler_params=pltpu.CompilerParams(vmem_limit_bytes=62 << 20),
-        cost_estimate=pl.CostEstimate(flops=100_000, bytes_accessed=200_000, transcendentals=0),
-        name="edge",
-    )(ids, qkv)
+    edge = qkv[:, rows - EDGE :, :]
+    edge = edge.at[0, 0, :rows].set(doc_ids.astype(BF16))
     edge = passed_along(edge, 1)
 
     shifts = ((taps - 1) * rows, rows)
@@ -334,7 +380,6 @@
         )(ids, delay, edge, sf, qkv, cotangent)
         sent.append((feats, passed_along(kv, 1), passed_along(grad, -1)))
 
-    results = []
     full = [
         jax.ShapeDtypeStruct((rows, chans), BF16),
         jax.ShapeDtypeStruct((3, rows, chans), BF16),
@@ -342,39 +387,61 @@
         jax.ShapeDtypeStruct((3, EDGE, chans), BF16),
         jax.ShapeDtypeStruct((chans // CHUNK, packed_rows, CHUNK), BF16),
     ]
+    edge_scratch = pltpu.VMEM(((taps - 1) * EDGE, rows), BF16)
+    results = []
     for part in range(PARTS):
         feats, kv_prev, grad_next = sent[part]
         filled = len(results)
-        results = pl.pallas_call(
-            functools.partial(mixer_kernel, part * count, filled),
-            in_specs=[VMEM] * 11 + [ANY] * filled,
+        out, *rest = pl.pallas_call(
+            functools.partial(query_kernel, part * count, filled),
+            in_specs=[VMEM] * 9 + [ANY] * filled,
             out_specs=[ANY] * 5,
             out_shape=full,
-            input_output_aliases={11 + k: k for k in range(filled)},
+            input_output_aliases={9 + k: k for k in range(filled)},
             scratch_shapes=[
                 pltpu.VMEM((rows, count), BF16),
-                pltpu.VMEM((3, rows, count), BF16),
-                pltpu.VMEM((3, EDGE, count), F32),
-                pltpu.VMEM((3, EDGE, count), BF16),
-                pltpu.VMEM((count // CHUNK, packed_rows, CHUNK), BF16),
-                pltpu.VMEM(((taps - 1) * EDGE, rows), BF16),
-                pltpu.VMEM((2 * rows, rows), BF16),
+                pltpu.VMEM((rows, count), BF16),
+                pltpu.VMEM((EDGE, count), F32),
+                pltpu.VMEM((EDGE, count), BF16),
+                pltpu.VMEM((count // CHUNK, PADDED, CHUNK), BF16),
+                pltpu.VMEM((count // CHUNK, packed_rows - 3 * PADDED, CHUNK), BF16),
+                edge_scratch,
                 pltpu.VMEM((2 * rows, rows), BF16),
                 pltpu.VMEM((rows, 2 * rows), F32),
-                pltpu.VMEM((2 * rows, LANES), BF16),
                 pltpu.VMEM((2 * rows, LANES), BF16),
                 pltpu.VMEM((rows, LANES), BF16),
                 pltpu.VMEM((step_groups, long_taps), F32),
                 pltpu.VMEM((LANES, 2 * rows), BF16),
+                pltpu.VMEM((LANES, rows), F32),
+                pltpu.SemaphoreType.DMA((6, count // LANES)),
+            ],
+            compiler_params=params,
+            cost_estimate=pl.CostEstimate(flops=4_000_000_000, bytes_accessed=4_000_000, transcendentals=0),
+            name="query",
+        )(ids, sf, long_filter, advance, qkv, cotangent, edge, feats, kv_prev, *results)
+        rest = pl.pallas_call(
+            functools.partial(pair_kernel, part * count, 4),
+            in_specs=[VMEM] * 9 + [ANY] * 4,
+            out_specs=[ANY] * 4,
+            out_shape=full[1:],
+            input_output_aliases={9 + k: k for k in range(4)},
+            scratch_shapes=[
+                pltpu.VMEM((2, rows, count), BF16),
+                pltpu.VMEM((2, EDGE, count), F32),
+                pltpu.VMEM((2, EDGE, count), BF16),
+                pltpu.VMEM((count // CHUNK, 2 * PADDED, CHUNK), BF16),
+                edge_scratch,
+                pltpu.VMEM((2 * rows, rows), BF16),
+                pltpu.VMEM((2 * rows, LANES), BF16),
                 pltpu.VMEM((LANES, 2 * rows), BF16),
                 pltpu.VMEM((LANES, rows), F32),
-                pltpu.VMEM((LANES, rows), F32),
-                pltpu.SemaphoreType.DMA((5, count // LANES)),
+                pltpu.SemaphoreType.DMA((4, count // LANES)),
             ],
             compiler_params=params,
-            cost_estimate=pl.CostEstimate(flops=8_000_000_000, bytes_accessed=8_000_000, transcendentals=0),
-            name="mixer",
-        )(ids, sf, long_filter, lf_rev, advance, qkv, cotangent, edge, feats, kv_prev, grad_next, *results)
+            cost_estimate=pl.CostEstimate(flops=4_000_000_000, bytes_accessed=4_000_000, transcendentals=0),
+            name="pair",
+        )(ids, sf, lf_rev, advance, qkv, cotangent, edge, feats, grad_next, *rest)
+        results = [out, *rest]
     out, qg, tail, part, packed = results
 
     part = passed_along(part, -1)

time: 62.3 us -> 61.6 us (0.989)
  starting transfers between devices: 26.8 us -> 23.1 us
  waiting for transfers between devices: 13.5 us -> 9.95 us
  local copies, waits for them, and re-layouts: 0.03 us -> 3.35 us
  Pallas kernels: 20.8 us -> 23.3 us
  other arithmetic: 0 us -> 0.66 us
    ppermute x6, waiting for transfers between devices: 13.1 us -> 9.29 us  [passed_along(): return lax.ppermute(block, 'ctx', route)]
    all_to_all x1, starting transfers between devices: 8.75 us -> 5.78 us  [shards(): got = lax.all_to_all(packed, 'ctx', 0, 0)]
    pallas_call x3 -> x4, Pallas kernels: 15.4 us -> 17.9 us  [the longest x2 10.7 us: shards(): pl.pallas_call(functools.partial(query_kernel, part * count, filled), in_...]
    unnamed x10 -> x14, local copies, waits for them, and re-layouts: 0.03 us -> 2.37 us
    slice x0 -> x1, local copies, waits for them, and re-layouts: none -> 0.9 us  [shards(): edge = qkv[:, rows - EDGE:, :]]
    ppermute x6, starting transfers between devices: 18.1 us -> 17.3 us  [passed_along(): return lax.ppermute(block, 'ctx', route)]
    another operation x0 -> x1, other arithmetic: none -> 0.66 us
  transfers between devices with their start and end apart: 7 -> 7, of which waited for: 5 -> 5; matrix products, arithmetic and copies ran while one was open for 0% -> 0% of each run, Pallas kernels for 14% -> 27%
where the time goes in v5:
time: 61.6 us; the launch traced here: 61.1 us
  Pallas kernels  23.3 us (38%)
  starting transfers between devices  23.1 us (38%)
  waiting for transfers between devices  9.95 us (16%)
  local copies, waits for them, and re-layouts  3.35 us (5%)
  between operations  0.79 us (1%)
  other arithmetic  0.66 us (1%)
    ppermute x6, starting transfers between devices, passed_along(): return lax.ppermute(block, 'ctx', route)  17.3 us
    pallas_call x2, Pallas kernels, shards(): pl.pallas_call(functools.partial(query_kernel, part * count, filled), in_...  10.7 us
    ppermute x6, waiting for transfers between devices, passed_along(): return lax.ppermute(block, 'ctx', route)  9.29 us
    pallas_call x2, Pallas kernels, shards(): pl.pallas_call(functools.partial(pair_kernel, part * count, 4), in_specs=...  7.25 us
    all_to_all x1, starting transfers between devices, shards(): got = lax.all_to_all(packed, 'ctx', 0, 0)  5.78 us
    pallas_call x2, Pallas kernels, shards(): pl.pallas_call(functools.partial(feature_kernel, part * count), in_specs=...  3.91 us
    unnamed x14, local copies, waits for them, and re-layouts  2.37 us
    pallas_call x1, Pallas kernels, shards(): pl.pallas_call(functools.partial(finish_kernel, grad_scale, taps), in_spe...  1.28 us
  transfers between devices with their start and end apart: 7, of which 5 were waited for; matrix products, arithmetic and copies ran while one was open for 0% of the time, Pallas kernels for 27%

profile of v5, /device:TPU:0, one launch (start us, length us, event | category | flops | bytes accessed | tf_op | source)
XLA Modules:
  0.0 61.1 jit_solution(17935901152601216807)
XLA Ops:
  0.6 0.9 %slice.26 = bf16[3,8,2048]{2,1,0:T(8,128)(2,1)S(1)} slice(bf16[3,128,2048]{2,1,0:T(8,128)(2,1)} %x_ref.7), slice={[0:3], [120:128], [0:2048]} | slice | bytes 196608 | tf_op jit(solution)/shard_map/slice | solution.py:339
  1.5 0.7 %convert_bitcast_fusion = bf16[1,1,128]{2,1,0:T(2,128)(2,1)S(1)} fusion(s32[128]{0:T(128)} %param.9), kind=kLoop, calls=%fused_computation | loop fusion | flops 128 | bytes 768 | tf_op jit(solution)/shard_map/reshape.24
  2.2 0.1 scatter.4
  2.3 4.8 %collective-permute-start = (bf16[3,8,2048]{2,1,0:T(8,128)(2,1)S(1)}, bf16[3,8,2048]{2,1,0:T(8,128)(2,1)S(1)}, u32[]{:S(2)}, u32[]{:S(2)}) collective-permute-start(bf16[3,8,2048]{2,1,0:T(8,128)(2,1)S(1)} %scatter.4), channel_id=1, source_target_pairs={{0,4},{4,8},{8,12},{12,16},{16,20},{20,24},{24,28},{1,5},{5,9},{9,... | collective-permute-start | bytes 294920 | tf_op jit(solution)/shard_map/ppermute | solution.py:27
  7.1 0.0 copy-start.3
  7.2 0.8 %copy-done.3 = f32[128,128]{1,0:T(8,128)S(1)} copy-done((f32[128,128]{1,0:T(8,128)S(1)}, f32[128,128]{1,0:T(8,128)}, u32[]{:S(2)}) %copy-start.3) | copy-done | bytes 65560
  8.0 0.0 copy-start.5
  8.0 0.7 %copy-done.5 = s32[128]{0:T(128)S(1)} copy-done((s32[128]{0:T(128)S(1)}, s32[128]{0:T(128)}, u32[]{:S(2)}) %copy-start.5) | copy-done | bytes 536
  8.6 0.0 copy-start
  8.6 0.0 copy-start.1
  8.6 0.0 copy-start.2
  8.6 0.0 copy-start.6
  8.6 0.2 prepare.1
  8.8 0.5 collective-permute-done.edge_ref
  9.3 0.7 %copy-done = bf16[3,128,2048]{2,1,0:T(8,128)(2,1)S(1)} copy-done((bf16[3,128,2048]{2,1,0:T(8,128)(2,1)S(1)}, bf16[3,128,2048]{2,1,0:T(8,128)(2,1)}, u32[]{:S(2)}) %copy-start) | copy-done | bytes 1572888
  10.0 0.1 copy-done.1
  10.2 0.0 copy-done.2
  10.2 0.0 copy-done.6
  10.2 1.9 %features.3 = (f32[3,128,1024]{2,1,0:T(8,128)S(1)}, bf16[128,1024]{1,0:T(8,128)(2,1)S(1)}, bf16[128,1024]{1,0:T(8,128)(2,1)S(1)}) custom-call(s32[1,128]{1,0:T(1,128)S(1)} %bitcast.12, bf16[768,128]{1,0:T(8,128)(2,1)S(1)} %get-tuple-element.47.delay_ref, bf16[3,8,2048]{2,1,0:T(8,128)(2,1)S(1)} %collective-permute-done.edge_ref, f32[3,7,2048]{2,1,0:T(8,128)S(1)} %bitcast.5, ...), custom_call_target="tpu_custom_call" | custom-call | flops 2000000000 | bytes 4000000 | tf_op jit(solution)/shard_map/features/pallas_call | solution.py:361
  12.2 3.5 %collective-permute-start.2 = (bf16[128,1024]{1,0:T(8,128)(2,1)S(1)}, bf16[128,1024]{1,0:T(8,128)(2,1)S(1)}, u32[]{:S(2)}, u32[]{:S(2)}) collective-permute-start(bf16[128,1024]{1,0:T(8,128)(2,1)S(1)} %get-tuple-element.51), channel_id=1, source_target_pairs={{0,4},{4,8},{8,12},{12,16},{16,20},{20,24},{24,28},{1,5},{5,9},{9,... | collective-permute-start | bytes 786440 | tf_op jit(solution)/shard_map/ppermute | solution.py:27
  15.6 0.0 copy-start.4
  15.7 1.4 %collective-permute-start.3 = (bf16[128,1024]{1,0:T(8,128)(2,1)S(1)}, bf16[128,1024]{1,0:T(8,128)(2,1)S(1)}, u32[]{:S(2)}, u32[]{:S(2)}) collective-permute-start(bf16[128,1024]{1,0:T(8,128)(2,1)S(1)} %get-tuple-element.54), channel_id=1, source_target_pairs={{4,0},{8,4},{12,8},{16,12},{20,16},{24,20},{28,24},{5,1},{9,5},{13... | collective-permute-start | bytes 786440 | tf_op jit(solution)/shard_map/ppermute | solution.py:27
  17.1 2.0 %features.2 = (f32[3,128,1024]{2,1,0:T(8,128)S(1)}, bf16[128,1024]{1,0:T(8,128)(2,1)S(1)}, bf16[128,1024]{1,0:T(8,128)(2,1)S(1)}) custom-call(s32[1,128]{1,0:T(1,128)S(1)} %bitcast.13, bf16[768,128]{1,0:T(8,128)(2,1)S(1)} %get-tuple-element.47.delay_ref, bf16[3,8,2048]{2,1,0:T(8,128)(2,1)S(1)} %collective-permute-done.edge_ref, f32[3,7,2048]{2,1,0:T(8,128)S(1)} %bitcast.6, ...), custom_call_target="tpu_custom_call" | custom-call | flops 2000000000 | bytes 4000000 | tf_op jit(solution)/shard_map/features/pallas_call | solution.py:361
  19.1 5.0 %collective-permute-start.1 = (bf16[128,1024]{1,0:T(8,128)(2,1)S(1)}, bf16[128,1024]{1,0:T(8,128)(2,1)S(1)}, u32[]{:S(2)}, u32[]{:S(2)}) collective-permute-start(bf16[128,1024]{1,0:T(8,128)(2,1)S(1)} %get-tuple-element.49), channel_id=1, source_target_pairs={{0,4},{4,8},{8,12},{12,16},{16,20},{20,24},{24,28},{1,5},{5,9},{9,... | collective-permute-start | bytes 786440 | tf_op jit(solution)/shard_map/ppermute | solution.py:27
  24.1 1.3 %collective-permute-start.4 = (bf16[128,1024]{1,0:T(8,128)(2,1)S(1)}, bf16[128,1024]{1,0:T(8,128)(2,1)S(1)}, u32[]{:S(2)}, u32[]{:S(2)}) collective-permute-start(bf16[128,1024]{1,0:T(8,128)(2,1)S(1)} %get-tuple-element.64), channel_id=1, source_target_pairs={{4,0},{8,4},{12,8},{16,12},{20,16},{24,20},{28,24},{5,1},{9,5},{13... | collective-permute-start | bytes 786440 | tf_op jit(solution)/shard_map/ppermute | solution.py:27
  25.4 2.3 %collective-permute-done.2.kvp_ref = bf16[128,1024]{1,0:T(8,128)(2,1)S(1)} collective-permute-done((bf16[128,1024]{1,0:T(8,128)(2,1)S(1)}, bf16[128,1024]{1,0:T(8,128)(2,1)S(1)}, u32[]{:S(2)}, u32[]{:S(2)}) %collective-permute-start.2) | collective-permute-done | bytes 262176 | tf_op jit(solution)/shard_map/ppermute | solution.py:27
  27.7 0.0 copy-done.4
  27.7 5.3 %query.2 = (bf16[128,2048]{1,0:T(8,128)(2,1)}, bf16[3,128,2048]{2,1,0:T(8,128)(2,1)}, f32[3,8,2048]{2,1,0:T(8,128)S(1)}, bf16[3,8,2048]{2,1,0:T(8,128)(2,1)S(1)}, bf16[8,32,256]{2,1,0:T(8,128)(2,1)}) custom-call(s32[1,128]{1,0:T(1,128)S(1)} %bitcast.14, f32[3,7,2048]{2,1,0:T(8,128)S(1)} %bitcast.7, f32[128,128]{1,0:T(8,128)S(1)} %copy-done.4, ...), custom_call_target="tpu_custom_call" | custom-call | flops 4000000000 | bytes 4000000 | tf_op jit(solution)/shard_map/query/pallas_call | solution.py:395
  33.0 0.0 collective-permute-done.3.gn_ref
  33.0 3.6 %pair.2 = (bf16[3,128,2048]{2,1,0:T(8,128)(2,1)}, f32[3,8,2048]{2,1,0:T(8,128)S(1)}, bf16[3,8,2048]{2,1,0:T(8,128)(2,1)S(1)}, bf16[8,32,256]{2,1,0:T(8,128)(2,1)}) custom-call(s32[1,128]{1,0:T(1,128)S(1)} %bitcast.15, f32[3,7,2048]{2,1,0:T(8,128)S(1)} %bitcast.8, ...), custom_call_target="tpu_custom_call", output_to_operand_aliasing={{0}: (9, {}), {1}: (10, {}), {2}: (11, {}), {3}: (12, {})} | custom-call | flops 4000000000 | bytes 4000000 | tf_op jit(solution)/shard_map/pair/pallas_call | solution.py:422
  36.7 1.1 %collective-permute-done.1.kvp_ref = bf16[128,1024]{1,0:T(8,128)(2,1)S(1)} collective-permute-done((bf16[128,1024]{1,0:T(8,128)(2,1)S(1)}, bf16[128,1024]{1,0:T(8,128)(2,1)S(1)}, u32[]{:S(2)}, u32[]{:S(2)}) %collective-permute-start.1) | collective-permute-done | bytes 262176 | tf_op jit(solution)/shard_map/ppermute | solution.py:27
  37.7 5.3 %query.3 = (bf16[128,2048]{1,0:T(8,128)(2,1)}, bf16[3,128,2048]{2,1,0:T(8,128)(2,1)}, f32[3,8,2048]{2,1,0:T(8,128)S(1)}, bf16[3,8,2048]{2,1,0:T(8,128)(2,1)S(1)}, bf16[8,32,256]{2,1,0:T(8,128)(2,1)}) custom-call(s32[1,128]{1,0:T(1,128)S(1)} %bitcast.16, ...), custom_call_target="tpu_custom_call", output_to_operand_aliasing={{0}: (9, {}), {1}: (10, {}), {2}: (11, {}), {3}: (12, {}), ... | custom-call | flops 4000000000 | bytes 4000000 | tf_op jit(solution)/shard_map/query/pallas_call | solution.py:395
  43.1 0.0 collective-permute-done.4.gn_ref
  43.1 3.6 %pair.3 = (bf16[3,128,2048]{2,1,0:T(8,128)(2,1)}, f32[3,8,2048]{2,1,0:T(8,128)S(1)}, bf16[3,8,2048]{2,1,0:T(8,128)(2,1)S(1)}, bf16[8,32,256]{2,1,0:T(8,128)(2,1)}) custom-call(s32[1,128]{1,0:T(1,128)S(1)} %bitcast.17, f32[3,7,2048]{2,1,0:T(8,128)S(1)} %bitcast.10, ...), custom_call_target="tpu_custom_call", output_to_operand_aliasing={{0}: (9, {}), {1}: (10, {}), {2}: (11, {}), {3}: (12, {})} | custom-call | flops 4000000000 | bytes 4000000 | tf_op jit(solution)/shard_map/pair/pallas_call | solution.py:422
  46.7 5.8 %all-to-all-start = ((bf16[8,32,256]{2,1,0:T(8,128)(2,1)}), bf16[8,32,256]{2,1,0:T(8,128)(2,1)S(1)}, u32[]{:S(2)}, u32[]{:S(2)}) async-start(bf16[8,32,256]{2,1,0:T(8,128)(2,1)} %get-tuple-element.69), calls=%async_computation | async-start | bytes 262144 | tf_op jit(solution)/shard_map/all_to_all | solution.py:450
  52.5 1.3 %collective-permute-start.5 = (bf16[3,8,2048]{2,1,0:T(8,128)(2,1)S(1)}, bf16[3,8,2048]{2,1,0:T(8,128)(2,1)S(1)}, u32[]{:S(2)}, u32[]{:S(2)}) collective-permute-start(bf16[3,8,2048]{2,1,0:T(8,128)(2,1)S(1)} %get-tuple-element.71), channel_id=1, source_target_pairs={{4,0},{8,4},{12,8},{16,12},{20,16},{24,20},{28,24},{5,1},{9,5},{13... | collective-permute-start | bytes 294920 | tf_op jit(solution)/shard_map/ppermute | solution.py:27
  53.8 5.4 %collective-permute-done.5.part_ref = bf16[3,8,2048]{2,1,0:T(8,128)(2,1)S(1)} collective-permute-done((bf16[3,8,2048]{2,1,0:T(8,128)(2,1)S(1)}, bf16[3,8,2048]{2,1,0:T(8,128)(2,1)S(1)}, u32[]{:S(2)}, u32[]{:S(2)}) %collective-permute-start.5) | collective-permute-done | bytes 98336 | tf_op jit(solution)/shard_map/ppermute | solution.py:27
  59.2 0.7 %all-to-all-done.got_ref = bf16[8,32,256]{2,1,0:T(8,128)(2,1)S(1)} async-done(((bf16[8,32,256]{2,1,0:T(8,128)(2,1)}), bf16[8,32,256]{2,1,0:T(8,128)(2,1)S(1)}, u32[]{:S(2)}, u32[]{:S(2)}) %all-to-all-start) | async-done | bytes 131104 | tf_op jit(solution)/shard_map/all_to_all | solution.py:450
  59.9 1.3 %finish.1 = (bf16[3,128,2048]{2,1,0:T(8,128)(2,1)}, f32[16,128]{1,0:T(8,128)}, f32[3,7,256]{2,1,0:T(8,128)}) custom-call(bf16[8,32,256]{2,1,0:T(8,128)(2,1)S(1)} %all-to-all-done.got_ref, f32[3,8,2048]{2,1,0:T(8,128)S(1)} %get-tuple-element.70.tail_ref, bf16[3,8,2048]{2,1,0:T(8,128)(2,1)S(1)} %collective-permute-done.5.part_ref, ...), custom_call_target="tpu_custom_call", output_to_operand_aliasing={{0}: (3, {})} | custom-call | flops 1000000 | bytes 200000 | tf_op jit(solution)/shard_map/finish/pallas_call | solution.py:451
Async XLA Ops:
  2.3 7.0 %collective-permute-start = (bf16[3,8,2048]{2,1,0:T(8,128)(2,1)S(1)}, bf16[3,8,2048]{2,1,0:T(8,128)(2,1)S(1)}, u32[]{:S(2)}, u32[]{:S(2)}) collective-permute-start(bf16[3,8,2048]{2,1,0:T(8,128)(2,1)S(1)} %scatter.4), channel_id=1, source_target_pairs={{0,4},{4,8},{8,12},{12,16},{16,20},{20,24},{24,28},{1,5},{5,9},{9,... | collective-permute-start | bytes 294920 | tf_op jit(solution)/shard_map/ppermute | solution.py:27
  7.1 0.8 %copy-start.3 = (f32[128,128]{1,0:T(8,128)S(1)}, f32[128,128]{1,0:T(8,128)}, u32[]{:S(2)}) copy-start(f32[128,128]{1,0:T(8,128)} %lf_ref.5) | copy-start | bytes 196612
  8.0 0.7 %copy-start.5 = (s32[128]{0:T(128)S(1)}, s32[128]{0:T(128)}, u32[]{:S(2)}) copy-start(s32[128]{0:T(128)} %param.9) | copy-start | bytes 1540
  8.6 1.4 %copy-start = (bf16[3,128,2048]{2,1,0:T(8,128)(2,1)S(1)}, bf16[3,128,2048]{2,1,0:T(8,128)(2,1)}, u32[]{:S(2)}) copy-start(bf16[3,128,2048]{2,1,0:T(8,128)(2,1)} %x_ref.7) | copy-start | bytes 4718596
  8.6 1.5 %copy-start.1 = (bf16[128,2048]{1,0:T(8,128)(2,1)S(1)}, bf16[128,2048]{1,0:T(8,128)(2,1)}, u32[]{:S(2)}) copy-start(bf16[128,2048]{1,0:T(8,128)(2,1)} %cot_ref.7) | copy-start | bytes 1572868
  8.6 1.6 %copy-start.2 = (f32[3,2048,7]{1,2,0:T(8,128)S(1)}, f32[3,2048,7]{1,2,0:T(8,128)}, u32[]{:S(2)}) copy-start(f32[3,2048,7]{1,2,0:T(8,128)} %param.10) | copy-start | bytes 516100
  8.6 1.6 %copy-start.6 = (s32[128]{0:T(128)S(1)}, s32[128]{0:T(128)}, u32[]{:S(2)}) copy-start(s32[128]{0:T(128)} %param.9) | copy-start | bytes 1540
  12.2 15.5 %collective-permute-start.2 = (bf16[128,1024]{1,0:T(8,128)(2,1)S(1)}, bf16[128,1024]{1,0:T(8,128)(2,1)S(1)}, u32[]{:S(2)}, u32[]{:S(2)}) collective-permute-start(bf16[128,1024]{1,0:T(8,128)(2,1)S(1)} %get-tuple-element.51), channel_id=1, source_target_pairs={{0,4},{4,8},{8,12},{12,16},{16,20},{20,24},{24,28},{1,5},{5,9},{9,... | collective-permute-start | bytes 786440 | tf_op jit(solution)/shard_map/ppermute | solution.py:27
  15.6 12.0 %copy-start.4 = (f32[128,128]{1,0:T(8,128)S(1)}, f32[128,128]{1,0:T(8,128)}, u32[]{:S(2)}) copy-start(f32[128,128]{1,0:T(8,128)} %lf_ref.5) | copy-start | bytes 196612
  15.7 17.4 %collective-permute-start.3 = (bf16[128,1024]{1,0:T(8,128)(2,1)S(1)}, bf16[128,1024]{1,0:T(8,128)(2,1)S(1)}, u32[]{:S(2)}, u32[]{:S(2)}) collective-permute-start(bf16[128,1024]{1,0:T(8,128)(2,1)S(1)} %get-tuple-element.54), channel_id=1, source_target_pairs={{4,0},{8,4},{12,8},{16,12},{20,16},{24,20},{28,24},{5,1},{9,5},{13... | collective-permute-start | bytes 786440 | tf_op jit(solution)/shard_map/ppermute | solution.py:27
  19.1 18.7 %collective-permute-start.1 = (bf16[128,1024]{1,0:T(8,128)(2,1)S(1)}, bf16[128,1024]{1,0:T(8,128)(2,1)S(1)}, u32[]{:S(2)}, u32[]{:S(2)}) collective-permute-start(bf16[128,1024]{1,0:T(8,128)(2,1)S(1)} %get-tuple-element.49), channel_id=1, source_target_pairs={{0,4},{4,8},{8,12},{12,16},{16,20},{20,24},{24,28},{1,5},{5,9},{9,... | collective-permute-start | bytes 786440 | tf_op jit(solution)/shard_map/ppermute | solution.py:27
  24.1 19.0 %collective-permute-start.4 = (bf16[128,1024]{1,0:T(8,128)(2,1)S(1)}, bf16[128,1024]{1,0:T(8,128)(2,1)S(1)}, u32[]{:S(2)}, u32[]{:S(2)}) collective-permute-start(bf16[128,1024]{1,0:T(8,128)(2,1)S(1)} %get-tuple-element.64), channel_id=1, source_target_pairs={{4,0},{8,4},{12,8},{16,12},{20,16},{24,20},{28,24},{5,1},{9,5},{13... | collective-permute-start | bytes 786440 | tf_op jit(solution)/shard_map/ppermute | solution.py:27
  46.7 13.1 %all-to-all-start = ((bf16[8,32,256]{2,1,0:T(8,128)(2,1)}), bf16[8,32,256]{2,1,0:T(8,128)(2,1)S(1)}, u32[]{:S(2)}, u32[]{:S(2)}) async-start(bf16[8,32,256]{2,1,0:T(8,128)(2,1)} %get-tuple-element.69), calls=%async_computation | async-start | bytes 262144 | tf_op jit(solution)/shard_map/all_to_all | solution.py:450
  52.5 6.7 %collective-permute-start.5 = (bf16[3,8,2048]{2,1,0:T(8,128)(2,1)S(1)}, bf16[3,8,2048]{2,1,0:T(8,128)(2,1)S(1)}, u32[]{:S(2)}, u32[]{:S(2)}) collective-permute-start(bf16[3,8,2048]{2,1,0:T(8,128)(2,1)S(1)} %get-tuple-element.71), channel_id=1, source_target_pairs={{4,0},{8,4},{12,8},{16,12},{20,16},{24,20},{28,24},{5,1},{9,5},{13... | collective-permute-start | bytes 294920 | tf_op jit(solution)/shard_map/ppermute | solution.py:27

commit v6 on v5

--- a/solution.py
+++ b/solution.py
@@ -115,12 +115,21 @@
     lax.fori_loop(0, steps, one_step, 0)
 
 
-def store_all(copies, steps):
+def run_steps(parts, steps):
+    def start(p, carry):
+        for one_step, copies in parts:
+            one_step(p)
+            for copy in copies(p):
+                copy.start()
+        return carry
+
     def drain(p, carry):
-        for copy in copies(p):
-            copy.wait()
+        for _, copies in parts:
+            for copy in copies(p):
+                copy.wait()
         return carry
 
+    lax.fori_loop(0, steps, start, 0)
     lax.fori_loop(0, steps, drain, 0)
 
 
@@ -154,12 +163,12 @@
     return acc, sent, jnp.concatenate(sums, 0)
 
 
-def query_kernel(first, filled, ids_ref, sf_ref, lf_ref, advance_ref, x_ref, cot_ref, edge_ref,
-                 feat_ref, kvp_ref, *refs):
-    (out_hbm, qg_hbm, tail_hbm, part_hbm, packed_hbm, out_ref, qg_ref, tail_ref, part_ref, short_ref, long_ref,
-     edge_shift, mask_y, mask_a, w_kv, g_rev, dh_ref, kv_turned, y_turned, sems) = refs[filled:]
+def query_part(first, shared, lf_ref, feat_ref, kvp_ref, outs, scratch):
+    ids_ref, sf_ref, advance_ref, x_ref, cot_ref, edge_ref = shared
+    out_hbm, qg_hbm, tail_hbm, part_hbm, packed_hbm = outs
+    (out_ref, qg_ref, tail_ref, part_ref, short_ref, long_ref,
+     edge_shift, mask_y, mask_a, w_kv, g_rev, dh_ref, kv_turned, y_turned, sems) = scratch
     rows = x_ref.shape[1]
-    count = kvp_ref.shape[1]
     width = x_ref.shape[2] // lf_ref.shape[0]
     half = rows
     per = half // width
@@ -193,7 +202,7 @@
         ]
         return [pltpu.make_async_copy(src, dst, sems.at[k, p]) for k, (src, dst) in enumerate(pairs)]
 
-    def one_step(p, carry):
+    def one_step(p):
         near = lane_range(p * LANES, LANES)
         cols = lane_range(first + p * LANES, LANES)
         cot = cot_ref[:, cols].astype(F32)
@@ -211,9 +220,7 @@
                 toeplitz = jnp.concatenate([taps, taps], 0) * mask_y[...]
                 y_turned[mine] = dot(kv_turned[mine], toeplitz)
                 g_sel = jnp.where(owner == j, g_rev[:, part], jnp.zeros((rows, half), BF16))
-                cross = lax.dot_general(
-                    g_sel, w_kv[:, part], (((1,), (1,)), ((), ())), preferred_element_type=F32
-                ) * mask_a[...]
+                cross = dot(g_sel, kv_turned[part, :]) * mask_a[...]
                 folded = cross[:, 0:rows] + cross[:, rows:]
                 folded = pltpu.roll(folded, 0, 1, stride=1, stride_axis=0)
                 dh_ref[q * per + j : q * per + j + 1] = jnp.sum(folded, 0, keepdims=True)
@@ -232,20 +239,16 @@
             short_ref[p * blocks + k] = sums[:, k * CHUNK : (k + 1) * CHUNK].astype(BF16)
             lines = range(k * (CHUNK // rows), (k + 1) * (CHUNK // rows))
             long_ref[p * blocks + k] = jnp.concatenate([dh[e * size : (e + 1) * size] for e in lines], 1).astype(BF16)
-        for copy in copies(p):
-            copy.start()
-        return carry
-
-    lax.fori_loop(0, count // LANES, one_step, 0)
-    store_all(copies, count // LANES)
-
-
-def pair_kernel(first, filled, ids_ref, sf_ref, lfr_ref, advance_ref, x_ref, cot_ref, edge_ref,
-                feat_ref, gn_ref, *refs):
-    (qg_hbm, tail_hbm, part_hbm, packed_hbm, qg_ref, tail_ref, part_ref, short_ref,
-     edge_shift, mask_g, w_g, g_turned, gm_turned, sems) = refs[filled:]
+
+    return one_step, copies
+
+
+def pair_part(first, shared, lfr_ref, feat_ref, gn_ref, outs, scratch):
+    ids_ref, sf_ref, advance_ref, x_ref, cot_ref, edge_ref = shared
+    _, qg_hbm, tail_hbm, part_hbm, packed_hbm = outs
+    (qg_ref, tail_ref, part_ref, short_ref,
+     edge_shift, mask_g, w_g, g_turned, gm_turned, sems) = scratch
     rows = x_ref.shape[1]
-    count = gn_ref.shape[1]
     width = x_ref.shape[2] // lfr_ref.shape[0]
     lag = iota2((rows, rows), 0) - iota2((rows, rows), 1)
     id_row = jnp.broadcast_to(ids_ref[...], (rows, rows)).astype(F32)
@@ -269,7 +272,7 @@
         ]
         return [pltpu.make_async_copy(src, dst, sems.at[k, p]) for k, (src, dst) in enumerate(pairs)]
 
-    def one_step(p, carry):
+    def one_step(p):
         near = lane_range(p * LANES, LANES)
         cols = lane_range(first + p * LANES, LANES)
         w_g[0:rows] = (cot_ref[:, cols].astype(F32) * feat_ref[0, :, near]).astype(BF16)
@@ -296,12 +299,25 @@
         for k in range(blocks):
             picked = [head[:, k * CHUNK : (k + 1) * CHUNK] for head in heads]
             short_ref[p * blocks + k] = jnp.concatenate(picked, 0).astype(BF16)
-        for copy in copies(p):
-            copy.start()
-        return carry
-
-    lax.fori_loop(0, count // LANES, one_step, 0)
-    store_all(copies, count // LANES)
+
+    return one_step, copies
+
+
+def mixer_kernel(query_first, pair_first, filled, *refs):
+    shared = refs[:6]
+    halves = [query_first, pair_first]
+    inputs = refs[6:]
+    used = 3 * sum(first is not None for first in halves)
+    outs = inputs[used + filled : used + filled + 5]
+    scratch = inputs[used + filled + 5 :]
+    parts = []
+    for first, make, size in zip(halves, (query_part, pair_part), (15, 10)):
+        if first is not None:
+            steps = inputs[2].shape[1] // LANES
+            parts.append(make(first, shared, *inputs[:3], outs, scratch[:size]))
+            inputs = inputs[3:]
+            scratch = scratch[size:]
+    run_steps(parts, steps)
 
 
 def finish_kernel(scale, taps, got_ref, tail_ref, part_ref, qg_in, qg_hbm, long_ref, short_ref, last_ref, sem):
@@ -388,60 +404,60 @@
         jax.ShapeDtypeStruct((chans // CHUNK, packed_rows, CHUNK), BF16),
     ]
     edge_scratch = pltpu.VMEM(((taps - 1) * EDGE, rows), BF16)
+    query_scratch = [
+        pltpu.VMEM((rows, count), BF16),
+        pltpu.VMEM((rows, count), BF16),
+        pltpu.VMEM((EDGE, count), F32),
+        pltpu.VMEM((EDGE, count), BF16),
+        pltpu.VMEM((count // CHUNK, PADDED, CHUNK), BF16),
+        pltpu.VMEM((count // CHUNK, packed_rows - 3 * PADDED, CHUNK), BF16),
+        edge_scratch,
+        pltpu.VMEM((2 * rows, rows), BF16),
+        pltpu.VMEM((rows, 2 * rows), F32),
+        pltpu.VMEM((2 * rows, LANES), BF16),
+        pltpu.VMEM((rows, LANES), BF16),
+        pltpu.VMEM((step_groups, long_taps), F32),
+        pltpu.VMEM((LANES, 2 * rows), BF16),
+        pltpu.VMEM((LANES, rows), F32),
+        pltpu.SemaphoreType.DMA((6, count // LANES)),
+    ]
+    pair_scratch = [
+        pltpu.VMEM((2, rows, count), BF16),
+        pltpu.VMEM((2, EDGE, count), F32),
+        pltpu.VMEM((2, EDGE, count), BF16),
+        pltpu.VMEM((count // CHUNK, 2 * PADDED, CHUNK), BF16),
+        edge_scratch,
+        pltpu.VMEM((2 * rows, rows), BF16),
+        pltpu.VMEM((2 * rows, LANES), BF16),
+        pltpu.VMEM((LANES, 2 * rows), BF16),
+        pltpu.VMEM((LANES, rows), F32),
+        pltpu.SemaphoreType.DMA((4, count // LANES)),
+    ]
     results = []
-    for part in range(PARTS):
-        feats, kv_prev, grad_next = sent[part]
+    for stage in range(PARTS + 1):
+        operands = [ids, sf, advance, qkv, cotangent, edge]
+        scratch = []
+        query_first = pair_first = None
+        if stage < PARTS:
+            query_first = stage * count
+            operands += [long_filter, sent[stage][0], sent[stage][1]]
+            scratch += query_scratch
+        if stage > 0:
+            pair_first = (stage - 1) * count
+            operands += [lf_rev, sent[stage - 1][0], sent[stage - 1][2]]
+            scratch += pair_scratch
         filled = len(results)
-        out, *rest = pl.pallas_call(
-            functools.partial(query_kernel, part * count, filled),
-            in_specs=[VMEM] * 9 + [ANY] * filled,
+        results = pl.pallas_call(
+            functools.partial(mixer_kernel, query_first, pair_first, filled),
+            in_specs=[VMEM] * len(operands) + [ANY] * filled,
             out_specs=[ANY] * 5,
             out_shape=full,
-            input_output_aliases={9 + k: k for k in range(filled)},
-            scratch_shapes=[
-                pltpu.VMEM((rows, count), BF16),
-                pltpu.VMEM((rows, count), BF16),
-                pltpu.VMEM((EDGE, count), F32),
-                pltpu.VMEM((EDGE, count), BF16),
-                pltpu.VMEM((count // CHUNK, PADDED, CHUNK), BF16),
-                pltpu.VMEM((count // CHUNK, packed_rows - 3 * PADDED, CHUNK), BF16),
-                edge_scratch,
-                pltpu.VMEM((2 * rows, rows), BF16),
-                pltpu.VMEM((rows, 2 * rows), F32),
-                pltpu.VMEM((2 * rows, LANES), BF16),
-                pltpu.VMEM((rows, LANES), BF16),
-                pltpu.VMEM((step_groups, long_taps), F32),
-                pltpu.VMEM((LANES, 2 * rows), BF16),
-                pltpu.VMEM((LANES, rows), F32),
-                pltpu.SemaphoreType.DMA((6, count // LANES)),
-            ],
+            input_output_aliases={len(operands) + k: k for k in range(filled)},
+            scratch_shapes=scratch,
             compiler_params=params,
             cost_estimate=pl.CostEstimate(flops=4_000_000_000, bytes_accessed=4_000_000, transcendentals=0),
-            name="query",
-        )(ids, sf, long_filter, advance, qkv, cotangent, edge, feats, kv_prev, *results)
-        rest = pl.pallas_call(
-            functools.partial(pair_kernel, part * count, 4),
-            in_specs=[VMEM] * 9 + [ANY] * 4,
-            out_specs=[ANY] * 4,
-            out_shape=full[1:],
-            input_output_aliases={9 + k: k for k in range(4)},
-            scratch_shapes=[
-                pltpu.VMEM((2, rows, count), BF16),
-                pltpu.VMEM((2, EDGE, count), F32),
-                pltpu.VMEM((2, EDGE, count), BF16),
-                pltpu.VMEM((count // CHUNK, 2 * PADDED, CHUNK), BF16),
-                edge_scratch,
-                pltpu.VMEM((2 * rows, rows), BF16),
-                pltpu.VMEM((2 * rows, LANES), BF16),
-                pltpu.VMEM((LANES, 2 * rows), BF16),
-                pltpu.VMEM((LANES, rows), F32),
-                pltpu.SemaphoreType.DMA((4, count // LANES)),
-            ],
-            compiler_params=params,
-            cost_estimate=pl.CostEstimate(flops=4_000_000_000, bytes_accessed=4_000_000, transcendentals=0),
-            name="pair",
-        )(ids, sf, lf_rev, advance, qkv, cotangent, edge, feats, grad_next, *rest)
-        results = [out, *rest]
+            name=f"mixer{stage}",
+        )(*operands, *results)
     out, qg, tail, part, packed = results
 
     part = passed_along(part, -1)

time: 61.6 us -> 65.2 us (1.058)
  waiting for transfers between devices: 9.95 us -> 13.9 us
  Pallas kernels: 23.3 us -> 22.2 us
  starting transfers between devices: 23.1 us -> 23.8 us
    ppermute x6, waiting for transfers between devices: 9.29 us -> 13.2 us  [passed_along(): return lax.ppermute(block, 'ctx', route)]
    pallas_call x4 -> x3, Pallas kernels: 17.9 us -> 16.9 us  [shards(): pl.pallas_call(functools.partial(mixer_kernel, query_first, pair_first, f...]
  transfers between devices with their start and end apart: 7 -> 7, of which waited for: 5 -> 4; matrix products, arithmetic and copies ran while one was open for 0% -> 0% of each run, Pallas kernels for 27% -> 24%
where the time goes in v6:
time: 65.2 us; the launch traced here: 64.7 us
  starting transfers between devices  23.8 us (37%)
  Pallas kernels  22.2 us (34%)
  waiting for transfers between devices  13.9 us (21%)
  local copies, waits for them, and re-layouts  3.4 us (5%)
  between operations  0.78 us (1%)
  other arithmetic  0.66 us (1%)
    ppermute x6, starting transfers between devices, passed_along(): return lax.ppermute(block, 'ctx', route)  18 us
    pallas_call x3, Pallas kernels, shards(): pl.pallas_call(functools.partial(mixer_kernel, query_first, pair_first, f...  16.9 us
    ppermute x6, waiting for transfers between devices, passed_along(): return lax.ppermute(block, 'ctx', route)  13.2 us
    all_to_all x1, starting transfers between devices, shards(): got = lax.all_to_all(packed, 'ctx', 0, 0)  5.82 us
    pallas_call x2, Pallas kernels, shards(): pl.pallas_call(functools.partial(feature_kernel, part * count), in_specs=...  3.9 us
    unnamed x14, local copies, waits for them, and re-layouts  2.37 us
  transfers between devices with their start and end apart: 7, of which 4 were waited for; matrix products, arithmetic and copies ran while one was open for 0% of the time, Pallas kernels for 24%

profile of v6, /device:TPU:0, one launch (start us, length us, event | category | flops | bytes accessed | tf_op | source)
XLA Modules:
  0.0 64.7 jit_solution(3026377493656912864)
XLA Ops:
  0.6 0.7 %convert_bitcast_fusion = bf16[1,1,128]{2,1,0:T(2,128)(2,1)S(1)} fusion(s32[128]{0:T(128)} %param.9), kind=kLoop, calls=%fused_computation | loop fusion | flops 128 | bytes 768 | tf_op jit(solution)/shard_map/reshape.24
  1.3 0.9 %slice.26 = bf16[3,8,2048]{2,1,0:T(8,128)(2,1)S(1)} slice(bf16[3,128,2048]{2,1,0:T(8,128)(2,1)} %refs_3_.5), slice={[0:3], [120:128], [0:2048]} | slice | bytes 196608 | tf_op jit(solution)/shard_map/slice | solution.py:355
  2.2 0.1 scatter.4
  2.3 4.8 %collective-permute-start = (bf16[3,8,2048]{2,1,0:T(8,128)(2,1)S(1)}, bf16[3,8,2048]{2,1,0:T(8,128)(2,1)S(1)}, u32[]{:S(2)}, u32[]{:S(2)}) collective-permute-start(bf16[3,8,2048]{2,1,0:T(8,128)(2,1)S(1)} %scatter.4), channel_id=1, source_target_pairs={{0,4},{4,8},{8,12},{12,16},{16,20},{20,24},{24,28},{1,5},{5,9},{9,... | collective-permute-start | bytes 294920 | tf_op jit(solution)/shard_map/ppermute | solution.py:27
  7.2 0.0 copy-start.3
  7.2 0.8 %copy-done.3 = f32[128,128]{1,0:T(8,128)S(1)} copy-done((f32[128,128]{1,0:T(8,128)S(1)}, f32[128,128]{1,0:T(8,128)}, u32[]{:S(2)}) %copy-start.3) | copy-done | bytes 65560
  8.0 0.0 copy-start.5
  8.0 0.7 %copy-done.5 = s32[128]{0:T(128)S(1)} copy-done((s32[128]{0:T(128)S(1)}, s32[128]{0:T(128)}, u32[]{:S(2)}) %copy-start.5) | copy-done | bytes 536
  8.7 0.0 copy-start
  8.7 0.0 copy-start.1
  8.7 0.0 copy-start.2
  8.7 0.0 copy-start.6
  8.7 0.2 prepare.1
  8.9 0.5 collective-permute-done.edge_ref.refs_5_
  9.4 0.7 %copy-done = bf16[3,128,2048]{2,1,0:T(8,128)(2,1)S(1)} copy-done((bf16[3,128,2048]{2,1,0:T(8,128)(2,1)S(1)}, bf16[3,128,2048]{2,1,0:T(8,128)(2,1)}, u32[]{:S(2)}) %copy-start) | copy-done | bytes 1572888
  10.1 0.1 copy-done.1
  10.2 0.0 copy-done.2
  10.2 0.0 copy-done.6
  10.2 1.9 %features.3 = (f32[3,128,1024]{2,1,0:T(8,128)S(1)}, bf16[128,1024]{1,0:T(8,128)(2,1)S(1)}, bf16[128,1024]{1,0:T(8,128)(2,1)S(1)}) custom-call(s32[1,128]{1,0:T(1,128)S(1)} %bitcast.11, bf16[768,128]{1,0:T(8,128)(2,1)S(1)} %get-tuple-element.45.delay_ref, bf16[3,8,2048]{2,1,0:T(8,128)(2,1)S(1)} %collective-permute-done.edge_ref.refs_5_, ...), custom_call_target="tpu_custom_call" | custom-call | flops 2000000000 | bytes 4000000 | tf_op jit(solution)/shard_map/features/pallas_call | solution.py:377
  12.2 3.5 %collective-permute-start.4 = (bf16[128,1024]{1,0:T(8,128)(2,1)S(1)}, bf16[128,1024]{1,0:T(8,128)(2,1)S(1)}, u32[]{:S(2)}, u32[]{:S(2)}) collective-permute-start(bf16[128,1024]{1,0:T(8,128)(2,1)S(1)} %get-tuple-element.51), channel_id=1, source_target_pairs={{0,4},{4,8},{8,12},{12,16},{16,20},{20,24},{24,28},{1,5},{5,9},{9,... | collective-permute-start | bytes 786440 | tf_op jit(solution)/shard_map/ppermute | solution.py:27
  15.7 0.0 copy-start.4
  15.7 1.4 %collective-permute-start.3 = (bf16[128,1024]{1,0:T(8,128)(2,1)S(1)}, bf16[128,1024]{1,0:T(8,128)(2,1)S(1)}, u32[]{:S(2)}, u32[]{:S(2)}) collective-permute-start(bf16[128,1024]{1,0:T(8,128)(2,1)S(1)} %get-tuple-element.50), channel_id=1, source_target_pairs={{4,0},{8,4},{12,8},{16,12},{20,16},{24,20},{28,24},{5,1},{9,5},{13... | collective-permute-start | bytes 786440 | tf_op jit(solution)/shard_map/ppermute | solution.py:27
  17.1 2.0 %features.2 = (f32[3,128,1024]{2,1,0:T(8,128)S(1)}, bf16[128,1024]{1,0:T(8,128)(2,1)S(1)}, bf16[128,1024]{1,0:T(8,128)(2,1)S(1)}) custom-call(s32[1,128]{1,0:T(1,128)S(1)} %bitcast.12, bf16[768,128]{1,0:T(8,128)(2,1)S(1)} %get-tuple-element.45.delay_ref, bf16[3,8,2048]{2,1,0:T(8,128)(2,1)S(1)} %collective-permute-done.edge_ref.refs_5_, ...), custom_call_target="tpu_custom_call" | custom-call | flops 2000000000 | bytes 4000000 | tf_op jit(solution)/shard_map/features/pallas_call | solution.py:377
  19.1 1.3 %collective-permute-start.1 = (bf16[128,1024]{1,0:T(8,128)(2,1)S(1)}, bf16[128,1024]{1,0:T(8,128)(2,1)S(1)}, u32[]{:S(2)}, u32[]{:S(2)}) collective-permute-start(bf16[128,1024]{1,0:T(8,128)(2,1)S(1)} %get-tuple-element.47), channel_id=1, source_target_pairs={{4,0},{8,4},{12,8},{16,12},{20,16},{24,20},{28,24},{5,1},{9,5},{13... | collective-permute-start | bytes 786440 | tf_op jit(solution)/shard_map/ppermute | solution.py:27
  20.4 5.6 %collective-permute-start.2 = (bf16[128,1024]{1,0:T(8,128)(2,1)S(1)}, bf16[128,1024]{1,0:T(8,128)(2,1)S(1)}, u32[]{:S(2)}, u32[]{:S(2)}) collective-permute-start(bf16[128,1024]{1,0:T(8,128)(2,1)S(1)} %get-tuple-element.48), channel_id=1, source_target_pairs={{0,4},{4,8},{8,12},{12,16},{16,20},{20,24},{24,28},{1,5},{5,9},{9,... | collective-permute-start | bytes 786440 | tf_op jit(solution)/shard_map/ppermute | solution.py:27
  26.0 7.3 %collective-permute-done.4.refs_8_ = bf16[128,1024]{1,0:T(8,128)(2,1)S(1)} collective-permute-done((bf16[128,1024]{1,0:T(8,128)(2,1)S(1)}, bf16[128,1024]{1,0:T(8,128)(2,1)S(1)}, u32[]{:S(2)}, u32[]{:S(2)}) %collective-permute-start.4) | collective-permute-done | bytes 262176 | tf_op jit(solution)/shard_map/ppermute | solution.py:27
  33.3 0.0 copy-done.4
  33.3 5.1 %mixer0.1 = (bf16[128,2048]{1,0:T(8,128)(2,1)}, bf16[3,128,2048]{2,1,0:T(8,128)(2,1)}, f32[3,8,2048]{2,1,0:T(8,128)S(1)}, bf16[3,8,2048]{2,1,0:T(8,128)(2,1)S(1)}, bf16[8,32,256]{2,1,0:T(8,128)(2,1)}) custom-call(s32[1,128]{1,0:T(1,128)S(1)} %bitcast.13, f32[3,7,2048]{2,1,0:T(8,128)S(1)} %bitcast.7, bf16[768,128]{1,0:T(8,128)(2,1)S(1)} %get-tuple-element.43.refs_2_, ...), custom_call_target="tpu_custom_call" | custom-call | flops 4000000000 | bytes 4000000 | tf_op jit(solution)/shard_map/mixer0/pallas_call | solution.py:450
  38.5 0.0 collective-permute-done.3.refs_11_
  38.5 0.0 collective-permute-done.2.refs_8_
  38.5 8.1 %mixer1.1 = (bf16[128,2048]{1,0:T(8,128)(2,1)}, bf16[3,128,2048]{2,1,0:T(8,128)(2,1)}, f32[3,8,2048]{2,1,0:T(8,128)S(1)}, bf16[3,8,2048]{2,1,0:T(8,128)(2,1)S(1)}, bf16[8,32,256]{2,1,0:T(8,128)(2,1)}) custom-call(s32[1,128]{1,0:T(1,128)S(1)} %bitcast.14, ...), custom_call_target="tpu_custom_call", output_to_operand_aliasing={{0}: (12, {}), {1}: (13, {}), {2}: (14, {}), {3}: (15, {}),... | custom-call | flops 4000000000 | bytes 4000000 | tf_op jit(solution)/shard_map/mixer1/pallas_call | solution.py:450
  46.6 0.0 collective-permute-done.1.refs_8_
  46.6 3.6 %mixer2.1 = (bf16[128,2048]{1,0:T(8,128)(2,1)}, bf16[3,128,2048]{2,1,0:T(8,128)(2,1)}, f32[3,8,2048]{2,1,0:T(8,128)S(1)}, bf16[3,8,2048]{2,1,0:T(8,128)(2,1)S(1)}, bf16[8,32,256]{2,1,0:T(8,128)(2,1)}) custom-call(s32[1,128]{1,0:T(1,128)S(1)} %bitcast.15, ...), custom_call_target="tpu_custom_call", output_to_operand_aliasing={{0}: (9, {}), {1}: (10, {}), {2}: (11, {}), {3}: (12, {}), ... | custom-call | flops 4000000000 | bytes 4000000 | tf_op jit(solution)/shard_map/mixer2/pallas_call | solution.py:450
  50.3 5.8 %all-to-all-start = ((bf16[8,32,256]{2,1,0:T(8,128)(2,1)}), bf16[8,32,256]{2,1,0:T(8,128)(2,1)S(1)}, u32[]{:S(2)}, u32[]{:S(2)}) async-start(bf16[8,32,256]{2,1,0:T(8,128)(2,1)} %get-tuple-element.63), calls=%async_computation | async-start | bytes 262144 | tf_op jit(solution)/shard_map/all_to_all | solution.py:466
  56.1 1.3 %collective-permute-start.5 = (bf16[3,8,2048]{2,1,0:T(8,128)(2,1)S(1)}, bf16[3,8,2048]{2,1,0:T(8,128)(2,1)S(1)}, u32[]{:S(2)}, u32[]{:S(2)}) collective-permute-start(bf16[3,8,2048]{2,1,0:T(8,128)(2,1)S(1)} %get-tuple-element.65), channel_id=1, source_target_pairs={{4,0},{8,4},{12,8},{16,12},{20,16},{24,20},{28,24},{5,1},{9,5},{13... | collective-permute-start | bytes 294920 | tf_op jit(solution)/shard_map/ppermute | solution.py:27
  57.4 5.4 %collective-permute-done.5.part_ref = bf16[3,8,2048]{2,1,0:T(8,128)(2,1)S(1)} collective-permute-done((bf16[3,8,2048]{2,1,0:T(8,128)(2,1)S(1)}, bf16[3,8,2048]{2,1,0:T(8,128)(2,1)S(1)}, u32[]{:S(2)}, u32[]{:S(2)}) %collective-permute-start.5) | collective-permute-done | bytes 98336 | tf_op jit(solution)/shard_map/ppermute | solution.py:27
  62.8 0.7 %all-to-all-done.got_ref = bf16[8,32,256]{2,1,0:T(8,128)(2,1)S(1)} async-done(((bf16[8,32,256]{2,1,0:T(8,128)(2,1)}), bf16[8,32,256]{2,1,0:T(8,128)(2,1)S(1)}, u32[]{:S(2)}, u32[]{:S(2)}) %all-to-all-start) | async-done | bytes 131104 | tf_op jit(solution)/shard_map/all_to_all | solution.py:466
  63.4 1.3 %finish.1 = (bf16[3,128,2048]{2,1,0:T(8,128)(2,1)}, f32[16,128]{1,0:T(8,128)}, f32[3,7,256]{2,1,0:T(8,128)}) custom-call(bf16[8,32,256]{2,1,0:T(8,128)(2,1)S(1)} %all-to-all-done.got_ref, f32[3,8,2048]{2,1,0:T(8,128)S(1)} %get-tuple-element.64.tail_ref, bf16[3,8,2048]{2,1,0:T(8,128)(2,1)S(1)} %collective-permute-done.5.part_ref, ...), custom_call_target="tpu_custom_call", output_to_operand_aliasing={{0}: (3, {})} | custom-call | flops 1000000 | bytes 200000 | tf_op jit(solution)/shard_map/finish/pallas_call | solution.py:467
Async XLA Ops:
  2.3 7.0 %collective-permute-start = (bf16[3,8,2048]{2,1,0:T(8,128)(2,1)S(1)}, bf16[3,8,2048]{2,1,0:T(8,128)(2,1)S(1)}, u32[]{:S(2)}, u32[]{:S(2)}) collective-permute-start(bf16[3,8,2048]{2,1,0:T(8,128)(2,1)S(1)} %scatter.4), channel_id=1, source_target_pairs={{0,4},{4,8},{8,12},{12,16},{16,20},{20,24},{24,28},{1,5},{5,9},{9,... | collective-permute-start | bytes 294920 | tf_op jit(solution)/shard_map/ppermute | solution.py:27
  7.2 0.8 %copy-start.3 = (f32[128,128]{1,0:T(8,128)S(1)}, f32[128,128]{1,0:T(8,128)}, u32[]{:S(2)}) copy-start(f32[128,128]{1,0:T(8,128)} %refs_6_.3) | copy-start | bytes 196612
  8.0 0.7 %copy-start.5 = (s32[128]{0:T(128)S(1)}, s32[128]{0:T(128)}, u32[]{:S(2)}) copy-start(s32[128]{0:T(128)} %param.9) | copy-start | bytes 1540
  8.7 1.4 %copy-start = (bf16[3,128,2048]{2,1,0:T(8,128)(2,1)S(1)}, bf16[3,128,2048]{2,1,0:T(8,128)(2,1)}, u32[]{:S(2)}) copy-start(bf16[3,128,2048]{2,1,0:T(8,128)(2,1)} %refs_3_.5) | copy-start | bytes 4718596
  8.7 1.5 %copy-start.1 = (bf16[128,2048]{1,0:T(8,128)(2,1)S(1)}, bf16[128,2048]{1,0:T(8,128)(2,1)}, u32[]{:S(2)}) copy-start(bf16[128,2048]{1,0:T(8,128)(2,1)} %refs_4_.5) | copy-start | bytes 1572868
  8.7 1.6 %copy-start.2 = (f32[3,2048,7]{1,2,0:T(8,128)S(1)}, f32[3,2048,7]{1,2,0:T(8,128)}, u32[]{:S(2)}) copy-start(f32[3,2048,7]{1,2,0:T(8,128)} %param.10) | copy-start | bytes 516100
  8.7 1.6 %copy-start.6 = (s32[128]{0:T(128)S(1)}, s32[128]{0:T(128)}, u32[]{:S(2)}) copy-start(s32[128]{0:T(128)} %param.9) | copy-start | bytes 1540
  12.2 21.1 %collective-permute-start.4 = (bf16[128,1024]{1,0:T(8,128)(2,1)S(1)}, bf16[128,1024]{1,0:T(8,128)(2,1)S(1)}, u32[]{:S(2)}, u32[]{:S(2)}) collective-permute-start(bf16[128,1024]{1,0:T(8,128)(2,1)S(1)} %get-tuple-element.51), channel_id=1, source_target_pairs={{0,4},{4,8},{8,12},{12,16},{16,20},{20,24},{24,28},{1,5},{5,9},{9,... | collective-permute-start | bytes 786440 | tf_op jit(solution)/shard_map/ppermute | solution.py:27
  15.7 17.6 %copy-start.4 = (f32[128,128]{1,0:T(8,128)S(1)}, f32[128,128]{1,0:T(8,128)}, u32[]{:S(2)}) copy-start(f32[128,128]{1,0:T(8,128)} %refs_6_.3) | copy-start | bytes 196612
  15.7 22.8 %collective-permute-start.3 = (bf16[128,1024]{1,0:T(8,128)(2,1)S(1)}, bf16[128,1024]{1,0:T(8,128)(2,1)S(1)}, u32[]{:S(2)}, u32[]{:S(2)}) collective-permute-start(bf16[128,1024]{1,0:T(8,128)(2,1)S(1)} %get-tuple-element.50), channel_id=1, source_target_pairs={{4,0},{8,4},{12,8},{16,12},{20,16},{24,20},{28,24},{5,1},{9,5},{13... | collective-permute-start | bytes 786440 | tf_op jit(solution)/shard_map/ppermute | solution.py:27
  19.1 27.5 %collective-permute-start.1 = (bf16[128,1024]{1,0:T(8,128)(2,1)S(1)}, bf16[128,1024]{1,0:T(8,128)(2,1)S(1)}, u32[]{:S(2)}, u32[]{:S(2)}) collective-permute-start(bf16[128,1024]{1,0:T(8,128)(2,1)S(1)} %get-tuple-element.47), channel_id=1, source_target_pairs={{4,0},{8,4},{12,8},{16,12},{20,16},{24,20},{28,24},{5,1},{9,5},{13... | collective-permute-start | bytes 786440 | tf_op jit(solution)/shard_map/ppermute | solution.py:27
  20.4 18.1 %collective-permute-start.2 = (bf16[128,1024]{1,0:T(8,128)(2,1)S(1)}, bf16[128,1024]{1,0:T(8,128)(2,1)S(1)}, u32[]{:S(2)}, u32[]{:S(2)}) collective-permute-start(bf16[128,1024]{1,0:T(8,128)(2,1)S(1)} %get-tuple-element.48), channel_id=1, source_target_pairs={{0,4},{4,8},{8,12},{12,16},{16,20},{20,24},{24,28},{1,5},{5,9},{9,... | collective-permute-start | bytes 786440 | tf_op jit(solution)/shard_map/ppermute | solution.py:27
  50.3 13.2 %all-to-all-start = ((bf16[8,32,256]{2,1,0:T(8,128)(2,1)}), bf16[8,32,256]{2,1,0:T(8,128)(2,1)S(1)}, u32[]{:S(2)}, u32[]{:S(2)}) async-start(bf16[8,32,256]{2,1,0:T(8,128)(2,1)} %get-tuple-element.63), calls=%async_computation | async-start | bytes 262144 | tf_op jit(solution)/shard_map/all_to_all | solution.py:466
  56.1 6.7 %collective-permute-start.5 = (bf16[3,8,2048]{2,1,0:T(8,128)(2,1)S(1)}, bf16[3,8,2048]{2,1,0:T(8,128)(2,1)S(1)}, u32[]{:S(2)}, u32[]{:S(2)}) collective-permute-start(bf16[3,8,2048]{2,1,0:T(8,128)(2,1)S(1)} %get-tuple-element.65), channel_id=1, source_target_pairs={{4,0},{8,4},{12,8},{16,12},{20,16},{24,20},{28,24},{5,1},{9,5},{13... | collective-permute-start | bytes 294920 | tf_op jit(solution)/shard_map/ppermute | solution.py:27

commit v7 on v6

--- a/solution.py
+++ b/solution.py
@@ -56,20 +56,23 @@
     lfr_ref[...] = dot(lf_ref[...].astype(BF16), backward.astype(BF16))
 
 
-def feature_kernel(first, ids_ref, delay_ref, edge_ref, sf_hbm, x_hbm, cot_hbm,
-                   feat_ref, kv_ref, g_ref, edge_shift, sf_ref, x_ref, cot_ref, sems):
+def feature_kernel(first, streams, ids_ref, delay_ref, edge_ref, sf_hbm, x_hbm, cot_hbm, _,
+                   feat_ref, sent_ref, edge_shift, sf_ref, x_ref, cot_ref, sems):
     rows = x_ref.shape[1]
     taps = sf_ref.shape[1]
-    steps = kv_ref.shape[1] // LANES
+    steps = sent_ref.shape[1] // LANES
+    pick = pl.ds(streams[0], len(streams))
+    gradient = len(streams) == 1
 
     def loads(p):
         near = lane_range(p * LANES, LANES)
         cols = lane_range(first + p * LANES, LANES)
         pairs = [
-            (sf_hbm.at[:, :, cols], sf_ref.at[:, :, near]),
-            (x_hbm.at[:, :, cols], x_ref.at[:, :, near]),
-            (cot_hbm.at[:, cols], cot_ref.at[:, near]),
+            (sf_hbm.at[pick, :, cols], sf_ref.at[:, :, near]),
+            (x_hbm.at[pick, :, cols], x_ref.at[:, :, near]),
         ]
+        if gradient:
+            pairs.append((cot_hbm.at[:, cols], cot_ref.at[:, near]))
         return [pltpu.make_async_copy(src, dst, sems.at[k, p]) for k, (src, dst) in enumerate(pairs)]
 
     for p in range(steps):
@@ -90,14 +93,14 @@
         for copy in loads(p):
             copy.wait()
         feats = []
-        for i in range(3):
+        for i, stream in enumerate(streams):
             x = x_ref[i, :, near]
             w = sf_ref[i, :, near]
             moved = dot(delay_ref[...], x)
             acc = w[0:1] * x.astype(F32)
             for t in range(1, taps):
                 acc = acc + w[t : t + 1] * moved[(t - 1) * rows : t * rows]
-            edge = edge_ref[i, :, cols].astype(F32)
+            edge = edge_ref[stream, :, cols].astype(F32)
             edge = jnp.concatenate([edge, jnp.zeros((rows - EDGE, LANES), F32)], 0)
             moved = dot(edge_shift[...].astype(BF16), edge.astype(BF16))
             fix = w[1:2] * moved[0:EDGE]
@@ -106,10 +109,12 @@
             acc = jnp.concatenate([acc[0:EDGE] + fix, acc[EDGE:]], 0)
             feat_ref[i, :, near] = acc
             feats.append(acc)
-        kv_ref[:, near] = (feats[1] * feats[2]).astype(BF16)
-        g = cot_ref[:, near].astype(F32) * feats[0]
-        last = iota2(g.shape, 0) == rows - 1
-        g_ref[:, near] = jnp.where(last, jnp.broadcast_to(id_wide, g.shape), g).astype(BF16)
+        if gradient:
+            g = cot_ref[:, near].astype(F32) * feats[0]
+            last = iota2(g.shape, 0) == rows - 1
+            sent_ref[:, near] = jnp.where(last, jnp.broadcast_to(id_wide, g.shape), g).astype(BF16)
+        else:
+            sent_ref[:, near] = (feats[0] * feats[1]).astype(BF16)
         return carry
 
     lax.fori_loop(0, steps, one_step, 0)
@@ -163,7 +168,7 @@
     return acc, sent, jnp.concatenate(sums, 0)
 
 
-def query_part(first, shared, lf_ref, feat_ref, kvp_ref, outs, scratch):
+def query_part(first, shared, lf_ref, q_ref, feat_ref, kvp_ref, outs, scratch):
     ids_ref, sf_ref, advance_ref, x_ref, cot_ref, edge_ref = shared
     out_hbm, qg_hbm, tail_hbm, part_hbm, packed_hbm = outs
     (out_ref, qg_ref, tail_ref, part_ref, short_ref, long_ref,
@@ -206,10 +211,10 @@
         near = lane_range(p * LANES, LANES)
         cols = lane_range(first + p * LANES, LANES)
         cot = cot_ref[:, cols].astype(F32)
-        w_kv[0:rows] = (feat_ref[1, :, near] * feat_ref[2, :, near]).astype(BF16)
+        w_kv[0:rows] = (feat_ref[0, :, near] * feat_ref[1, :, near]).astype(BF16)
         w_kv[rows:] = kvp_ref[:, near]
         kv_turned[...] = w_kv[...].T
-        g_rev[...] = dot(mirror, (cot * feat_ref[0, :, near]).astype(BF16)).astype(BF16)
+        g_rev[...] = dot(mirror, (cot * q_ref[0, :, near]).astype(BF16)).astype(BF16)
         for q in range(LANES // half):
             part = slice(q * half, (q + 1) * half)
             base = pl.multiple_of((first // half) * per + p * (LANES // width) + q * per, per)
@@ -226,7 +231,7 @@
                 dh_ref[q * per + j : q * per + j + 1] = jnp.sum(folded, 0, keepdims=True)
         dh = dot(dh_ref[...].astype(BF16), mirror)
         y = y_turned[...].T
-        out_ref[:, near] = (feat_ref[0, :, near] * y).astype(BF16)
+        out_ref[:, near] = (q_ref[0, :, near] * y).astype(BF16)
         acc, sent, sums = short_stage(
             cot * y, sf_ref[0, :, cols], x_ref[0, :, cols].astype(F32), edge_ref[0, :, cols].astype(F32),
             advance_ref, edge_shift,
@@ -243,7 +248,7 @@
     return one_step, copies
 
 
-def pair_part(first, shared, lfr_ref, feat_ref, gn_ref, outs, scratch):
+def pair_part(first, shared, lfr_ref, q_ref, feat_ref, gn_ref, outs, scratch):
     ids_ref, sf_ref, advance_ref, x_ref, cot_ref, edge_ref = shared
     _, qg_hbm, tail_hbm, part_hbm, packed_hbm = outs
     (qg_ref, tail_ref, part_ref, short_ref,
@@ -275,7 +280,7 @@
     def one_step(p):
         near = lane_range(p * LANES, LANES)
         cols = lane_range(first + p * LANES, LANES)
-        w_g[0:rows] = (cot_ref[:, cols].astype(F32) * feat_ref[0, :, near]).astype(BF16)
+        w_g[0:rows] = (cot_ref[:, cols].astype(F32) * q_ref[0, :, near]).astype(BF16)
         w_g[rows:] = gn_ref[:, near]
         g_turned[...] = w_g[...].T
         for j in range(LANES // width):
@@ -289,7 +294,7 @@
         heads = []
         for i in (1, 2):
             acc, sent, sums = short_stage(
-                gm * feat_ref[3 - i, :, near], sf_ref[i, :, cols], x_ref[i, :, cols].astype(F32),
+                gm * feat_ref[2 - i, :, near], sf_ref[i, :, cols], x_ref[i, :, cols].astype(F32),
                 edge_ref[i, :, cols].astype(F32), advance_ref, edge_shift,
             )
             qg_ref[i - 1, :, near] = acc.astype(BF16)
@@ -307,15 +312,15 @@
     shared = refs[:6]
     halves = [query_first, pair_first]
     inputs = refs[6:]
-    used = 3 * sum(first is not None for first in halves)
+    used = 4 * sum(first is not None for first in halves)
     outs = inputs[used + filled : used + filled + 5]
     scratch = inputs[used + filled + 5 :]
     parts = []
     for first, make, size in zip(halves, (query_part, pair_part), (15, 10)):
         if first is not None:
-            steps = inputs[2].shape[1] // LANES
-            parts.append(make(first, shared, *inputs[:3], outs, scratch[:size]))
-            inputs = inputs[3:]
+            steps = inputs[3].shape[1] // LANES
+            parts.append(make(first, shared, *inputs[:4], outs, scratch[:size]))
+            inputs = inputs[4:]
             scratch = scratch[size:]
     run_steps(parts, steps)
 
@@ -372,29 +377,31 @@
     )(ids, long_filter)
 
     count = chans // PARTS
-    sent = []
-    for part in range(PARTS):
-        feats, kv, grad = pl.pallas_call(
-            functools.partial(feature_kernel, part * count),
-            in_specs=[VMEM] * 3 + [HBM] * 3,
-            out_specs=[VMEM] * 3,
-            out_shape=[
-                jax.ShapeDtypeStruct((3, rows, count), F32),
-                jax.ShapeDtypeStruct((rows, count), BF16),
-                jax.ShapeDtypeStruct((rows, count), BF16),
-            ],
-            scratch_shapes=[
-                pltpu.VMEM(((taps - 1) * EDGE, rows), F32),
-                pltpu.VMEM((3, taps, count), F32),
-                pltpu.VMEM((3, rows, count), BF16),
-                pltpu.VMEM((rows, count), BF16),
-                pltpu.SemaphoreType.DMA((3, count // LANES)),
-            ],
-            compiler_params=params,
-            cost_estimate=pl.CostEstimate(flops=2_000_000_000, bytes_accessed=4_000_000, transcendentals=0),
-            name="features",
-        )(ids, delay, edge, sf, qkv, cotangent)
-        sent.append((feats, passed_along(kv, 1), passed_along(grad, -1)))
+    after = ids
+    features = []
+    for streams, distance in (((1, 2), 1), ((0,), -1)):
+        for part in range(PARTS):
+            feats, message = pl.pallas_call(
+                functools.partial(feature_kernel, part * count, streams),
+                in_specs=[VMEM] * 3 + [HBM] * 3 + [ANY],
+                out_specs=[VMEM] * 2,
+                out_shape=[
+                    jax.ShapeDtypeStruct((len(streams), rows, count), F32),
+                    jax.ShapeDtypeStruct((rows, count), BF16),
+                ],
+                scratch_shapes=[
+                    pltpu.VMEM(((taps - 1) * EDGE, rows), F32),
+                    pltpu.VMEM((len(streams), taps, count), F32),
+                    pltpu.VMEM((len(streams), rows, count), BF16),
+                    pltpu.VMEM((rows, count), BF16),
+                    pltpu.SemaphoreType.DMA((3, count // LANES)),
+                ],
+                compiler_params=params,
+                cost_estimate=pl.CostEstimate(flops=2_000_000_000, bytes_accessed=4_000_000, transcendentals=0),
+                name="features",
+            )(ids, delay, edge, sf, qkv, cotangent, after)
+            after = message
+            features.append((feats, passed_along(message, distance)))
 
     full = [
         jax.ShapeDtypeStruct((rows, chans), BF16),
@@ -434,17 +441,18 @@
         pltpu.SemaphoreType.DMA((4, count // LANES)),
     ]
     results = []
-    for stage in range(PARTS + 1):
+    stages = [(stage, None) for stage in range(PARTS)] + [(None, stage) for stage in range(PARTS)]
+    for query, pair in stages:
         operands = [ids, sf, advance, qkv, cotangent, edge]
         scratch = []
         query_first = pair_first = None
-        if stage < PARTS:
-            query_first = stage * count
-            operands += [long_filter, sent[stage][0], sent[stage][1]]
+        if query is not None:
+            query_first = query * count
+            operands += [long_filter, features[PARTS + query][0], *features[query]]
             scratch += query_scratch
-        if stage > 0:
-            pair_first = (stage - 1) * count
-            operands += [lf_rev, sent[stage - 1][0], sent[stage - 1][2]]
+        if pair is not None:
+            pair_first = pair * count
+            operands += [lf_rev, features[PARTS + pair][0], features[pair][0], features[PARTS + pair][1]]
             scratch += pair_scratch
         filled = len(results)
         results = pl.pallas_call(
@@ -456,7 +464,7 @@
             scratch_shapes=scratch,
             compiler_params=params,
             cost_estimate=pl.CostEstimate(flops=4_000_000_000, bytes_accessed=4_000_000, transcendentals=0),
-            name=f"mixer{stage}",
+            name="query" if pair is None else "pair",
         )(*operands, *results)
     out, qg, tail, part, packed = results
 

time: 65.2 us -> 64.5 us (0.989)
  Pallas kernels: 22.2 us -> 23.8 us
  starting transfers between devices: 23.8 us -> 22.5 us
  waiting for transfers between devices: 13.9 us -> 12.9 us
    ppermute x6, starting transfers between devices: 18 us -> 16.7 us  [passed_along(): return lax.ppermute(block, 'ctx', route)]
    pallas_call x2 -> x4, Pallas kernels: 3.9 us -> 4.89 us  [shards(): pl.pallas_call(functools.partial(feature_kernel, part * count, streams),...]
    ppermute x6, waiting for transfers between devices: 13.2 us -> 12.3 us  [passed_along(): return lax.ppermute(block, 'ctx', route)]
    pallas_call x3 -> x4, Pallas kernels: 16.9 us -> 17.5 us  [shards(): pl.pallas_call(functools.partial(mixer_kernel, query_first, pair_first, f...]
  transfers between devices with their start and end apart: 7 -> 7, of which waited for: 4 -> 4; matrix products, arithmetic and copies ran while one was open for 0% -> 0% of each run, Pallas kernels for 24% -> 27%
where the time goes in v7:
time: 64.5 us; the launch traced here: 64.1 us
  Pallas kernels  23.8 us (37%)
  starting transfers between devices  22.5 us (35%)
  waiting for transfers between devices  12.9 us (20%)
  local copies, waits for them, and re-layouts  3.4 us (5%)
  between operations  0.82 us (1%)
  other arithmetic  0.66 us (1%)
    pallas_call x4, Pallas kernels, shards(): pl.pallas_call(functools.partial(mixer_kernel, query_first, pair_first, f...  17.5 us
    ppermute x6, starting transfers between devices, passed_along(): return lax.ppermute(block, 'ctx', route)  16.7 us
    ppermute x6, waiting for transfers between devices, passed_along(): return lax.ppermute(block, 'ctx', route)  12.3 us
    all_to_all x1, starting transfers between devices, shards(): got = lax.all_to_all(packed, 'ctx', 0, 0)  5.79 us
    pallas_call x4, Pallas kernels, shards(): pl.pallas_call(functools.partial(feature_kernel, part * count, streams),...  4.89 us
    unnamed x14, local copies, waits for them, and re-layouts  2.37 us
  transfers between devices with their start and end apart: 7, of which 4 were waited for; matrix products, arithmetic and copies ran while one was open for 0% of the time, Pallas kernels for 27%

profile of v7, /device:TPU:0, one launch (start us, length us, event | category | flops | bytes accessed | tf_op | source)
XLA Modules:
  0.0 64.1 jit_solution(6267943418586451808)
XLA Ops:
  0.6 0.7 %convert_bitcast_fusion = bf16[1,1,128]{2,1,0:T(2,128)(2,1)S(1)} fusion(s32[128]{0:T(128)} %param.9), kind=kLoop, calls=%fused_computation | loop fusion | flops 128 | bytes 768 | tf_op jit(solution)/shard_map/reshape.24
  1.3 0.9 %slice.26 = bf16[3,8,2048]{2,1,0:T(8,128)(2,1)S(1)} slice(bf16[3,128,2048]{2,1,0:T(8,128)(2,1)} %refs_3_.7), slice={[0:3], [120:128], [0:2048]} | slice | bytes 196608 | tf_op jit(solution)/shard_map/slice | solution.py:360
  2.2 0.1 scatter.4
  2.3 4.8 %collective-permute-start = (bf16[3,8,2048]{2,1,0:T(8,128)(2,1)S(1)}, bf16[3,8,2048]{2,1,0:T(8,128)(2,1)S(1)}, u32[]{:S(2)}, u32[]{:S(2)}) collective-permute-start(bf16[3,8,2048]{2,1,0:T(8,128)(2,1)S(1)} %scatter.4), channel_id=1, source_target_pairs={{0,4},{4,8},{8,12},{12,16},{16,20},{20,24},{24,28},{1,5},{5,9},{9,... | collective-permute-start | bytes 294920 | tf_op jit(solution)/shard_map/ppermute | solution.py:27
  7.2 0.0 copy-start.3
  7.2 0.8 %copy-done.3 = f32[128,128]{1,0:T(8,128)S(1)} copy-done((f32[128,128]{1,0:T(8,128)S(1)}, f32[128,128]{1,0:T(8,128)}, u32[]{:S(2)}) %copy-start.3) | copy-done | bytes 65560
  8.0 0.0 copy-start.5
  8.0 0.7 %copy-done.5 = s32[128]{0:T(128)S(1)} copy-done((s32[128]{0:T(128)S(1)}, s32[128]{0:T(128)}, u32[]{:S(2)}) %copy-start.5) | copy-done | bytes 536
  8.7 0.0 copy-start
  8.7 0.0 copy-start.1
  8.7 0.0 copy-start.2
  8.7 0.0 copy-start.6
  8.7 0.2 prepare.1
  8.9 0.5 collective-permute-done.edge_ref.refs_5_
  9.4 0.7 %copy-done = bf16[3,128,2048]{2,1,0:T(8,128)(2,1)S(1)} copy-done((bf16[3,128,2048]{2,1,0:T(8,128)(2,1)S(1)}, bf16[3,128,2048]{2,1,0:T(8,128)(2,1)}, u32[]{:S(2)}) %copy-start) | copy-done | bytes 1572888
  10.1 0.1 copy-done.1
  10.2 0.0 copy-done.2
  10.2 0.0 copy-done.6
  10.2 1.4 %features.4 = (f32[2,128,1024]{2,1,0:T(8,128)S(1)}, bf16[128,1024]{1,0:T(8,128)(2,1)S(1)}) custom-call(s32[1,128]{1,0:T(1,128)S(1)} %bitcast.14, bf16[768,128]{1,0:T(8,128)(2,1)S(1)} %get-tuple-element.52.delay_ref, bf16[3,8,2048]{2,1,0:T(8,128)(2,1)S(1)} %collective-permute-done.edge_ref.refs_5_, f32[3,7,2048]{2,1,0:T(8,128)S(1)} %bitcast.5, ...), custom_call_target="tpu_custom_call" | custom-call | flops 2000000000 | bytes 4000000 | tf_op jit(solution)/shard_map/features/pallas_call | solution.py:384
  11.7 3.5 %collective-permute-start.4 = (bf16[128,1024]{1,0:T(8,128)(2,1)S(1)}, bf16[128,1024]{1,0:T(8,128)(2,1)S(1)}, u32[]{:S(2)}, u32[]{:S(2)}) collective-permute-start(bf16[128,1024]{1,0:T(8,128)(2,1)S(1)} %get-tuple-element.53._), channel_id=1, source_target_pairs={{0,4},{4,8},{8,12},{12,16},{16,20},{20,24},{24,28},{1,5},{5,9},{9,... | collective-permute-start | bytes 786440 | tf_op jit(solution)/shard_map/ppermute | solution.py:27
  15.2 1.4 %features.5 = (f32[2,128,1024]{2,1,0:T(8,128)S(1)}, bf16[128,1024]{1,0:T(8,128)(2,1)S(1)}) custom-call(s32[1,128]{1,0:T(1,128)S(1)} %bitcast.16, bf16[768,128]{1,0:T(8,128)(2,1)S(1)} %get-tuple-element.52.delay_ref, bf16[3,8,2048]{2,1,0:T(8,128)(2,1)S(1)} %collective-permute-done.edge_ref.refs_5_, f32[3,7,2048]{2,1,0:T(8,128)S(1)} %bitcast.6, ...), custom_call_target="tpu_custom_call" | custom-call | flops 2000000000 | bytes 4000000 | tf_op jit(solution)/shard_map/features/pallas_call | solution.py:384
  16.6 4.4 %collective-permute-start.3 = (bf16[128,1024]{1,0:T(8,128)(2,1)S(1)}, bf16[128,1024]{1,0:T(8,128)(2,1)S(1)}, u32[]{:S(2)}, u32[]{:S(2)}) collective-permute-start(bf16[128,1024]{1,0:T(8,128)(2,1)S(1)} %get-tuple-element.54._), channel_id=1, source_target_pairs={{0,4},{4,8},{8,12},{12,16},{16,20},{20,24},{24,28},{1,5},{5,9},{9,... | collective-permute-start | bytes 786440 | tf_op jit(solution)/shard_map/ppermute | solution.py:27
  21.0 1.0 %features.6 = (f32[1,128,1024]{2,1,0:T(8,128)S(1)}, bf16[128,1024]{1,0:T(8,128)(2,1)S(1)}) custom-call(s32[1,128]{1,0:T(1,128)S(1)} %bitcast.17, bf16[768,128]{1,0:T(8,128)(2,1)S(1)} %get-tuple-element.52.delay_ref, bf16[3,8,2048]{2,1,0:T(8,128)(2,1)S(1)} %collective-permute-done.edge_ref.refs_5_, f32[3,7,2048]{2,1,0:T(8,128)S(1)} %bitcast.7, ...), custom_call_target="tpu_custom_call" | custom-call | flops 2000000000 | bytes 4000000 | tf_op jit(solution)/shard_map/features/pallas_call | solution.py:384
  22.0 0.0 copy-start.4
  22.0 1.4 %collective-permute-start.2 = (bf16[128,1024]{1,0:T(8,128)(2,1)S(1)}, bf16[128,1024]{1,0:T(8,128)(2,1)S(1)}, u32[]{:S(2)}, u32[]{:S(2)}) collective-permute-start(bf16[128,1024]{1,0:T(8,128)(2,1)S(1)} %get-tuple-element.55._), channel_id=1, source_target_pairs={{4,0},{8,4},{12,8},{16,12},{20,16},{24,20},{28,24},{5,1},{9,5},{13... | collective-permute-start | bytes 786440 | tf_op jit(solution)/shard_map/ppermute | solution.py:27
  23.5 1.0 %features.7 = (f32[1,128,1024]{2,1,0:T(8,128)S(1)}, bf16[128,1024]{1,0:T(8,128)(2,1)S(1)}) custom-call(s32[1,128]{1,0:T(1,128)S(1)} %bitcast.18, bf16[768,128]{1,0:T(8,128)(2,1)S(1)} %get-tuple-element.52.delay_ref, bf16[3,8,2048]{2,1,0:T(8,128)(2,1)S(1)} %collective-permute-done.edge_ref.refs_5_, f32[3,7,2048]{2,1,0:T(8,128)S(1)} %bitcast.8, ...), custom_call_target="tpu_custom_call" | custom-call | flops 2000000000 | bytes 4000000 | tf_op jit(solution)/shard_map/features/pallas_call | solution.py:384
  24.5 1.3 %collective-permute-start.1 = (bf16[128,1024]{1,0:T(8,128)(2,1)S(1)}, bf16[128,1024]{1,0:T(8,128)(2,1)S(1)}, u32[]{:S(2)}, u32[]{:S(2)}) collective-permute-start(bf16[128,1024]{1,0:T(8,128)(2,1)S(1)} %get-tuple-element.58), channel_id=1, source_target_pairs={{4,0},{8,4},{12,8},{16,12},{20,16},{24,20},{28,24},{5,1},{9,5},{13... | collective-permute-start | bytes 786440 | tf_op jit(solution)/shard_map/ppermute | solution.py:27
  25.8 0.0 collective-permute-done.4.refs_9_
  25.8 0.0 copy-done.4
  25.8 5.1 %query.2 = (bf16[128,2048]{1,0:T(8,128)(2,1)}, bf16[3,128,2048]{2,1,0:T(8,128)(2,1)}, f32[3,8,2048]{2,1,0:T(8,128)S(1)}, bf16[3,8,2048]{2,1,0:T(8,128)(2,1)S(1)}, bf16[8,32,256]{2,1,0:T(8,128)(2,1)}) custom-call(s32[1,128]{1,0:T(1,128)S(1)} %bitcast.19, f32[3,7,2048]{2,1,0:T(8,128)S(1)} %bitcast.9, bf16[768,128]{1,0:T(8,128)(2,1)S(1)} %get-tuple-element.50.refs_2_, ...), custom_call_target="tpu_custom_call" | custom-call | flops 4000000000 | bytes 4000000 | tf_op jit(solution)/shard_map/query/pallas_call | solution.py:458
  30.9 6.3 %collective-permute-done.3.refs_9_ = bf16[128,1024]{1,0:T(8,128)(2,1)S(1)} collective-permute-done((bf16[128,1024]{1,0:T(8,128)(2,1)S(1)}, bf16[128,1024]{1,0:T(8,128)(2,1)S(1)}, u32[]{:S(2)}, u32[]{:S(2)}) %collective-permute-start.3) | collective-permute-done | bytes 262176 | tf_op jit(solution)/shard_map/ppermute | solution.py:27
  37.2 5.1 %query.3 = (bf16[128,2048]{1,0:T(8,128)(2,1)}, bf16[3,128,2048]{2,1,0:T(8,128)(2,1)}, f32[3,8,2048]{2,1,0:T(8,128)S(1)}, bf16[3,8,2048]{2,1,0:T(8,128)(2,1)S(1)}, bf16[8,32,256]{2,1,0:T(8,128)(2,1)}) custom-call(s32[1,128]{1,0:T(1,128)S(1)} %bitcast.20, ...), custom_call_target="tpu_custom_call", output_to_operand_aliasing={{0}: (10, {}), {1}: (11, {}), {2}: (12, {}), {3}: (13, {}),... | custom-call | flops 4000000000 | bytes 4000000 | tf_op jit(solution)/shard_map/query/pallas_call | solution.py:458
  42.3 0.0 collective-permute-done.2.refs_9_
  42.4 3.6 %pair.2 = (bf16[128,2048]{1,0:T(8,128)(2,1)}, bf16[3,128,2048]{2,1,0:T(8,128)(2,1)}, f32[3,8,2048]{2,1,0:T(8,128)S(1)}, bf16[3,8,2048]{2,1,0:T(8,128)(2,1)S(1)}, bf16[8,32,256]{2,1,0:T(8,128)(2,1)}) custom-call(s32[1,128]{1,0:T(1,128)S(1)} %bitcast.21, ...), custom_call_target="tpu_custom_call", output_to_operand_aliasing={{0}: (10, {}), {1}: (11, {}), {2}: (12, {}), {3}: (13, {}),... | custom-call | flops 4000000000 | bytes 4000000 | tf_op jit(solution)/shard_map/pair/pallas_call | solution.py:458
  46.0 0.0 collective-permute-done.1.refs_9_
  46.0 3.6 %pair.3 = (bf16[128,2048]{1,0:T(8,128)(2,1)}, bf16[3,128,2048]{2,1,0:T(8,128)(2,1)}, f32[3,8,2048]{2,1,0:T(8,128)S(1)}, bf16[3,8,2048]{2,1,0:T(8,128)(2,1)S(1)}, bf16[8,32,256]{2,1,0:T(8,128)(2,1)}) custom-call(s32[1,128]{1,0:T(1,128)S(1)} %bitcast.22, ...), custom_call_target="tpu_custom_call", output_to_operand_aliasing={{0}: (10, {}), {1}: (11, {}), {2}: (12, {}), {3}: (13, {}),... | custom-call | flops 4000000000 | bytes 4000000 | tf_op jit(solution)/shard_map/pair/pallas_call | solution.py:458
  49.6 5.8 %all-to-all-start = ((bf16[8,32,256]{2,1,0:T(8,128)(2,1)}), bf16[8,32,256]{2,1,0:T(8,128)(2,1)S(1)}, u32[]{:S(2)}, u32[]{:S(2)}) async-start(bf16[8,32,256]{2,1,0:T(8,128)(2,1)} %get-tuple-element.77), calls=%async_computation | async-start | bytes 262144 | tf_op jit(solution)/shard_map/all_to_all | solution.py:474
  55.4 1.3 %collective-permute-start.5 = (bf16[3,8,2048]{2,1,0:T(8,128)(2,1)S(1)}, bf16[3,8,2048]{2,1,0:T(8,128)(2,1)S(1)}, u32[]{:S(2)}, u32[]{:S(2)}) collective-permute-start(bf16[3,8,2048]{2,1,0:T(8,128)(2,1)S(1)} %get-tuple-element.79), channel_id=1, source_target_pairs={{4,0},{8,4},{12,8},{16,12},{20,16},{24,20},{28,24},{5,1},{9,5},{13... | collective-permute-start | bytes 294920 | tf_op jit(solution)/shard_map/ppermute | solution.py:27
  56.7 5.4 %collective-permute-done.5.part_ref = bf16[3,8,2048]{2,1,0:T(8,128)(2,1)S(1)} collective-permute-done((bf16[3,8,2048]{2,1,0:T(8,128)(2,1)S(1)}, bf16[3,8,2048]{2,1,0:T(8,128)(2,1)S(1)}, u32[]{:S(2)}, u32[]{:S(2)}) %collective-permute-start.5) | collective-permute-done | bytes 98336 | tf_op jit(solution)/shard_map/ppermute | solution.py:27
  62.1 0.7 %all-to-all-done.got_ref = bf16[8,32,256]{2,1,0:T(8,128)(2,1)S(1)} async-done(((bf16[8,32,256]{2,1,0:T(8,128)(2,1)}), bf16[8,32,256]{2,1,0:T(8,128)(2,1)S(1)}, u32[]{:S(2)}, u32[]{:S(2)}) %all-to-all-start) | async-done | bytes 131104 | tf_op jit(solution)/shard_map/all_to_all | solution.py:474
  62.8 1.3 %finish.1 = (bf16[3,128,2048]{2,1,0:T(8,128)(2,1)}, f32[16,128]{1,0:T(8,128)}, f32[3,7,256]{2,1,0:T(8,128)}) custom-call(bf16[8,32,256]{2,1,0:T(8,128)(2,1)S(1)} %all-to-all-done.got_ref, f32[3,8,2048]{2,1,0:T(8,128)S(1)} %get-tuple-element.78.tail_ref, bf16[3,8,2048]{2,1,0:T(8,128)(2,1)S(1)} %collective-permute-done.5.part_ref, ...), custom_call_target="tpu_custom_call", output_to_operand_aliasing={{0}: (3, {})} | custom-call | flops 1000000 | bytes 200000 | tf_op jit(solution)/shard_map/finish/pallas_call | solution.py:475
Async XLA Ops:
  2.3 7.0 %collective-permute-start = (bf16[3,8,2048]{2,1,0:T(8,128)(2,1)S(1)}, bf16[3,8,2048]{2,1,0:T(8,128)(2,1)S(1)}, u32[]{:S(2)}, u32[]{:S(2)}) collective-permute-start(bf16[3,8,2048]{2,1,0:T(8,128)(2,1)S(1)} %scatter.4), channel_id=1, source_target_pairs={{0,4},{4,8},{8,12},{12,16},{16,20},{20,24},{24,28},{1,5},{5,9},{9,... | collective-permute-start | bytes 294920 | tf_op jit(solution)/shard_map/ppermute | solution.py:27
  7.2 0.8 %copy-start.3 = (f32[128,128]{1,0:T(8,128)S(1)}, f32[128,128]{1,0:T(8,128)}, u32[]{:S(2)}) copy-start(f32[128,128]{1,0:T(8,128)} %refs_6_.3) | copy-start | bytes 196612
  8.0 0.7 %copy-start.5 = (s32[128]{0:T(128)S(1)}, s32[128]{0:T(128)}, u32[]{:S(2)}) copy-start(s32[128]{0:T(128)} %param.9) | copy-start | bytes 1540
  8.7 1.4 %copy-start = (bf16[3,128,2048]{2,1,0:T(8,128)(2,1)S(1)}, bf16[3,128,2048]{2,1,0:T(8,128)(2,1)}, u32[]{:S(2)}) copy-start(bf16[3,128,2048]{2,1,0:T(8,128)(2,1)} %refs_3_.7) | copy-start | bytes 4718596
  8.7 1.5 %copy-start.1 = (bf16[128,2048]{1,0:T(8,128)(2,1)S(1)}, bf16[128,2048]{1,0:T(8,128)(2,1)}, u32[]{:S(2)}) copy-start(bf16[128,2048]{1,0:T(8,128)(2,1)} %refs_4_.7) | copy-start | bytes 1572868
  8.7 1.6 %copy-start.2 = (f32[3,2048,7]{1,2,0:T(8,128)S(1)}, f32[3,2048,7]{1,2,0:T(8,128)}, u32[]{:S(2)}) copy-start(f32[3,2048,7]{1,2,0:T(8,128)} %param.10) | copy-start | bytes 516100
  8.7 1.6 %copy-start.6 = (s32[128]{0:T(128)S(1)}, s32[128]{0:T(128)}, u32[]{:S(2)}) copy-start(s32[128]{0:T(128)} %param.9) | copy-start | bytes 1540
  11.7 14.1 %collective-permute-start.4 = (bf16[128,1024]{1,0:T(8,128)(2,1)S(1)}, bf16[128,1024]{1,0:T(8,128)(2,1)S(1)}, u32[]{:S(2)}, u32[]{:S(2)}) collective-permute-start(bf16[128,1024]{1,0:T(8,128)(2,1)S(1)} %get-tuple-element.53._), channel_id=1, source_target_pairs={{0,4},{4,8},{8,12},{12,16},{16,20},{20,24},{24,28},{1,5},{5,9},{9,... | collective-permute-start | bytes 786440 | tf_op jit(solution)/shard_map/ppermute | solution.py:27
  16.6 20.6 %collective-permute-start.3 = (bf16[128,1024]{1,0:T(8,128)(2,1)S(1)}, bf16[128,1024]{1,0:T(8,128)(2,1)S(1)}, u32[]{:S(2)}, u32[]{:S(2)}) collective-permute-start(bf16[128,1024]{1,0:T(8,128)(2,1)S(1)} %get-tuple-element.54._), channel_id=1, source_target_pairs={{0,4},{4,8},{8,12},{12,16},{16,20},{20,24},{24,28},{1,5},{5,9},{9,... | collective-permute-start | bytes 786440 | tf_op jit(solution)/shard_map/ppermute | solution.py:27
  22.0 3.8 %copy-start.4 = (f32[128,128]{1,0:T(8,128)S(1)}, f32[128,128]{1,0:T(8,128)}, u32[]{:S(2)}) copy-start(f32[128,128]{1,0:T(8,128)} %refs_6_.3) | copy-start | bytes 196612
  22.0 20.3 %collective-permute-start.2 = (bf16[128,1024]{1,0:T(8,128)(2,1)S(1)}, bf16[128,1024]{1,0:T(8,128)(2,1)S(1)}, u32[]{:S(2)}, u32[]{:S(2)}) collective-permute-start(bf16[128,1024]{1,0:T(8,128)(2,1)S(1)} %get-tuple-element.55._), channel_id=1, source_target_pairs={{4,0},{8,4},{12,8},{16,12},{20,16},{24,20},{28,24},{5,1},{9,5},{13... | collective-permute-start | bytes 786440 | tf_op jit(solution)/shard_map/ppermute | solution.py:27
  24.5 21.5 %collective-permute-start.1 = (bf16[128,1024]{1,0:T(8,128)(2,1)S(1)}, bf16[128,1024]{1,0:T(8,128)(2,1)S(1)}, u32[]{:S(2)}, u32[]{:S(2)}) collective-permute-start(bf16[128,1024]{1,0:T(8,128)(2,1)S(1)} %get-tuple-element.58), channel_id=1, source_target_pairs={{4,0},{8,4},{12,8},{16,12},{20,16},{24,20},{28,24},{5,1},{9,5},{13... | collective-permute-start | bytes 786440 | tf_op jit(solution)/shard_map/ppermute | solution.py:27
  49.6 13.1 %all-to-all-start = ((bf16[8,32,256]{2,1,0:T(8,128)(2,1)}), bf16[8,32,256]{2,1,0:T(8,128)(2,1)S(1)}, u32[]{:S(2)}, u32[]{:S(2)}) async-start(bf16[8,32,256]{2,1,0:T(8,128)(2,1)} %get-tuple-element.77), calls=%async_computation | async-start | bytes 262144 | tf_op jit(solution)/shard_map/all_to_all | solution.py:474
  55.4 6.7 %collective-permute-start.5 = (bf16[3,8,2048]{2,1,0:T(8,128)(2,1)S(1)}, bf16[3,8,2048]{2,1,0:T(8,128)(2,1)S(1)}, u32[]{:S(2)}, u32[]{:S(2)}) collective-permute-start(bf16[3,8,2048]{2,1,0:T(8,128)(2,1)S(1)} %get-tuple-element.79), channel_id=1, source_target_pairs={{4,0},{8,4},{12,8},{16,12},{20,16},{24,20},{28,24},{5,1},{9,5},{13... | collective-permute-start | bytes 294920 | tf_op jit(solution)/shard_map/ppermute | solution.py:27

commit v8 on v7

--- a/solution.py
+++ b/solution.py
@@ -56,68 +56,75 @@
     lfr_ref[...] = dot(lf_ref[...].astype(BF16), backward.astype(BF16))
 
 
-def feature_kernel(first, streams, ids_ref, delay_ref, edge_ref, sf_hbm, x_hbm, cot_hbm, _,
-                   feat_ref, sent_ref, edge_shift, sf_ref, x_ref, cot_ref, sems):
+def local_kernel(first, ids_ref, delay_ref, sf_hbm, x_hbm, _, feat_ref, sf_ref, x_ref, sems):
     rows = x_ref.shape[1]
     taps = sf_ref.shape[1]
-    steps = sent_ref.shape[1] // LANES
-    pick = pl.ds(streams[0], len(streams))
-    gradient = len(streams) == 1
+    steps = feat_ref.shape[2] // LANES
 
     def loads(p):
         near = lane_range(p * LANES, LANES)
         cols = lane_range(first + p * LANES, LANES)
         pairs = [
-            (sf_hbm.at[pick, :, cols], sf_ref.at[:, :, near]),
-            (x_hbm.at[pick, :, cols], x_ref.at[:, :, near]),
+            (sf_hbm.at[:, :, cols], sf_ref.at[:, :, near]),
+            (x_hbm.at[:, :, cols], x_ref.at[:, :, near]),
         ]
-        if gradient:
-            pairs.append((cot_hbm.at[:, cols], cot_ref.at[:, near]))
         return [pltpu.make_async_copy(src, dst, sems.at[k, p]) for k, (src, dst) in enumerate(pairs)]
 
     for p in range(steps):
         for copy in loads(p):
             copy.start()
-    id_row = jnp.broadcast_to(ids_ref[...], (rows, rows)).astype(F32)
-    head_ids = id_row.T[0:EDGE]
-    before = jnp.broadcast_to(edge_ref[0, 0:1, 0:rows].astype(F32), (EDGE, rows))
-    before = pltpu.roll(before, EDGE, 1)
-    lag = iota2((EDGE, rows), 0) + EDGE - iota2((EDGE, rows), 1)
-    for t in range(1, taps):
-        edge_shift[(t - 1) * EDGE : t * EDGE] = ones_where((lag == t) & (before == head_ids))
-    id_wide = jnp.concatenate([ids_ref[...].astype(F32)] * (LANES // rows), 1)
 
     def one_step(p, carry):
         near = lane_range(p * LANES, LANES)
-        cols = lane_range(first + p * LANES, LANES)
         for copy in loads(p):
             copy.wait()
-        feats = []
-        for i, stream in enumerate(streams):
+        for i in range(3):
             x = x_ref[i, :, near]
             w = sf_ref[i, :, near]
             moved = dot(delay_ref[...], x)
             acc = w[0:1] * x.astype(F32)
             for t in range(1, taps):
                 acc = acc + w[t : t + 1] * moved[(t - 1) * rows : t * rows]
+            feat_ref[i, :, near] = acc
+        return carry
+
+    lax.fori_loop(0, steps, one_step, 0)
+
+
+def message_kernel(first, streams, ids_ref, prev_ref, edge_ref, sf_ref, cot_ref, local_ref, _,
+                   head_ref, sent_ref, edge_shift):
+    rows = local_ref.shape[1]
+    taps = sf_ref.shape[1]
+    head_ids = jnp.broadcast_to(ids_ref[...], (rows, rows)).astype(F32).T[0:EDGE]
+    before = pltpu.roll(jnp.broadcast_to(prev_ref[...].astype(F32), (EDGE, rows)), EDGE, 1)
+    lag = iota2((EDGE, rows), 0) + EDGE - iota2((EDGE, rows), 1)
+    for t in range(1, taps):
+        edge_shift[(t - 1) * EDGE : t * EDGE] = ones_where((lag == t) & (before == head_ids))
+    id_wide = jnp.concatenate([ids_ref[...].astype(F32)] * (LANES // rows), 1)
+
+    def one_step(p, carry):
+        near = lane_range(p * LANES, LANES)
+        cols = lane_range(first + p * LANES, LANES)
+        feats = []
+        for i, stream in enumerate(streams):
+            w = sf_ref[stream, :, cols]
             edge = edge_ref[stream, :, cols].astype(F32)
             edge = jnp.concatenate([edge, jnp.zeros((rows - EDGE, LANES), F32)], 0)
             moved = dot(edge_shift[...].astype(BF16), edge.astype(BF16))
-            fix = w[1:2] * moved[0:EDGE]
+            head = local_ref[stream, 0:EDGE, near] + w[1:2] * moved[0:EDGE]
             for t in range(2, taps):
-                fix = fix + w[t : t + 1] * moved[(t - 1) * EDGE : t * EDGE]
-            acc = jnp.concatenate([acc[0:EDGE] + fix, acc[EDGE:]], 0)
-            feat_ref[i, :, near] = acc
-            feats.append(acc)
-        if gradient:
-            g = cot_ref[:, near].astype(F32) * feats[0]
+                head = head + w[t : t + 1] * moved[(t - 1) * EDGE : t * EDGE]
+            head_ref[i, :, near] = head
+            feats.append(jnp.concatenate([head, local_ref[stream, EDGE:, near]], 0))
+        if len(streams) == 1:
+            g = cot_ref[:, cols].astype(F32) * feats[0]
             last = iota2(g.shape, 0) == rows - 1
             sent_ref[:, near] = jnp.where(last, jnp.broadcast_to(id_wide, g.shape), g).astype(BF16)
         else:
             sent_ref[:, near] = (feats[0] * feats[1]).astype(BF16)
         return carry
 
-    lax.fori_loop(0, steps, one_step, 0)
+    lax.fori_loop(0, sent_ref.shape[1] // LANES, one_step, 0)
 
 
 def run_steps(parts, steps):
@@ -138,11 +145,15 @@
     lax.fori_loop(0, steps, drain, 0)
 
 
-def edge_shifts(ids_ref, edge_ref, edge_shift):
+def joined(head, local):
+    return jnp.concatenate([head, local[EDGE:]], 0)
+
+
+def edge_shifts(ids_ref, prev_ref, edge_shift):
     rows = edge_shift.shape[1]
     taps = edge_shift.shape[0] // EDGE + 1
     id_head = jnp.broadcast_to(ids_ref[...], (EDGE, rows)).astype(F32)
-    prev = jnp.broadcast_to(edge_ref[0, 0:1, 0:rows].astype(F32), (rows, rows)).T
+    prev = jnp.broadcast_to(prev_ref[...], (rows, rows)).astype(F32).T
     lag = iota2((EDGE, rows), 1) + EDGE - iota2((EDGE, rows), 0)
     same = prev[rows - EDGE :] == id_head
     pieces = [ones_where((lag == t) & same) for t in range(1, taps)]
@@ -168,8 +179,8 @@
     return acc, sent, jnp.concatenate(sums, 0)
 
 
-def query_part(first, shared, lf_ref, q_ref, feat_ref, kvp_ref, outs, scratch):
-    ids_ref, sf_ref, advance_ref, x_ref, cot_ref, edge_ref = shared
+def query_part(first, shared, lf_ref, local_ref, q_head_ref, kv_head_ref, kvp_ref, outs, scratch):
+    ids_ref, prev_ref, sf_ref, advance_ref, x_ref, cot_ref, edge_ref = shared
     out_hbm, qg_hbm, tail_hbm, part_hbm, packed_hbm = outs
     (out_ref, qg_ref, tail_ref, part_ref, short_ref, long_ref,
      edge_shift, mask_y, mask_a, w_kv, g_rev, dh_ref, kv_turned, y_turned, sems) = scratch
@@ -181,13 +192,13 @@
     mirror = ones_where(iota2((rows, rows), 0) + iota2((rows, rows), 1) == rows - 1).astype(BF16)
     id_row = jnp.broadcast_to(ids_ref[...], (rows, rows)).astype(F32)
     id_col = id_row.T
-    prev_row = jnp.broadcast_to(edge_ref[0, 0:1, 0:rows].astype(F32), (rows, rows))
+    prev_row = jnp.broadcast_to(prev_ref[...], (rows, rows)).astype(F32)
     same = id_row == id_col
     mask_y[0:rows] = ones_where((lag <= 0) & same).astype(BF16)
     mask_y[rows:] = ones_where((lag > 0) & (prev_row.T == id_row)).astype(BF16)
     mask_a[:, 0:rows] = dot(mirror, ones_where((lag >= 0) & same).astype(BF16))
     mask_a[:, rows:] = dot(mirror, ones_where((lag < 0) & (prev_row == id_col)).astype(BF16))
-    edge_shifts(ids_ref, edge_ref, edge_shift)
+    edge_shifts(ids_ref, prev_ref, edge_shift)
     owner = iota2((rows, half), 1) // width
     blocks = LANES // CHUNK
     head = 3 * PADDED
@@ -211,15 +222,18 @@
         near = lane_range(p * LANES, LANES)
         cols = lane_range(first + p * LANES, LANES)
         cot = cot_ref[:, cols].astype(F32)
-        w_kv[0:rows] = (feat_ref[0, :, near] * feat_ref[1, :, near]).astype(BF16)
+        q = joined(q_head_ref[0, :, near], local_ref[0, :, near])
+        k = joined(kv_head_ref[0, :, near], local_ref[1, :, near])
+        v = joined(kv_head_ref[1, :, near], local_ref[2, :, near])
+        w_kv[0:rows] = (k * v).astype(BF16)
         w_kv[rows:] = kvp_ref[:, near]
         kv_turned[...] = w_kv[...].T
-        g_rev[...] = dot(mirror, (cot * q_ref[0, :, near]).astype(BF16)).astype(BF16)
-        for q in range(LANES // half):
-            part = slice(q * half, (q + 1) * half)
-            base = pl.multiple_of((first // half) * per + p * (LANES // width) + q * per, per)
+        g_rev[...] = dot(mirror, (cot * q).astype(BF16)).astype(BF16)
+        for h in range(LANES // half):
+            part = slice(h * half, (h + 1) * half)
+            base = pl.multiple_of((first // half) * per + p * (LANES // width) + h * per, per)
             for j in range(per):
-                mine = slice((q * per + j) * width, (q * per + j + 1) * width)
+                mine = slice((h * per + j) * width, (h * per + j + 1) * width)
                 taps = jnp.broadcast_to(lf_ref[pl.ds(base + j, 1), :], (rows, rows))
                 taps = pltpu.roll(taps, 0, 1, stride=1, stride_axis=0).astype(BF16)
                 toeplitz = jnp.concatenate([taps, taps], 0) * mask_y[...]
@@ -228,10 +242,10 @@
                 cross = dot(g_sel, kv_turned[part, :]) * mask_a[...]
                 folded = cross[:, 0:rows] + cross[:, rows:]
                 folded = pltpu.roll(folded, 0, 1, stride=1, stride_axis=0)
-                dh_ref[q * per + j : q * per + j + 1] = jnp.sum(folded, 0, keepdims=True)
+                dh_ref[h * per + j : h * per + j + 1] = jnp.sum(folded, 0, keepdims=True)
         dh = dot(dh_ref[...].astype(BF16), mirror)
         y = y_turned[...].T
-        out_ref[:, near] = (q_ref[0, :, near] * y).astype(BF16)
+        out_ref[:, near] = (q * y).astype(BF16)
         acc, sent, sums = short_stage(
             cot * y, sf_ref[0, :, cols], x_ref[0, :, cols].astype(F32), edge_ref[0, :, cols].astype(F32),
             advance_ref, edge_shift,
@@ -248,8 +262,8 @@
     return one_step, copies
 
 
-def pair_part(first, shared, lfr_ref, q_ref, feat_ref, gn_ref, outs, scratch):
-    ids_ref, sf_ref, advance_ref, x_ref, cot_ref, edge_ref = shared
+def pair_part(first, shared, lfr_ref, local_ref, q_head_ref, kv_head_ref, gn_ref, outs, scratch):
+    ids_ref, prev_ref, sf_ref, advance_ref, x_ref, cot_ref, edge_ref = shared
     _, qg_hbm, tail_hbm, part_hbm, packed_hbm = outs
     (qg_ref, tail_ref, part_ref, short_ref,
      edge_shift, mask_g, w_g, g_turned, gm_turned, sems) = scratch
@@ -260,7 +274,7 @@
     next_col = jnp.broadcast_to(gn_ref[rows - 1 : rows, 0:rows].astype(F32), (rows, rows)).T
     mask_g[0:rows] = ones_where((lag >= 0) & (id_row == id_row.T)).astype(BF16)
     mask_g[rows:] = ones_where((lag < 0) & (next_col == id_row)).astype(BF16)
-    edge_shifts(ids_ref, edge_ref, edge_shift)
+    edge_shifts(ids_ref, prev_ref, edge_shift)
     blocks = LANES // CHUNK
 
     def copies(p):
@@ -280,7 +294,8 @@
     def one_step(p):
         near = lane_range(p * LANES, LANES)
         cols = lane_range(first + p * LANES, LANES)
-        w_g[0:rows] = (cot_ref[:, cols].astype(F32) * q_ref[0, :, near]).astype(BF16)
+        q = joined(q_head_ref[0, :, near], local_ref[0, :, near])
+        w_g[0:rows] = (cot_ref[:, cols].astype(F32) * q).astype(BF16)
         w_g[rows:] = gn_ref[:, near]
         g_turned[...] = w_g[...].T
         for j in range(LANES // width):
@@ -294,7 +309,7 @@
         heads = []
         for i in (1, 2):
             acc, sent, sums = short_stage(
-                gm * feat_ref[2 - i, :, near], sf_ref[i, :, cols], x_ref[i, :, cols].astype(F32),
+                gm * joined(kv_head_ref[2 - i, :, near], local_ref[3 - i, :, near]), sf_ref[i, :, cols], x_ref[i, :, cols].astype(F32),
                 edge_ref[i, :, cols].astype(F32), advance_ref, edge_shift,
             )
             qg_ref[i - 1, :, near] = acc.astype(BF16)
@@ -309,18 +324,18 @@
 
 
 def mixer_kernel(query_first, pair_first, filled, *refs):
-    shared = refs[:6]
+    shared = refs[:7]
     halves = [query_first, pair_first]
-    inputs = refs[6:]
-    used = 4 * sum(first is not None for first in halves)
+    inputs = refs[7:]
+    used = 5 * sum(first is not None for first in halves)
     outs = inputs[used + filled : used + filled + 5]
     scratch = inputs[used + filled + 5 :]
     parts = []
     for first, make, size in zip(halves, (query_part, pair_part), (15, 10)):
         if first is not None:
-            steps = inputs[3].shape[1] // LANES
-            parts.append(make(first, shared, *inputs[:4], outs, scratch[:size]))
-            inputs = inputs[4:]
+            steps = inputs[4].shape[1] // LANES
+            parts.append(make(first, shared, *inputs[:5], outs, scratch[:size]))
+            inputs = inputs[5:]
             scratch = scratch[size:]
     run_steps(parts, steps)
 
@@ -357,9 +372,8 @@
     sf = jnp.transpose(short_filter, (0, 2, 1))
 
     small = pltpu.CompilerParams(vmem_limit_bytes=8 << 20)
-    edge = qkv[:, rows - EDGE :, :]
-    edge = edge.at[0, 0, :rows].set(doc_ids.astype(BF16))
-    edge = passed_along(edge, 1)
+    edge = passed_along(qkv[:, rows - EDGE :, :], 1)
+    prev_ids = passed_along(doc_ids, 1).reshape(1, rows)
 
     shifts = ((taps - 1) * rows, rows)
     delay, advance, lf_rev = pl.pallas_call(
@@ -379,29 +393,40 @@
     count = chans // PARTS
     after = ids
     features = []
-    for streams, distance in (((1, 2), 1), ((0,), -1)):
-        for part in range(PARTS):
-            feats, message = pl.pallas_call(
-                functools.partial(feature_kernel, part * count, streams),
-                in_specs=[VMEM] * 3 + [HBM] * 3 + [ANY],
+    for part in range(PARTS):
+        local = pl.pallas_call(
+            functools.partial(local_kernel, part * count),
+            in_specs=[VMEM] * 2 + [HBM] * 2 + [ANY],
+            out_specs=VMEM,
+            out_shape=jax.ShapeDtypeStruct((3, rows, count), F32),
+            scratch_shapes=[
+                pltpu.VMEM((3, taps, count), F32),
+                pltpu.VMEM((3, rows, count), BF16),
+                pltpu.SemaphoreType.DMA((2, count // LANES)),
+            ],
+            compiler_params=params,
+            cost_estimate=pl.CostEstimate(flops=2_000_000_000, bytes_accessed=4_000_000, transcendentals=0),
+            name="local",
+        )(ids, delay, sf, qkv, after)
+        made = [local]
+        after = ids
+        for streams, distance in (((1, 2), 1), ((0,), -1)):
+            head, message = pl.pallas_call(
+                functools.partial(message_kernel, part * count, streams),
+                in_specs=[VMEM] * 6 + [ANY],
                 out_specs=[VMEM] * 2,
                 out_shape=[
-                    jax.ShapeDtypeStruct((len(streams), rows, count), F32),
+                    jax.ShapeDtypeStruct((len(streams), EDGE, count), F32),
                     jax.ShapeDtypeStruct((rows, count), BF16),
                 ],
-                scratch_shapes=[
-                    pltpu.VMEM(((taps - 1) * EDGE, rows), F32),
-                    pltpu.VMEM((len(streams), taps, count), F32),
-                    pltpu.VMEM((len(streams), rows, count), BF16),
-                    pltpu.VMEM((rows, count), BF16),
-                    pltpu.SemaphoreType.DMA((3, count // LANES)),
-                ],
+                scratch_shapes=[pltpu.VMEM(((taps - 1) * EDGE, rows), F32)],
                 compiler_params=params,
-                cost_estimate=pl.CostEstimate(flops=2_000_000_000, bytes_accessed=4_000_000, transcendentals=0),
-                name="features",
-            )(ids, delay, edge, sf, qkv, cotangent, after)
+                cost_estimate=pl.CostEstimate(flops=500_000_000, bytes_accessed=1_000_000, transcendentals=0),
+                name="message",
+            )(ids, prev_ids, edge, sf, cotangent, local, after)
             after = message
-            features.append((feats, passed_along(message, distance)))
+            made += [head, passed_along(message, distance)]
+        features.append(made)
 
     full = [
         jax.ShapeDtypeStruct((rows, chans), BF16),
@@ -441,18 +466,20 @@
         pltpu.SemaphoreType.DMA((4, count // LANES)),
     ]
     results = []
-    stages = [(stage, None) for stage in range(PARTS)] + [(None, stage) for stage in range(PARTS)]
+    stages = [pair for stage in range(PARTS) for pair in ((stage, None), (None, stage))]
     for query, pair in stages:
-        operands = [ids, sf, advance, qkv, cotangent, edge]
+        operands = [ids, prev_ids, sf, advance, qkv, cotangent, edge]
         scratch = []
         query_first = pair_first = None
         if query is not None:
             query_first = query * count
-            operands += [long_filter, features[PARTS + query][0], *features[query]]
+            local, kv_head, kv_prev, q_head, grad_next = features[query]
+            operands += [long_filter, local, q_head, kv_head, kv_prev]
             scratch += query_scratch
         if pair is not None:
             pair_first = pair * count
-            operands += [lf_rev, features[PARTS + pair][0], features[pair][0], features[PARTS + pair][1]]
+            local, kv_head, kv_prev, q_head, grad_next = features[pair]
+            operands += [lf_rev, local, q_head, kv_head, grad_next]
             scratch += pair_scratch
         filled = len(results)
         results = pl.pallas_call(

time: 64.5 us -> 68.9 us (1.068)
  starting transfers between devices: 22.5 us -> 31 us
  waiting for transfers between devices: 12.9 us -> 8.8 us
    all_to_all x1, starting transfers between devices: 5.79 us -> 10.7 us  [shards(): got = lax.all_to_all(packed, 'ctx', 0, 0)]
    ppermute x6 -> x7, waiting for transfers between devices: 12.3 us -> 8.14 us  [passed_along(): return lax.ppermute(block, 'ctx', route)]
    ppermute x6 -> x7, starting transfers between devices: 16.7 us -> 20.3 us  [passed_along(): return lax.ppermute(block, 'ctx', route)]
    pallas_call x4 -> x6, Pallas kernels: 4.89 us -> 5.12 us  [the longest x2 3.39 us: shards(): pl.pallas_call(functools.partial(local_kernel, part * count), in_specs=[V...]
  transfers between devices with their start and end apart: 7 -> 8, of which waited for: 4 -> 4; matrix products, arithmetic and copies ran while one was open for 0% -> 0% of each run, Pallas kernels for 27% -> 27%
where the time goes in v8:
time: 68.9 us; the launch traced here: 68.4 us
  starting transfers between devices  31 us (45%)
  Pallas kernels  24 us (35%)
  waiting for transfers between devices  8.8 us (13%)
  local copies, waits for them, and re-layouts  3.79 us (6%)
  between operations  0.83 us (1%)
    ppermute x7, starting transfers between devices, passed_along(): return lax.ppermute(block, 'ctx', route)  20.3 us
    pallas_call x4, Pallas kernels, shards(): pl.pallas_call(functools.partial(mixer_kernel, query_first, pair_first, f...  17.5 us
    all_to_all x1, starting transfers between devices, shards(): got = lax.all_to_all(packed, 'ctx', 0, 0)  10.7 us
    ppermute x7, waiting for transfers between devices, passed_along(): return lax.ppermute(block, 'ctx', route)  8.14 us
    pallas_call x2, Pallas kernels, shards(): pl.pallas_call(functools.partial(local_kernel, part * count), in_specs=[V...  3.39 us
    unnamed x14, local copies, waits for them, and re-layouts  2.88 us
    pallas_call x4, Pallas kernels, shards(): pl.pallas_call(functools.partial(message_kernel, part * count, streams),...  1.74 us
  transfers between devices with their start and end apart: 8, of which 4 were waited for; matrix products, arithmetic and copies ran while one was open for 0% of the time, Pallas kernels for 27%

profile of v8, /device:TPU:0, one launch (start us, length us, event | category | flops | bytes accessed | tf_op | source)
XLA Modules:
  0.0 68.4 jit_solution(8927761081016704826)
XLA Ops:
  0.6 0.9 %slice.3 = bf16[3,8,2048]{2,1,0:T(8,128)(2,1)S(1)} slice(bf16[3,128,2048]{2,1,0:T(8,128)(2,1)} %refs_4_.7), slice={[0:3], [120:128], [0:2048]} | slice | bytes 196608 | tf_op jit(solution)/shard_map/slice | solution.py:375
  1.5 4.8 %collective-permute-start.1 = (bf16[3,8,2048]{2,1,0:T(8,128)(2,1)S(1)}, bf16[3,8,2048]{2,1,0:T(8,128)(2,1)S(1)}, u32[]{:S(2)}, u32[]{:S(2)}) collective-permute-start(bf16[3,8,2048]{2,1,0:T(8,128)(2,1)S(1)} %slice.3), channel_id=1, source_target_pairs={{0,4},{4,8},{8,12},{12,16},{16,20},{20,24},{24,28},{1,5},{5,9},{9,... | collective-permute-start | bytes 294920 | tf_op jit(solution)/shard_map/ppermute | solution.py:27
  6.4 3.5 %collective-permute-start = (s32[128]{0:T(128)}, s32[128]{0:T(128)S(1)}, u32[]{:S(2)}, u32[]{:S(2)}) collective-permute-start(s32[128]{0:T(128)} %param.7), channel_id=1, source_target_pairs={{0,4},{4,8},{8,12},{12,16},{16,20},{20,24},{24,28},{1,5},{5,9},{9,... | collective-permute-start | bytes 1544 | tf_op jit(solution)/shard_map/ppermute | solution.py:27
  9.8 0.0 copy-start.2
  9.8 0.7 copy-done.2
  10.5 0.0 copy-start.5
  10.5 0.8 %copy-done.5 = f32[128,128]{1,0:T(8,128)S(1)} copy-done((f32[128,128]{1,0:T(8,128)S(1)}, f32[128,128]{1,0:T(8,128)}, u32[]{:S(2)}) %copy-start.5) | copy-done | bytes 65560
  11.3 0.0 copy-start.1
  11.4 0.0 copy-start.3
  11.4 0.0 copy-start.4
  11.4 0.2 prepare.1
  11.5 0.8 %copy-done.1 = f32[3,2048,7]{1,2,0:T(8,128)S(1)} copy-done((f32[3,2048,7]{1,2,0:T(8,128)S(1)}, f32[3,2048,7]{1,2,0:T(8,128)}, u32[]{:S(2)}) %copy-start.1) | copy-done | bytes 172056
  12.3 0.0 copy-done.3
  12.3 0.6 copy-done.4
  12.9 0.0 copy-start
  12.9 1.7 %local.2.local_ref.refs_8_ = f32[3,128,1024]{2,1,0:T(8,128)S(1)} custom-call(s32[1,128]{1,0:T(1,128)S(1)} %bitcast.15, bf16[768,128]{1,0:T(8,128)(2,1)S(1)} %get-tuple-element.40.delay_ref, f32[3,7,2048]{2,1,0:T(8,128)S(1)} %bitcast.4, bf16[3,128,2048]{2,1,0:T(8,128)(2,1)S(1)} %copy-done.4, s32[1,128]{1,0:T(1,128)S(1)} %bitcast.16), custom_call_target="tpu_custom_call" | custom-call | flops 2000000000 | bytes 4000000 | tf_op jit(solution)/shard_map/local/pallas_call | solution.py:397
  14.6 0.0 collective-permute-done
  14.6 0.0 collective-permute-done.1.edge_ref.refs_6_
  14.6 0.0 copy-done
  14.6 0.4 message.4
  15.1 3.4 %collective-permute-start.5 = (bf16[128,1024]{1,0:T(8,128)(2,1)S(1)}, bf16[128,1024]{1,0:T(8,128)(2,1)S(1)}, u32[]{:S(2)}, u32[]{:S(2)}) collective-permute-start(bf16[128,1024]{1,0:T(8,128)(2,1)S(1)} %get-tuple-element.41._), channel_id=1, source_target_pairs={{0,4},{4,8},{8,12},{12,16},{16,20},{20,24},{24,28},{1,5},{5,9},{9,... | collective-permute-start | bytes 786440 | tf_op jit(solution)/shard_map/ppermute | solution.py:27
  18.5 0.4 message.5
  18.9 1.3 %collective-permute-start.4 = (bf16[128,1024]{1,0:T(8,128)(2,1)S(1)}, bf16[128,1024]{1,0:T(8,128)(2,1)S(1)}, u32[]{:S(2)}, u32[]{:S(2)}) collective-permute-start(bf16[128,1024]{1,0:T(8,128)(2,1)S(1)} %get-tuple-element.42._), channel_id=1, source_target_pairs={{4,0},{8,4},{12,8},{16,12},{20,16},{24,20},{28,24},{5,1},{9,5},{13... | collective-permute-start | bytes 786440 | tf_op jit(solution)/shard_map/ppermute | solution.py:27
  20.2 1.7 %local.3.local_ref.refs_8_ = f32[3,128,1024]{2,1,0:T(8,128)S(1)} custom-call(s32[1,128]{1,0:T(1,128)S(1)} %bitcast.20, bf16[768,128]{1,0:T(8,128)(2,1)S(1)} %get-tuple-element.40.delay_ref, f32[3,7,2048]{2,1,0:T(8,128)S(1)} %bitcast.7, bf16[3,128,2048]{2,1,0:T(8,128)(2,1)S(1)} %copy-done.4, bf16[128,1024]{1,0:T(8,128)(2,1)S(1)} %get-tuple-element.42._), custom_call_target="tpu_custom_call" | custom-call | flops 2000000000 | bytes 4000000 | tf_op jit(solution)/shard_map/local/pallas_call | solution.py:397
  21.9 0.4 message.6
  22.4 0.0 copy-start.6
  22.4 4.7 %collective-permute-start.3 = (bf16[128,1024]{1,0:T(8,128)(2,1)S(1)}, bf16[128,1024]{1,0:T(8,128)(2,1)S(1)}, u32[]{:S(2)}, u32[]{:S(2)}) collective-permute-start(bf16[128,1024]{1,0:T(8,128)(2,1)S(1)} %get-tuple-element.43._), channel_id=1, source_target_pairs={{0,4},{4,8},{8,12},{12,16},{16,20},{20,24},{24,28},{1,5},{5,9},{9,... | collective-permute-start | bytes 786440 | tf_op jit(solution)/shard_map/ppermute | solution.py:27
  27.1 0.4 message.7
  27.5 1.3 %collective-permute-start.2 = (bf16[128,1024]{1,0:T(8,128)(2,1)S(1)}, bf16[128,1024]{1,0:T(8,128)(2,1)S(1)}, u32[]{:S(2)}, u32[]{:S(2)}) collective-permute-start(bf16[128,1024]{1,0:T(8,128)(2,1)S(1)} %get-tuple-element.46), channel_id=1, source_target_pairs={{4,0},{8,4},{12,8},{16,12},{20,16},{24,20},{28,24},{5,1},{9,5},{13... | collective-permute-start | bytes 786440 | tf_op jit(solution)/shard_map/ppermute | solution.py:27
  28.8 1.2 %collective-permute-done.5.refs_11_ = bf16[128,1024]{1,0:T(8,128)(2,1)S(1)} collective-permute-done((bf16[128,1024]{1,0:T(8,128)(2,1)S(1)}, bf16[128,1024]{1,0:T(8,128)(2,1)S(1)}, u32[]{:S(2)}, u32[]{:S(2)}) %collective-permute-start.5) | collective-permute-done | bytes 262176 | tf_op jit(solution)/shard_map/ppermute | solution.py:27
  30.0 0.0 copy-done.6
  30.0 5.1 %query.2 = (bf16[128,2048]{1,0:T(8,128)(2,1)}, bf16[3,128,2048]{2,1,0:T(8,128)(2,1)}, f32[3,8,2048]{2,1,0:T(8,128)S(1)}, bf16[3,8,2048]{2,1,0:T(8,128)(2,1)S(1)}, bf16[8,32,256]{2,1,0:T(8,128)(2,1)}) custom-call(s32[1,128]{1,0:T(1,128)S(1)} %bitcast.24, s32[1,128]{1,0:T(1,128)S(1)} %bitcast.32, f32[3,7,2048]{2,1,0:T(8,128)S(1)} %bitcast.10, ...), custom_call_target="tpu_custom_call" | custom-call | flops 4000000000 | bytes 4000000 | tf_op jit(solution)/shard_map/query/pallas_call | solution.py:485
  35.1 0.0 collective-permute-done.4.refs_11_
  35.2 3.6 %pair.2 = (bf16[128,2048]{1,0:T(8,128)(2,1)}, bf16[3,128,2048]{2,1,0:T(8,128)(2,1)}, f32[3,8,2048]{2,1,0:T(8,128)S(1)}, bf16[3,8,2048]{2,1,0:T(8,128)(2,1)S(1)}, bf16[8,32,256]{2,1,0:T(8,128)(2,1)}) custom-call(s32[1,128]{1,0:T(1,128)S(1)} %bitcast.25, ...), custom_call_target="tpu_custom_call", output_to_operand_aliasing={{0}: (12, {}), {1}: (13, {}), {2}: (14, {}), {3}: (15, {}),... | custom-call | flops 4000000000 | bytes 4000000 | tf_op jit(solution)/shard_map/pair/pallas_call | solution.py:485
  38.8 1.5 %collective-permute-done.3.refs_11_ = bf16[128,1024]{1,0:T(8,128)(2,1)S(1)} collective-permute-done((bf16[128,1024]{1,0:T(8,128)(2,1)S(1)}, bf16[128,1024]{1,0:T(8,128)(2,1)S(1)}, u32[]{:S(2)}, u32[]{:S(2)}) %collective-permute-start.3) | collective-permute-done | bytes 262176 | tf_op jit(solution)/shard_map/ppermute | solution.py:27
  40.3 5.1 %query.3 = (bf16[128,2048]{1,0:T(8,128)(2,1)}, bf16[3,128,2048]{2,1,0:T(8,128)(2,1)}, f32[3,8,2048]{2,1,0:T(8,128)S(1)}, bf16[3,8,2048]{2,1,0:T(8,128)(2,1)S(1)}, bf16[8,32,256]{2,1,0:T(8,128)(2,1)}) custom-call(s32[1,128]{1,0:T(1,128)S(1)} %bitcast.26, ...), custom_call_target="tpu_custom_call", output_to_operand_aliasing={{0}: (12, {}), {1}: (13, {}), {2}: (14, {}), {3}: (15, {}),... | custom-call | flops 4000000000 | bytes 4000000 | tf_op jit(solution)/shard_map/query/pallas_call | solution.py:485
  45.5 0.0 collective-permute-done.2.refs_11_
  45.5 3.6 %pair.3 = (bf16[128,2048]{1,0:T(8,128)(2,1)}, bf16[3,128,2048]{2,1,0:T(8,128)(2,1)}, f32[3,8,2048]{2,1,0:T(8,128)S(1)}, bf16[3,8,2048]{2,1,0:T(8,128)(2,1)S(1)}, bf16[8,32,256]{2,1,0:T(8,128)(2,1)}) custom-call(s32[1,128]{1,0:T(1,128)S(1)} %bitcast.27, ...), custom_call_target="tpu_custom_call", output_to_operand_aliasing={{0}: (12, {}), {1}: (13, {}), {2}: (14, {}), {3}: (15, {}),... | custom-call | flops 4000000000 | bytes 4000000 | tf_op jit(solution)/shard_map/pair/pallas_call | solution.py:485
  49.1 10.7 %all-to-all-start = ((bf16[8,32,256]{2,1,0:T(8,128)(2,1)}), bf16[8,32,256]{2,1,0:T(8,128)(2,1)S(1)}, u32[]{:S(2)}, u32[]{:S(2)}) async-start(bf16[8,32,256]{2,1,0:T(8,128)(2,1)} %get-tuple-element.65), calls=%async_computation | async-start | bytes 262144 | tf_op jit(solution)/shard_map/all_to_all | solution.py:501
  59.8 1.3 %collective-permute-start.6 = (bf16[3,8,2048]{2,1,0:T(8,128)(2,1)S(1)}, bf16[3,8,2048]{2,1,0:T(8,128)(2,1)S(1)}, u32[]{:S(2)}, u32[]{:S(2)}) collective-permute-start(bf16[3,8,2048]{2,1,0:T(8,128)(2,1)S(1)} %get-tuple-element.67), channel_id=1, source_target_pairs={{4,0},{8,4},{12,8},{16,12},{20,16},{24,20},{28,24},{5,1},{9,5},{13... | collective-permute-start | bytes 294920 | tf_op jit(solution)/shard_map/ppermute | solution.py:27
  61.1 5.4 %collective-permute-done.6.part_ref = bf16[3,8,2048]{2,1,0:T(8,128)(2,1)S(1)} collective-permute-done((bf16[3,8,2048]{2,1,0:T(8,128)(2,1)S(1)}, bf16[3,8,2048]{2,1,0:T(8,128)(2,1)S(1)}, u32[]{:S(2)}, u32[]{:S(2)}) %collective-permute-start.6) | collective-permute-done | bytes 98336 | tf_op jit(solution)/shard_map/ppermute | solution.py:27
  66.4 0.7 all-to-all-done.got_ref
  67.1 1.3 %finish.1 = (bf16[3,128,2048]{2,1,0:T(8,128)(2,1)}, f32[16,128]{1,0:T(8,128)}, f32[3,7,256]{2,1,0:T(8,128)}) custom-call(bf16[8,32,256]{2,1,0:T(8,128)(2,1)S(1)} %all-to-all-done.got_ref, f32[3,8,2048]{2,1,0:T(8,128)S(1)} %get-tuple-element.66.tail_ref, bf16[3,8,2048]{2,1,0:T(8,128)(2,1)S(1)} %collective-permute-done.6.part_ref, ...), custom_call_target="tpu_custom_call", output_to_operand_aliasing={{0}: (3, {})} | custom-call | flops 1000000 | bytes 200000 | tf_op jit(solution)/shard_map/finish/pallas_call | solution.py:502
Async XLA Ops:
  1.5 13.1 %collective-permute-start.1 = (bf16[3,8,2048]{2,1,0:T(8,128)(2,1)S(1)}, bf16[3,8,2048]{2,1,0:T(8,128)(2,1)S(1)}, u32[]{:S(2)}, u32[]{:S(2)}) collective-permute-start(bf16[3,8,2048]{2,1,0:T(8,128)(2,1)S(1)} %slice.3), channel_id=1, source_target_pairs={{0,4},{4,8},{8,12},{12,16},{16,20},{20,24},{24,28},{1,5},{5,9},{9,... | collective-permute-start | bytes 294920 | tf_op jit(solution)/shard_map/ppermute | solution.py:27
  6.4 8.2 %collective-permute-start = (s32[128]{0:T(128)}, s32[128]{0:T(128)S(1)}, u32[]{:S(2)}, u32[]{:S(2)}) collective-permute-start(s32[128]{0:T(128)} %param.7), channel_id=1, source_target_pairs={{0,4},{4,8},{8,12},{12,16},{16,20},{20,24},{24,28},{1,5},{5,9},{9,... | collective-permute-start | bytes 1544 | tf_op jit(solution)/shard_map/ppermute | solution.py:27
  9.8 0.7 copy-start.2
  10.5 0.8 %copy-start.5 = (f32[128,128]{1,0:T(8,128)S(1)}, f32[128,128]{1,0:T(8,128)}, u32[]{:S(2)}) copy-start(f32[128,128]{1,0:T(8,128)} %refs_7_.3) | copy-start | bytes 196612
  11.3 0.9 %copy-start.1 = (f32[3,2048,7]{1,2,0:T(8,128)S(1)}, f32[3,2048,7]{1,2,0:T(8,128)}, u32[]{:S(2)}) copy-start(f32[3,2048,7]{1,2,0:T(8,128)} %param.8) | copy-start | bytes 516100
  11.4 0.9 %copy-start.3 = (s32[128]{0:T(128)S(1)}, s32[128]{0:T(128)}, u32[]{:S(2)}) copy-start(s32[128]{0:T(128)} %param.7) | copy-start | bytes 1540
  11.4 1.5 %copy-start.4 = (bf16[3,128,2048]{2,1,0:T(8,128)(2,1)S(1)}, bf16[3,128,2048]{2,1,0:T(8,128)(2,1)}, u32[]{:S(2)}) copy-start(bf16[3,128,2048]{2,1,0:T(8,128)(2,1)} %refs_4_.7) | copy-start | bytes 4718596
  12.9 1.7 %copy-start = (bf16[128,2048]{1,0:T(8,128)(2,1)S(1)}, bf16[128,2048]{1,0:T(8,128)(2,1)}, u32[]{:S(2)}) copy-start(bf16[128,2048]{1,0:T(8,128)(2,1)} %refs_5_.7) | copy-start | bytes 1572868
  15.1 14.9 %collective-permute-start.5 = (bf16[128,1024]{1,0:T(8,128)(2,1)S(1)}, bf16[128,1024]{1,0:T(8,128)(2,1)S(1)}, u32[]{:S(2)}, u32[]{:S(2)}) collective-permute-start(bf16[128,1024]{1,0:T(8,128)(2,1)S(1)} %get-tuple-element.41._), channel_id=1, source_target_pairs={{0,4},{4,8},{8,12},{12,16},{16,20},{20,24},{24,28},{1,5},{5,9},{9,... | collective-permute-start | bytes 786440 | tf_op jit(solution)/shard_map/ppermute | solution.py:27
  18.9 16.2 %collective-permute-start.4 = (bf16[128,1024]{1,0:T(8,128)(2,1)S(1)}, bf16[128,1024]{1,0:T(8,128)(2,1)S(1)}, u32[]{:S(2)}, u32[]{:S(2)}) collective-permute-start(bf16[128,1024]{1,0:T(8,128)(2,1)S(1)} %get-tuple-element.42._), channel_id=1, source_target_pairs={{4,0},{8,4},{12,8},{16,12},{20,16},{24,20},{28,24},{5,1},{9,5},{13... | collective-permute-start | bytes 786440 | tf_op jit(solution)/shard_map/ppermute | solution.py:27
  22.4 7.6 %copy-start.6 = (f32[128,128]{1,0:T(8,128)S(1)}, f32[128,128]{1,0:T(8,128)}, u32[]{:S(2)}) copy-start(f32[128,128]{1,0:T(8,128)} %refs_7_.3) | copy-start | bytes 196612
  22.4 17.9 %collective-permute-start.3 = (bf16[128,1024]{1,0:T(8,128)(2,1)S(1)}, bf16[128,1024]{1,0:T(8,128)(2,1)S(1)}, u32[]{:S(2)}, u32[]{:S(2)}) collective-permute-start(bf16[128,1024]{1,0:T(8,128)(2,1)S(1)} %get-tuple-element.43._), channel_id=1, source_target_pairs={{0,4},{4,8},{8,12},{12,16},{16,20},{20,24},{24,28},{1,5},{5,9},{9,... | collective-permute-start | bytes 786440 | tf_op jit(solution)/shard_map/ppermute | solution.py:27
  27.5 17.9 %collective-permute-start.2 = (bf16[128,1024]{1,0:T(8,128)(2,1)S(1)}, bf16[128,1024]{1,0:T(8,128)(2,1)S(1)}, u32[]{:S(2)}, u32[]{:S(2)}) collective-permute-start(bf16[128,1024]{1,0:T(8,128)(2,1)S(1)} %get-tuple-element.46), channel_id=1, source_target_pairs={{4,0},{8,4},{12,8},{16,12},{20,16},{24,20},{28,24},{5,1},{9,5},{13... | collective-permute-start | bytes 786440 | tf_op jit(solution)/shard_map/ppermute | solution.py:27
  49.1 18.0 %all-to-all-start = ((bf16[8,32,256]{2,1,0:T(8,128)(2,1)}), bf16[8,32,256]{2,1,0:T(8,128)(2,1)S(1)}, u32[]{:S(2)}, u32[]{:S(2)}) async-start(bf16[8,32,256]{2,1,0:T(8,128)(2,1)} %get-tuple-element.65), calls=%async_computation | async-start | bytes 262144 | tf_op jit(solution)/shard_map/all_to_all | solution.py:501
  59.8 6.7 %collective-permute-start.6 = (bf16[3,8,2048]{2,1,0:T(8,128)(2,1)S(1)}, bf16[3,8,2048]{2,1,0:T(8,128)(2,1)S(1)}, u32[]{:S(2)}, u32[]{:S(2)}) collective-permute-start(bf16[3,8,2048]{2,1,0:T(8,128)(2,1)S(1)} %get-tuple-element.67), channel_id=1, source_target_pairs={{4,0},{8,4},{12,8},{16,12},{20,16},{24,20},{28,24},{5,1},{9,5},{13... | collective-permute-start | bytes 294920 | tf_op jit(solution)/shard_map/ppermute | solution.py:27

commit v9 on v8

--- a/solution.py
+++ b/solution.py
@@ -43,7 +43,7 @@
     return jnp.where(cond, 1.0, 0.0)
 
 
-def prepare_kernel(ids_ref, lf_ref, delay_ref, advance_ref, lfr_ref):
+def prepare_kernel(ids_ref, delay_ref, advance_ref):
     rows = delay_ref.shape[1]
     taps = delay_ref.shape[0] // rows + 1
     id_row = jnp.broadcast_to(ids_ref[...], (rows, rows)).astype(F32)
@@ -52,8 +52,6 @@
     for t in range(1, taps):
         delay_ref[(t - 1) * rows : t * rows] = ones_where((lag == t) & same).astype(BF16)
         advance_ref[(t - 1) * rows : t * rows] = ones_where((lag == -t) & same).astype(BF16)
-    backward = ones_where((iota2((rows, rows), 0) + iota2((rows, rows), 1)) % rows == 0)
-    lfr_ref[...] = dot(lf_ref[...].astype(BF16), backward.astype(BF16))
 
 
 def local_kernel(first, ids_ref, delay_ref, sf_hbm, x_hbm, _, feat_ref, sf_ref, x_ref, sems):
@@ -91,12 +89,12 @@
     lax.fori_loop(0, steps, one_step, 0)
 
 
-def message_kernel(first, streams, ids_ref, prev_ref, edge_ref, sf_ref, cot_ref, local_ref, _,
+def message_kernel(first, streams, ids_ref, edge_ref, sf_ref, cot_ref, local_ref, _,
                    head_ref, sent_ref, edge_shift):
     rows = local_ref.shape[1]
     taps = sf_ref.shape[1]
     head_ids = jnp.broadcast_to(ids_ref[...], (rows, rows)).astype(F32).T[0:EDGE]
-    before = pltpu.roll(jnp.broadcast_to(prev_ref[...].astype(F32), (EDGE, rows)), EDGE, 1)
+    before = pltpu.roll(jnp.broadcast_to(edge_ref[0, 0:1, 0:rows].astype(F32), (EDGE, rows)), EDGE, 1)
     lag = iota2((EDGE, rows), 0) + EDGE - iota2((EDGE, rows), 1)
     for t in range(1, taps):
         edge_shift[(t - 1) * EDGE : t * EDGE] = ones_where((lag == t) & (before == head_ids))
@@ -149,11 +147,11 @@
     return jnp.concatenate([head, local[EDGE:]], 0)
 
 
-def edge_shifts(ids_ref, prev_ref, edge_shift):
+def edge_shifts(ids_ref, edge_ref, edge_shift):
     rows = edge_shift.shape[1]
     taps = edge_shift.shape[0] // EDGE + 1
     id_head = jnp.broadcast_to(ids_ref[...], (EDGE, rows)).astype(F32)
-    prev = jnp.broadcast_to(prev_ref[...], (rows, rows)).astype(F32).T
+    prev = jnp.broadcast_to(edge_ref[0, 0:1, 0:rows].astype(F32), (rows, rows)).T
     lag = iota2((EDGE, rows), 1) + EDGE - iota2((EDGE, rows), 0)
     same = prev[rows - EDGE :] == id_head
     pieces = [ones_where((lag == t) & same) for t in range(1, taps)]
@@ -180,7 +178,7 @@
 
 
 def query_part(first, shared, lf_ref, local_ref, q_head_ref, kv_head_ref, kvp_ref, outs, scratch):
-    ids_ref, prev_ref, sf_ref, advance_ref, x_ref, cot_ref, edge_ref = shared
+    ids_ref, sf_ref, advance_ref, x_ref, cot_ref, edge_ref = shared
     out_hbm, qg_hbm, tail_hbm, part_hbm, packed_hbm = outs
     (out_ref, qg_ref, tail_ref, part_ref, short_ref, long_ref,
      edge_shift, mask_y, mask_a, w_kv, g_rev, dh_ref, kv_turned, y_turned, sems) = scratch
@@ -192,13 +190,13 @@
     mirror = ones_where(iota2((rows, rows), 0) + iota2((rows, rows), 1) == rows - 1).astype(BF16)
     id_row = jnp.broadcast_to(ids_ref[...], (rows, rows)).astype(F32)
     id_col = id_row.T
-    prev_row = jnp.broadcast_to(prev_ref[...], (rows, rows)).astype(F32)
+    prev_row = jnp.broadcast_to(edge_ref[0, 0:1, 0:rows].astype(F32), (rows, rows))
     same = id_row == id_col
     mask_y[0:rows] = ones_where((lag <= 0) & same).astype(BF16)
     mask_y[rows:] = ones_where((lag > 0) & (prev_row.T == id_row)).astype(BF16)
     mask_a[:, 0:rows] = dot(mirror, ones_where((lag >= 0) & same).astype(BF16))
     mask_a[:, rows:] = dot(mirror, ones_where((lag < 0) & (prev_row == id_col)).astype(BF16))
-    edge_shifts(ids_ref, prev_ref, edge_shift)
+    edge_shifts(ids_ref, edge_ref, edge_shift)
     owner = iota2((rows, half), 1) // width
     blocks = LANES // CHUNK
     head = 3 * PADDED
@@ -262,19 +260,21 @@
     return one_step, copies
 
 
-def pair_part(first, shared, lfr_ref, local_ref, q_head_ref, kv_head_ref, gn_ref, outs, scratch):
-    ids_ref, prev_ref, sf_ref, advance_ref, x_ref, cot_ref, edge_ref = shared
+def pair_part(first, shared, lf_ref, local_ref, q_head_ref, kv_head_ref, gn_ref, outs, scratch):
+    ids_ref, sf_ref, advance_ref, x_ref, cot_ref, edge_ref = shared
     _, qg_hbm, tail_hbm, part_hbm, packed_hbm = outs
     (qg_ref, tail_ref, part_ref, short_ref,
-     edge_shift, mask_g, w_g, g_turned, gm_turned, sems) = scratch
+     edge_shift, mask_g, w_g, g_turned, gm_turned, lfr_ref, sems) = scratch
     rows = x_ref.shape[1]
     width = x_ref.shape[2] // lfr_ref.shape[0]
     lag = iota2((rows, rows), 0) - iota2((rows, rows), 1)
     id_row = jnp.broadcast_to(ids_ref[...], (rows, rows)).astype(F32)
     next_col = jnp.broadcast_to(gn_ref[rows - 1 : rows, 0:rows].astype(F32), (rows, rows)).T
+    backward = ones_where((iota2((rows, rows), 0) + iota2((rows, rows), 1)) % rows == 0)
+    lfr_ref[...] = dot(lf_ref[...].astype(BF16), backward.astype(BF16))
     mask_g[0:rows] = ones_where((lag >= 0) & (id_row == id_row.T)).astype(BF16)
     mask_g[rows:] = ones_where((lag < 0) & (next_col == id_row)).astype(BF16)
-    edge_shifts(ids_ref, prev_ref, edge_shift)
+    edge_shifts(ids_ref, edge_ref, edge_shift)
     blocks = LANES // CHUNK
 
     def copies(p):
@@ -324,14 +324,14 @@
 
 
 def mixer_kernel(query_first, pair_first, filled, *refs):
-    shared = refs[:7]
+    shared = refs[:6]
     halves = [query_first, pair_first]
-    inputs = refs[7:]
+    inputs = refs[6:]
     used = 5 * sum(first is not None for first in halves)
     outs = inputs[used + filled : used + filled + 5]
     scratch = inputs[used + filled + 5 :]
     parts = []
-    for first, make, size in zip(halves, (query_part, pair_part), (15, 10)):
+    for first, make, size in zip(halves, (query_part, pair_part), (15, 11)):
         if first is not None:
             steps = inputs[4].shape[1] // LANES
             parts.append(make(first, shared, *inputs[:5], outs, scratch[:size]))
@@ -340,11 +340,15 @@
     run_steps(parts, steps)
 
 
-def finish_kernel(scale, taps, got_ref, tail_ref, part_ref, qg_in, qg_hbm, long_ref, short_ref, last_ref, sem):
+def last_rows_kernel(tail_ref, part_ref, qg_in, _, qg_hbm, last_ref, sem):
     rows = qg_hbm.shape[1]
     last_ref[...] = (tail_ref[...] + part_ref[...].astype(F32)).astype(BF16)
     copy = pltpu.make_async_copy(last_ref, qg_hbm.at[:, rows - EDGE :, :], sem)
     copy.start()
+    copy.wait()
+
+
+def total_kernel(scale, taps, got_ref, long_ref, short_ref):
     total = got_ref[0].astype(F32)
     for k in range(1, got_ref.shape[0]):
         total = total + got_ref[k].astype(F32)
@@ -355,7 +359,6 @@
     lags = long_ref.shape[1]
     for p in range(total.shape[1] // lags):
         long_ref[p * size : (p + 1) * size] = total[3 * PADDED :, p * lags : (p + 1) * lags]
-    copy.wait()
 
 
 def shards(qkv, cotangent, doc_ids, short_filter, long_filter):
@@ -372,23 +375,19 @@
     sf = jnp.transpose(short_filter, (0, 2, 1))
 
     small = pltpu.CompilerParams(vmem_limit_bytes=8 << 20)
-    edge = passed_along(qkv[:, rows - EDGE :, :], 1)
-    prev_ids = passed_along(doc_ids, 1).reshape(1, rows)
+    edge = qkv[:, rows - EDGE :, :]
+    edge = passed_along(edge.at[0, 0, :rows].set(doc_ids.astype(BF16)), 1)
 
     shifts = ((taps - 1) * rows, rows)
-    delay, advance, lf_rev = pl.pallas_call(
+    delay, advance = pl.pallas_call(
         prepare_kernel,
-        in_specs=[VMEM] * 2,
-        out_specs=[VMEM] * 3,
-        out_shape=[
-            jax.ShapeDtypeStruct(shifts, BF16),
-            jax.ShapeDtypeStruct(shifts, BF16),
-            jax.ShapeDtypeStruct((groups, long_taps), F32),
-        ],
+        in_specs=[VMEM],
+        out_specs=[VMEM] * 2,
+        out_shape=[jax.ShapeDtypeStruct(shifts, BF16), jax.ShapeDtypeStruct(shifts, BF16)],
         cost_estimate=pl.CostEstimate(flops=6_000_000_000, bytes_accessed=16_000_000, transcendentals=0),
         compiler_params=small,
         name="prepare",
-    )(ids, long_filter)
+    )(ids)
 
     count = chans // PARTS
     after = ids
@@ -413,7 +412,7 @@
         for streams, distance in (((1, 2), 1), ((0,), -1)):
             head, message = pl.pallas_call(
                 functools.partial(message_kernel, part * count, streams),
-                in_specs=[VMEM] * 6 + [ANY],
+                in_specs=[VMEM] * 5 + [ANY],
                 out_specs=[VMEM] * 2,
                 out_shape=[
                     jax.ShapeDtypeStruct((len(streams), EDGE, count), F32),
@@ -423,7 +422,7 @@
                 compiler_params=params,
                 cost_estimate=pl.CostEstimate(flops=500_000_000, bytes_accessed=1_000_000, transcendentals=0),
                 name="message",
-            )(ids, prev_ids, edge, sf, cotangent, local, after)
+            )(ids, edge, sf, cotangent, local, after)
             after = message
             made += [head, passed_along(message, distance)]
         features.append(made)
@@ -463,12 +462,13 @@
         pltpu.VMEM((2 * rows, LANES), BF16),
         pltpu.VMEM((LANES, 2 * rows), BF16),
         pltpu.VMEM((LANES, rows), F32),
+        pltpu.VMEM((groups, long_taps), F32),
         pltpu.SemaphoreType.DMA((4, count // LANES)),
     ]
     results = []
     stages = [pair for stage in range(PARTS) for pair in ((stage, None), (None, stage))]
     for query, pair in stages:
-        operands = [ids, prev_ids, sf, advance, qkv, cotangent, edge]
+        operands = [ids, sf, advance, qkv, cotangent, edge]
         scratch = []
         query_first = pair_first = None
         if query is not None:
@@ -479,7 +479,7 @@
         if pair is not None:
             pair_first = pair * count
             local, kv_head, kv_prev, q_head, grad_next = features[pair]
-            operands += [lf_rev, local, q_head, kv_head, grad_next]
+            operands += [long_filter, local, q_head, kv_head, grad_next]
             scratch += pair_scratch
         filled = len(results)
         results = pl.pallas_call(
@@ -499,32 +499,40 @@
     per = chans // devices
     if per == CHUNK:
         got = lax.all_to_all(packed, "ctx", 0, 0)
-        qg, long_grad, short_grad = pl.pallas_call(
-            functools.partial(finish_kernel, grad_scale, taps),
-            in_specs=[VMEM, VMEM, VMEM, ANY],
-            out_specs=[ANY, VMEM, VMEM],
+        long_grad, short_grad = pl.pallas_call(
+            functools.partial(total_kernel, grad_scale, taps),
+            in_specs=[VMEM],
+            out_specs=[VMEM] * 2,
             out_shape=[
-                jax.ShapeDtypeStruct(qg.shape, BF16),
                 jax.ShapeDtypeStruct((groups // devices, long_taps), F32),
                 jax.ShapeDtypeStruct((3, taps, per), F32),
             ],
-            input_output_aliases={3: 0},
-            scratch_shapes=[pltpu.VMEM((3, EDGE, chans), BF16), pltpu.SemaphoreType.DMA],
             compiler_params=small,
             cost_estimate=pl.CostEstimate(flops=1_000_000, bytes_accessed=200_000, transcendentals=0),
-            name="finish",
-        )(got, tail, part, qg)
-        return (out, qg, long_grad, short_grad.transpose(0, 2, 1))
-    qg = lax.dynamic_update_slice(qg, (tail + part.astype(F32)).astype(BF16), (0, rows - EDGE, 0))
-    head = 3 * PADDED
-    short_part = packed[:, :head].transpose(1, 0, 2).reshape(head, devices, per)
-    long_part = packed[:, head:].reshape(-1, packed_rows - head, CHUNK // long_taps, long_taps)
-    long_part = long_part.transpose(0, 2, 1, 3).reshape(devices, -1, per)
-    got = jnp.concatenate([short_part.transpose(1, 0, 2), long_part], 1)
-    got = lax.all_to_all(got, "ctx", 0, 0)
-    total = jnp.sum(got.astype(F32), 0) * grad_scale
-    short_grad = total[:head].reshape(3, PADDED, per)[:, :taps].transpose(0, 2, 1)
-    long_grad = total[head:].reshape(groups // devices, long_taps)
+            name="total",
+        )(got)
+        short_grad = short_grad.transpose(0, 2, 1)
+    else:
+        head = 3 * PADDED
+        short_part = packed[:, :head].transpose(1, 0, 2).reshape(head, devices, per)
+        long_part = packed[:, head:].reshape(-1, packed_rows - head, CHUNK // long_taps, long_taps)
+        long_part = long_part.transpose(0, 2, 1, 3).reshape(devices, -1, per)
+        got = jnp.concatenate([short_part.transpose(1, 0, 2), long_part], 1)
+        got = lax.all_to_all(got, "ctx", 0, 0)
+        total = jnp.sum(got.astype(F32), 0) * grad_scale
+        short_grad = total[:head].reshape(3, PADDED, per)[:, :taps].transpose(0, 2, 1)
+        long_grad = total[head:].reshape(groups // devices, long_taps)
+    qg = pl.pallas_call(
+        last_rows_kernel,
+        in_specs=[VMEM, VMEM, ANY, ANY],
+        out_specs=ANY,
+        out_shape=jax.ShapeDtypeStruct(qg.shape, BF16),
+        input_output_aliases={2: 0},
+        scratch_shapes=[pltpu.VMEM((3, EDGE, chans), BF16), pltpu.SemaphoreType.DMA],
+        compiler_params=small,
+        cost_estimate=pl.CostEstimate(flops=100_000, bytes_accessed=200_000, transcendentals=0),
+        name="last_rows",
+    )(tail, part, qg, got)
     return (out, qg, long_grad, short_grad)
 
 

time: 68.9 us -> 60.7 us (0.88)
  starting transfers between devices: 31 us -> 22.7 us
  local copies, waits for them, and re-layouts: 3.79 us -> 3.04 us
    all_to_all x1, waiting for transfers between devices: 0.66 us -> 6.06 us  [shards(): got = lax.all_to_all(packed, 'ctx', 0, 0)]
    ppermute x7 -> x6, waiting for transfers between devices: 8.14 us -> 3 us  [passed_along(): return lax.ppermute(block, 'ctx', route)]
    all_to_all x1, starting transfers between devices: 10.7 us -> 5.78 us  [shards(): got = lax.all_to_all(packed, 'ctx', 0, 0)]
    ppermute x7 -> x6, starting transfers between devices: 20.3 us -> 16.9 us  [passed_along(): return lax.ppermute(block, 'ctx', route)]
    unnamed x14 -> x12, local copies, waits for them, and re-layouts: 2.88 us -> 2.06 us
    pallas_call x2 -> x3, Pallas kernels: 1.44 us -> 1.43 us  [the longest x1 0.67 us: shards(): pl.pallas_call(last_rows_kernel, in_specs=[VMEM, VMEM, ANY, ANY], out_spe...]
  transfers between devices with their start and end apart: 8 -> 7, of which waited for: 4 -> 3; matrix products, arithmetic and copies ran while one was open for 0% -> 0% of each run, Pallas kernels for 27% -> 32%
where the time goes in v9:
time: 60.7 us; the launch traced here: 60.3 us
  Pallas kernels  24.1 us (40%)
  starting transfers between devices  22.7 us (37%)
  waiting for transfers between devices  9.05 us (15%)
  local copies, waits for them, and re-layouts  3.04 us (5%)
  between operations  0.82 us (1%)
  other arithmetic  0.66 us (1%)
    pallas_call x4, Pallas kernels, shards(): pl.pallas_call(functools.partial(mixer_kernel, query_first, pair_first, f...  17.5 us
    ppermute x6, starting transfers between devices, passed_along(): return lax.ppermute(block, 'ctx', route)  16.9 us
    all_to_all x1, waiting for transfers between devices, shards(): got = lax.all_to_all(packed, 'ctx', 0, 0)  6.06 us
    all_to_all x1, starting transfers between devices, shards(): got = lax.all_to_all(packed, 'ctx', 0, 0)  5.78 us
    pallas_call x2, Pallas kernels, shards(): pl.pallas_call(functools.partial(local_kernel, part * count), in_specs=[V...  3.42 us
    ppermute x6, waiting for transfers between devices, passed_along(): return lax.ppermute(block, 'ctx', route)  3 us
    unnamed x12, local copies, waits for them, and re-layouts  2.06 us
    pallas_call x4, Pallas kernels, shards(): pl.pallas_call(functools.partial(message_kernel, part * count, streams),...  1.74 us
  transfers between devices with their start and end apart: 7, of which 3 were waited for; matrix products, arithmetic and copies ran while one was open for 0% of the time, Pallas kernels for 32%

profile of v9, /device:TPU:0, one launch (start us, length us, event | category | flops | bytes accessed | tf_op | source)
XLA Modules:
  0.0 60.3 jit_solution(15347228681428751451)
XLA Ops:
  0.6 0.9 %slice.26 = bf16[3,8,2048]{2,1,0:T(8,128)(2,1)S(1)} slice(bf16[3,128,2048]{2,1,0:T(8,128)(2,1)} %refs_3_.7), slice={[0:3], [120:128], [0:2048]} | slice | bytes 196608 | tf_op jit(solution)/shard_map/slice | solution.py:378
  1.5 0.7 %convert_bitcast_fusion = bf16[1,1,128]{2,1,0:T(2,128)(2,1)S(1)} fusion(s32[128]{0:T(128)} %param.9), kind=kLoop, calls=%fused_computation | loop fusion | flops 128 | bytes 768 | tf_op jit(solution)/shard_map/reshape.24
  2.2 0.1 scatter.4
  2.3 4.8 %collective-permute-start = (bf16[3,8,2048]{2,1,0:T(8,128)(2,1)S(1)}, bf16[3,8,2048]{2,1,0:T(8,128)(2,1)S(1)}, u32[]{:S(2)}, u32[]{:S(2)}) collective-permute-start(bf16[3,8,2048]{2,1,0:T(8,128)(2,1)S(1)} %scatter.4), channel_id=1, source_target_pairs={{0,4},{4,8},{8,12},{12,16},{16,20},{20,24},{24,28},{1,5},{5,9},{9,... | collective-permute-start | bytes 294920 | tf_op jit(solution)/shard_map/ppermute | solution.py:27
  7.1 0.0 copy-start.2
  7.2 0.6 %copy-done.2 = s32[128]{0:T(128)S(1)} copy-done((s32[128]{0:T(128)S(1)}, s32[128]{0:T(128)}, u32[]{:S(2)}) %copy-start.2) | copy-done | bytes 536
  7.8 0.0 copy-start.1
  7.8 0.0 copy-start.3
  7.8 0.0 copy-start.4
  7.8 0.1 prepare.1
  7.9 0.8 %copy-done.1 = f32[3,2048,7]{1,2,0:T(8,128)S(1)} copy-done((f32[3,2048,7]{1,2,0:T(8,128)S(1)}, f32[3,2048,7]{1,2,0:T(8,128)}, u32[]{:S(2)}) %copy-start.1) | copy-done | bytes 172056
  8.7 0.0 copy-done.3
  8.7 0.6 %copy-done.4 = bf16[3,128,2048]{2,1,0:T(8,128)(2,1)S(1)} copy-done((bf16[3,128,2048]{2,1,0:T(8,128)(2,1)S(1)}, bf16[3,128,2048]{2,1,0:T(8,128)(2,1)}, u32[]{:S(2)}) %copy-start.4) | copy-done | bytes 1572888
  9.3 0.0 copy-start
  9.3 1.7 %local.2.local_ref.refs_7_ = f32[3,128,1024]{2,1,0:T(8,128)S(1)} custom-call(s32[1,128]{1,0:T(1,128)S(1)} %bitcast.16, bf16[768,128]{1,0:T(8,128)(2,1)S(1)} %get-tuple-element.49.delay_ref, f32[3,7,2048]{2,1,0:T(8,128)S(1)} %bitcast.5, bf16[3,128,2048]{2,1,0:T(8,128)(2,1)S(1)} %copy-done.4, s32[1,128]{1,0:T(1,128)S(1)} %bitcast.17), custom_call_target="tpu_custom_call" | custom-call | flops 2000000000 | bytes 4000000 | tf_op jit(solution)/shard_map/local/pallas_call | solution.py:396
  11.1 0.0 collective-permute-done.edge_ref.refs_5_
  11.1 0.0 copy-done
  11.1 0.4 message.4
  11.5 3.5 %collective-permute-start.4 = (bf16[128,1024]{1,0:T(8,128)(2,1)S(1)}, bf16[128,1024]{1,0:T(8,128)(2,1)S(1)}, u32[]{:S(2)}, u32[]{:S(2)}) collective-permute-start(bf16[128,1024]{1,0:T(8,128)(2,1)S(1)} %get-tuple-element.50._), channel_id=1, source_target_pairs={{0,4},{4,8},{8,12},{12,16},{16,20},{20,24},{24,28},{1,5},{5,9},{9,... | collective-permute-start | bytes 786440 | tf_op jit(solution)/shard_map/ppermute | solution.py:27
  15.0 0.4 message.5
  15.4 1.3 %collective-permute-start.3 = (bf16[128,1024]{1,0:T(8,128)(2,1)S(1)}, bf16[128,1024]{1,0:T(8,128)(2,1)S(1)}, u32[]{:S(2)}, u32[]{:S(2)}) collective-permute-start(bf16[128,1024]{1,0:T(8,128)(2,1)S(1)} %get-tuple-element.51._), channel_id=1, source_target_pairs={{4,0},{8,4},{12,8},{16,12},{20,16},{24,20},{28,24},{5,1},{9,5},{13... | collective-permute-start | bytes 786440 | tf_op jit(solution)/shard_map/ppermute | solution.py:27
  16.7 1.7 %local.3.local_ref.refs_7_ = f32[3,128,1024]{2,1,0:T(8,128)S(1)} custom-call(s32[1,128]{1,0:T(1,128)S(1)} %bitcast.21, bf16[768,128]{1,0:T(8,128)(2,1)S(1)} %get-tuple-element.49.delay_ref, f32[3,7,2048]{2,1,0:T(8,128)S(1)} %bitcast.8, bf16[3,128,2048]{2,1,0:T(8,128)(2,1)S(1)} %copy-done.4, bf16[128,1024]{1,0:T(8,128)(2,1)S(1)} %get-tuple-element.51._), custom_call_target="tpu_custom_call" | custom-call | flops 2000000000 | bytes 4000000 | tf_op jit(solution)/shard_map/local/pallas_call | solution.py:396
  18.5 0.4 message.6
  18.9 0.0 copy-start.5
  18.9 4.7 %collective-permute-start.2 = (bf16[128,1024]{1,0:T(8,128)(2,1)S(1)}, bf16[128,1024]{1,0:T(8,128)(2,1)S(1)}, u32[]{:S(2)}, u32[]{:S(2)}) collective-permute-start(bf16[128,1024]{1,0:T(8,128)(2,1)S(1)} %get-tuple-element.52._), channel_id=1, source_target_pairs={{0,4},{4,8},{8,12},{12,16},{16,20},{20,24},{24,28},{1,5},{5,9},{9,... | collective-permute-start | bytes 786440 | tf_op jit(solution)/shard_map/ppermute | solution.py:27
  23.6 0.4 message.7
  24.0 1.3 %collective-permute-start.1 = (bf16[128,1024]{1,0:T(8,128)(2,1)S(1)}, bf16[128,1024]{1,0:T(8,128)(2,1)S(1)}, u32[]{:S(2)}, u32[]{:S(2)}) collective-permute-start(bf16[128,1024]{1,0:T(8,128)(2,1)S(1)} %get-tuple-element.55), channel_id=1, source_target_pairs={{4,0},{8,4},{12,8},{16,12},{20,16},{24,20},{28,24},{5,1},{9,5},{13... | collective-permute-start | bytes 786440 | tf_op jit(solution)/shard_map/ppermute | solution.py:27
  25.3 1.5 %collective-permute-done.4.refs_10_ = bf16[128,1024]{1,0:T(8,128)(2,1)S(1)} collective-permute-done((bf16[128,1024]{1,0:T(8,128)(2,1)S(1)}, bf16[128,1024]{1,0:T(8,128)(2,1)S(1)}, u32[]{:S(2)}, u32[]{:S(2)}) %collective-permute-start.4) | collective-permute-done | bytes 262176 | tf_op jit(solution)/shard_map/ppermute | solution.py:27
  26.8 0.0 copy-done.5
  26.8 5.1 %query.2 = (bf16[128,2048]{1,0:T(8,128)(2,1)}, bf16[3,128,2048]{2,1,0:T(8,128)(2,1)}, f32[3,8,2048]{2,1,0:T(8,128)S(1)}, bf16[3,8,2048]{2,1,0:T(8,128)(2,1)S(1)}, bf16[8,32,256]{2,1,0:T(8,128)(2,1)}) custom-call(s32[1,128]{1,0:T(1,128)S(1)} %bitcast.25, f32[3,7,2048]{2,1,0:T(8,128)S(1)} %bitcast.11, bf16[768,128]{1,0:T(8,128)(2,1)S(1)} %get-tuple-element.48.refs_2_, ...), custom_call_target="tpu_custom_call" | custom-call | flops 4000000000 | bytes 4000000 | tf_op jit(solution)/shard_map/query/pallas_call | solution.py:485
  31.9 0.0 collective-permute-done.3.refs_10_
  32.0 3.6 %pair.2 = (bf16[128,2048]{1,0:T(8,128)(2,1)}, bf16[3,128,2048]{2,1,0:T(8,128)(2,1)}, f32[3,8,2048]{2,1,0:T(8,128)S(1)}, bf16[3,8,2048]{2,1,0:T(8,128)(2,1)S(1)}, bf16[8,32,256]{2,1,0:T(8,128)(2,1)}) custom-call(s32[1,128]{1,0:T(1,128)S(1)} %bitcast.26, ...), custom_call_target="tpu_custom_call", output_to_operand_aliasing={{0}: (11, {}), {1}: (12, {}), {2}: (13, {}), {3}: (14, {}),... | custom-call | flops 4000000000 | bytes 4000000 | tf_op jit(solution)/shard_map/pair/pallas_call | solution.py:485
  35.6 1.5 %collective-permute-done.2.refs_10_ = bf16[128,1024]{1,0:T(8,128)(2,1)S(1)} collective-permute-done((bf16[128,1024]{1,0:T(8,128)(2,1)S(1)}, bf16[128,1024]{1,0:T(8,128)(2,1)S(1)}, u32[]{:S(2)}, u32[]{:S(2)}) %collective-permute-start.2) | collective-permute-done | bytes 262176 | tf_op jit(solution)/shard_map/ppermute | solution.py:27
  37.1 5.1 %query.3 = (bf16[128,2048]{1,0:T(8,128)(2,1)}, bf16[3,128,2048]{2,1,0:T(8,128)(2,1)}, f32[3,8,2048]{2,1,0:T(8,128)S(1)}, bf16[3,8,2048]{2,1,0:T(8,128)(2,1)S(1)}, bf16[8,32,256]{2,1,0:T(8,128)(2,1)}) custom-call(s32[1,128]{1,0:T(1,128)S(1)} %bitcast.27, ...), custom_call_target="tpu_custom_call", output_to_operand_aliasing={{0}: (11, {}), {1}: (12, {}), {2}: (13, {}), {3}: (14, {}),... | custom-call | flops 4000000000 | bytes 4000000 | tf_op jit(solution)/shard_map/query/pallas_call | solution.py:485
  42.2 0.0 collective-permute-done.1.refs_10_
  42.2 3.6 %pair.3 = (bf16[128,2048]{1,0:T(8,128)(2,1)}, bf16[3,128,2048]{2,1,0:T(8,128)(2,1)}, f32[3,8,2048]{2,1,0:T(8,128)S(1)}, bf16[3,8,2048]{2,1,0:T(8,128)(2,1)S(1)}, bf16[8,32,256]{2,1,0:T(8,128)(2,1)}) custom-call(s32[1,128]{1,0:T(1,128)S(1)} %bitcast.28, ...), custom_call_target="tpu_custom_call", output_to_operand_aliasing={{0}: (11, {}), {1}: (12, {}), {2}: (13, {}), {3}: (14, {}),... | custom-call | flops 4000000000 | bytes 4000000 | tf_op jit(solution)/shard_map/pair/pallas_call | solution.py:485
  45.9 5.8 %all-to-all-start = ((bf16[8,32,256]{2,1,0:T(8,128)(2,1)}), bf16[8,32,256]{2,1,0:T(8,128)(2,1)S(1)}, u32[]{:S(2)}, u32[]{:S(2)}) async-start(bf16[8,32,256]{2,1,0:T(8,128)(2,1)} %get-tuple-element.77), calls=%async_computation | async-start | bytes 262144 | tf_op jit(solution)/shard_map/all_to_all | solution.py:501
  51.7 1.3 %collective-permute-start.5 = (bf16[3,8,2048]{2,1,0:T(8,128)(2,1)S(1)}, bf16[3,8,2048]{2,1,0:T(8,128)(2,1)S(1)}, u32[]{:S(2)}, u32[]{:S(2)}) collective-permute-start(bf16[3,8,2048]{2,1,0:T(8,128)(2,1)S(1)} %get-tuple-element.75), channel_id=1, source_target_pairs={{4,0},{8,4},{12,8},{16,12},{20,16},{24,20},{28,24},{5,1},{9,5},{13... | collective-permute-start | bytes 294920 | tf_op jit(solution)/shard_map/ppermute | solution.py:27
  52.9 6.1 %all-to-all-done._.got_ref = bf16[8,32,256]{2,1,0:T(8,128)(2,1)S(1)} async-done(((bf16[8,32,256]{2,1,0:T(8,128)(2,1)}), bf16[8,32,256]{2,1,0:T(8,128)(2,1)S(1)}, u32[]{:S(2)}, u32[]{:S(2)}) %all-to-all-start) | async-done | bytes 131104 | tf_op jit(solution)/shard_map/all_to_all | solution.py:501
  59.0 0.6 %total.1 = (f32[16,128]{1,0:T(8,128)}, f32[3,7,256]{2,1,0:T(8,128)}) custom-call(bf16[8,32,256]{2,1,0:T(8,128)(2,1)S(1)} %all-to-all-done._.got_ref), custom_call_target="tpu_custom_call" | custom-call | flops 1000000 | bytes 200000 | tf_op jit(solution)/shard_map/total/pallas_call | solution.py:502
  59.6 0.0 collective-permute-done.5.part_ref
  59.6 0.7 %last_rows.1 = bf16[3,128,2048]{2,1,0:T(8,128)(2,1)} custom-call(f32[3,8,2048]{2,1,0:T(8,128)S(1)} %get-tuple-element.74.tail_ref, bf16[3,8,2048]{2,1,0:T(8,128)(2,1)S(1)} %collective-permute-done.5.part_ref, bf16[3,128,2048]{2,1,0:T(8,128)(2,1)} %get-tuple-element.76.qg_in, ...), custom_call_target="tpu_custom_call", output_to_operand_aliasing={{}: (2, {})} | custom-call | flops 100000 | bytes 200000 | tf_op jit(solution)/shard_map/last_rows/pallas_call | solution.py:525
Async XLA Ops:
  2.3 8.8 %collective-permute-start = (bf16[3,8,2048]{2,1,0:T(8,128)(2,1)S(1)}, bf16[3,8,2048]{2,1,0:T(8,128)(2,1)S(1)}, u32[]{:S(2)}, u32[]{:S(2)}) collective-permute-start(bf16[3,8,2048]{2,1,0:T(8,128)(2,1)S(1)} %scatter.4), channel_id=1, source_target_pairs={{0,4},{4,8},{8,12},{12,16},{16,20},{20,24},{24,28},{1,5},{5,9},{9,... | collective-permute-start | bytes 294920 | tf_op jit(solution)/shard_map/ppermute | solution.py:27
  7.1 0.7 %copy-start.2 = (s32[128]{0:T(128)S(1)}, s32[128]{0:T(128)}, u32[]{:S(2)}) copy-start(s32[128]{0:T(128)} %param.9) | copy-start | bytes 1540
  7.8 0.9 %copy-start.1 = (f32[3,2048,7]{1,2,0:T(8,128)S(1)}, f32[3,2048,7]{1,2,0:T(8,128)}, u32[]{:S(2)}) copy-start(f32[3,2048,7]{1,2,0:T(8,128)} %param.10) | copy-start | bytes 516100
  7.8 0.9 %copy-start.3 = (s32[128]{0:T(128)S(1)}, s32[128]{0:T(128)}, u32[]{:S(2)}) copy-start(s32[128]{0:T(128)} %param.9) | copy-start | bytes 1540
  7.8 1.5 %copy-start.4 = (bf16[3,128,2048]{2,1,0:T(8,128)(2,1)S(1)}, bf16[3,128,2048]{2,1,0:T(8,128)(2,1)}, u32[]{:S(2)}) copy-start(bf16[3,128,2048]{2,1,0:T(8,128)(2,1)} %refs_3_.7) | copy-start | bytes 4718596
  9.3 1.7 %copy-start = (bf16[128,2048]{1,0:T(8,128)(2,1)S(1)}, bf16[128,2048]{1,0:T(8,128)(2,1)}, u32[]{:S(2)}) copy-start(bf16[128,2048]{1,0:T(8,128)(2,1)} %refs_4_.7) | copy-start | bytes 1572868
  11.5 15.3 %collective-permute-start.4 = (bf16[128,1024]{1,0:T(8,128)(2,1)S(1)}, bf16[128,1024]{1,0:T(8,128)(2,1)S(1)}, u32[]{:S(2)}, u32[]{:S(2)}) collective-permute-start(bf16[128,1024]{1,0:T(8,128)(2,1)S(1)} %get-tuple-element.50._), channel_id=1, source_target_pairs={{0,4},{4,8},{8,12},{12,16},{16,20},{20,24},{24,28},{1,5},{5,9},{9,... | collective-permute-start | bytes 786440 | tf_op jit(solution)/shard_map/ppermute | solution.py:27
  15.4 16.5 %collective-permute-start.3 = (bf16[128,1024]{1,0:T(8,128)(2,1)S(1)}, bf16[128,1024]{1,0:T(8,128)(2,1)S(1)}, u32[]{:S(2)}, u32[]{:S(2)}) collective-permute-start(bf16[128,1024]{1,0:T(8,128)(2,1)S(1)} %get-tuple-element.51._), channel_id=1, source_target_pairs={{4,0},{8,4},{12,8},{16,12},{20,16},{24,20},{28,24},{5,1},{9,5},{13... | collective-permute-start | bytes 786440 | tf_op jit(solution)/shard_map/ppermute | solution.py:27
  18.9 7.9 %copy-start.5 = (f32[128,128]{1,0:T(8,128)S(1)}, f32[128,128]{1,0:T(8,128)}, u32[]{:S(2)}) copy-start(f32[128,128]{1,0:T(8,128)} %refs_6_.7) | copy-start | bytes 196612
  18.9 18.2 %collective-permute-start.2 = (bf16[128,1024]{1,0:T(8,128)(2,1)S(1)}, bf16[128,1024]{1,0:T(8,128)(2,1)S(1)}, u32[]{:S(2)}, u32[]{:S(2)}) collective-permute-start(bf16[128,1024]{1,0:T(8,128)(2,1)S(1)} %get-tuple-element.52._), channel_id=1, source_target_pairs={{0,4},{4,8},{8,12},{12,16},{16,20},{20,24},{24,28},{1,5},{5,9},{9,... | collective-permute-start | bytes 786440 | tf_op jit(solution)/shard_map/ppermute | solution.py:27
  24.0 18.2 %collective-permute-start.1 = (bf16[128,1024]{1,0:T(8,128)(2,1)S(1)}, bf16[128,1024]{1,0:T(8,128)(2,1)S(1)}, u32[]{:S(2)}, u32[]{:S(2)}) collective-permute-start(bf16[128,1024]{1,0:T(8,128)(2,1)S(1)} %get-tuple-element.55), channel_id=1, source_target_pairs={{4,0},{8,4},{12,8},{16,12},{20,16},{24,20},{28,24},{5,1},{9,5},{13... | collective-permute-start | bytes 786440 | tf_op jit(solution)/shard_map/ppermute | solution.py:27
  45.9 13.1 %all-to-all-start = ((bf16[8,32,256]{2,1,0:T(8,128)(2,1)}), bf16[8,32,256]{2,1,0:T(8,128)(2,1)S(1)}, u32[]{:S(2)}, u32[]{:S(2)}) async-start(bf16[8,32,256]{2,1,0:T(8,128)(2,1)} %get-tuple-element.77), calls=%async_computation | async-start | bytes 262144 | tf_op jit(solution)/shard_map/all_to_all | solution.py:501
  51.7 8.0 %collective-permute-start.5 = (bf16[3,8,2048]{2,1,0:T(8,128)(2,1)S(1)}, bf16[3,8,2048]{2,1,0:T(8,128)(2,1)S(1)}, u32[]{:S(2)}, u32[]{:S(2)}) collective-permute-start(bf16[3,8,2048]{2,1,0:T(8,128)(2,1)S(1)} %get-tuple-element.75), channel_id=1, source_target_pairs={{4,0},{8,4},{12,8},{16,12},{20,16},{24,20},{28,24},{5,1},{9,5},{13... | collective-permute-start | bytes 294920 | tf_op jit(solution)/shard_map/ppermute | solution.py:27

commit v10 on v9

--- a/solution.py
+++ b/solution.py
@@ -72,7 +72,7 @@
         for copy in loads(p):
             copy.start()
 
-    def one_step(p, carry):
+    def one_step(p):
         near = lane_range(p * LANES, LANES)
         for copy in loads(p):
             copy.wait()
@@ -84,9 +84,9 @@
             for t in range(1, taps):
                 acc = acc + w[t : t + 1] * moved[(t - 1) * rows : t * rows]
             feat_ref[i, :, near] = acc
-        return carry
-
-    lax.fori_loop(0, steps, one_step, 0)
+
+    for p in range(steps):
+        one_step(p)
 
 
 def message_kernel(first, streams, ids_ref, edge_ref, sf_ref, cot_ref, local_ref, _,
@@ -100,7 +100,7 @@
         edge_shift[(t - 1) * EDGE : t * EDGE] = ones_where((lag == t) & (before == head_ids))
     id_wide = jnp.concatenate([ids_ref[...].astype(F32)] * (LANES // rows), 1)
 
-    def one_step(p, carry):
+    def one_step(p):
         near = lane_range(p * LANES, LANES)
         cols = lane_range(first + p * LANES, LANES)
         feats = []
@@ -120,27 +120,21 @@
             sent_ref[:, near] = jnp.where(last, jnp.broadcast_to(id_wide, g.shape), g).astype(BF16)
         else:
             sent_ref[:, near] = (feats[0] * feats[1]).astype(BF16)
-        return carry
-
-    lax.fori_loop(0, sent_ref.shape[1] // LANES, one_step, 0)
+
+    for p in range(sent_ref.shape[1] // LANES):
+        one_step(p)
 
 
 def run_steps(parts, steps):
-    def start(p, carry):
+    for p in range(steps):
         for one_step, copies in parts:
             one_step(p)
             for copy in copies(p):
                 copy.start()
-        return carry
-
-    def drain(p, carry):
+    for p in range(steps):
         for _, copies in parts:
             for copy in copies(p):
                 copy.wait()
-        return carry
-
-    lax.fori_loop(0, steps, start, 0)
-    lax.fori_loop(0, steps, drain, 0)
 
 
 def joined(head, local):

time: 60.7 us -> 60.7 us (level)
    pallas_call x4, Pallas kernels: 1.74 us -> 1.02 us  [shards(): pl.pallas_call(functools.partial(message_kernel, part * count, streams),...]
where the time goes in v10:
time: 60.7 us; the launch traced here: 60.3 us
  Pallas kernels  23.5 us (39%)
  starting transfers between devices  22.7 us (37%)
  waiting for transfers between devices  9.47 us (16%)
  local copies, waits for them, and re-layouts  3.04 us (5%)
  between operations  0.97 us (2%)
  other arithmetic  0.66 us (1%)
    pallas_call x4, Pallas kernels, shards(): pl.pallas_call(functools.partial(mixer_kernel, query_first, pair_first, f...  17.5 us
    ppermute x6, starting transfers between devices, passed_along(): return lax.ppermute(block, 'ctx', route)  16.9 us
    all_to_all x1, waiting for transfers between devices, shards(): got = lax.all_to_all(packed, 'ctx', 0, 0)  6.06 us
    all_to_all x1, starting transfers between devices, shards(): got = lax.all_to_all(packed, 'ctx', 0, 0)  5.8 us
    pallas_call x2, Pallas kernels, shards(): pl.pallas_call(functools.partial(local_kernel, part * count), in_specs=[V...  3.51 us
    ppermute x6, waiting for transfers between devices, passed_along(): return lax.ppermute(block, 'ctx', route)  3.41 us
    unnamed x12, local copies, waits for them, and re-layouts  2.06 us
  transfers between devices with their start and end apart: 7, of which 3 were waited for; matrix products, arithmetic and copies ran while one was open for 0% of the time, Pallas kernels for 32%

profile of v10, /device:TPU:0, one launch (start us, length us, event | category | flops | bytes accessed | tf_op | source)
XLA Modules:
  0.0 60.3 jit_solution(5226585648181673976)
XLA Ops:
  0.6 0.9 %slice.26 = bf16[3,8,2048]{2,1,0:T(8,128)(2,1)S(1)} slice(bf16[3,128,2048]{2,1,0:T(8,128)(2,1)} %refs_3_.7), slice={[0:3], [120:128], [0:2048]} | slice | bytes 196608 | tf_op jit(solution)/shard_map/slice | solution.py:372
  1.5 0.7 %convert_bitcast_fusion = bf16[1,1,128]{2,1,0:T(2,128)(2,1)S(1)} fusion(s32[128]{0:T(128)} %param.9), kind=kLoop, calls=%fused_computation | loop fusion | flops 128 | bytes 768 | tf_op jit(solution)/shard_map/reshape.24
  2.2 0.1 scatter.4
  2.3 4.8 %collective-permute-start = (bf16[3,8,2048]{2,1,0:T(8,128)(2,1)S(1)}, bf16[3,8,2048]{2,1,0:T(8,128)(2,1)S(1)}, u32[]{:S(2)}, u32[]{:S(2)}) collective-permute-start(bf16[3,8,2048]{2,1,0:T(8,128)(2,1)S(1)} %scatter.4), channel_id=1, source_target_pairs={{0,4},{4,8},{8,12},{12,16},{16,20},{20,24},{24,28},{1,5},{5,9},{9,... | collective-permute-start | bytes 294920 | tf_op jit(solution)/shard_map/ppermute | solution.py:27
  7.1 0.0 copy-start.2
  7.2 0.6 %copy-done.2 = s32[128]{0:T(128)S(1)} copy-done((s32[128]{0:T(128)S(1)}, s32[128]{0:T(128)}, u32[]{:S(2)}) %copy-start.2) | copy-done | bytes 536
  7.8 0.0 copy-start.1
  7.8 0.0 copy-start.3
  7.8 0.0 copy-start.4
  7.8 0.1 prepare.1
  7.9 0.8 %copy-done.1 = f32[3,2048,7]{1,2,0:T(8,128)S(1)} copy-done((f32[3,2048,7]{1,2,0:T(8,128)S(1)}, f32[3,2048,7]{1,2,0:T(8,128)}, u32[]{:S(2)}) %copy-start.1) | copy-done | bytes 172056
  8.7 0.0 copy-done.3
  8.7 0.6 %copy-done.4 = bf16[3,128,2048]{2,1,0:T(8,128)(2,1)S(1)} copy-done((bf16[3,128,2048]{2,1,0:T(8,128)(2,1)S(1)}, bf16[3,128,2048]{2,1,0:T(8,128)(2,1)}, u32[]{:S(2)}) %copy-start.4) | copy-done | bytes 1572888
  9.3 0.0 copy-start
  9.3 1.7 %local.2.local_ref.refs_7_ = f32[3,128,1024]{2,1,0:T(8,128)S(1)} custom-call(s32[1,128]{1,0:T(1,128)S(1)} %bitcast.16, bf16[768,128]{1,0:T(8,128)(2,1)S(1)} %get-tuple-element.49.delay_ref, f32[3,7,2048]{2,1,0:T(8,128)S(1)} %bitcast.5, bf16[3,128,2048]{2,1,0:T(8,128)(2,1)S(1)} %copy-done.4, s32[1,128]{1,0:T(1,128)S(1)} %bitcast.17), custom_call_target="tpu_custom_call" | custom-call | flops 2000000000 | bytes 4000000 | tf_op jit(solution)/shard_map/local/pallas_call | solution.py:390
  11.1 0.0 collective-permute-done.edge_ref.refs_5_
  11.1 0.0 copy-done
  11.1 0.3 message.4
  11.4 3.5 %collective-permute-start.4 = (bf16[128,1024]{1,0:T(8,128)(2,1)S(1)}, bf16[128,1024]{1,0:T(8,128)(2,1)S(1)}, u32[]{:S(2)}, u32[]{:S(2)}) collective-permute-start(bf16[128,1024]{1,0:T(8,128)(2,1)S(1)} %get-tuple-element.50._), channel_id=1, source_target_pairs={{0,4},{4,8},{8,12},{12,16},{16,20},{20,24},{24,28},{1,5},{5,9},{9,... | collective-permute-start | bytes 786440 | tf_op jit(solution)/shard_map/ppermute | solution.py:27
  14.9 0.2 message.5
  15.1 1.3 %collective-permute-start.3 = (bf16[128,1024]{1,0:T(8,128)(2,1)S(1)}, bf16[128,1024]{1,0:T(8,128)(2,1)S(1)}, u32[]{:S(2)}, u32[]{:S(2)}) collective-permute-start(bf16[128,1024]{1,0:T(8,128)(2,1)S(1)} %get-tuple-element.51._), channel_id=1, source_target_pairs={{4,0},{8,4},{12,8},{16,12},{20,16},{24,20},{28,24},{5,1},{9,5},{13... | collective-permute-start | bytes 786440 | tf_op jit(solution)/shard_map/ppermute | solution.py:27
  16.4 1.8 %local.3.local_ref.refs_7_ = f32[3,128,1024]{2,1,0:T(8,128)S(1)} custom-call(s32[1,128]{1,0:T(1,128)S(1)} %bitcast.21, bf16[768,128]{1,0:T(8,128)(2,1)S(1)} %get-tuple-element.49.delay_ref, f32[3,7,2048]{2,1,0:T(8,128)S(1)} %bitcast.8, bf16[3,128,2048]{2,1,0:T(8,128)(2,1)S(1)} %copy-done.4, bf16[128,1024]{1,0:T(8,128)(2,1)S(1)} %get-tuple-element.51._), custom_call_target="tpu_custom_call" | custom-call | flops 2000000000 | bytes 4000000 | tf_op jit(solution)/shard_map/local/pallas_call | solution.py:390
  18.2 0.3 message.6
  18.4 0.0 copy-start.5
  18.5 4.7 %collective-permute-start.2 = (bf16[128,1024]{1,0:T(8,128)(2,1)S(1)}, bf16[128,1024]{1,0:T(8,128)(2,1)S(1)}, u32[]{:S(2)}, u32[]{:S(2)}) collective-permute-start(bf16[128,1024]{1,0:T(8,128)(2,1)S(1)} %get-tuple-element.52._), channel_id=1, source_target_pairs={{0,4},{4,8},{8,12},{12,16},{16,20},{20,24},{24,28},{1,5},{5,9},{9,... | collective-permute-start | bytes 786440 | tf_op jit(solution)/shard_map/ppermute | solution.py:27
  23.2 0.2 message.7
  23.4 1.3 %collective-permute-start.1 = (bf16[128,1024]{1,0:T(8,128)(2,1)S(1)}, bf16[128,1024]{1,0:T(8,128)(2,1)S(1)}, u32[]{:S(2)}, u32[]{:S(2)}) collective-permute-start(bf16[128,1024]{1,0:T(8,128)(2,1)S(1)} %get-tuple-element.55), channel_id=1, source_target_pairs={{4,0},{8,4},{12,8},{16,12},{20,16},{24,20},{28,24},{5,1},{9,5},{13... | collective-permute-start | bytes 786440 | tf_op jit(solution)/shard_map/ppermute | solution.py:27
  24.7 2.2 %collective-permute-done.4.refs_10_ = bf16[128,1024]{1,0:T(8,128)(2,1)S(1)} collective-permute-done((bf16[128,1024]{1,0:T(8,128)(2,1)S(1)}, bf16[128,1024]{1,0:T(8,128)(2,1)S(1)}, u32[]{:S(2)}, u32[]{:S(2)}) %collective-permute-start.4) | collective-permute-done | bytes 262176 | tf_op jit(solution)/shard_map/ppermute | solution.py:27
  26.9 0.0 copy-done.5
  26.9 5.4 %query.2 = (bf16[128,2048]{1,0:T(8,128)(2,1)}, bf16[3,128,2048]{2,1,0:T(8,128)(2,1)}, f32[3,8,2048]{2,1,0:T(8,128)S(1)}, bf16[3,8,2048]{2,1,0:T(8,128)(2,1)S(1)}, bf16[8,32,256]{2,1,0:T(8,128)(2,1)}) custom-call(s32[1,128]{1,0:T(1,128)S(1)} %bitcast.25, f32[3,7,2048]{2,1,0:T(8,128)S(1)} %bitcast.11, bf16[768,128]{1,0:T(8,128)(2,1)S(1)} %get-tuple-element.48.refs_2_, ...), custom_call_target="tpu_custom_call" | custom-call | flops 4000000000 | bytes 4000000 | tf_op jit(solution)/shard_map/query/pallas_call | solution.py:479
  32.3 0.0 collective-permute-done.3.refs_10_
  32.3 3.5 %pair.2 = (bf16[128,2048]{1,0:T(8,128)(2,1)}, bf16[3,128,2048]{2,1,0:T(8,128)(2,1)}, f32[3,8,2048]{2,1,0:T(8,128)S(1)}, bf16[3,8,2048]{2,1,0:T(8,128)(2,1)S(1)}, bf16[8,32,256]{2,1,0:T(8,128)(2,1)}) custom-call(s32[1,128]{1,0:T(1,128)S(1)} %bitcast.26, ...), custom_call_target="tpu_custom_call", output_to_operand_aliasing={{0}: (11, {}), {1}: (12, {}), {2}: (13, {}), {3}: (14, {}),... | custom-call | flops 4000000000 | bytes 4000000 | tf_op jit(solution)/shard_map/pair/pallas_call | solution.py:479
  35.8 1.2 %collective-permute-done.2.refs_10_ = bf16[128,1024]{1,0:T(8,128)(2,1)S(1)} collective-permute-done((bf16[128,1024]{1,0:T(8,128)(2,1)S(1)}, bf16[128,1024]{1,0:T(8,128)(2,1)S(1)}, u32[]{:S(2)}, u32[]{:S(2)}) %collective-permute-start.2) | collective-permute-done | bytes 262176 | tf_op jit(solution)/shard_map/ppermute | solution.py:27
  37.0 5.2 %query.3 = (bf16[128,2048]{1,0:T(8,128)(2,1)}, bf16[3,128,2048]{2,1,0:T(8,128)(2,1)}, f32[3,8,2048]{2,1,0:T(8,128)S(1)}, bf16[3,8,2048]{2,1,0:T(8,128)(2,1)S(1)}, bf16[8,32,256]{2,1,0:T(8,128)(2,1)}) custom-call(s32[1,128]{1,0:T(1,128)S(1)} %bitcast.27, ...), custom_call_target="tpu_custom_call", output_to_operand_aliasing={{0}: (11, {}), {1}: (12, {}), {2}: (13, {}), {3}: (14, {}),... | custom-call | flops 4000000000 | bytes 4000000 | tf_op jit(solution)/shard_map/query/pallas_call | solution.py:479
  42.2 0.0 collective-permute-done.1.refs_10_
  42.2 3.5 %pair.3 = (bf16[128,2048]{1,0:T(8,128)(2,1)}, bf16[3,128,2048]{2,1,0:T(8,128)(2,1)}, f32[3,8,2048]{2,1,0:T(8,128)S(1)}, bf16[3,8,2048]{2,1,0:T(8,128)(2,1)S(1)}, bf16[8,32,256]{2,1,0:T(8,128)(2,1)}) custom-call(s32[1,128]{1,0:T(1,128)S(1)} %bitcast.28, ...), custom_call_target="tpu_custom_call", output_to_operand_aliasing={{0}: (11, {}), {1}: (12, {}), {2}: (13, {}), {3}: (14, {}),... | custom-call | flops 4000000000 | bytes 4000000 | tf_op jit(solution)/shard_map/pair/pallas_call | solution.py:479
  45.7 5.8 %all-to-all-start = ((bf16[8,32,256]{2,1,0:T(8,128)(2,1)}), bf16[8,32,256]{2,1,0:T(8,128)(2,1)S(1)}, u32[]{:S(2)}, u32[]{:S(2)}) async-start(bf16[8,32,256]{2,1,0:T(8,128)(2,1)} %get-tuple-element.77), calls=%async_computation | async-start | bytes 262144 | tf_op jit(solution)/shard_map/all_to_all | solution.py:495
  51.5 1.3 %collective-permute-start.5 = (bf16[3,8,2048]{2,1,0:T(8,128)(2,1)S(1)}, bf16[3,8,2048]{2,1,0:T(8,128)(2,1)S(1)}, u32[]{:S(2)}, u32[]{:S(2)}) collective-permute-start(bf16[3,8,2048]{2,1,0:T(8,128)(2,1)S(1)} %get-tuple-element.75), channel_id=1, source_target_pairs={{4,0},{8,4},{12,8},{16,12},{20,16},{24,20},{28,24},{5,1},{9,5},{13... | collective-permute-start | bytes 294920 | tf_op jit(solution)/shard_map/ppermute | solution.py:27
  52.8 6.1 %all-to-all-done._.got_ref = bf16[8,32,256]{2,1,0:T(8,128)(2,1)S(1)} async-done(((bf16[8,32,256]{2,1,0:T(8,128)(2,1)}), bf16[8,32,256]{2,1,0:T(8,128)(2,1)S(1)}, u32[]{:S(2)}, u32[]{:S(2)}) %all-to-all-start) | async-done | bytes 131104 | tf_op jit(solution)/shard_map/all_to_all | solution.py:495
  58.8 0.6 %total.1 = (f32[16,128]{1,0:T(8,128)}, f32[3,7,256]{2,1,0:T(8,128)}) custom-call(bf16[8,32,256]{2,1,0:T(8,128)(2,1)S(1)} %all-to-all-done._.got_ref), custom_call_target="tpu_custom_call" | custom-call | flops 1000000 | bytes 200000 | tf_op jit(solution)/shard_map/total/pallas_call | solution.py:496
  59.4 0.0 collective-permute-done.5.part_ref
  59.4 0.7 %last_rows.1 = bf16[3,128,2048]{2,1,0:T(8,128)(2,1)} custom-call(f32[3,8,2048]{2,1,0:T(8,128)S(1)} %get-tuple-element.74.tail_ref, bf16[3,8,2048]{2,1,0:T(8,128)(2,1)S(1)} %collective-permute-done.5.part_ref, bf16[3,128,2048]{2,1,0:T(8,128)(2,1)} %get-tuple-element.76.qg_in, ...), custom_call_target="tpu_custom_call", output_to_operand_aliasing={{}: (2, {})} | custom-call | flops 100000 | bytes 200000 | tf_op jit(solution)/shard_map/last_rows/pallas_call | solution.py:519
Async XLA Ops:
  2.3 8.8 %collective-permute-start = (bf16[3,8,2048]{2,1,0:T(8,128)(2,1)S(1)}, bf16[3,8,2048]{2,1,0:T(8,128)(2,1)S(1)}, u32[]{:S(2)}, u32[]{:S(2)}) collective-permute-start(bf16[3,8,2048]{2,1,0:T(8,128)(2,1)S(1)} %scatter.4), channel_id=1, source_target_pairs={{0,4},{4,8},{8,12},{12,16},{16,20},{20,24},{24,28},{1,5},{5,9},{9,... | collective-permute-start | bytes 294920 | tf_op jit(solution)/shard_map/ppermute | solution.py:27
  7.1 0.7 %copy-start.2 = (s32[128]{0:T(128)S(1)}, s32[128]{0:T(128)}, u32[]{:S(2)}) copy-start(s32[128]{0:T(128)} %param.9) | copy-start | bytes 1540
  7.8 0.9 %copy-start.1 = (f32[3,2048,7]{1,2,0:T(8,128)S(1)}, f32[3,2048,7]{1,2,0:T(8,128)}, u32[]{:S(2)}) copy-start(f32[3,2048,7]{1,2,0:T(8,128)} %param.10) | copy-start | bytes 516100
  7.8 0.9 %copy-start.3 = (s32[128]{0:T(128)S(1)}, s32[128]{0:T(128)}, u32[]{:S(2)}) copy-start(s32[128]{0:T(128)} %param.9) | copy-start | bytes 1540
  7.8 1.5 %copy-start.4 = (bf16[3,128,2048]{2,1,0:T(8,128)(2,1)S(1)}, bf16[3,128,2048]{2,1,0:T(8,128)(2,1)}, u32[]{:S(2)}) copy-start(bf16[3,128,2048]{2,1,0:T(8,128)(2,1)} %refs_3_.7) | copy-start | bytes 4718596
  9.3 1.8 %copy-start = (bf16[128,2048]{1,0:T(8,128)(2,1)S(1)}, bf16[128,2048]{1,0:T(8,128)(2,1)}, u32[]{:S(2)}) copy-start(bf16[128,2048]{1,0:T(8,128)(2,1)} %refs_4_.7) | copy-start | bytes 1572868
  11.4 15.5 %collective-permute-start.4 = (bf16[128,1024]{1,0:T(8,128)(2,1)S(1)}, bf16[128,1024]{1,0:T(8,128)(2,1)S(1)}, u32[]{:S(2)}, u32[]{:S(2)}) collective-permute-start(bf16[128,1024]{1,0:T(8,128)(2,1)S(1)} %get-tuple-element.50._), channel_id=1, source_target_pairs={{0,4},{4,8},{8,12},{12,16},{16,20},{20,24},{24,28},{1,5},{5,9},{9,... | collective-permute-start | bytes 786440 | tf_op jit(solution)/shard_map/ppermute | solution.py:27
  15.1 17.2 %collective-permute-start.3 = (bf16[128,1024]{1,0:T(8,128)(2,1)S(1)}, bf16[128,1024]{1,0:T(8,128)(2,1)S(1)}, u32[]{:S(2)}, u32[]{:S(2)}) collective-permute-start(bf16[128,1024]{1,0:T(8,128)(2,1)S(1)} %get-tuple-element.51._), channel_id=1, source_target_pairs={{4,0},{8,4},{12,8},{16,12},{20,16},{24,20},{28,24},{5,1},{9,5},{13... | collective-permute-start | bytes 786440 | tf_op jit(solution)/shard_map/ppermute | solution.py:27
  18.4 8.5 %copy-start.5 = (f32[128,128]{1,0:T(8,128)S(1)}, f32[128,128]{1,0:T(8,128)}, u32[]{:S(2)}) copy-start(f32[128,128]{1,0:T(8,128)} %refs_6_.7) | copy-start | bytes 196612
  18.5 18.5 %collective-permute-start.2 = (bf16[128,1024]{1,0:T(8,128)(2,1)S(1)}, bf16[128,1024]{1,0:T(8,128)(2,1)S(1)}, u32[]{:S(2)}, u32[]{:S(2)}) collective-permute-start(bf16[128,1024]{1,0:T(8,128)(2,1)S(1)} %get-tuple-element.52._), channel_id=1, source_target_pairs={{0,4},{4,8},{8,12},{12,16},{16,20},{20,24},{24,28},{1,5},{5,9},{9,... | collective-permute-start | bytes 786440 | tf_op jit(solution)/shard_map/ppermute | solution.py:27
  23.4 18.8 %collective-permute-start.1 = (bf16[128,1024]{1,0:T(8,128)(2,1)S(1)}, bf16[128,1024]{1,0:T(8,128)(2,1)S(1)}, u32[]{:S(2)}, u32[]{:S(2)}) collective-permute-start(bf16[128,1024]{1,0:T(8,128)(2,1)S(1)} %get-tuple-element.55), channel_id=1, source_target_pairs={{4,0},{8,4},{12,8},{16,12},{20,16},{24,20},{28,24},{5,1},{9,5},{13... | collective-permute-start | bytes 786440 | tf_op jit(solution)/shard_map/ppermute | solution.py:27
  45.7 13.1 %all-to-all-start = ((bf16[8,32,256]{2,1,0:T(8,128)(2,1)}), bf16[8,32,256]{2,1,0:T(8,128)(2,1)S(1)}, u32[]{:S(2)}, u32[]{:S(2)}) async-start(bf16[8,32,256]{2,1,0:T(8,128)(2,1)} %get-tuple-element.77), calls=%async_computation | async-start | bytes 262144 | tf_op jit(solution)/shard_map/all_to_all | solution.py:495
  51.5 8.0 %collective-permute-start.5 = (bf16[3,8,2048]{2,1,0:T(8,128)(2,1)S(1)}, bf16[3,8,2048]{2,1,0:T(8,128)(2,1)S(1)}, u32[]{:S(2)}, u32[]{:S(2)}) collective-permute-start(bf16[3,8,2048]{2,1,0:T(8,128)(2,1)S(1)} %get-tuple-element.75), channel_id=1, source_target_pairs={{4,0},{8,4},{12,8},{16,12},{20,16},{24,20},{28,24},{5,1},{9,5},{13... | collective-permute-start | bytes 294920 | tf_op jit(solution)/shard_map/ppermute | solution.py:27

commit v11 on v10

--- a/solution.py
+++ b/solution.py
@@ -46,7 +46,7 @@
 def prepare_kernel(ids_ref, delay_ref, advance_ref):
     rows = delay_ref.shape[1]
     taps = delay_ref.shape[0] // rows + 1
-    id_row = jnp.broadcast_to(ids_ref[...], (rows, rows)).astype(F32)
+    id_row = jnp.broadcast_to(ids_ref[...].astype(F32), (rows, rows))
     same = id_row == id_row.T
     lag = iota2((rows, rows), 0) - iota2((rows, rows), 1)
     for t in range(1, taps):
@@ -54,7 +54,7 @@
         advance_ref[(t - 1) * rows : t * rows] = ones_where((lag == -t) & same).astype(BF16)
 
 
-def local_kernel(first, ids_ref, delay_ref, sf_hbm, x_hbm, _, feat_ref, sf_ref, x_ref, sems):
+def local_kernel(first, delay_ref, sf_hbm, x_hbm, _, feat_ref, sf_ref, x_ref, sems):
     rows = x_ref.shape[1]
     taps = sf_ref.shape[1]
     steps = feat_ref.shape[2] // LANES
@@ -93,7 +93,7 @@
                    head_ref, sent_ref, edge_shift):
     rows = local_ref.shape[1]
     taps = sf_ref.shape[1]
-    head_ids = jnp.broadcast_to(ids_ref[...], (rows, rows)).astype(F32).T[0:EDGE]
+    head_ids = jnp.broadcast_to(ids_ref[...].astype(F32), (rows, rows)).T[0:EDGE]
     before = pltpu.roll(jnp.broadcast_to(edge_ref[0, 0:1, 0:rows].astype(F32), (EDGE, rows)), EDGE, 1)
     lag = iota2((EDGE, rows), 0) + EDGE - iota2((EDGE, rows), 1)
     for t in range(1, taps):
@@ -144,7 +144,7 @@
 def edge_shifts(ids_ref, edge_ref, edge_shift):
     rows = edge_shift.shape[1]
     taps = edge_shift.shape[0] // EDGE + 1
-    id_head = jnp.broadcast_to(ids_ref[...], (EDGE, rows)).astype(F32)
+    id_head = jnp.broadcast_to(ids_ref[...].astype(F32), (EDGE, rows))
     prev = jnp.broadcast_to(edge_ref[0, 0:1, 0:rows].astype(F32), (rows, rows)).T
     lag = iota2((EDGE, rows), 1) + EDGE - iota2((EDGE, rows), 0)
     same = prev[rows - EDGE :] == id_head
@@ -182,7 +182,7 @@
     per = half // width
     lag = iota2((rows, rows), 0) - iota2((rows, rows), 1)
     mirror = ones_where(iota2((rows, rows), 0) + iota2((rows, rows), 1) == rows - 1).astype(BF16)
-    id_row = jnp.broadcast_to(ids_ref[...], (rows, rows)).astype(F32)
+    id_row = jnp.broadcast_to(ids_ref[...].astype(F32), (rows, rows))
     id_col = id_row.T
     prev_row = jnp.broadcast_to(edge_ref[0, 0:1, 0:rows].astype(F32), (rows, rows))
     same = id_row == id_col
@@ -262,7 +262,7 @@
     rows = x_ref.shape[1]
     width = x_ref.shape[2] // lfr_ref.shape[0]
     lag = iota2((rows, rows), 0) - iota2((rows, rows), 1)
-    id_row = jnp.broadcast_to(ids_ref[...], (rows, rows)).astype(F32)
+    id_row = jnp.broadcast_to(ids_ref[...].astype(F32), (rows, rows))
     next_col = jnp.broadcast_to(gn_ref[rows - 1 : rows, 0:rows].astype(F32), (rows, rows)).T
     backward = ones_where((iota2((rows, rows), 0) + iota2((rows, rows), 1)) % rows == 0)
     lfr_ref[...] = dot(lf_ref[...].astype(BF16), backward.astype(BF16))
@@ -365,12 +365,12 @@
     step_groups = LANES * groups // chans
     params = pltpu.CompilerParams(vmem_limit_bytes=24 << 20)
 
-    ids = doc_ids.reshape(1, rows)
+    ids = doc_ids.astype(BF16).reshape(1, rows)
     sf = jnp.transpose(short_filter, (0, 2, 1))
 
     small = pltpu.CompilerParams(vmem_limit_bytes=8 << 20)
     edge = qkv[:, rows - EDGE :, :]
-    edge = passed_along(edge.at[0, 0, :rows].set(doc_ids.astype(BF16)), 1)
+    edge = passed_along(edge.at[0, 0, :rows].set(ids[0]), 1)
 
     shifts = ((taps - 1) * rows, rows)
     delay, advance = pl.pallas_call(
@@ -389,7 +389,7 @@
     for part in range(PARTS):
         local = pl.pallas_call(
             functools.partial(local_kernel, part * count),
-            in_specs=[VMEM] * 2 + [HBM] * 2 + [ANY],
+            in_specs=[VMEM] + [HBM] * 2 + [ANY],
             out_specs=VMEM,
             out_shape=jax.ShapeDtypeStruct((3, rows, count), F32),
             scratch_shapes=[
@@ -400,7 +400,7 @@
             compiler_params=params,
             cost_estimate=pl.CostEstimate(flops=2_000_000_000, bytes_accessed=4_000_000, transcendentals=0),
             name="local",
-        )(ids, delay, sf, qkv, after)
+        )(delay, sf, qkv, after)
         made = [local]
         after = ids
         for streams, distance in (((1, 2), 1), ((0,), -1)):

time: 60.7 us -> 60 us (0.988)
  local copies, waits for them, and re-layouts: 3.04 us -> 2.41 us
    unnamed x12 -> x8, local copies, waits for them, and re-layouts: 2.06 us -> 1.38 us
where the time goes in v11:
time: 60 us; the launch traced here: 59.6 us
  Pallas kernels  23.4 us (39%)
  starting transfers between devices  22.9 us (38%)
  waiting for transfers between devices  9.28 us (15%)
  local copies, waits for them, and re-layouts  2.41 us (4%)
  between operations  0.98 us (2%)
  other arithmetic  0.66 us (1%)
    pallas_call x4, Pallas kernels, shards(): pl.pallas_call(functools.partial(mixer_kernel, query_first, pair_first, f...  17.5 us
    ppermute x6, starting transfers between devices, passed_along(): return lax.ppermute(block, 'ctx', route)  17.1 us
    all_to_all x1, waiting for transfers between devices, shards(): got = lax.all_to_all(packed, 'ctx', 0, 0)  6.06 us
    all_to_all x1, starting transfers between devices, shards(): got = lax.all_to_all(packed, 'ctx', 0, 0)  5.79 us
    pallas_call x2, Pallas kernels, shards(): pl.pallas_call(functools.partial(local_kernel, part * count), in_specs=[V...  3.44 us
    ppermute x6, waiting for transfers between devices, passed_along(): return lax.ppermute(block, 'ctx', route)  3.23 us
    unnamed x8, local copies, waits for them, and re-layouts  1.38 us
  transfers between devices with their start and end apart: 7, of which 3 were waited for; matrix products, arithmetic and copies ran while one was open for 0% of the time, Pallas kernels for 32%

profile of v11, /device:TPU:0, one launch (start us, length us, event | category | flops | bytes accessed | tf_op | source)
XLA Modules:
  0.0 59.6 jit_solution(7672908809261892844)
XLA Ops:
  0.6 0.7 %convert_bitcast_fusion = (bf16[1,1,128]{2,1,0:T(2,128)(2,1)S(1)}, bf16[1,128]{1,0:T(2,128)(2,1)S(1)}) fusion(s32[128]{0:T(128)} %param.9), kind=kLoop, calls=%fused_computation | loop fusion | flops 128 | bytes 1024 | tf_op jit(solution)/shard_map/reshape.24
  1.3 0.9 %slice.26 = bf16[3,8,2048]{2,1,0:T(8,128)(2,1)S(1)} slice(bf16[3,128,2048]{2,1,0:T(8,128)(2,1)} %refs_3_.7), slice={[0:3], [120:128], [0:2048]} | slice | bytes 196608 | tf_op jit(solution)/shard_map/slice | solution.py:372
  2.2 0.1 scatter.4
  2.3 4.8 %collective-permute-start = (bf16[3,8,2048]{2,1,0:T(8,128)(2,1)S(1)}, bf16[3,8,2048]{2,1,0:T(8,128)(2,1)S(1)}, u32[]{:S(2)}, u32[]{:S(2)}) collective-permute-start(bf16[3,8,2048]{2,1,0:T(8,128)(2,1)S(1)} %scatter.4), channel_id=1, source_target_pairs={{0,4},{4,8},{8,12},{12,16},{16,20},{20,24},{24,28},{1,5},{5,9},{9,... | collective-permute-start | bytes 294920 | tf_op jit(solution)/shard_map/ppermute | solution.py:27
  7.2 0.0 copy-start.1
  7.2 0.0 copy-start.2
  7.2 0.1 prepare.1
  7.4 0.8 %copy-done.1 = f32[3,2048,7]{1,2,0:T(8,128)S(1)} copy-done((f32[3,2048,7]{1,2,0:T(8,128)S(1)}, f32[3,2048,7]{1,2,0:T(8,128)}, u32[]{:S(2)}) %copy-start.1) | copy-done | bytes 172056
  8.1 0.6 %copy-done.2 = bf16[3,128,2048]{2,1,0:T(8,128)(2,1)S(1)} copy-done((bf16[3,128,2048]{2,1,0:T(8,128)(2,1)S(1)}, bf16[3,128,2048]{2,1,0:T(8,128)(2,1)}, u32[]{:S(2)}) %copy-start.2) | copy-done | bytes 1572888
  8.7 0.0 copy-start
  8.7 1.7 %local.2.local_ref.refs_7_ = f32[3,128,1024]{2,1,0:T(8,128)S(1)} custom-call(bf16[768,128]{1,0:T(8,128)(2,1)S(1)} %get-tuple-element.49.delay_ref, f32[3,7,2048]{2,1,0:T(8,128)S(1)} %bitcast.6, bf16[3,128,2048]{2,1,0:T(8,128)(2,1)S(1)} %copy-done.2, bf16[1,128]{1,0:T(2,128)(2,1)S(1)} %get-tuple-element.81.ids_ref._.refs_0_), custom_call_target="tpu_custom_call" | custom-call | flops 2000000000 | bytes 4000000 | tf_op jit(solution)/shard_map/local/pallas_call | solution.py:390
  10.4 0.0 collective-permute-done.edge_ref.refs_5_
  10.4 0.0 copy-done
  10.5 0.3 message.4
  10.7 3.5 %collective-permute-start.4 = (bf16[128,1024]{1,0:T(8,128)(2,1)S(1)}, bf16[128,1024]{1,0:T(8,128)(2,1)S(1)}, u32[]{:S(2)}, u32[]{:S(2)}) collective-permute-start(bf16[128,1024]{1,0:T(8,128)(2,1)S(1)} %get-tuple-element.50._), channel_id=1, source_target_pairs={{0,4},{4,8},{8,12},{12,16},{16,20},{20,24},{24,28},{1,5},{5,9},{9,... | collective-permute-start | bytes 786440 | tf_op jit(solution)/shard_map/ppermute | solution.py:27
  14.2 0.2 message.5
  14.4 1.3 %collective-permute-start.3 = (bf16[128,1024]{1,0:T(8,128)(2,1)S(1)}, bf16[128,1024]{1,0:T(8,128)(2,1)S(1)}, u32[]{:S(2)}, u32[]{:S(2)}) collective-permute-start(bf16[128,1024]{1,0:T(8,128)(2,1)S(1)} %get-tuple-element.51._), channel_id=1, source_target_pairs={{4,0},{8,4},{12,8},{16,12},{20,16},{24,20},{28,24},{5,1},{9,5},{13... | collective-permute-start | bytes 786440 | tf_op jit(solution)/shard_map/ppermute | solution.py:27
  15.7 1.7 %local.3.local_ref.refs_7_ = f32[3,128,1024]{2,1,0:T(8,128)S(1)} custom-call(bf16[768,128]{1,0:T(8,128)(2,1)S(1)} %get-tuple-element.49.delay_ref, f32[3,7,2048]{2,1,0:T(8,128)S(1)} %bitcast.9, bf16[3,128,2048]{2,1,0:T(8,128)(2,1)S(1)} %copy-done.2, bf16[128,1024]{1,0:T(8,128)(2,1)S(1)} %get-tuple-element.51._), custom_call_target="tpu_custom_call" | custom-call | flops 2000000000 | bytes 4000000 | tf_op jit(solution)/shard_map/local/pallas_call | solution.py:390
  17.5 0.3 message.6
  17.8 0.0 copy-start.3
  17.8 4.9 %collective-permute-start.2 = (bf16[128,1024]{1,0:T(8,128)(2,1)S(1)}, bf16[128,1024]{1,0:T(8,128)(2,1)S(1)}, u32[]{:S(2)}, u32[]{:S(2)}) collective-permute-start(bf16[128,1024]{1,0:T(8,128)(2,1)S(1)} %get-tuple-element.52._), channel_id=1, source_target_pairs={{0,4},{4,8},{8,12},{12,16},{16,20},{20,24},{24,28},{1,5},{5,9},{9,... | collective-permute-start | bytes 786440 | tf_op jit(solution)/shard_map/ppermute | solution.py:27
  22.7 0.2 message.7
  22.9 1.3 %collective-permute-start.1 = (bf16[128,1024]{1,0:T(8,128)(2,1)S(1)}, bf16[128,1024]{1,0:T(8,128)(2,1)S(1)}, u32[]{:S(2)}, u32[]{:S(2)}) collective-permute-start(bf16[128,1024]{1,0:T(8,128)(2,1)S(1)} %get-tuple-element.55), channel_id=1, source_target_pairs={{4,0},{8,4},{12,8},{16,12},{20,16},{24,20},{28,24},{5,1},{9,5},{13... | collective-permute-start | bytes 786440 | tf_op jit(solution)/shard_map/ppermute | solution.py:27
  24.2 2.1 %collective-permute-done.4.refs_10_ = bf16[128,1024]{1,0:T(8,128)(2,1)S(1)} collective-permute-done((bf16[128,1024]{1,0:T(8,128)(2,1)S(1)}, bf16[128,1024]{1,0:T(8,128)(2,1)S(1)}, u32[]{:S(2)}, u32[]{:S(2)}) %collective-permute-start.4) | collective-permute-done | bytes 262176 | tf_op jit(solution)/shard_map/ppermute | solution.py:27
  26.3 0.0 copy-done.3
  26.3 5.4 %query.2 = (bf16[128,2048]{1,0:T(8,128)(2,1)}, bf16[3,128,2048]{2,1,0:T(8,128)(2,1)}, f32[3,8,2048]{2,1,0:T(8,128)S(1)}, bf16[3,8,2048]{2,1,0:T(8,128)(2,1)S(1)}, bf16[8,32,256]{2,1,0:T(8,128)(2,1)}) custom-call(bf16[1,128]{1,0:T(2,128)(2,1)S(1)} %get-tuple-element.81.ids_ref._.refs_0_, f32[3,7,2048]{2,1,0:T(8,128)S(1)} %bitcast.12, ...), custom_call_target="tpu_custom_call" | custom-call | flops 4000000000 | bytes 4000000 | tf_op jit(solution)/shard_map/query/pallas_call | solution.py:479
  31.6 0.0 collective-permute-done.3.refs_10_
  31.7 3.5 %pair.2 = (bf16[128,2048]{1,0:T(8,128)(2,1)}, bf16[3,128,2048]{2,1,0:T(8,128)(2,1)}, f32[3,8,2048]{2,1,0:T(8,128)S(1)}, bf16[3,8,2048]{2,1,0:T(8,128)(2,1)S(1)}, bf16[8,32,256]{2,1,0:T(8,128)(2,1)}) custom-call(bf16[1,128]{1,0:T(2,128)(2,1)S(1)} %get-tuple-element.81.ids_ref._.refs_0_,, ...), custom_call_target="tpu_custom_call", output_to_operand_aliasing={{0}: (11, {}), {1}: (12, {}), {2}: (13, {}), {3}: (14, {}),... | custom-call | flops 4000000000 | bytes 4000000 | tf_op jit(solution)/shard_map/pair/pallas_call | solution.py:479
  35.2 1.2 %collective-permute-done.2.refs_10_ = bf16[128,1024]{1,0:T(8,128)(2,1)S(1)} collective-permute-done((bf16[128,1024]{1,0:T(8,128)(2,1)S(1)}, bf16[128,1024]{1,0:T(8,128)(2,1)S(1)}, u32[]{:S(2)}, u32[]{:S(2)}) %collective-permute-start.2) | collective-permute-done | bytes 262176 | tf_op jit(solution)/shard_map/ppermute | solution.py:27
  36.3 5.2 %query.3 = (bf16[128,2048]{1,0:T(8,128)(2,1)}, bf16[3,128,2048]{2,1,0:T(8,128)(2,1)}, f32[3,8,2048]{2,1,0:T(8,128)S(1)}, bf16[3,8,2048]{2,1,0:T(8,128)(2,1)S(1)}, bf16[8,32,256]{2,1,0:T(8,128)(2,1)}) custom-call(bf16[1,128]{1,0:T(2,128)(2,1)S(1)} %get-tuple-element.81.ids_ref._.refs_0_, ...), custom_call_target="tpu_custom_call", output_to_operand_aliasing={{0}: (11, {}), {1}: (12, {}), {2}: (13, {}), {3}: (14, {}),... | custom-call | flops 4000000000 | bytes 4000000 | tf_op jit(solution)/shard_map/query/pallas_call | solution.py:479
  41.5 0.0 collective-permute-done.1.refs_10_
  41.5 3.5 %pair.3 = (bf16[128,2048]{1,0:T(8,128)(2,1)}, bf16[3,128,2048]{2,1,0:T(8,128)(2,1)}, f32[3,8,2048]{2,1,0:T(8,128)S(1)}, bf16[3,8,2048]{2,1,0:T(8,128)(2,1)S(1)}, bf16[8,32,256]{2,1,0:T(8,128)(2,1)}) custom-call(bf16[1,128]{1,0:T(2,128)(2,1)S(1)} %get-tuple-element.81.ids_ref._.refs_0_,, ...), custom_call_target="tpu_custom_call", output_to_operand_aliasing={{0}: (11, {}), {1}: (12, {}), {2}: (13, {}), {3}: (14, {}),... | custom-call | flops 4000000000 | bytes 4000000 | tf_op jit(solution)/shard_map/pair/pallas_call | solution.py:479
  45.0 5.8 %all-to-all-start = ((bf16[8,32,256]{2,1,0:T(8,128)(2,1)}), bf16[8,32,256]{2,1,0:T(8,128)(2,1)S(1)}, u32[]{:S(2)}, u32[]{:S(2)}) async-start(bf16[8,32,256]{2,1,0:T(8,128)(2,1)} %get-tuple-element.77), calls=%async_computation | async-start | bytes 262144 | tf_op jit(solution)/shard_map/all_to_all | solution.py:495
  50.8 1.3 %collective-permute-start.5 = (bf16[3,8,2048]{2,1,0:T(8,128)(2,1)S(1)}, bf16[3,8,2048]{2,1,0:T(8,128)(2,1)S(1)}, u32[]{:S(2)}, u32[]{:S(2)}) collective-permute-start(bf16[3,8,2048]{2,1,0:T(8,128)(2,1)S(1)} %get-tuple-element.75), channel_id=1, source_target_pairs={{4,0},{8,4},{12,8},{16,12},{20,16},{24,20},{28,24},{5,1},{9,5},{13... | collective-permute-start | bytes 294920 | tf_op jit(solution)/shard_map/ppermute | solution.py:27
  52.1 6.1 %all-to-all-done._.got_ref = bf16[8,32,256]{2,1,0:T(8,128)(2,1)S(1)} async-done(((bf16[8,32,256]{2,1,0:T(8,128)(2,1)}), bf16[8,32,256]{2,1,0:T(8,128)(2,1)S(1)}, u32[]{:S(2)}, u32[]{:S(2)}) %all-to-all-start) | async-done | bytes 131104 | tf_op jit(solution)/shard_map/all_to_all | solution.py:495
  58.2 0.6 %total.1 = (f32[16,128]{1,0:T(8,128)}, f32[3,7,256]{2,1,0:T(8,128)}) custom-call(bf16[8,32,256]{2,1,0:T(8,128)(2,1)S(1)} %all-to-all-done._.got_ref), custom_call_target="tpu_custom_call" | custom-call | flops 1000000 | bytes 200000 | tf_op jit(solution)/shard_map/total/pallas_call | solution.py:496
  58.8 0.0 collective-permute-done.5.part_ref
  58.8 0.7 %last_rows.1 = bf16[3,128,2048]{2,1,0:T(8,128)(2,1)} custom-call(f32[3,8,2048]{2,1,0:T(8,128)S(1)} %get-tuple-element.74.tail_ref, bf16[3,8,2048]{2,1,0:T(8,128)(2,1)S(1)} %collective-permute-done.5.part_ref, bf16[3,128,2048]{2,1,0:T(8,128)(2,1)} %get-tuple-element.76.qg_in, ...), custom_call_target="tpu_custom_call", output_to_operand_aliasing={{}: (2, {})} | custom-call | flops 100000 | bytes 200000 | tf_op jit(solution)/shard_map/last_rows/pallas_call | solution.py:519
Async XLA Ops:
  2.3 8.1 %collective-permute-start = (bf16[3,8,2048]{2,1,0:T(8,128)(2,1)S(1)}, bf16[3,8,2048]{2,1,0:T(8,128)(2,1)S(1)}, u32[]{:S(2)}, u32[]{:S(2)}) collective-permute-start(bf16[3,8,2048]{2,1,0:T(8,128)(2,1)S(1)} %scatter.4), channel_id=1, source_target_pairs={{0,4},{4,8},{8,12},{12,16},{16,20},{20,24},{24,28},{1,5},{5,9},{9,... | collective-permute-start | bytes 294920 | tf_op jit(solution)/shard_map/ppermute | solution.py:27
  7.2 0.9 %copy-start.1 = (f32[3,2048,7]{1,2,0:T(8,128)S(1)}, f32[3,2048,7]{1,2,0:T(8,128)}, u32[]{:S(2)}) copy-start(f32[3,2048,7]{1,2,0:T(8,128)} %param.10) | copy-start | bytes 516100
  7.2 1.5 %copy-start.2 = (bf16[3,128,2048]{2,1,0:T(8,128)(2,1)S(1)}, bf16[3,128,2048]{2,1,0:T(8,128)(2,1)}, u32[]{:S(2)}) copy-start(bf16[3,128,2048]{2,1,0:T(8,128)(2,1)} %refs_3_.7) | copy-start | bytes 4718596
  8.7 1.7 %copy-start = (bf16[128,2048]{1,0:T(8,128)(2,1)S(1)}, bf16[128,2048]{1,0:T(8,128)(2,1)}, u32[]{:S(2)}) copy-start(bf16[128,2048]{1,0:T(8,128)(2,1)} %refs_4_.7) | copy-start | bytes 1572868
  10.7 15.5 %collective-permute-start.4 = (bf16[128,1024]{1,0:T(8,128)(2,1)S(1)}, bf16[128,1024]{1,0:T(8,128)(2,1)S(1)}, u32[]{:S(2)}, u32[]{:S(2)}) collective-permute-start(bf16[128,1024]{1,0:T(8,128)(2,1)S(1)} %get-tuple-element.50._), channel_id=1, source_target_pairs={{0,4},{4,8},{8,12},{12,16},{16,20},{20,24},{24,28},{1,5},{5,9},{9,... | collective-permute-start | bytes 786440 | tf_op jit(solution)/shard_map/ppermute | solution.py:27
  14.4 17.2 %collective-permute-start.3 = (bf16[128,1024]{1,0:T(8,128)(2,1)S(1)}, bf16[128,1024]{1,0:T(8,128)(2,1)S(1)}, u32[]{:S(2)}, u32[]{:S(2)}) collective-permute-start(bf16[128,1024]{1,0:T(8,128)(2,1)S(1)} %get-tuple-element.51._), channel_id=1, source_target_pairs={{4,0},{8,4},{12,8},{16,12},{20,16},{24,20},{28,24},{5,1},{9,5},{13... | collective-permute-start | bytes 786440 | tf_op jit(solution)/shard_map/ppermute | solution.py:27
  17.8 8.5 %copy-start.3 = (f32[128,128]{1,0:T(8,128)S(1)}, f32[128,128]{1,0:T(8,128)}, u32[]{:S(2)}) copy-start(f32[128,128]{1,0:T(8,128)} %refs_6_.7) | copy-start | bytes 196612
  17.8 18.5 %collective-permute-start.2 = (bf16[128,1024]{1,0:T(8,128)(2,1)S(1)}, bf16[128,1024]{1,0:T(8,128)(2,1)S(1)}, u32[]{:S(2)}, u32[]{:S(2)}) collective-permute-start(bf16[128,1024]{1,0:T(8,128)(2,1)S(1)} %get-tuple-element.52._), channel_id=1, source_target_pairs={{0,4},{4,8},{8,12},{12,16},{16,20},{20,24},{24,28},{1,5},{5,9},{9,... | collective-permute-start | bytes 786440 | tf_op jit(solution)/shard_map/ppermute | solution.py:27
  22.9 18.6 %collective-permute-start.1 = (bf16[128,1024]{1,0:T(8,128)(2,1)S(1)}, bf16[128,1024]{1,0:T(8,128)(2,1)S(1)}, u32[]{:S(2)}, u32[]{:S(2)}) collective-permute-start(bf16[128,1024]{1,0:T(8,128)(2,1)S(1)} %get-tuple-element.55), channel_id=1, source_target_pairs={{4,0},{8,4},{12,8},{16,12},{20,16},{24,20},{28,24},{5,1},{9,5},{13... | collective-permute-start | bytes 786440 | tf_op jit(solution)/shard_map/ppermute | solution.py:27
  45.0 13.1 %all-to-all-start = ((bf16[8,32,256]{2,1,0:T(8,128)(2,1)}), bf16[8,32,256]{2,1,0:T(8,128)(2,1)S(1)}, u32[]{:S(2)}, u32[]{:S(2)}) async-start(bf16[8,32,256]{2,1,0:T(8,128)(2,1)} %get-tuple-element.77), calls=%async_computation | async-start | bytes 262144 | tf_op jit(solution)/shard_map/all_to_all | solution.py:495
  50.8 8.0 %collective-permute-start.5 = (bf16[3,8,2048]{2,1,0:T(8,128)(2,1)S(1)}, bf16[3,8,2048]{2,1,0:T(8,128)(2,1)S(1)}, u32[]{:S(2)}, u32[]{:S(2)}) collective-permute-start(bf16[3,8,2048]{2,1,0:T(8,128)(2,1)S(1)} %get-tuple-element.75), channel_id=1, source_target_pairs={{4,0},{8,4},{12,8},{16,12},{20,16},{24,20},{28,24},{5,1},{9,5},{13... | collective-permute-start | bytes 294920 | tf_op jit(solution)/shard_map/ppermute | solution.py:27
